TPU v7x, 32 devices: a whole 2x2x4 slice. The times are simulated.
32 devices in a mesh: rad: 2 (over core), azi: 16 (over z, y, x).
Axes of the slice: x: 2, y: 2, z: 4, core: 2. Of those that a mesh axis runs over, the one named last changes fastest.
Arguments:
- density: float32 [4, 64, 16384], P(None, 'rad', 'azi'), may hold values from -6 to 6
- radial_velocity: float32 [4, 64, 16384], P(None, 'rad', 'azi'), may hold values from -6 to 6
- azimuthal_velocity: float32 [4, 64, 16384], P(None, 'rad', 'azi'), may hold values from -6 to 6
- cycle_shift: int32 [64], P('rad'), may hold values from 0 to 16383
- remainder: float32 [64], P('rad'), may hold values from 0 to 1
- kernel: bfloat16 [2048, 64, 64], P(('rad', 'azi')), may hold values from -0.75 to 0.75
Outputs:
- density_next: float32 [4, 64, 16384], P(None, 'rad', 'azi')
- radial_next: float32 [4, 64, 16384], P(None, 'rad', 'azi')
- azimuthal_next: float32 [4, 64, 16384], P(None, 'rad', 'azi')
- potential: float32 [64, 16384], P(('rad', 'azi'))
All inputs are finite; a program needn't handle non-finite values.
Results may differ from a plain program's by a relative error of at most 0.0003.
The roundings to bfloat16 on the way count: a program that leaves them out, or rounds other values in their place, can miss the bound.
Values may be sent and summed in bfloat16 or wider, within the bound.
No kernel may reach another device: no remote copies, remote signals or barrier semaphores. Data moves between devices by JAX's collectives and lax.ppermute only.
A program may use at most 256 MiB of HBM per device.

v0:
```python
import math

import jax
import jax.numpy as jnp
from jax import lax
from jax.sharding import PartitionSpec as P

NPHI = 16384
MODES = 2048
SPLIT = 128


RADIAL_COURANT = 0.3
VISCOSITY = 0.08
HIGHEST_PRECISION = lax.Precision.HIGHEST


def padded_2(cells, sides, width):
    for axis, dim in sides:
        count = lax.axis_size(axis)
        head = lax.slice_in_dim(cells, 0, width, axis=dim)
        tail = lax.slice_in_dim(cells, cells.shape[dim] - width, cells.shape[dim], axis=dim)
        cells = jnp.concatenate(
            [
                lax.ppermute(tail, axis, [(i, (i + 1) % count) for i in range(count)]),
                cells,
                lax.ppermute(head, axis, [((i + 1) % count, i) for i in range(count)]),
            ],
            axis=dim,
        )
    return cells


def from_behind(block, axis, distance):
    devices = range(lax.axis_size(axis))
    route = [((i - distance) % len(devices), i) for i in devices]
    return lax.ppermute(block, axis, route)


def cycle_coeffs(first_row, row_count, cycle_total):
    cycle_index = first_row + lax.broadcasted_iota(jnp.int32, (row_count, 1), 0)
    radius = 1.0 + 4.0 * (cycle_index.astype(jnp.float32) + 0.5) / cycle_total
    return (0.3 / radius, 0.2 * radius ** (-1.5), 0.05 * radius ** (-1.5))


def rates(padded, coeffs):
    courant, coriolis, epicycle = coeffs
    extended = jnp.concatenate([padded[:, :1], padded, padded[:, -1:]], axis=1)
    center = extended[:, 1:-1, 1:-1, 1:-1]
    rad_diff = 0.5 * (extended[:, 1:-1, 2:, 1:-1] - extended[:, 1:-1, :-2, 1:-1])
    azi_diff = 0.5 * (extended[:, 1:-1, 1:-1, 2:] - extended[:, 1:-1, 1:-1, :-2])
    spread = (
        extended[:, 2:, 1:-1, 1:-1]
        + extended[:, :-2, 1:-1, 1:-1]
        + extended[:, 1:-1, 2:, 1:-1]
        + extended[:, 1:-1, :-2, 1:-1]
        + extended[:, 1:-1, 1:-1, 2:]
        + extended[:, 1:-1, 1:-1, :-2]
        - 6.0 * center
    )
    change_rho = -(RADIAL_COURANT * rad_diff[1] + courant * azi_diff[2]) + VISCOSITY * spread[0]
    change_radial = coriolis * center[2] - RADIAL_COURANT * rad_diff[0] + VISCOSITY * spread[1]
    change_azimuthal = -epicycle * center[1] - courant * azi_diff[0] + VISCOSITY * spread[2]
    return (jnp.stack([change_rho, change_radial, change_azimuthal]), center)


def clamp_edges(padded, width):
    row_count = padded.shape[2]
    row_id = lax.broadcasted_iota(jnp.int32, (1, 1, row_count, 1), 2)
    at_inner = (lax.axis_index("rad") == 0) & (row_id < width)
    at_outer = (lax.axis_index("rad") == lax.axis_size("rad") - 1) & (row_id >= row_count - width)
    padded = jnp.where(at_inner, padded[:, :, width : width + 1], padded)
    return jnp.where(at_outer, padded[:, :, row_count - width - 1 : row_count - width], padded)


def cubic_weights(remainder):
    moved = -remainder[:, None]
    w_next = moved * (moved + 1.0) * (moved + 2.0) / 6.0
    w_here = -(moved - 1.0) * (moved + 1.0) * (moved + 2.0) / 2.0
    w_prev = (moved - 1.0) * moved * (moved + 2.0) / 2.0
    w_prev_two = -(moved - 1.0) * moved * (moved + 1.0) / 6.0
    return (w_next, w_here, w_prev, w_prev_two)


def rotate_cycles(joined, offsets, length):
    return jax.vmap(
        lambda one_cycle, offset: lax.dynamic_slice_in_dim(one_cycle, offset, length, 2),
        in_axes=(2, 0),
        out_axes=2,
    )(joined, offsets)


def inner_tables(outer):
    left = lax.broadcasted_iota(jnp.int32, (outer, outer), 0)
    right = lax.broadcasted_iota(jnp.int32, (outer, outer), 1)
    angle = 2.0 * math.pi / outer * (left * right % outer).astype(jnp.float32)
    return (jnp.cos(angle), jnp.sin(angle))


def twiddle_tables(outer):
    blocks = MODES // outer
    upper = lax.broadcasted_iota(jnp.int32, (blocks, outer, SPLIT), 0)
    lower = lax.broadcasted_iota(jnp.int32, (blocks, outer, SPLIT), 1)
    sample = lax.broadcasted_iota(jnp.int32, (blocks, outer, SPLIT), 2)
    angle = 2.0 * math.pi / NPHI * ((lower + outer * upper) * sample % NPHI).astype(jnp.float32)
    return (jnp.cos(angle), jnp.sin(angle))


def forward_modes(surface):
    cycle_count = surface.shape[0]
    outer = NPHI // SPLIT
    grid = surface.reshape(cycle_count, outer, SPLIT)
    small_cos, small_sin = inner_tables(outer)
    part_real = jnp.einsum("bqn,qk->bnk", grid, small_cos, precision=HIGHEST_PRECISION)
    part_imag = -jnp.einsum("bqn,qk->bnk", grid, small_sin, precision=HIGHEST_PRECISION)
    turn_cos, turn_sin = twiddle_tables(outer)
    real_part = jnp.einsum(
        "bnk,jkn->jkb", part_real, turn_cos, precision=HIGHEST_PRECISION
    ) + jnp.einsum("bnk,jkn->jkb", part_imag, turn_sin, precision=HIGHEST_PRECISION)
    imag_part = jnp.einsum(
        "bnk,jkn->jkb", part_imag, turn_cos, precision=HIGHEST_PRECISION
    ) - jnp.einsum("bnk,jkn->jkb", part_real, turn_sin, precision=HIGHEST_PRECISION)
    return jnp.stack(
        [real_part.reshape(MODES, cycle_count), imag_part.reshape(MODES, cycle_count)], axis=1
    )


def inverse_modes(mode_values):
    cycle_count = mode_values.shape[2]
    outer = NPHI // SPLIT
    mode_id = lax.broadcasted_iota(jnp.int32, (MODES, 1), 0)
    factor = jnp.where(mode_id == 0, 1.0, 2.0) / NPHI
    scaled_real = (mode_values[:, 0, :] * factor).reshape(MODES // outer, outer, cycle_count)
    scaled_imag = (mode_values[:, 1, :] * factor).reshape(MODES // outer, outer, cycle_count)
    turn_cos, turn_sin = twiddle_tables(outer)
    mid_real = jnp.einsum(
        "jkb,jkn->bnk", scaled_real, turn_cos, precision=HIGHEST_PRECISION
    ) - jnp.einsum("jkb,jkn->bnk", scaled_imag, turn_sin, precision=HIGHEST_PRECISION)
    mid_imag = jnp.einsum(
        "jkb,jkn->bnk", scaled_real, turn_sin, precision=HIGHEST_PRECISION
    ) + jnp.einsum("jkb,jkn->bnk", scaled_imag, turn_cos, precision=HIGHEST_PRECISION)
    small_cos, small_sin = inner_tables(outer)
    values = jnp.einsum(
        "bnk,qk->bqn", mid_real, small_cos, precision=HIGHEST_PRECISION
    ) - jnp.einsum("bnk,qk->bqn", mid_imag, small_sin, precision=HIGHEST_PRECISION)
    return values.reshape(cycle_count, NPHI)


def body(density, radial_velocity, azimuthal_velocity, cycle_shift, remainder, kernel):
    fields = jnp.stack([density, radial_velocity, azimuthal_velocity])
    slab = fields.shape[2]
    seg_len = fields.shape[3]
    cycle_total = slab * lax.axis_size("rad")
    first_row = lax.axis_index("rad") * slab
    coeffs = cycle_coeffs(first_row, slab, cycle_total)
    padded = padded_2(fields, (("rad", 2), ("azi", 3)), 2)
    padded = clamp_edges(padded, 2)
    change, center = rates(padded, cycle_coeffs(first_row - 1, slab + 2, cycle_total))
    section_one = clamp_edges(center + change, 1)
    change_two = rates(section_one, coeffs)[0]
    hydro = 0.5 * fields + 0.5 * (section_one[:, :, 1:-1, 1:-1] + change_two)
    per_device = slab // lax.axis_size("azi")
    whole_segments = cycle_shift // seg_len
    within = cycle_shift % seg_len
    turned = hydro
    for bit_number in range((lax.axis_size("azi") - 1).bit_length()):
        arrived = from_behind(turned, "azi", 1 << bit_number)
        chosen = whole_segments // (1 << bit_number) % 2 == 1
        turned = jnp.where(chosen[None, None, :, None], arrived, turned)
    previous = from_behind(turned, "azi", 1)
    rotated = rotate_cycles(jnp.concatenate([previous, turned], axis=3), seg_len - within, seg_len)
    margin = padded_2(rotated, (("azi", 3),), 2)
    w_next, w_here, w_prev, w_prev_two = cubic_weights(remainder)
    moved = (
        w_next * margin[:, :, :, 3 : seg_len + 3]
        + w_here * margin[:, :, :, 2 : seg_len + 2]
        + w_prev * margin[:, :, :, 1 : seg_len + 1]
        + w_prev_two * margin[:, :, :, 0:seg_len]
    )
    block_surface = jnp.sum(moved[0], axis=0)
    surface = lax.all_to_all(block_surface, "azi", split_axis=0, concat_axis=1, tiled=True)
    spectrum = forward_modes(surface).astype(jnp.bfloat16)
    outgoing = spectrum.reshape(MODES, 2, 1, 1, per_device)
    arrived_modes = lax.all_to_all(
        lax.all_to_all(outgoing, "rad", split_axis=0, concat_axis=2, tiled=True),
        "azi",
        split_axis=0,
        concat_axis=3,
        tiled=True,
    )
    local_modes = arrived_modes.shape[0]
    columns = arrived_modes.reshape(local_modes, 2, cycle_total)
    mode_potential = jnp.einsum("mrs,mcs->mcr", kernel, columns, preferred_element_type=jnp.float32)
    returning = mode_potential.reshape(
        1, 1, local_modes, 2, lax.axis_size("rad"), lax.axis_size("azi"), per_device
    )
    back = lax.all_to_all(
        lax.all_to_all(returning, "rad", split_axis=4, concat_axis=0, tiled=True),
        "azi",
        split_axis=5,
        concat_axis=1,
        tiled=True,
    )
    potential = inverse_modes(back.reshape(MODES, 2, per_device))
    return (moved[0], moved[1], moved[2], potential)


def solution(mesh):
    in_specs = (
        P(None, "rad", "azi"),
        P(None, "rad", "azi"),
        P(None, "rad", "azi"),
        P("rad"),
        P("rad"),
        P(("rad", "azi"), None, None),
    )
    out_specs = (
        P(None, "rad", "azi"),
        P(None, "rad", "azi"),
        P(None, "rad", "azi"),
        P(("rad", "azi"), None),
    )
    return jax.shard_map(body, mesh=mesh, in_specs=in_specs, out_specs=out_specs, check_vma=False)
```

profile of v0, /device:TPU:0, one launch (start us, length us, event | category | flops | bytes accessed | tf_op | source)
XLA Modules:
  0.0 561.3 jit_solution(15048122779493492218)
XLA Ops:
  7.2 2.7 collective-permute-start.2
  9.9 4.3 collective-permute-start.3
  14.2 5.8 %collective-permute-done.2 = f32[3,4,36,2]{3,1,0,2:T(4,128)S(1)} collective-permute-done((f32[3,4,36,2]{3,1,0,2:T(4,128)S(1)}, f32[3,4,36,2]{3,1,0,2:T(4,128)S(1)}, u32[]{:S(2)}, u32[]{:S(2)}) %collective-permute-start.2) | collective-permute-done | bytes 3488 | tf_op jit(solution)/shard_map/ppermute | solution.py:25
  21.8 4.7 concatenate.44
  28.6 8.8 %subtract_multiply_fusion.1 = (f32[3,4,34,1026]{3,1,0,2:T(4,128)S(1)}, f32[3,4,34,1026]{3,1,0,2:T(4,128)S(1)}, f32[3,4,34,1026]{3,1,0,2:T(4,128)S(1)}) fusion(f32[3,4,36,1028]{3,1,0,2:T(4,128)S(1)} %broadcast_select_fusion, f32[3,1,36,1028]{3,1,0,2:T(1,128)S(1)} %get-tuple-element.34, f32[3,1,36,1028]{3,1,0,2:T(1,128)S(1)} %get-tuple-element.33), kind=kLoop, calls=%fused_computation.13 | loop fusion | flops 5441904 | bytes 17409600 | tf_op jit(solution)/shard_map/mul | solution.py:50
  43.0 7.3 %subtract_multiply_fusion.3 = (f32[3,4,32,1024]{3,1,0,2:T(4,128)S(1)}, f32[3,4,32,1024]{3,1,0,2:T(4,128)S(1)}, f32[3,4,32,1024]{3,1,0,2:T(4,128)S(1)}) fusion(f32[3,4,34,1026]{3,1,0,2:T(4,128)S(1)} %broadcast_select_fusion.2, f32[3,1,34,1026]{3,1,0,2:T(1,128)S(1)} %get-tuple-element.39, f32[3,1,34,1026]{3,1,0,2:T(1,128)S(1)} %get-tuple-element.38), kind=kLoop, calls=%fused_computation.42 | loop fusion | flops 5111808 | bytes 15403008 | tf_op jit(solution)/shard_map/mul | solution.py:50
  54.4 37.9 %collective-permute-done.4 = f32[3,4,32,1024]{3,1,0,2:T(4,128)S(1)} collective-permute-done((f32[3,4,32,1024]{3,1,0,2:T(4,128)S(1)}, f32[3,4,32,1024]{3,1,0,2:T(4,128)S(1)}, u32[]{:S(2)}, u32[]{:S(2)}) %collective-permute-start.4) | collective-permute-done | bytes 1572896 | tf_op jit(solution)/shard_map/ppermute | solution.py:37
  93.8 37.6 %collective-permute-done.5 = f32[3,4,32,1024]{3,1,0,2:T(4,128)S(1)} collective-permute-done((f32[3,4,32,1024]{3,1,0,2:T(4,128)S(1)}, f32[3,4,32,1024]{3,1,0,2:T(4,128)S(1)}, u32[]{:S(2)}, u32[]{:S(2)}) %collective-permute-start.5) | collective-permute-done | bytes 1572896 | tf_op jit(solution)/shard_map/ppermute | solution.py:37
  132.2 36.5 %collective-permute-done.6 = f32[3,4,32,1024]{3,1,0,2:T(4,128)S(1)} collective-permute-done((f32[3,4,32,1024]{3,1,0,2:T(4,128)S(1)}, f32[3,4,32,1024]{3,1,0,2:T(4,128)S(1)}, u32[]{:S(2)}, u32[]{:S(2)}) %collective-permute-start.6) | collective-permute-done | bytes 1572896 | tf_op jit(solution)/shard_map/ppermute | solution.py:37
  169.5 66.0 %collective-permute-done.7 = f32[3,4,32,1024]{3,1,0,2:T(4,128)S(1)} collective-permute-done((f32[3,4,32,1024]{3,1,0,2:T(4,128)S(1)}, f32[3,4,32,1024]{3,1,0,2:T(4,128)S(1)}, u32[]{:S(2)}, u32[]{:S(2)}) %collective-permute-start.7) | collective-permute-done | bytes 1572896 | tf_op jit(solution)/shard_map/ppermute | solution.py:37
  236.3 40.0 %collective-permute-done.8 = f32[3,4,32,1024]{3,1,0,2:T(4,128)} collective-permute-done((f32[3,4,32,1024]{3,1,0,2:T(4,128)S(1)}, f32[3,4,32,1024]{3,1,0,2:T(4,128)}, u32[]{:S(2)}, u32[]{:S(2)}) %collective-permute-start.8) | collective-permute-done | bytes 1572896 | tf_op jit(solution)/shard_map/ppermute | solution.py:37
  276.3 4.2 maximum_bitcast_fusion
  280.5 152.3 %while.1 = (s32[]{:T(128)}, f32[32,3,4,2048]{3,2,1,0:T(4,128)}, s32[32,4]{0,1:T(4,128)S(1)}, f32[32,3,4,1024]{3,0,2,1:T(8,128)}, s32[]{:T(128)}, /*index=5*/s32[]{:T(128)}) while((s32[]{:T(128)}, f32[32,3,4,2048]{3,2,1,0:T(4,128)}, s32[32,4]{0,1:T(4,128)S(1)}, f32[32,3,4,1024]{3,0,2,1:T(8,128)}, s32[]{:T(128)}, /*index=5*/s32[]{:T(128)}) %tuple.49), condition=%wide.while_cond, body=%wide.while_body.sunk | while | flops 2 | bytes 295045 | solution.py:87
  281.0 2.2 constant_dynamic-slice_fusion.5
  290.6 2.2 constant_dynamic-slice_fusion.5
  295.3 2.2 constant_dynamic-slice_fusion.5
  300.1 2.2 constant_dynamic-slice_fusion.5
  304.8 2.2 constant_dynamic-slice_fusion.5
  309.6 2.2 constant_dynamic-slice_fusion.5
  314.4 2.2 constant_dynamic-slice_fusion.5
  319.1 2.2 constant_dynamic-slice_fusion.5
  323.9 2.2 constant_dynamic-slice_fusion.5
  328.7 2.2 constant_dynamic-slice_fusion.5
  333.4 2.2 constant_dynamic-slice_fusion.5
  338.2 2.2 constant_dynamic-slice_fusion.5
  342.9 2.2 constant_dynamic-slice_fusion.5
  347.7 2.2 constant_dynamic-slice_fusion.5
  352.5 2.2 constant_dynamic-slice_fusion.5
  357.2 2.2 constant_dynamic-slice_fusion.5
  362.0 2.2 constant_dynamic-slice_fusion.5
  366.7 2.2 constant_dynamic-slice_fusion.5
  371.5 2.2 constant_dynamic-slice_fusion.5
  376.3 2.2 constant_dynamic-slice_fusion.5
  381.0 2.2 constant_dynamic-slice_fusion.5
  385.8 2.2 constant_dynamic-slice_fusion.5
  390.5 2.2 constant_dynamic-slice_fusion.5
  395.3 2.2 constant_dynamic-slice_fusion.5
  400.1 2.2 constant_dynamic-slice_fusion.5
  404.8 2.2 constant_dynamic-slice_fusion.5
  409.6 2.2 constant_dynamic-slice_fusion.5
  414.3 2.2 constant_dynamic-slice_fusion.5
  419.1 2.2 constant_dynamic-slice_fusion.5
  423.9 2.2 constant_dynamic-slice_fusion.5
  428.6 2.2 constant_dynamic-slice_fusion.5
  434.0 5.6 collective-permute-start.9
  439.6 3.9 collective-permute-done.10
  443.6 4.7 fusion.9
  450.2 7.2 %all-to-all-start = ((f32[16,2,1024]{2,1,0:T(2,128)}), f32[16,2,1024]{2,1,0:T(2,128)S(1)}, u32[]{:S(2)}, u32[]{:S(2)}) async-start(f32[16,2,1024]{2,1,0:T(2,128)} %all_to_all.60), calls=%async_computation | async-start | bytes 262144 | tf_op jit(solution)/shard_map/all_to_all | solution.py:181
  457.4 7.8 %all-to-all-done = f32[16,2,1024]{2,1,0:T(2,128)S(1)} async-done(((f32[16,2,1024]{2,1,0:T(2,128)}), f32[16,2,1024]{2,1,0:T(2,128)S(1)}, u32[]{:S(2)}, u32[]{:S(2)}) %all-to-all-start) | async-done | bytes 131104 | tf_op jit(solution)/shard_map/all_to_all | solution.py:181
  466.6 6.3 %fusion.52 = f32[128,16,2]{1,2,0:T(2,128)S(1)} fusion(f32[2,128,128]{1,0,2:T(2,128)S(1)} %copy.90, s32[16]{0:T(128)S(1)} %iota_multiply_fusion), kind=kOutput, calls=%fused_computation.108 | convolution fusion | flops 10223616 | bytes 147520 | tf_op jit(solution)/shard_map/bnk,jkn->jkb/dot_general | solution.py:117
  472.9 6.3 %fusion.50 = f32[128,16,2]{1,2,0:T(2,128)S(1)} fusion(f32[2,128,128]{1,0,2:T(2,128)S(1)} %copy.92, s32[16]{0:T(128)S(1)} %iota_multiply_fusion), kind=kOutput, calls=%fused_computation.107 | convolution fusion | flops 10223616 | bytes 147520 | tf_op jit(solution)/shard_map/bnk,jkn->jkb/dot_general | solution.py:120
  479.1 6.3 %fusion.27 = bf16[16,128,2]{0,2,1:T(2,128)(2,1)S(1)} fusion(f32[128,16,2]{1,2,0:T(2,128)S(1)} %fusion.52, f32[2,128,128]{1,0,2:T(2,128)S(1)} %copy.92, s32[16]{0:T(128)S(1)} %iota_multiply_fusion), kind=kOutput, calls=%fused_computation.55 | convolution fusion | flops 10231808 | bytes 155712 | tf_op jit(solution)/shard_map/bnk,jkn->jkb/dot_general | solution.py:119
  485.5 6.3 %fusion.26 = bf16[16,128,2]{0,2,1:T(2,128)(2,1)S(1)} fusion(f32[128,16,2]{1,2,0:T(2,128)S(1)} %fusion.50, f32[2,128,128]{1,0,2:T(2,128)S(1)} %copy.90, s32[16]{0:T(128)S(1)} %iota_multiply_fusion), kind=kOutput, calls=%fused_computation.54 | convolution fusion | flops 10231808 | bytes 155712 | tf_op jit(solution)/shard_map/bnk,jkn->jkb/dot_general | solution.py:122
  494.5 3.7 all_to_all.82
  498.2 2.2 reshape.236
  503.9 9.9 %all_to_all.83 = bf16[16,2,256]{2,1,0:T(2,128)(2,1)S(1)} all-to-all(bf16[16,2,256]{2,1,0:T(2,128)(2,1)S(1)} %reshape.237), channel_id=1, replica_groups=mesh['rad'=2,'azi'=16] {'azi'}, dimensions={0} | all-to-all | bytes 32768 | tf_op jit(solution)/shard_map/all_to_all | solution.py:184
  513.9 2.2 reshape.238
  518.7 3.7 all_to_all.84
  524.5 3.5 all-to-all-start.4
  528.0 7.3 %all-to-all-done.4 = f32[16,1,512]{2,1,0:T(1,128)S(1)} async-done(((f32[16,1,512]{2,1,0:T(1,128)}), f32[16,1,512]{2,1,0:T(1,128)S(1)}, u32[]{:S(2)}, u32[]{:S(2)}) %all-to-all-start.4) | async-done | bytes 32800 | tf_op jit(solution)/shard_map/all_to_all | solution.py:197
  536.4 5.7 %fusion.54 = f32[128,128,2]{1,2,0:T(2,128)S(1)} fusion(s32[16]{0:T(128)S(1)} %iota_multiply_fusion, f32[16,128,2]{0,2,1:T(2,128)S(1)} %copy.107, f32[16,128]{0,1:T(8,128)S(1)} %select_multiply_fusion), kind=kOutput, calls=%fused_computation.109 | convolution fusion | flops 10227712 | bytes 155712 | tf_op jit(solution)/shard_map/jkb,jkn->bnk/dot_general | solution.py:139
  542.1 5.7 %fusion.48 = f32[128,128,2]{1,2,0:T(2,128)S(1)} fusion(s32[16]{0:T(128)S(1)} %iota_multiply_fusion, f32[16,128,2]{0,2,1:T(2,128)S(1)} %copy.107, f32[16,128]{0,1:T(8,128)S(1)} %select_multiply_fusion), kind=kOutput, calls=%fused_computation.106 | convolution fusion | flops 10227712 | bytes 155712 | tf_op jit(solution)/shard_map/jkb,jkn->bnk/dot_general | solution.py:136
  547.9 5.7 %fusion.22 = f32[2,128,128]{1,0,2:T(2,128)S(1)} fusion(f32[128,128,2]{1,2,0:T(2,128)S(1)} %fusion.54, s32[16]{0:T(128)S(1)} %iota_multiply_fusion, f32[16,128,2]{0,2,1:T(2,128)S(1)} %copy.108, f32[16,128]{0,1:T(8,128)S(1)} %select_multiply_fusion), kind=kOutput, calls=%fused_computation.46 | convolution fusion | flops 10260480 | bytes 286784 | tf_op jit(solution)/shard_map/jkb,jkn->bnk/dot_general | solution.py:141
  553.6 5.7 %fusion.23 = f32[2,128,128]{1,0,2:T(2,128)S(1)} fusion(f32[128,128,2]{1,2,0:T(2,128)S(1)} %fusion.48, s32[16]{0:T(128)S(1)} %iota_multiply_fusion, f32[16,128,2]{0,2,1:T(2,128)S(1)} %copy.108, f32[16,128]{0,1:T(8,128)S(1)} %select_multiply_fusion), kind=kOutput, calls=%fused_computation.48 | convolution fusion | flops 10260480 | bytes 286784 | tf_op jit(solution)/shard_map/jkb,jkn->bnk/dot_general | solution.py:138
  (246 shorter events, 125.7 us)
Async XLA Ops:
  0.6 517.2 %copy-start = (bf16[64,64,64]{2,1,0:T(8,128)(2,1)S(1)}, bf16[64,64,64]{2,1,0:T(8,128)(2,1)}, u32[]{:S(2)}) copy-start(bf16[64,64,64]{2,1,0:T(8,128)(2,1)} %param.11) | copy-start | bytes 1572868
  2.1 4.4 copy-start.1
  4.2 2.3 copy-start.3
  4.2 2.3 copy-start.5
  4.7 1.5 collective-permute-start
  5.2 1.3 collective-permute-start.1
  7.0 12.9 %copy-start.7 = (f32[3,4,36,1024]{3,1,0,2:T(4,128)}, f32[3,4,36,1024]{3,1,0,2:T(4,128)S(1)}, u32[]{:S(2)}) copy-start(f32[3,4,36,1024]{3,1,0,2:T(4,128)S(1)} %pad_maximum_fusion.2) | copy-start | bytes 5308420
  7.2 12.7 %collective-permute-start.2 = (f32[3,4,36,2]{3,1,0,2:T(4,128)S(1)}, f32[3,4,36,2]{3,1,0,2:T(4,128)S(1)}, u32[]{:S(2)}, u32[]{:S(2)}) collective-permute-start(f32[3,4,36,2]{3,1,0,2:T(4,128)S(1)} %get-tuple-element.41), channel_id=1, source_target_pairs={{0,1},{1,2},{2,3},{3,4},{4,5},{5,6},{6,7},{7,8},{8,9},{9,10},{10,1... | collective-permute-start | bytes 10376 | tf_op jit(solution)/shard_map/ppermute | solution.py:25
  9.9 11.9 %collective-permute-start.3 = (f32[3,4,36,2]{3,1,0,2:T(4,128)S(1)}, f32[3,4,36,2]{3,1,0,2:T(4,128)S(1)}, u32[]{:S(2)}, u32[]{:S(2)}) collective-permute-start(f32[3,4,36,2]{3,1,0,2:T(4,128)S(1)} %get-tuple-element.40), channel_id=1, source_target_pairs={{1,0},{2,1},{3,2},{4,3},{5,4},{6,5},{7,6},{8,7},{9,8},{10,9},{11,1... | collective-permute-start | bytes 10376 | tf_op jit(solution)/shard_map/ppermute | solution.py:27
  50.3 1.2 copy-start.2
  50.3 1.2 copy-start.4
  50.4 1.3 copy-start.6
  51.7 2.7 copy-start.9
  52.8 39.4 %collective-permute-start.4 = (f32[3,4,32,1024]{3,1,0,2:T(4,128)S(1)}, f32[3,4,32,1024]{3,1,0,2:T(4,128)S(1)}, u32[]{:S(2)}, u32[]{:S(2)}) collective-permute-start(f32[3,4,32,1024]{3,1,0,2:T(4,128)S(1)} %fusion.20), channel_id=1, source_target_pairs={{15,0},{0,1},{1,2},{2,3},{3,4},{4,5},{5,6},{6,7},{7,8},{8,9},{9,10... | collective-permute-start | bytes 4718600 | tf_op jit(solution)/shard_map/ppermute | solution.py:37
  93.7 37.7 %collective-permute-start.5 = (f32[3,4,32,1024]{3,1,0,2:T(4,128)S(1)}, f32[3,4,32,1024]{3,1,0,2:T(4,128)S(1)}, u32[]{:S(2)}, u32[]{:S(2)}) collective-permute-start(f32[3,4,32,1024]{3,1,0,2:T(4,128)S(1)} %broadcast_select_fusion.4), channel_id=1, source_target_pairs={{14,0},{15,1},{0,2},{1,3},{2,4},{3,5},{4,6},{5,7},{6,8},{7,9},{8,1... | collective-permute-start | bytes 4718600 | tf_op jit(solution)/shard_map/ppermute | solution.py:37
  132.1 36.5 %collective-permute-start.6 = (f32[3,4,32,1024]{3,1,0,2:T(4,128)S(1)}, f32[3,4,32,1024]{3,1,0,2:T(4,128)S(1)}, u32[]{:S(2)}, u32[]{:S(2)}) collective-permute-start(f32[3,4,32,1024]{3,1,0,2:T(4,128)S(1)} %broadcast_select_fusion.5), channel_id=1, source_target_pairs={{12,0},{13,1},{14,2},{15,3},{0,4},{1,5},{2,6},{3,7},{4,8},{5,9},{6... | collective-permute-start | bytes 4718600 | tf_op jit(solution)/shard_map/ppermute | solution.py:37
  169.4 66.1 %collective-permute-start.7 = (f32[3,4,32,1024]{3,1,0,2:T(4,128)S(1)}, f32[3,4,32,1024]{3,1,0,2:T(4,128)S(1)}, u32[]{:S(2)}, u32[]{:S(2)}) collective-permute-start(f32[3,4,32,1024]{3,1,0,2:T(4,128)S(1)} %broadcast_select_fusion.6), channel_id=1, source_target_pairs={{8,0},{9,1},{10,2},{11,3},{12,4},{13,5},{14,6},{15,7},{0,8},{1,9},... | collective-permute-start | bytes 4718600 | tf_op jit(solution)/shard_map/ppermute | solution.py:37
  236.2 40.1 %collective-permute-start.8 = (f32[3,4,32,1024]{3,1,0,2:T(4,128)S(1)}, f32[3,4,32,1024]{3,1,0,2:T(4,128)}, u32[]{:S(2)}, u32[]{:S(2)}) collective-permute-start(f32[3,4,32,1024]{3,1,0,2:T(4,128)S(1)} %broadcast_select_fusion.7), channel_id=1, source_target_pairs={{15,0},{0,1},{1,2},{2,3},{3,4},{4,5},{5,6},{6,7},{7,8},{8,9},{9,10... | collective-permute-start | bytes 4718600 | tf_op jit(solution)/shard_map/ppermute | solution.py:37
  280.4 159.2 %copy-start.8 = (f32[32]{0:T(128)S(1)}, f32[32]{0:T(128)}, u32[]{:S(2)}) copy-start(f32[32]{0:T(128)} %param.10) | copy-start | bytes 388
  433.9 9.6 %collective-permute-start.10 = (f32[3,4,32,2]{3,2,1,0:T(8,128)S(1)}, f32[3,4,32,2]{3,2,1,0:T(8,128)S(1)}, u32[]{:S(2)}, u32[]{:S(2)}) collective-permute-start(f32[3,4,32,2]{3,2,1,0:T(8,128)S(1)} %get-tuple-element.47), channel_id=1, source_target_pairs={{0,1},{1,2},{2,3},{3,4},{4,5},{5,6},{6,7},{7,8},{8,9},{9,10},{10,1... | collective-permute-start | bytes 9224 | tf_op jit(solution)/shard_map/ppermute | solution.py:25
  434.0 9.6 %collective-permute-start.9 = (f32[3,4,32,2]{3,2,1,0:T(8,128)S(1)}, f32[3,4,32,2]{3,2,1,0:T(8,128)S(1)}, u32[]{:S(2)}, u32[]{:S(2)}) collective-permute-start(f32[3,4,32,2]{3,2,1,0:T(8,128)S(1)} %get-tuple-element.46), channel_id=1, source_target_pairs={{1,0},{2,1},{3,2},{4,3},{5,4},{6,5},{7,6},{8,7},{9,8},{10,9},{11,1... | collective-permute-start | bytes 9224 | tf_op jit(solution)/shard_map/ppermute | solution.py:27
  450.2 15.0 %all-to-all-start = ((f32[16,2,1024]{2,1,0:T(2,128)}), f32[16,2,1024]{2,1,0:T(2,128)S(1)}, u32[]{:S(2)}, u32[]{:S(2)}) async-start(f32[16,2,1024]{2,1,0:T(2,128)} %all_to_all.60), calls=%async_computation | async-start | bytes 262144 | tf_op jit(solution)/shard_map/all_to_all | solution.py:181
  524.5 10.9 %all-to-all-start.4 = ((f32[16,1,512]{2,1,0:T(1,128)}), f32[16,1,512]{2,1,0:T(1,128)S(1)}, u32[]{:S(2)}, u32[]{:S(2)}) async-start(f32[16,1,512]{2,1,0:T(1,128)} %reshape.241), calls=%async_computation.4 | async-start | bytes 65536 | tf_op jit(solution)/shard_map/all_to_all | solution.py:197
where the time goes:
time: 567 us; the launch traced here: 561 us
  waiting for transfers between devices  246 us (43%)
  local copies, waits for them, and re-layouts  179 us (32%)
  matrix products  50.7 us (9%)
  other arithmetic  40.5 us (7%)
  starting transfers between devices  25.7 us (5%)
  blocking collectives  17.4 us (3%)
    ppermute x5, waiting for transfers between devices, from_behind(): return lax.ppermute(block, axis, route)  218 us
    gather x160, local copies, waits for them, and re-layouts  152 us
    mul x2, other arithmetic, rates(): 0.5 * (extended[:, 1:-1, 2:, 1:-1] - extended[:, 1:-1, :-2, 1:-1])  16.1 us
  transfers between devices with their start and end apart: 13, of which 12 were waited for; matrix products, arithmetic and copies ran while one was open for 0% of the time, Pallas kernels for 0%

commit v1 on v0

v1 whole, which is shorter than its diff:
```python
import functools
import math

import jax
import jax.numpy as jnp
import numpy as np
from jax import lax
from jax.experimental import pallas as pl
from jax.experimental.pallas import tpu as pltpu
from jax.sharding import PartitionSpec as P

RADIAL_COURANT = 0.3
VISCOSITY = 0.08
LANES = 128
SUB = 8
EXACT = lax.Precision.HIGHEST
F32 = jnp.float32
BF16 = jnp.bfloat16

POWER = 12
TOP = 2.0**10.5
GAIN = 1.25


def encode(value, scale):
    scaled = value * scale
    second = scaled * scaled
    fourth = second * second
    size = fourth * fourth * fourth
    return jnp.where(scaled < 0.0, -size, size)


def decode(code, scale):
    size = jnp.abs(code)
    root = jnp.exp2(jnp.log2(jnp.maximum(size, 1e-37)) * (1.0 / POWER)) * scale
    return jnp.where(size < 2e-38, 0.0, jnp.where(code < 0.0, -root, root))


def row_iota(shape):
    return lax.broadcasted_iota(jnp.int32, shape, 0)


def lane_iota(shape):
    return lax.broadcasted_iota(jnp.int32, shape, 1)


def row_layout(per, tiles):
    used = per * tiles + per + 1
    return -(-used // SUB) * SUB


def hydro_kernel(per, rho, ur, up, low, high, bulk, surf, field, stage, block):
    nz, slab, seg = rho.shape
    width = seg + LANES
    first = 2 * SUB
    last_tile = slab // SUB + 2
    tiles = seg // LANES
    rad = lax.axis_index("rad")
    rad_count = lax.axis_size("rad")
    total = slab * rad_count
    for c, ref in enumerate((rho, ur, up)):
        for z in range(nz):
            field[c, z, SUB : slab + 3 * SUB, seg:width] = jnp.zeros((slab + 2 * SUB, LANES), F32)
            field[c, z, first : first + slab, 0:seg] = ref[z]
            inner = jnp.broadcast_to(ref[z, 0:1, :], (2, seg))
            outer = jnp.broadcast_to(ref[z, slab - 1 : slab, :], (2, seg))
            field[c, z, first - 2 : first, 0:seg] = jnp.where(rad == 0, inner, low[c, z])
            field[c, z, first + slab : first + slab + 2, 0:seg] = jnp.where(
                rad == rad_count - 1, outer, high[c, z]
            )
    sub = row_iota((SUB, width))

    def rates_at(ref, tile, z):
        cycle = rad * slab - first + tile * SUB + row_iota((SUB, LANES))
        radius = 1.0 + 4.0 * (cycle.astype(F32) + 0.5) / total
        power = 1.0 / (radius * jnp.sqrt(radius))
        wide = lambda x: jnp.concatenate([x] * (width // LANES), axis=1)
        courant = wide(0.5 * (0.3 / radius))
        coriolis, epicycle = wide(0.2 * power), wide(0.05 * power)
        here = pl.ds(pl.multiple_of(tile * SUB, SUB), SUB)
        before = pl.ds(pl.multiple_of((tile - 1) * SUB, SUB), SUB)
        after = pl.ds(pl.multiple_of((tile + 1) * SUB, SUB), SUB)
        z_up, z_down = min(z + 1, nz - 1), max(z - 1, 0)
        center, rad_diff, azi_diff, spread = [], [], [], []
        for c in range(3):
            cur = ref[c, z, here, :]
            inward = pltpu.roll(jnp.where(sub == SUB - 1, ref[c, z, before, :], cur), 1, 0)
            outward = pltpu.roll(jnp.where(sub == 0, ref[c, z, after, :], cur), SUB - 1, 0)
            ahead = pltpu.roll(cur, width - 1, 1)
            behind = pltpu.roll(cur, 1, 1)
            near = ref[c, z_up, here, :] + ref[c, z_down, here, :] + inward + outward + ahead + behind
            spread.append(VISCOSITY * near - (6.0 * VISCOSITY) * cur)
            rad_diff.append(outward - inward)
            azi_diff.append(ahead - behind)
            center.append(cur)
        half = 0.5 * RADIAL_COURANT
        return center, (
            spread[0] - (half * rad_diff[1] + courant * azi_diff[2]),
            coriolis * center[2] - half * rad_diff[0] + spread[1],
            spread[2] - epicycle * center[1] - courant * azi_diff[0],
        )

    def first_section(tile, carry):
        for z in range(nz):
            center, change = rates_at(field, tile, z)
            for c in range(3):
                stage[c, z, pl.ds(pl.multiple_of(tile * SUB, SUB), SUB), :] = center[c] + change[c]
        return carry

    lax.fori_loop(1, last_tile + 1, first_section, 0)

    @pl.when(rad == 0)
    def _():
        for c in range(3):
            for z in range(nz):
                stage[c, z, first - 1 : first, :] = stage[c, z, first : first + 1, :]

    @pl.when(rad == rad_count - 1)
    def _():
        for c in range(3):
            for z in range(nz):
                stage[c, z, first + slab : first + slab + 1, :] = stage[
                    c, z, first + slab - 1 : first + slab, :
                ]

    def second_section(tile, largest):
        here = pl.ds(pl.multiple_of(tile * SUB, SUB), SUB)
        for z in range(nz):
            center, change = rates_at(stage, tile, z)
            for c in range(3):
                value = 0.5 * field[c, z, here, :] + 0.5 * (center[c] + change[c])
                field[c, z, here, :] = value
                largest = jnp.maximum(largest, jnp.abs(value))
        return largest

    largest = lax.fori_loop(2, last_tile, second_section, jnp.zeros((SUB, width), F32))
    peak = jnp.maximum(jnp.max(largest, keepdims=True), 1e-30)
    scale = TOP / peak
    dests = SUB // per

    def pack(tile, carry):
        here = pl.ds(pl.multiple_of(tile * SUB, SUB), SUB)
        overflow = jnp.zeros((SUB, LANES), F32)
        column = jnp.zeros((SUB, seg), F32)
        for c in range(3):
            for z in range(nz):
                value = field[c, z, here, 0:seg]
                if c == 0:
                    column = column + value
                code = encode(value, scale)
                plane = c * nz + z
                for d in range(dests):
                    block[(tile - 2) * dests + d, plane * per : (plane + 1) * per, :] = code[
                        d * per : (d + 1) * per, :
                    ]
                overflow = overflow + pltpu.roll(field[c, z, here, seg:width], 2 + 4 * plane, 1)
        rows = surf.shape[1]
        for d in range(dests):
            dest = (tile - 2) * dests + d
            for k in range(per):
                row = d * per + k
                for b in range(tiles):
                    surf[dest, k * tiles + b : k * tiles + b + 1, :] = column[
                        row : row + 1, b * LANES : (b + 1) * LANES
                    ]
                at = per * tiles + k
                surf[dest, at : at + 1, :] = overflow[row : row + 1, :]
            spare = per * tiles + per
            surf[dest, spare:rows, :] = jnp.broadcast_to(peak, (rows - spare, LANES))
        return carry

    lax.fori_loop(2, last_tile, pack, 0)

    def narrow(d, carry):
        bulk[d] = block[d].astype(BF16)
        return carry

    lax.fori_loop(0, bulk.shape[0], narrow, 0)


def advect_kernel(per, nz, shift, remainder, bulk, surf, out, ring, tapped, over):
    sources, rows, seg = bulk.shape
    tiles = seg // LANES
    count = sources * tiles
    group = nz * per
    spare = per * tiles + per
    me = lax.axis_index("azi")

    def widen(a, carry):
        unit = surf[a, spare : spare + 1, :] * (1.0 / TOP)
        unit = jnp.concatenate([unit] * tiles, axis=1)
        value = decode(bulk[a].astype(F32), unit)
        for c in range(3):
            for b in range(tiles):
                ring[c, a * tiles + b] = value[
                    c * group : (c + 1) * group, b * LANES : (b + 1) * LANES
                ]
        packed = surf[a, per * tiles : per * tiles + per, :]
        for c in range(3):
            for z in range(nz):
                turned = pltpu.roll(packed, LANES - 2 - 4 * (c * nz + z), 1)
                over[c, a, z * per : (z + 1) * per, :] = turned
        return carry

    lax.fori_loop(0, sources, widen, 0)
    lane = lane_iota((group, LANES))
    cycle = row_iota((group, LANES)) % per

    def spill(a, carry):
        after = lax.rem((a + 1) * tiles, count)
        before = lax.rem(a * tiles + count - 1, count)
        for c in range(3):
            extra = over[c, a]
            ring[c, after] = ring[c, after] + jnp.where(lane < 2, extra, 0.0)
            ring[c, before] = ring[c, before] + jnp.where(lane >= LANES - 2, extra, 0.0)
        return carry

    lax.fori_loop(0, sources, spill, 0)
    x = jnp.zeros((group, LANES), F32)
    whole, part = [], []
    for k in range(per):
        x = jnp.where(cycle == k, -remainder[me * per + k], x)
        amount = shift[me * per + k]
        whole.append(amount // LANES)
        part.append(lax.rem(amount, LANES))
    w_next = x * (x + 1.0) * (x + 2.0) / 6.0
    w_here = -(x - 1.0) * (x + 1.0) * (x + 2.0) / 2.0
    w_prev = (x - 1.0) * x * (x + 2.0) / 2.0
    w_prev_two = -(x - 1.0) * x * (x + 1.0) / 6.0

    def tap(t, carry):
        after = lax.rem(t + 1, count)
        before = lax.rem(t + count - 1, count)
        for c in range(3):
            cur, nxt, prv = ring[c, t], ring[c, after], ring[c, before]
            next_one = pltpu.roll(jnp.where(lane == 0, nxt, cur), LANES - 1, 1)
            prev_one = pltpu.roll(jnp.where(lane == LANES - 1, prv, cur), 1, 1)
            prev_two = pltpu.roll(jnp.where(lane >= LANES - 2, prv, cur), 2, 1)
            tapped[c, t] = w_next * next_one + w_here * cur + w_prev * prev_one + w_prev_two * prev_two
        return carry

    lax.fori_loop(0, count, tap, 0)
    peak = jnp.max(surf[:, spare, :], axis=0, keepdims=True)
    scale = (TOP / GAIN) / peak

    def turned_tile(c, k, t):
        source = lax.rem(t - whole[k] + 2 * count, count)
        return pltpu.roll(tapped[c, source], part[k], 1)

    def turn(dest, carry):
        carry = list(carry)
        pieces = [[None] * tiles for _ in range(3)]
        for b in range(tiles):
            t = dest * tiles + b
            for c in range(3):
                joined = jnp.zeros((group, LANES), F32)
                for k in range(per):
                    now = turned_tile(c, k, t)
                    value = jnp.where(lane < part[k], carry[c * per + k], now)
                    joined = value if per == 1 else jnp.where(cycle == k, value, joined)
                    carry[c * per + k] = now
                pieces[c][b] = encode(joined, scale)
        columns = [jnp.concatenate([pieces[c][b] for b in range(tiles)], axis=1) for c in range(3)]
        out[dest] = jnp.concatenate(columns, axis=0).astype(BF16)
        return tuple(carry)

    start = tuple(turned_tile(c, k, -1) for c in range(3) for k in range(per))
    lax.fori_loop(0, sources, turn, start)


def settle_kernel(per, bulk, surf, rho, ur, up):
    nz = rho.shape[0]
    sources, rows, seg = bulk.shape
    tiles = seg // LANES
    spare = per * tiles + per
    peak = jnp.max(surf[:, spare, :], axis=0, keepdims=True)
    unit = jnp.concatenate([peak * (GAIN / TOP)] * tiles, axis=1)
    for a in range(sources):
        value = decode(bulk[a].astype(F32), unit)
        for c, ref in enumerate((rho, ur, up)):
            for z in range(nz):
                plane = c * nz + z
                ref[z, a * per : (a + 1) * per, :] = value[plane * per : (plane + 1) * per, :]


def forward_kernel(per, nz, modes, shift, remainder, surf, circle, twiddle, short, out, rows_out):
    sources = surf.shape[0]
    nq = circle.shape[0]
    tiles = nq // sources
    length = nq * LANES
    upper = modes // nq
    dests = out.shape[0]
    me = lax.axis_index("azi")
    lane = lane_iota((sources, LANES))
    q_id, a_id = row_iota((nq, sources)), lane_iota((nq, sources))
    to_after = (q_id == lax.rem((a_id + 1) * tiles, nq)).astype(F32)
    to_before = (q_id == lax.rem(a_id * tiles + nq - 1, nq)).astype(F32)
    mode = row_iota((upper, nq)) * nq + lane_iota((upper, nq))
    dot = functools.partial(jnp.dot, precision=EXACT, preferred_element_type=F32)
    for k in range(per):
        packed = surf[:, per * tiles + k, :]
        extra = jnp.zeros((sources, LANES), F32)
        for z in range(nz):
            extra = extra + pltpu.roll(packed, LANES - 2 - 4 * z, 1)
        grid = surf[:, k * tiles : (k + 1) * tiles, :].reshape(nq, LANES)
        grid = grid + dot(to_after, jnp.where(lane < 2, extra, 0.0))
        grid = grid + dot(to_before, jnp.where(lane >= LANES - 2, extra, 0.0))
        inner = dot(grid.T, circle[...])
        cos_part, sin_part = inner[:, :nq], inner[:, nq:]
        turn_cos, turn_sin = twiddle[:, :nq], twiddle[:, nq:]
        real = cos_part * turn_cos - sin_part * turn_sin
        imag = -(sin_part * turn_cos + cos_part * turn_sin)
        outer = dot(short[...], jnp.concatenate([real, imag], axis=1))
        real = outer[:upper, :nq] + outer[upper:, nq:]
        imag = outer[:upper, nq:] - outer[upper:, :nq]
        amount = shift[me * per + k]
        x = jnp.full((upper, nq), -remainder[me * per + k], F32)
        weights = (
            (-1, x * (x + 1.0) * (x + 2.0) / 6.0),
            (0, -(x - 1.0) * (x + 1.0) * (x + 2.0) / 2.0),
            (1, (x - 1.0) * x * (x + 2.0) / 2.0),
            (2, -(x - 1.0) * x * (x + 1.0) / 6.0),
        )
        gain_cos = jnp.zeros((upper, nq), F32)
        gain_sin = jnp.zeros((upper, nq), F32)
        for offset, weight in weights:
            steps = lax.rem(mode * (amount + offset + length), length)
            angle = steps.astype(F32) * (2.0 * math.pi / length)
            gain_cos = gain_cos + weight * jnp.cos(angle)
            gain_sin = gain_sin + weight * jnp.sin(angle)
        rows_out[:, k, :] = real * gain_cos + imag * gain_sin
        rows_out[:, per + k, :] = imag * gain_cos - real * gain_sin
    share = dests // upper
    for d in range(dests):
        out[d] = rows_out[d // share, 0 : 2 * per, :].astype(BF16)


def couple_kernel(per, local, columns, kernel, out, lines):
    sources, parts, nq = columns.shape
    total = sources * per
    me = lax.axis_index("rad") * lax.axis_size("azi") + lax.axis_index("azi")
    offset = lax.rem(me * local, nq)
    row, col = row_iota((total, total)), lane_iota((total, total))
    spread = (row == lax.rem(col, sources) * per + col // sources).astype(F32)
    lines[...] = columns[...].astype(F32)
    lane = lane_iota((total, nq))
    sides = []
    for c in range(2):
        stacked = jnp.concatenate([lines[:, c * per + k, :] for k in range(per)], axis=0)
        ordered = jnp.dot(spread, stacked, preferred_element_type=F32)
        sides.append(pltpu.roll(ordered, lax.rem(nq - offset + c * local, nq), 1))
    weights = jnp.where(lane < local, sides[0], sides[1]).astype(BF16)
    result = jnp.zeros((total, nq), F32)
    for m in range(local):
        product = jnp.dot(kernel[m], weights, preferred_element_type=F32)
        result = jnp.where((lane == m) | (lane == local + m), product, result)
    out[...] = result


def inverse_kernel(per, local, blocks, mixed, circle, twiddle, across, out):
    count = blocks.shape[0] // per
    nq = circle.shape[0]
    length = nq * LANES
    share = nq // local
    dot = functools.partial(jnp.dot, precision=EXACT, preferred_element_type=F32)
    block_id = row_iota((count, nq))
    first = (block_id == 0) & (lane_iota((count, nq)) % local == 0)
    factor = jnp.where(first, 1.0, 2.0) / length
    for k in range(per):
        values = blocks[pl.ds(k, count, stride=per), :] if per > 1 else blocks[...]
        values = values * factor
        real, imag = [], []
        for h in range(share):
            chosen = jnp.where(block_id % share == h, values, 0.0)
            mid = dot(chosen.T, mixed[...])
            top, bottom = mid[0:local, :], mid[local : 2 * local, :]
            real.append(top[:, :LANES] - bottom[:, LANES:])
            imag.append(top[:, LANES:] + bottom[:, :LANES])
        real = jnp.concatenate(real, axis=0)
        imag = jnp.concatenate(imag, axis=0)
        turn_cos, turn_sin = twiddle[:, :LANES], twiddle[:, LANES:]
        turned = jnp.concatenate(
            [real * turn_cos - imag * turn_sin, real * turn_sin + imag * turn_cos], axis=0
        )
        wave = dot(across[...], turned)
        for q in range(nq):
            out[k : k + 1, q * LANES : (q + 1) * LANES] = wave[q : q + 1, :]


def cos_sin(rows, columns, length):
    steps = np.outer(rows, columns) % length
    angle = 2.0 * np.pi * steps / length
    return np.cos(angle).astype(np.float32), np.sin(angle).astype(np.float32)


def call(body, out_shape, in_specs=None, scratch=(), name=None, **cost):
    return pl.pallas_call(
        body,
        out_shape=out_shape,
        **({} if in_specs is None else {"in_specs": in_specs}),
        scratch_shapes=list(scratch),
        name=name,
        cost_estimate=pl.CostEstimate(**{"flops": 0, "bytes_accessed": 0, "transcendentals": 0, **cost}),
    )


def shape_of(shape, dtype=F32):
    return jax.ShapeDtypeStruct(shape, dtype)


def body(density, radial_velocity, azimuthal_velocity, cycle_shift, remainder, kernel):
    nz, slab, seg = density.shape
    azi, rad = lax.axis_size("azi"), lax.axis_size("rad")
    devices = azi * rad
    per = slab // azi
    tiles = seg // LANES
    length = seg * azi
    nq = length // LANES
    local = kernel.shape[0]
    modes = local * devices
    upper = modes // nq
    width = seg + LANES
    group = nz * per
    rows = row_layout(per, tiles)
    both = ("rad", "azi")
    vmem, smem = pl.BlockSpec(memory_space=pltpu.VMEM), pl.BlockSpec(memory_space=pltpu.SMEM)

    fields = (density, radial_velocity, azimuthal_velocity)
    tail = jnp.stack([f[:, slab - 2 :, :] for f in fields])
    head = jnp.stack([f[:, :2, :] for f in fields])
    low = lax.ppermute(tail, "rad", [(i, (i + 1) % rad) for i in range(rad)])
    high = lax.ppermute(head, "rad", [((i + 1) % rad, i) for i in range(rad)])
    bulk, surf = call(
        functools.partial(hydro_kernel, per),
        (shape_of((azi, 3 * group, seg), BF16), shape_of((azi, rows, LANES))),
        scratch=(
            pltpu.VMEM((3, nz, slab + 4 * SUB, width), F32),
            pltpu.VMEM((3, nz, slab + 4 * SUB, width), F32),
            pltpu.VMEM((azi, 3 * group, seg), F32),
        ),
        name="hydro",
        flops=100 * 3 * nz * slab * seg,
        bytes_accessed=24 * nz * slab * seg,
    )(*fields, low, high)

    surf = lax.all_to_all(surf, "azi", 0, 0, tiled=True)
    bulk = lax.all_to_all(bulk, "azi", 0, 0, tiled=True)

    k_id, l_id = np.arange(nq), np.arange(LANES)
    circle = np.concatenate(cos_sin(k_id, k_id, nq), axis=1)
    twiddle = np.concatenate(cos_sin(l_id, k_id, length), axis=1)
    short = np.concatenate(cos_sin(np.arange(upper), l_id, LANES), axis=0)
    spectrum = call(
        functools.partial(forward_kernel, per, nz, modes),
        shape_of((devices, 2 * per, nq), BF16),
        in_specs=[smem, smem, vmem, vmem, vmem, vmem],
        scratch=(pltpu.VMEM((upper, 2 * per, nq), F32),),
        name="forward",
        flops=100_000_000,
        bytes_accessed=1_000_000,
    )(cycle_shift, remainder, surf, jnp.asarray(circle), jnp.asarray(twiddle), jnp.asarray(short))
    columns = lax.all_to_all(spectrum, both, 0, 0, tiled=True)
    total = devices * per
    coupled = call(
        functools.partial(couple_kernel, per, local),
        shape_of((total, nq)),
        scratch=(pltpu.VMEM((devices, 2 * per, nq), F32),),
        name="couple",
        flops=100_000_000,
        bytes_accessed=1_000_000,
    )(columns, kernel)
    blocks = lax.all_to_all(coupled, both, 0, 0, tiled=True)
    j_of_block = np.arange(devices) * local // nq
    mixed = np.concatenate(cos_sin(j_of_block, l_id, LANES), axis=1)
    turn = np.concatenate(cos_sin(k_id, l_id, length), axis=1)
    cosine, sine = cos_sin(k_id, k_id, nq)
    across = np.concatenate([cosine, -sine], axis=1)
    potential = call(
        functools.partial(inverse_kernel, per, local),
        shape_of((per, length)),
        name="inverse",
        flops=100_000_000,
        bytes_accessed=1_000_000,
    )(blocks, jnp.asarray(mixed), jnp.asarray(circle), jnp.asarray(turn), jnp.asarray(across))

    moved = call(
        functools.partial(advect_kernel, per, nz),
        shape_of((azi, 3 * group, seg), BF16),
        in_specs=[smem, smem, vmem, vmem],
        scratch=(
            pltpu.VMEM((3, nq, group, LANES), F32),
            pltpu.VMEM((3, nq, group, LANES), F32),
            pltpu.VMEM((3, azi, group, LANES), F32),
        ),
        name="advect",
        flops=50 * 3 * nz * slab * seg,
        bytes_accessed=12 * nz * slab * seg,
    )(cycle_shift, remainder, bulk, surf)
    moved = lax.all_to_all(moved, "azi", 0, 0, tiled=True)
    results = call(
        functools.partial(settle_kernel, per),
        tuple(shape_of((nz, slab, seg)) for _ in range(3)),
        name="settle",
        flops=20 * 3 * nz * slab * seg,
        bytes_accessed=18 * nz * slab * seg,
    )(moved, surf)
    return (*results, potential)


def solution(mesh):
    split = P(None, "rad", "azi")
    in_specs = (split, split, split, P("rad"), P("rad"), P(("rad", "azi"), None, None))
    out_specs = (split, split, split, P(("rad", "azi"), None))
    return jax.shard_map(body, mesh=mesh, in_specs=in_specs, out_specs=out_specs, check_vma=False)
```

time: 567 us -> 120 us (0.21)
  waiting for transfers between devices: 246 us -> 35.7 us
  local copies, waits for them, and re-layouts: 179 us -> 4.47 us
  matrix products: 50.7 us -> 0 us
  other arithmetic: 40.5 us -> 0.09 us
  Pallas kernels: 0 us -> 36 us
  starting transfers between devices: 25.7 us -> 15 us
  blocking collectives: 17.4 us -> 27.7 us
    ppermute x11 -> x2, waiting for transfers between devices: 231 us -> 1.28 us  [the longest x1 0.81 us: body(): high = lax.ppermute(head, 'rad', [((i + 1) % rad, i) for i in range(rad)])]
    gather x160 -> x0, local copies, waits for them, and re-layouts: 152 us -> none
    dot_general x13 -> x0, matrix products: 50.7 us -> none  [the longest x1 6.3 us: forward_modes(): jnp.einsum('bnk,jkn->jkb', part_imag, turn_sin, precision=HIGHEST_PRECISION)]
    pallas_call x0 -> x6, Pallas kernels: none -> 36 us  [the longest x1 16.5 us: body(): call(functools.partial(advect_kernel, per, nz), shape_of((azi, 3 * group,...]
    all_to_all x2 -> x3, waiting for transfers between devices: 15.1 us -> 34.4 us  [the longest x1 17.4 us: body(): bulk = lax.all_to_all(bulk, 'azi', 0, 0, tiled=True)]
    mul x3 -> x0, other arithmetic: 16.1 us -> none  [the longest x2 16.1 us: rates(): 0.5 * (extended[:, 1:-1, 2:, 1:-1] - extended[:, 1:-1, :-2, 1:-1])]
    ppermute x11 -> x2, starting transfers between devices: 15 us -> 0.64 us  [the longest x1 0.56 us: body(): high = lax.ppermute(head, 'rad', [((i + 1) % rad, i) for i in range(rad)])]
    all_to_all x3 -> x2, blocking collectives: 17.4 us -> 27.7 us  [the longest x1 17.3 us: body(): surf = lax.all_to_all(surf, 'azi', 0, 0, tiled=True)]
  transfers between devices with their start and end apart: 13 -> 5, of which waited for: 12 -> 4; matrix products, arithmetic and copies ran while one was open for 0% -> 0% of each run, Pallas kernels for 0% -> 18%
where the time goes in v1:
time: 120 us
  Pallas kernels  36 us (30%)
  waiting for transfers between devices  35.7 us (30%)
  blocking collectives  27.7 us (23%)
  starting transfers between devices  15 us (12%)
  local copies, waits for them, and re-layouts  4.47 us (4%)
    all_to_all x1, waiting for transfers between devices, body(): bulk = lax.all_to_all(bulk, 'azi', 0, 0, tiled=True)  17.4 us
    all_to_all x1, blocking collectives, body(): surf = lax.all_to_all(surf, 'azi', 0, 0, tiled=True)  17.3 us
    all_to_all x1, waiting for transfers between devices, body(): moved = lax.all_to_all(moved, 'azi', 0, 0, tiled=True)  17.1 us
    pallas_call x1, Pallas kernels, body(): call(functools.partial(advect_kernel, per, nz), shape_of((azi, 3 * group,...  16.5 us
    all_to_all x1, blocking collectives, body(): columns = lax.all_to_all(spectrum, both, 0, 0, tiled=True)  10.5 us
    pallas_call x1, Pallas kernels, body(): call(functools.partial(hydro_kernel, per), (shape_of((azi, 3 * group, seg...  7.76 us
    all_to_all x1, starting transfers between devices, body(): moved = lax.all_to_all(moved, 'azi', 0, 0, tiled=True)  6.85 us
    all_to_all x1, starting transfers between devices, body(): blocks = lax.all_to_all(coupled, both, 0, 0, tiled=True)  3.88 us
  transfers between devices with their start and end apart: 5, of which 4 were waited for; matrix products, arithmetic and copies ran while one was open for 0% of the time, Pallas kernels for 18%

profile of v1, /device:TPU:0, one launch (start us, length us, event | category | flops | bytes accessed | tf_op | source)
XLA Modules:
  0.0 119.7 jit_solution(5882552277200232267)
XLA Ops:
  0.6 1.0 slice_bitcast_fusion.2
  1.6 1.1 slice_bitcast_fusion
  2.8 0.6 collective-permute-start.1
  3.4 0.1 collective-permute-start
  3.5 0.8 collective-permute-done.1.high
  4.3 0.0 copy-start.3
  4.3 0.5 collective-permute-done.low
  4.8 0.2 copy-done.3
  5.0 0.0 copy-start.4
  5.0 0.6 copy-done.4
  5.6 7.8 %hydro.1 = (bf16[16,24,1024]{2,1,0:T(8,128)(2,1)}, f32[16,24,128]{2,1,0:T(8,128)}) custom-call(f32[4,32,1024]{2,1,0:T(8,128)} %rho.1, f32[4,32,1024]{2,1,0:T(8,128)} %ur.1, f32[4,32,1024]{2,1,0:T(8,128)} %up.1, f32[3,4,2,1024]{3,2,1,0:T(2,128)} %copy-done.4, f32[3,4,2,1024]{3,2,1,0:T(2,128)} %copy-done.3), custom_call_target="tpu_custom_call" | custom-call | flops 39321600 | bytes 3145728 | tf_op jit(solution)/shard_map/hydro/pallas_call | solution.py:433
  13.4 17.3 %all_to_all.31.surf = f32[16,24,128]{2,1,0:T(8,128)} all-to-all(f32[16,24,128]{2,1,0:T(8,128)} %get-tuple-element.10), channel_id=1, replica_groups=mesh['rad'=2,'azi'=16] {'azi'}, dimensions={0} | all-to-all | bytes 393216 | tf_op jit(solution)/shard_map/all_to_all | solution.py:446
  30.6 3.4 %forward.1 = bf16[32,4,128]{2,1,0:T(4,128)(2,1)} custom-call(s32[32]{0:T(128)} %shift.3, f32[32]{0:T(128)} %remainder.3, f32[16,24,128]{2,1,0:T(8,128)} %all_to_all.31.surf, f32[128,256]{1,0:T(8,128)} %constant.10.clone.circle, f32[128,256]{1,0:T(8,128)} %constant.11.clone.twiddle, f32[32,128]{1,0:T(8,128)} %constant.12.clone.short), custom_call_target="tpu_custom_call" | custom-call | flops 100000000 | bytes 1000000 | tf_op jit(solution)/shard_map/forward/pallas_call | solution.py:453
  34.0 10.5 %all_to_all.32.columns = bf16[32,4,128]{2,1,0:T(4,128)(2,1)} all-to-all(bf16[32,4,128]{2,1,0:T(4,128)(2,1)} %forward.1), channel_id=1, replica_groups=mesh['rad'=2,'azi'=16] {'rad','azi'}, dimensions={0} | all-to-all | bytes 65536 | tf_op jit(solution)/shard_map/all_to_all | solution.py:462
  44.5 3.6 %all-to-all-start = ((bf16[16,24,1024]{2,1,0:T(8,128)(2,1)}), bf16[16,24,1024]{2,1,0:T(8,128)(2,1)S(1)}, u32[]{:S(2)}, u32[]{:S(2)}) async-start(bf16[16,24,1024]{2,1,0:T(8,128)(2,1)} %get-tuple-element.9), calls=%async_computation | async-start | bytes 1572864 | tf_op jit(solution)/shard_map/all_to_all | solution.py:447
  48.1 2.5 %couple.1 = f32[64,128]{1,0:T(8,128)} custom-call(bf16[32,4,128]{2,1,0:T(4,128)(2,1)} %all_to_all.32.columns, bf16[64,64,64]{2,1,0:T(8,128)(2,1)} %kernel.1), custom_call_target="tpu_custom_call" | custom-call | flops 100000000 | bytes 1000000 | tf_op jit(solution)/shard_map/couple/pallas_call | solution.py:464
  50.7 17.4 %all-to-all-done.bulk = bf16[16,24,1024]{2,1,0:T(8,128)(2,1)S(1)} async-done(((bf16[16,24,1024]{2,1,0:T(8,128)(2,1)}), bf16[16,24,1024]{2,1,0:T(8,128)(2,1)S(1)}, u32[]{:S(2)}, u32[]{:S(2)}) %all-to-all-start) | async-done | bytes 786464 | tf_op jit(solution)/shard_map/all_to_all | solution.py:447
  68.0 0.0 copy-start
  68.0 3.9 %all-to-all-start.4 = ((f32[32,2,128]{2,1,0:T(2,128)}), f32[32,2,128]{2,1,0:T(2,128)S(1)}, u32[]{:S(2)}, u32[]{:S(2)}) async-start(f32[32,2,128]{2,1,0:T(2,128)} %bitcast.15), calls=%async_computation.4 | async-start | bytes 65536 | tf_op jit(solution)/shard_map/all_to_all | solution.py:472
  71.9 0.0 copy-done
  71.9 16.5 %advect.1 = bf16[16,24,1024]{2,1,0:T(8,128)(2,1)} custom-call(s32[32]{0:T(128)} %shift.3, f32[32]{0:T(128)} %remainder.3, bf16[16,24,1024]{2,1,0:T(8,128)(2,1)} %copy-done, f32[16,24,128]{2,1,0:T(8,128)} %all_to_all.31.surf), custom_call_target="tpu_custom_call" | custom-call | flops 19660800 | bytes 1572864 | tf_op jit(solution)/shard_map/advect/pallas_call | solution.py:486
  88.4 0.0 all-to-all-done.4
  88.4 0.0 copy-start.2
  88.4 0.6 copy-done.2
  89.0 6.8 %all-to-all-start.2 = ((bf16[16,24,1024]{2,1,0:T(8,128)(2,1)}), bf16[16,24,1024]{2,1,0:T(8,128)(2,1)S(1)}, u32[]{:S(2)}, u32[]{:S(2)}) async-start(bf16[16,24,1024]{2,1,0:T(8,128)(2,1)} %advect.1), calls=%async_computation.2 | async-start | bytes 1572864 | tf_op jit(solution)/shard_map/all_to_all | solution.py:499
  95.9 2.9 %inverse.1 = f32[2,16384]{1,0:T(2,128)} custom-call(f32[64,128]{1,0:T(8,128)} %bitcast.14, f32[32,256]{1,0:T(8,128)} %constant.13.clone.mixed, f32[128,256]{1,0:T(8,128)} %constant.10.clone.circle, f32[128,256]{1,0:T(8,128)} %constant.11.clone.twiddle, f32[128,256]{1,0:T(8,128)} %constant.14.clone.across), custom_call_target="tpu_custom_call" | custom-call | flops 100000000 | bytes 1000000 | tf_op jit(solution)/shard_map/inverse/pallas_call | solution.py:478
  98.8 17.1 %all-to-all-done.2.bulk = bf16[16,24,1024]{2,1,0:T(8,128)(2,1)S(1)} async-done(((bf16[16,24,1024]{2,1,0:T(8,128)(2,1)}), bf16[16,24,1024]{2,1,0:T(8,128)(2,1)S(1)}, u32[]{:S(2)}, u32[]{:S(2)}) %all-to-all-start.2) | async-done | bytes 786464 | tf_op jit(solution)/shard_map/all_to_all | solution.py:499
  115.9 0.0 copy-start.1
  115.9 0.9 copy-done.1
  116.8 3.0 %settle.1 = (f32[4,32,1024]{2,1,0:T(8,128)}, f32[4,32,1024]{2,1,0:T(8,128)}, f32[4,32,1024]{2,1,0:T(8,128)}) custom-call(bf16[16,24,1024]{2,1,0:T(8,128)(2,1)} %copy-done.1, f32[16,24,128]{2,1,0:T(8,128)} %all_to_all.31.surf), custom_call_target="tpu_custom_call" | custom-call | flops 7864320 | bytes 2359296 | tf_op jit(solution)/shard_map/settle/pallas_call | solution.py:500
  (2 shorter events, 0.1 us)
Async XLA Ops:
  2.8 1.5 %collective-permute-start.1 = (f32[3,4,2,1024]{3,2,1,0:T(2,128)S(1)}, f32[3,4,2,1024]{3,2,1,0:T(2,128)S(1)}, u32[]{:S(2)}, u32[]{:S(2)}) collective-permute-start(f32[3,4,2,1024]{3,2,1,0:T(2,128)S(1)} %pad_maximum_fusion.1), channel_id=1, source_target_pairs={{16,0},{0,16},{17,1},{1,17},{18,2},{2,18},{19,3},{3,19},{20,4},{4,... | collective-permute-start | bytes 294920 | tf_op jit(solution)/shard_map/ppermute | solution.py:432
  3.4 1.4 %collective-permute-start = (f32[3,4,2,1024]{3,2,1,0:T(2,128)S(1)}, f32[3,4,2,1024]{3,2,1,0:T(2,128)S(1)}, u32[]{:S(2)}, u32[]{:S(2)}) collective-permute-start(f32[3,4,2,1024]{3,2,1,0:T(2,128)S(1)} %pad_maximum_fusion), channel_id=1, source_target_pairs={{0,16},{16,0},{1,17},{17,1},{2,18},{18,2},{3,19},{19,3},{4,20},{20... | collective-permute-start | bytes 294920 | tf_op jit(solution)/shard_map/ppermute | solution.py:431
  4.3 0.6 copy-start.3
  5.0 0.6 copy-start.4
  44.5 23.5 %all-to-all-start = ((bf16[16,24,1024]{2,1,0:T(8,128)(2,1)}), bf16[16,24,1024]{2,1,0:T(8,128)(2,1)S(1)}, u32[]{:S(2)}, u32[]{:S(2)}) async-start(bf16[16,24,1024]{2,1,0:T(8,128)(2,1)} %get-tuple-element.9), calls=%async_computation | async-start | bytes 1572864 | tf_op jit(solution)/shard_map/all_to_all | solution.py:447
  68.0 3.9 %copy-start = (bf16[16,24,1024]{2,1,0:T(8,128)(2,1)}, bf16[16,24,1024]{2,1,0:T(8,128)(2,1)S(1)}, u32[]{:S(2)}) copy-start(bf16[16,24,1024]{2,1,0:T(8,128)(2,1)S(1)} %all-to-all-done.bulk) | copy-start | bytes 2359300
  68.0 20.4 %all-to-all-start.4 = ((f32[32,2,128]{2,1,0:T(2,128)}), f32[32,2,128]{2,1,0:T(2,128)S(1)}, u32[]{:S(2)}, u32[]{:S(2)}) async-start(f32[32,2,128]{2,1,0:T(2,128)} %bitcast.15), calls=%async_computation.4 | async-start | bytes 65536 | tf_op jit(solution)/shard_map/all_to_all | solution.py:472
  88.4 0.6 copy-start.2
  89.0 26.8 %all-to-all-start.2 = ((bf16[16,24,1024]{2,1,0:T(8,128)(2,1)}), bf16[16,24,1024]{2,1,0:T(8,128)(2,1)S(1)}, u32[]{:S(2)}, u32[]{:S(2)}) async-start(bf16[16,24,1024]{2,1,0:T(8,128)(2,1)} %advect.1), calls=%async_computation.2 | async-start | bytes 1572864 | tf_op jit(solution)/shard_map/all_to_all | solution.py:499
  115.9 0.9 copy-start.1

commit v2 on v1

--- a/solution.py
+++ b/solution.py
@@ -9,6 +9,7 @@
 from jax.experimental.pallas import tpu as pltpu
 from jax.sharding import PartitionSpec as P
 
+
 RADIAL_COURANT = 0.3
 VISCOSITY = 0.08
 LANES = 128
@@ -44,12 +45,18 @@
     return lax.broadcasted_iota(jnp.int32, shape, 1)
 
 
-def row_layout(per, tiles):
-    used = per * tiles + per + 1
-    return -(-used // SUB) * SUB
-
-
-def hydro_kernel(per, rho, ur, up, low, high, bulk, surf, field, stage, block):
+def parts_of(value):
+    high = value.astype(BF16).astype(F32)
+    middle = (value - high).astype(BF16).astype(F32)
+    return high, middle, (value - high - middle).astype(BF16).astype(F32)
+
+
+def joined_parts(tile, per):
+    rows = tile.shape[0]
+    return tile + pltpu.roll(tile, rows - per, 0) + pltpu.roll(tile, rows - 2 * per, 0)
+
+
+def hydro_kernel(per, rho, ur, up, low, high, bulk, field, stage, block):
     nz, slab, seg = rho.shape
     width = seg + LANES
     first = 2 * SUB
@@ -154,19 +161,21 @@
                         d * per : (d + 1) * per, :
                     ]
                 overflow = overflow + pltpu.roll(field[c, z, here, seg:width], 2 + 4 * plane, 1)
-        rows = surf.shape[1]
-        for d in range(dests):
-            dest = (tile - 2) * dests + d
-            for k in range(per):
-                row = d * per + k
-                for b in range(tiles):
-                    surf[dest, k * tiles + b : k * tiles + b + 1, :] = column[
-                        row : row + 1, b * LANES : (b + 1) * LANES
-                    ]
-                at = per * tiles + k
-                surf[dest, at : at + 1, :] = overflow[row : row + 1, :]
-            spare = per * tiles + per
-            surf[dest, spare:rows, :] = jnp.broadcast_to(peak, (rows - spare, LANES))
+        overflow = jnp.where(lane_iota((SUB, LANES)) < LANES // 2, overflow, peak)
+        base = bulk.shape[1] - SUB
+        for part, (tall, over) in enumerate(zip(parts_of(column), parts_of(overflow))):
+            for d in range(dests):
+                dest = (tile - 2) * dests + d
+                for k in range(per):
+                    row = d * per + k
+                    at = pl.ds((part * per + k) * LANES, LANES)
+                    for b in range(tiles):
+                        block[dest, base + b : base + b + 1, at] = tall[
+                            row : row + 1, b * LANES : (b + 1) * LANES
+                        ]
+                    at = pl.ds(3 * per * LANES, LANES)
+                    line = base + part * per + k
+                    block[dest, line : line + 1, at] = over[row : row + 1, :]
         return carry
 
     lax.fori_loop(2, last_tile, pack, 0)
@@ -178,31 +187,34 @@
     lax.fori_loop(0, bulk.shape[0], narrow, 0)
 
 
-def advect_kernel(per, nz, shift, remainder, bulk, surf, out, ring, tapped, over):
-    sources, rows, seg = bulk.shape
+def advect_kernel(per, nz, shift, remainder, bulk, out, top, ring, tapped, over):
+    sources, _, seg = bulk.shape
     tiles = seg // LANES
     count = sources * tiles
     group = nz * per
-    spare = per * tiles + per
+    base = bulk.shape[1] - SUB
     me = lax.axis_index("azi")
 
-    def widen(a, carry):
-        unit = surf[a, spare : spare + 1, :] * (1.0 / TOP)
-        unit = jnp.concatenate([unit] * tiles, axis=1)
-        value = decode(bulk[a].astype(F32), unit)
+    def widen(a, peak):
+        whole_block = bulk[a].astype(F32)
+        at = 3 * per * LANES
+        packed = joined_parts(whole_block[base : base + SUB, at : at + LANES], per)[0:per, :]
+        mine = jnp.where(lane_iota((1, LANES)) >= LANES // 2, packed[0:1, :], 0.0)
+        mine = jnp.max(mine, keepdims=True)
+        value = decode(whole_block[0:base, :], mine * (1.0 / TOP))
         for c in range(3):
             for b in range(tiles):
                 ring[c, a * tiles + b] = value[
                     c * group : (c + 1) * group, b * LANES : (b + 1) * LANES
                 ]
-        packed = surf[a, per * tiles : per * tiles + per, :]
         for c in range(3):
             for z in range(nz):
                 turned = pltpu.roll(packed, LANES - 2 - 4 * (c * nz + z), 1)
                 over[c, a, z * per : (z + 1) * per, :] = turned
-        return carry
-
-    lax.fori_loop(0, sources, widen, 0)
+        return jnp.maximum(peak, mine)
+
+    peak = lax.fori_loop(0, sources, widen, jnp.zeros((1, 1), F32))
+    top[...] = jnp.broadcast_to(peak, top.shape)
     lane = lane_iota((group, LANES))
     cycle = row_iota((group, LANES)) % per
 
@@ -228,19 +240,24 @@
     w_prev = (x - 1.0) * x * (x + 2.0) / 2.0
     w_prev_two = -(x - 1.0) * x * (x + 1.0) / 6.0
 
-    def tap(t, carry):
-        after = lax.rem(t + 1, count)
-        before = lax.rem(t + count - 1, count)
-        for c in range(3):
-            cur, nxt, prv = ring[c, t], ring[c, after], ring[c, before]
-            next_one = pltpu.roll(jnp.where(lane == 0, nxt, cur), LANES - 1, 1)
-            prev_one = pltpu.roll(jnp.where(lane == LANES - 1, prv, cur), 1, 1)
-            prev_two = pltpu.roll(jnp.where(lane >= LANES - 2, prv, cur), 2, 1)
-            tapped[c, t] = w_next * next_one + w_here * cur + w_prev * prev_one + w_prev_two * prev_two
+    def tap(a, carry):
+        before = lax.rem(a * tiles + count - 1, count)
+        after = lax.rem((a + 1) * tiles, count)
+        for c in range(3):
+            line = [ring[c, before]]
+            line += [ring[c, a * tiles + b] for b in range(tiles)]
+            line += [ring[c, after]]
+            for b in range(tiles):
+                prv, cur, nxt = line[b : b + 3]
+                next_one = pltpu.roll(jnp.where(lane == 0, nxt, cur), LANES - 1, 1)
+                prev_one = pltpu.roll(jnp.where(lane == LANES - 1, prv, cur), 1, 1)
+                prev_two = pltpu.roll(jnp.where(lane >= LANES - 2, prv, cur), 2, 1)
+                tapped[c, a * tiles + b] = (
+                    w_next * next_one + w_here * cur + w_prev * prev_one + w_prev_two * prev_two
+                )
         return carry
 
-    lax.fori_loop(0, count, tap, 0)
-    peak = jnp.max(surf[:, spare, :], axis=0, keepdims=True)
+    lax.fori_loop(0, sources, tap, 0)
     scale = (TOP / GAIN) / peak
 
     def turned_tile(c, k, t):
@@ -268,13 +285,10 @@
     lax.fori_loop(0, sources, turn, start)
 
 
-def settle_kernel(per, bulk, surf, rho, ur, up):
+def settle_kernel(per, bulk, top, rho, ur, up):
     nz = rho.shape[0]
-    sources, rows, seg = bulk.shape
-    tiles = seg // LANES
-    spare = per * tiles + per
-    peak = jnp.max(surf[:, spare, :], axis=0, keepdims=True)
-    unit = jnp.concatenate([peak * (GAIN / TOP)] * tiles, axis=1)
+    sources, _, seg = bulk.shape
+    unit = jnp.concatenate([top[0:1, :] * (GAIN / TOP)] * (seg // LANES), axis=1)
     for a in range(sources):
         value = decode(bulk[a].astype(F32), unit)
         for c, ref in enumerate((rho, ur, up)):
@@ -283,8 +297,8 @@
                 ref[z, a * per : (a + 1) * per, :] = value[plane * per : (plane + 1) * per, :]
 
 
-def forward_kernel(per, nz, modes, shift, remainder, surf, circle, twiddle, short, out, rows_out):
-    sources = surf.shape[0]
+def forward_kernel(per, nz, modes, shift, remainder, side, circle, twiddle, short, out, rows_out):
+    sources = side.shape[0]
     nq = circle.shape[0]
     tiles = nq // sources
     length = nq * LANES
@@ -298,11 +312,23 @@
     mode = row_iota((upper, nq)) * nq + lane_iota((upper, nq))
     dot = functools.partial(jnp.dot, precision=EXACT, preferred_element_type=F32)
     for k in range(per):
-        packed = surf[:, per * tiles + k, :]
+        at = 3 * per * LANES
+        folded = [
+            joined_parts(side[a, :, at : at + LANES].astype(F32), per)[k : k + 1, :]
+            for a in range(sources)
+        ]
+        packed = jnp.concatenate(folded, axis=0)
         extra = jnp.zeros((sources, LANES), F32)
         for z in range(nz):
             extra = extra + pltpu.roll(packed, LANES - 2 - 4 * z, 1)
-        grid = surf[:, k * tiles : (k + 1) * tiles, :].reshape(nq, LANES)
+        grid = []
+        for a in range(sources):
+            tile = jnp.zeros((SUB, LANES), F32)
+            for part in range(3):
+                at = (part * per + k) * LANES
+                tile = tile + side[a, :, at : at + LANES].astype(F32)
+            grid.append(tile[0:tiles, :])
+        grid = jnp.concatenate(grid, axis=0)
         grid = grid + dot(to_after, jnp.where(lane < 2, extra, 0.0))
         grid = grid + dot(to_before, jnp.where(lane >= LANES - 2, extra, 0.0))
         inner = dot(grid.T, circle[...])
@@ -336,7 +362,7 @@
 
 
 def couple_kernel(per, local, columns, kernel, out, lines):
-    sources, parts, nq = columns.shape
+    sources, _, nq = columns.shape
     total = sources * per
     me = lax.axis_index("rad") * lax.axis_size("azi") + lax.axis_index("azi")
     offset = lax.rem(me * local, nq)
@@ -393,15 +419,19 @@
     return np.cos(angle).astype(np.float32), np.sin(angle).astype(np.float32)
 
 
-def call(body, out_shape, in_specs=None, scratch=(), name=None, **cost):
+def call(body, out_shape, in_specs=None, scratch=(), grid=(), **cost):
     return pl.pallas_call(
         body,
         out_shape=out_shape,
+        grid=grid,
         **({} if in_specs is None else {"in_specs": in_specs}),
         scratch_shapes=list(scratch),
-        name=name,
         cost_estimate=pl.CostEstimate(**{"flops": 0, "bytes_accessed": 0, "transcendentals": 0, **cost}),
     )
+
+
+def exchange(array, axes):
+    return lax.all_to_all(array, axes, 0, 0, tiled=True)
 
 
 def shape_of(shape, dtype=F32):
@@ -413,7 +443,6 @@
     azi, rad = lax.axis_size("azi"), lax.axis_size("rad")
     devices = azi * rad
     per = slab // azi
-    tiles = seg // LANES
     length = seg * azi
     nq = length // LANES
     local = kernel.shape[0]
@@ -421,7 +450,8 @@
     upper = modes // nq
     width = seg + LANES
     group = nz * per
-    rows = row_layout(per, tiles)
+    base = -(-3 * group // SUB) * SUB
+    rows = base + SUB
     both = ("rad", "azi")
     vmem, smem = pl.BlockSpec(memory_space=pltpu.VMEM), pl.BlockSpec(memory_space=pltpu.SMEM)
 
@@ -430,46 +460,44 @@
     head = jnp.stack([f[:, :2, :] for f in fields])
     low = lax.ppermute(tail, "rad", [(i, (i + 1) % rad) for i in range(rad)])
     high = lax.ppermute(head, "rad", [((i + 1) % rad, i) for i in range(rad)])
-    bulk, surf = call(
+    bulk = call(
         functools.partial(hydro_kernel, per),
-        (shape_of((azi, 3 * group, seg), BF16), shape_of((azi, rows, LANES))),
+        shape_of((azi, rows, seg), BF16),
         scratch=(
             pltpu.VMEM((3, nz, slab + 4 * SUB, width), F32),
             pltpu.VMEM((3, nz, slab + 4 * SUB, width), F32),
-            pltpu.VMEM((azi, 3 * group, seg), F32),
+            pltpu.VMEM((azi, rows, seg), F32),
         ),
-        name="hydro",
         flops=100 * 3 * nz * slab * seg,
         bytes_accessed=24 * nz * slab * seg,
     )(*fields, low, high)
 
-    surf = lax.all_to_all(surf, "azi", 0, 0, tiled=True)
-    bulk = lax.all_to_all(bulk, "azi", 0, 0, tiled=True)
+    bulk = exchange(bulk, "azi")
 
     k_id, l_id = np.arange(nq), np.arange(LANES)
     circle = np.concatenate(cos_sin(k_id, k_id, nq), axis=1)
     twiddle = np.concatenate(cos_sin(l_id, k_id, length), axis=1)
     short = np.concatenate(cos_sin(np.arange(upper), l_id, LANES), axis=0)
+    side = pl.BlockSpec((azi, SUB, seg), lambda i: (0, base // SUB, 0))
     spectrum = call(
         functools.partial(forward_kernel, per, nz, modes),
         shape_of((devices, 2 * per, nq), BF16),
-        in_specs=[smem, smem, vmem, vmem, vmem, vmem],
+        in_specs=[smem, smem, side, vmem, vmem, vmem],
         scratch=(pltpu.VMEM((upper, 2 * per, nq), F32),),
-        name="forward",
+        grid=(1,),
         flops=100_000_000,
         bytes_accessed=1_000_000,
-    )(cycle_shift, remainder, surf, jnp.asarray(circle), jnp.asarray(twiddle), jnp.asarray(short))
-    columns = lax.all_to_all(spectrum, both, 0, 0, tiled=True)
+    )(cycle_shift, remainder, bulk, jnp.asarray(circle), jnp.asarray(twiddle), jnp.asarray(short))
+    columns = exchange(spectrum, both)
     total = devices * per
     coupled = call(
         functools.partial(couple_kernel, per, local),
         shape_of((total, nq)),
         scratch=(pltpu.VMEM((devices, 2 * per, nq), F32),),
-        name="couple",
         flops=100_000_000,
         bytes_accessed=1_000_000,
     )(columns, kernel)
-    blocks = lax.all_to_all(coupled, both, 0, 0, tiled=True)
+    blocks = exchange(coupled, both)
     j_of_block = np.arange(devices) * local // nq
     mixed = np.concatenate(cos_sin(j_of_block, l_id, LANES), axis=1)
     turn = np.concatenate(cos_sin(k_id, l_id, length), axis=1)
@@ -478,32 +506,29 @@
     potential = call(
         functools.partial(inverse_kernel, per, local),
         shape_of((per, length)),
-        name="inverse",
         flops=100_000_000,
         bytes_accessed=1_000_000,
     )(blocks, jnp.asarray(mixed), jnp.asarray(circle), jnp.asarray(turn), jnp.asarray(across))
 
-    moved = call(
+    moved, top = call(
         functools.partial(advect_kernel, per, nz),
-        shape_of((azi, 3 * group, seg), BF16),
-        in_specs=[smem, smem, vmem, vmem],
+        (shape_of((azi, 3 * group, seg), BF16), shape_of((SUB, LANES))),
+        in_specs=[smem, smem, vmem],
         scratch=(
             pltpu.VMEM((3, nq, group, LANES), F32),
             pltpu.VMEM((3, nq, group, LANES), F32),
             pltpu.VMEM((3, azi, group, LANES), F32),
         ),
-        name="advect",
         flops=50 * 3 * nz * slab * seg,
         bytes_accessed=12 * nz * slab * seg,
-    )(cycle_shift, remainder, bulk, surf)
-    moved = lax.all_to_all(moved, "azi", 0, 0, tiled=True)
+    )(cycle_shift, remainder, bulk)
+    moved = exchange(moved, "azi")
     results = call(
         functools.partial(settle_kernel, per),
         tuple(shape_of((nz, slab, seg)) for _ in range(3)),
-        name="settle",
         flops=20 * 3 * nz * slab * seg,
         bytes_accessed=18 * nz * slab * seg,
-    )(moved, surf)
+    )(moved, top)
     return (*results, potential)
 
 
@@ -511,4 +536,5 @@
     split = P(None, "rad", "azi")
     in_specs = (split, split, split, P("rad"), P("rad"), P(("rad", "azi"), None, None))
     out_specs = (split, split, split, P(("rad", "azi"), None))
+
     return jax.shard_map(body, mesh=mesh, in_specs=in_specs, out_specs=out_specs, check_vma=False)

time: 120 us -> 109 us (0.908)
  blocking collectives: 27.7 us -> 45.3 us
  waiting for transfers between devices: 35.7 us -> 18.4 us
  Pallas kernels: 36 us -> 29.5 us
  starting transfers between devices: 15 us -> 10.1 us
    all_to_all x2, blocking collectives: 27.7 us -> 45.3 us  [exchange(): return lax.all_to_all(array, axes, 0, 0, tiled=True)]
    all_to_all x3 -> x2, waiting for transfers between devices: 34.4 us -> 17.1 us  [exchange(): return lax.all_to_all(array, axes, 0, 0, tiled=True)]
    pallas_call x2, Pallas kernels: 24.3 us -> 17.7 us  [the longest x1 9.64 us: body(): call(functools.partial(advect_kernel, per, nz), (shape_of((azi, 3 * group...]
    all_to_all x3 -> x2, starting transfers between devices: 14.3 us -> 9.42 us  [exchange(): return lax.all_to_all(array, axes, 0, 0, tiled=True)]
  transfers between devices with their start and end apart: 5 -> 4, of which waited for: 4 -> 3; matrix products, arithmetic and copies ran while one was open for 0% -> 0% of each run, Pallas kernels for 18% -> 12%
where the time goes in v2:
time: 109 us; the launch traced here: 108 us
  blocking collectives  45.3 us (42%)
  Pallas kernels  29.5 us (27%)
  waiting for transfers between devices  18.4 us (17%)
  starting transfers between devices  10.1 us (9%)
  local copies, waits for them, and re-layouts  4.46 us (4%)
    all_to_all x2, blocking collectives, exchange(): return lax.all_to_all(array, axes, 0, 0, tiled=True)  45.3 us
    all_to_all x2, waiting for transfers between devices, exchange(): return lax.all_to_all(array, axes, 0, 0, tiled=True)  17.1 us
    pallas_call x1, Pallas kernels, body(): call(functools.partial(advect_kernel, per, nz), (shape_of((azi, 3 * group...  9.64 us
    all_to_all x2, starting transfers between devices, exchange(): return lax.all_to_all(array, axes, 0, 0, tiled=True)  9.42 us
    pallas_call x1, Pallas kernels, body(): call(functools.partial(hydro_kernel, per), shape_of((azi, rows, seg), BF1...  8.1 us
    pallas_call x1, Pallas kernels, body(): call(functools.partial(forward_kernel, per, nz, modes), shape_of((devices...  3.39 us
    pallas_call x1, Pallas kernels, body(): call(functools.partial(settle_kernel, per), tuple((shape_of((nz, slab, se...  2.94 us
    pallas_call x1, Pallas kernels, body(): call(functools.partial(inverse_kernel, per, local), shape_of((per, length...  2.9 us
  transfers between devices with their start and end apart: 4, of which 3 were waited for; matrix products, arithmetic and copies ran while one was open for 0% of the time, Pallas kernels for 12%

profile of v2, /device:TPU:0, one launch (start us, length us, event | category | flops | bytes accessed | tf_op | source)
XLA Modules:
  0.0 108.4 jit_solution(11700844411395265859)
XLA Ops:
  0.6 1.0 slice_bitcast_fusion.2
  1.6 1.1 %slice_bitcast_fusion = (f32[1,4,2,1024]{3,2,1,0:T(2,128)S(1)}, f32[1,4,2,1024]{3,2,1,0:T(2,128)S(1)}, f32[1,4,2,1024]{3,2,1,0:T(2,128)S(1)}, f32[1,4,2,1024]{3,2,1,0:T(2,128)S(1)}) fusion(f32[4,32,1024]{2,1,0:T(8,128)} %up.1, f32[4,32,1024]{2,1,0:T(8,128)} %ur.1), kind=kLoop, calls=%fused_computation.2 | loop fusion | bytes 262144 | tf_op jit(solution)/shard_map/stack | solution.py:460
  2.8 0.6 collective-permute-start
  3.4 0.1 collective-permute-start.1
  3.5 0.8 collective-permute-done.low
  4.3 0.0 copy-start.2
  4.3 0.5 collective-permute-done.1.high
  4.8 0.2 copy-done.2
  5.0 0.0 copy-start.3
  5.0 0.6 copy-done.3
  5.6 8.1 %shard_map.147 = bf16[16,32,1024]{2,1,0:T(8,128)(2,1)} custom-call(f32[4,32,1024]{2,1,0:T(8,128)} %rho.1, f32[4,32,1024]{2,1,0:T(8,128)} %ur.1, f32[4,32,1024]{2,1,0:T(8,128)} %up.1, f32[3,4,2,1024]{3,2,1,0:T(2,128)} %copy-done.2, f32[3,4,2,1024]{3,2,1,0:T(2,128)} %copy-done.3), custom_call_target="tpu_custom_call" | custom-call | flops 39321600 | bytes 3145728 | tf_op jit(solution)/shard_map/pallas_call | solution.py:463
  13.7 34.9 %all_to_all.26.bulk.side = bf16[16,32,1024]{2,1,0:T(8,128)(2,1)} all-to-all(bf16[16,32,1024]{2,1,0:T(8,128)(2,1)} %shard_map.147), channel_id=1, replica_groups=mesh['rad'=2,'azi'=16] {'azi'}, dimensions={0} | all-to-all | bytes 2097152 | tf_op jit(solution)/shard_map/all_to_all | solution.py:434
  48.7 3.4 %shard_map.150 = bf16[32,4,128]{2,1,0:T(4,128)(2,1)} custom-call(s32[32]{0:T(128)} %shift.3, f32[32]{0:T(128)} %remainder.3, bf16[16,32,1024]{2,1,0:T(8,128)(2,1)} %all_to_all.26.bulk.side, f32[128,256]{1,0:T(8,128)} %constant.10.clone.circle, f32[128,256]{1,0:T(8,128)} %constant.11.clone.twiddle, f32[32,128]{1,0:T(8,128)} %constant.12.clone.short), custom_call_target="tpu_custom_call" | custom-call | flops 100000000 | bytes 1000000 | tf_op jit(solution)/shard_map/pallas_call | solution.py:482
  52.1 10.3 %all_to_all.27.columns = bf16[32,4,128]{2,1,0:T(4,128)(2,1)} all-to-all(bf16[32,4,128]{2,1,0:T(4,128)(2,1)} %shard_map.150), channel_id=1, replica_groups=mesh['rad'=2,'azi'=16] {'rad','azi'}, dimensions={0} | all-to-all | bytes 65536 | tf_op jit(solution)/shard_map/all_to_all | solution.py:434
  62.4 2.5 %shard_map.151 = f32[64,128]{1,0:T(8,128)} custom-call(bf16[32,4,128]{2,1,0:T(4,128)(2,1)} %all_to_all.27.columns, bf16[64,64,64]{2,1,0:T(8,128)(2,1)} %kernel.1), custom_call_target="tpu_custom_call" | custom-call | flops 100000000 | bytes 1000000 | tf_op jit(solution)/shard_map/pallas_call | solution.py:493
  64.9 2.6 %all-to-all-start.3 = ((f32[32,2,128]{2,1,0:T(2,128)}), f32[32,2,128]{2,1,0:T(2,128)S(1)}, u32[]{:S(2)}, u32[]{:S(2)}) async-start(f32[32,2,128]{2,1,0:T(2,128)} %bitcast.15), calls=%async_computation.3 | async-start | bytes 65536 | tf_op jit(solution)/shard_map/all_to_all | solution.py:434
  67.5 9.6 %shard_map.148 = (bf16[16,24,1024]{2,1,0:T(8,128)(2,1)}, f32[8,128]{1,0:T(8,128)}) custom-call(s32[32]{0:T(128)} %shift.3, f32[32]{0:T(128)} %remainder.3, bf16[16,32,1024]{2,1,0:T(8,128)(2,1)} %all_to_all.26.bulk.side), custom_call_target="tpu_custom_call" | custom-call | flops 19660800 | bytes 1572864 | tf_op jit(solution)/shard_map/pallas_call | solution.py:513
  77.1 0.0 all-to-all-done.3
  77.1 0.0 copy-start.1
  77.1 0.6 copy-done.1
  77.7 6.8 %all-to-all-start.1 = ((bf16[16,24,1024]{2,1,0:T(8,128)(2,1)}), bf16[16,24,1024]{2,1,0:T(8,128)(2,1)S(1)}, u32[]{:S(2)}, u32[]{:S(2)}) async-start(bf16[16,24,1024]{2,1,0:T(8,128)(2,1)} %get-tuple-element.9), calls=%async_computation.1 | async-start | bytes 1572864 | tf_op jit(solution)/shard_map/all_to_all | solution.py:434
  84.6 2.9 %shard_map.152 = f32[2,16384]{1,0:T(2,128)} custom-call(f32[64,128]{1,0:T(8,128)} %bitcast.14, f32[32,256]{1,0:T(8,128)} %constant.13.clone.mixed, f32[128,256]{1,0:T(8,128)} %constant.10.clone.circle, f32[128,256]{1,0:T(8,128)} %constant.11.clone.twiddle, f32[128,256]{1,0:T(8,128)} %constant.14.clone.across), custom_call_target="tpu_custom_call" | custom-call | flops 100000000 | bytes 1000000 | tf_op jit(solution)/shard_map/pallas_call | solution.py:506
  87.5 17.1 %all-to-all-done.1.bulk = bf16[16,24,1024]{2,1,0:T(8,128)(2,1)S(1)} async-done(((bf16[16,24,1024]{2,1,0:T(8,128)(2,1)}), bf16[16,24,1024]{2,1,0:T(8,128)(2,1)S(1)}, u32[]{:S(2)}, u32[]{:S(2)}) %all-to-all-start.1) | async-done | bytes 786464 | tf_op jit(solution)/shard_map/all_to_all | solution.py:434
  104.6 0.0 copy-start
  104.6 0.9 copy-done
  105.5 2.9 %shard_map.149 = (f32[4,32,1024]{2,1,0:T(8,128)}, f32[4,32,1024]{2,1,0:T(8,128)}, f32[4,32,1024]{2,1,0:T(8,128)}) custom-call(bf16[16,24,1024]{2,1,0:T(8,128)(2,1)} %copy-done, f32[8,128]{1,0:T(8,128)} %get-tuple-element.10.top), custom_call_target="tpu_custom_call" | custom-call | flops 7864320 | bytes 2359296 | tf_op jit(solution)/shard_map/pallas_call | solution.py:526
  (2 shorter events, 0.1 us)
Async XLA Ops:
  2.8 1.5 %collective-permute-start = (f32[3,4,2,1024]{3,2,1,0:T(2,128)S(1)}, f32[3,4,2,1024]{3,2,1,0:T(2,128)S(1)}, u32[]{:S(2)}, u32[]{:S(2)}) collective-permute-start(f32[3,4,2,1024]{3,2,1,0:T(2,128)S(1)} %pad_maximum_fusion), channel_id=1, source_target_pairs={{0,16},{16,0},{1,17},{17,1},{2,18},{18,2},{3,19},{19,3},{4,20},{20... | collective-permute-start | bytes 294920 | tf_op jit(solution)/shard_map/ppermute | solution.py:461
  3.4 1.4 %collective-permute-start.1 = (f32[3,4,2,1024]{3,2,1,0:T(2,128)S(1)}, f32[3,4,2,1024]{3,2,1,0:T(2,128)S(1)}, u32[]{:S(2)}, u32[]{:S(2)}) collective-permute-start(f32[3,4,2,1024]{3,2,1,0:T(2,128)S(1)} %pad_maximum_fusion.1), channel_id=1, source_target_pairs={{16,0},{0,16},{17,1},{1,17},{18,2},{2,18},{19,3},{3,19},{20,4},{4,... | collective-permute-start | bytes 294920 | tf_op jit(solution)/shard_map/ppermute | solution.py:462
  4.3 0.6 copy-start.2
  5.0 0.6 copy-start.3
  64.9 12.2 %all-to-all-start.3 = ((f32[32,2,128]{2,1,0:T(2,128)}), f32[32,2,128]{2,1,0:T(2,128)S(1)}, u32[]{:S(2)}, u32[]{:S(2)}) async-start(f32[32,2,128]{2,1,0:T(2,128)} %bitcast.15), calls=%async_computation.3 | async-start | bytes 65536 | tf_op jit(solution)/shard_map/all_to_all | solution.py:434
  77.1 0.6 copy-start.1
  77.7 26.8 %all-to-all-start.1 = ((bf16[16,24,1024]{2,1,0:T(8,128)(2,1)}), bf16[16,24,1024]{2,1,0:T(8,128)(2,1)S(1)}, u32[]{:S(2)}, u32[]{:S(2)}) async-start(bf16[16,24,1024]{2,1,0:T(8,128)(2,1)} %get-tuple-element.9), calls=%async_computation.1 | async-start | bytes 1572864 | tf_op jit(solution)/shard_map/all_to_all | solution.py:434
  104.6 0.9 copy-start

commit v3 on v2

--- a/solution.py
+++ b/solution.py
@@ -47,16 +47,29 @@
 
 def parts_of(value):
     high = value.astype(BF16).astype(F32)
-    middle = (value - high).astype(BF16).astype(F32)
-    return high, middle, (value - high - middle).astype(BF16).astype(F32)
+    return high, (value - high).astype(BF16).astype(F32)
+
+
+PARTS = 2
 
 
 def joined_parts(tile, per):
-    rows = tile.shape[0]
-    return tile + pltpu.roll(tile, rows - per, 0) + pltpu.roll(tile, rows - 2 * per, 0)
-
-
-def hydro_kernel(per, rho, ur, up, low, high, bulk, field, stage, block):
+    return tile + pltpu.roll(tile, tile.shape[0] - per, 0)
+
+
+def load_kernel(rho, ur, up, rho_near, ur_near, up_near, tail, head, sems):
+    slab = rho.shape[1]
+    pairs = ((rho, rho_near), (ur, ur_near), (up, up_near))
+    copies = [pltpu.make_async_copy(far, near, sems.at[c]) for c, (far, near) in enumerate(pairs)]
+    for copy in copies:
+        copy.start()
+    for c, (_, near) in enumerate(pairs):
+        copies[c].wait()
+        tail[c] = near[:, slab - 2 :, :]
+        head[c] = near[:, 0:2, :]
+
+
+def hydro_kernel(per, rho, ur, up, low, high, bulk, field, stage, block, narrow, sems):
     nz, slab, seg = rho.shape
     width = seg + LANES
     first = 2 * SUB
@@ -142,8 +155,16 @@
 
     largest = lax.fori_loop(2, last_tile, second_section, jnp.zeros((SUB, width), F32))
     peak = jnp.maximum(jnp.max(largest, keepdims=True), 1e-30)
+    peak = sum(parts_of(peak))
     scale = TOP / peak
     dests = SUB // per
+    stride = -(-3 * nz * per // SUB) * SUB
+    base = tiles * stride
+    lines = base + PARTS * per * SUB
+
+    def send(index):
+        at = pl.ds(index * dests, dests)
+        return pltpu.make_async_copy(narrow.at[at], bulk.at[at], sems.at[index])
 
     def pack(tile, carry):
         here = pl.ds(pl.multiple_of(tile * SUB, SUB), SUB)
@@ -157,56 +178,55 @@
                 code = encode(value, scale)
                 plane = c * nz + z
                 for d in range(dests):
-                    block[(tile - 2) * dests + d, plane * per : (plane + 1) * per, :] = code[
-                        d * per : (d + 1) * per, :
-                    ]
+                    for b in range(tiles):
+                        line = b * stride + plane * per
+                        block[(tile - 2) * dests + d, line : line + per, :] = code[
+                            d * per : (d + 1) * per, b * LANES : (b + 1) * LANES
+                        ]
                 overflow = overflow + pltpu.roll(field[c, z, here, seg:width], 2 + 4 * plane, 1)
         overflow = jnp.where(lane_iota((SUB, LANES)) < LANES // 2, overflow, peak)
-        base = bulk.shape[1] - SUB
         for part, (tall, over) in enumerate(zip(parts_of(column), parts_of(overflow))):
             for d in range(dests):
                 dest = (tile - 2) * dests + d
                 for k in range(per):
                     row = d * per + k
-                    at = pl.ds((part * per + k) * LANES, LANES)
+                    at = base + (part * per + k) * SUB
                     for b in range(tiles):
-                        block[dest, base + b : base + b + 1, at] = tall[
+                        block[dest, at + b : at + b + 1, :] = tall[
                             row : row + 1, b * LANES : (b + 1) * LANES
                         ]
-                    at = pl.ds(3 * per * LANES, LANES)
-                    line = base + part * per + k
-                    block[dest, line : line + 1, at] = over[row : row + 1, :]
+                    line = lines + part * per + k
+                    block[dest, line : line + 1, :] = over[row : row + 1, :]
+        for d in range(dests):
+            dest = (tile - 2) * dests + d
+            narrow[dest] = block[dest].astype(BF16)
+        send(tile - 2).start()
         return carry
 
     lax.fori_loop(2, last_tile, pack, 0)
-
-    def narrow(d, carry):
-        bulk[d] = block[d].astype(BF16)
-        return carry
-
-    lax.fori_loop(0, bulk.shape[0], narrow, 0)
+    for index in range(slab // SUB):
+        send(index).wait()
 
 
 def advect_kernel(per, nz, shift, remainder, bulk, out, top, ring, tapped, over):
-    sources, _, seg = bulk.shape
-    tiles = seg // LANES
-    count = sources * tiles
+    sources = bulk.shape[0]
+    count = ring.shape[1]
+    tiles = count // sources
     group = nz * per
-    base = bulk.shape[1] - SUB
+    stride = -(-3 * group // SUB) * SUB
+    lines = tiles * stride + PARTS * per * SUB
     me = lax.axis_index("azi")
 
     def widen(a, peak):
         whole_block = bulk[a].astype(F32)
-        at = 3 * per * LANES
-        packed = joined_parts(whole_block[base : base + SUB, at : at + LANES], per)[0:per, :]
+        packed = joined_parts(whole_block[lines : lines + SUB, :], per)[0:per, :]
         mine = jnp.where(lane_iota((1, LANES)) >= LANES // 2, packed[0:1, :], 0.0)
         mine = jnp.max(mine, keepdims=True)
-        value = decode(whole_block[0:base, :], mine * (1.0 / TOP))
-        for c in range(3):
-            for b in range(tiles):
-                ring[c, a * tiles + b] = value[
-                    c * group : (c + 1) * group, b * LANES : (b + 1) * LANES
-                ]
+        unit = mine * (1.0 / TOP)
+        for b in range(tiles):
+            value = decode(whole_block[b * stride : (b + 1) * stride, :], unit)
+            for c in range(3):
+                ring[c, a * tiles + b] = value[c * group : (c + 1) * group, :]
         for c in range(3):
             for z in range(nz):
                 turned = pltpu.roll(packed, LANES - 2 - 4 * (c * nz + z), 1)
@@ -227,7 +247,7 @@
             ring[c, before] = ring[c, before] + jnp.where(lane >= LANES - 2, extra, 0.0)
         return carry
 
-    lax.fori_loop(0, sources, spill, 0)
+    lax.fori_loop(0, sources, spill, 0, unroll=4)
     x = jnp.zeros((group, LANES), F32)
     whole, part = [], []
     for k in range(per):
@@ -304,6 +324,8 @@
     length = nq * LANES
     upper = modes // nq
     dests = out.shape[0]
+    base = tiles * (-(-3 * nz * per // SUB) * SUB)
+    lines = base + PARTS * per * SUB
     me = lax.axis_index("azi")
     lane = lane_iota((sources, LANES))
     q_id, a_id = row_iota((nq, sources)), lane_iota((nq, sources))
@@ -312,9 +334,8 @@
     mode = row_iota((upper, nq)) * nq + lane_iota((upper, nq))
     dot = functools.partial(jnp.dot, precision=EXACT, preferred_element_type=F32)
     for k in range(per):
-        at = 3 * per * LANES
         folded = [
-            joined_parts(side[a, :, at : at + LANES].astype(F32), per)[k : k + 1, :]
+            joined_parts(side[a, lines : lines + SUB, :].astype(F32), per)[k : k + 1, :]
             for a in range(sources)
         ]
         packed = jnp.concatenate(folded, axis=0)
@@ -324,9 +345,9 @@
         grid = []
         for a in range(sources):
             tile = jnp.zeros((SUB, LANES), F32)
-            for part in range(3):
-                at = (part * per + k) * LANES
-                tile = tile + side[a, :, at : at + LANES].astype(F32)
+            for part in range(PARTS):
+                at = base + (part * per + k) * SUB
+                tile = tile + side[a, at : at + SUB, :].astype(F32)
             grid.append(tile[0:tiles, :])
         grid = jnp.concatenate(grid, axis=0)
         grid = grid + dot(to_after, jnp.where(lane < 2, extra, 0.0))
@@ -361,7 +382,31 @@
         out[d] = rows_out[d // share, 0 : 2 * per, :].astype(BF16)
 
 
-def couple_kernel(per, local, columns, kernel, out, lines):
+def pick(values, index):
+    chosen = values[0]
+    for i, value in enumerate(values[1:]):
+        chosen = jnp.where(index == i + 1, value, chosen)
+    return chosen
+
+
+def route_kernel(size, middle, inner, where, *rest):
+    count = (len(rest) - 1 - size)
+    sources, outs, sorted_rows = rest[:count], rest[count:-1], rest[-1]
+    for i, source in enumerate(sources):
+        value = source[...]
+        for m in range(middle):
+            for dest in range(size):
+                at = (m * size + dest) * inner
+                to = (i * middle + m) * inner
+                sorted_rows[dest, to : to + inner, :] = value[at : at + inner, :]
+    choices = [sorted_rows[dest] for dest in range(size)]
+    index = where()
+    for offset, out in enumerate(outs):
+        out[...] = pick(choices, lax.rem(index + offset, size))
+
+
+def couple_kernel(per, local, columns, kernel, *rest):
+    outs, lines = rest[:-1], rest[-1]
     sources, _, nq = columns.shape
     total = sources * per
     me = lax.axis_index("rad") * lax.axis_size("azi") + lax.axis_index("azi")
@@ -380,20 +425,37 @@
     for m in range(local):
         product = jnp.dot(kernel[m], weights, preferred_element_type=F32)
         result = jnp.where((lane == m) | (lane == local + m), product, result)
-    out[...] = result
-
-
-def inverse_kernel(per, local, blocks, mixed, circle, twiddle, across, out):
-    count = blocks.shape[0] // per
+    rad = lax.axis_index("rad")
+    share = total // len(outs)
+    slabs = [result[i * share : (i + 1) * share, :] for i in range(len(outs))]
+    for offset, out in enumerate(outs):
+        out[...] = pick(slabs, lax.rem(rad + offset, len(outs)))
+
+
+def inverse_kernel(per, local, fast, *rest):
+    blocks, (circle, twiddle, mixed, out) = rest[:-4], rest[-4:]
+    slow = len(blocks)
     nq = circle.shape[0]
     length = nq * LANES
     share = nq // local
+    rad_count = lax.axis_size("rad")
+    count = slow * fast * rad_count
     dot = functools.partial(jnp.dot, precision=EXACT, preferred_element_type=F32)
     block_id = row_iota((count, nq))
     first = (block_id == 0) & (lane_iota((count, nq)) % local == 0)
     factor = jnp.where(first, 1.0, 2.0) / length
+    azi, rad = lax.axis_index("azi"), lax.axis_index("rad")
+    place = lane_iota((count, count))
+    from_rad = lax.rem(rad - place % rad_count + rad_count, rad_count)
+    from_fast = lax.rem(azi % fast - place // rad_count % fast + fast, fast)
+    from_slow = lax.rem(azi // fast - place // (rad_count * fast) + slow, slow)
+    source = (from_rad * slow + from_slow) * fast + from_fast
+    order = (source == row_iota((count, count))).astype(F32)
     for k in range(per):
-        values = blocks[pl.ds(k, count, stride=per), :] if per > 1 else blocks[...]
+        picked = [
+            ref[pl.ds(k, fast * rad_count, stride=per), :] if per > 1 else ref[...] for ref in blocks
+        ]
+        values = dot(order, jnp.concatenate(picked, axis=0))
         values = values * factor
         real, imag = [], []
         for h in range(share):
@@ -406,9 +468,9 @@
         imag = jnp.concatenate(imag, axis=0)
         turn_cos, turn_sin = twiddle[:, :LANES], twiddle[:, LANES:]
         turned = jnp.concatenate(
-            [real * turn_cos - imag * turn_sin, real * turn_sin + imag * turn_cos], axis=0
+            [real * turn_cos - imag * turn_sin, -(real * turn_sin + imag * turn_cos)], axis=0
         )
-        wave = dot(across[...], turned)
+        wave = dot(circle[...], turned)
         for q in range(nq):
             out[k : k + 1, q * LANES : (q + 1) * LANES] = wave[q : q + 1, :]
 
@@ -419,15 +481,24 @@
     return np.cos(angle).astype(np.float32), np.sin(angle).astype(np.float32)
 
 
-def call(body, out_shape, in_specs=None, scratch=(), grid=(), **cost):
-    return pl.pallas_call(
+def call(body, out_shape, in_specs=None, out_specs=None, scratch=(), name=None, **cost):
+    kernel = pl.pallas_call(
         body,
         out_shape=out_shape,
-        grid=grid,
         **({} if in_specs is None else {"in_specs": in_specs}),
+        **({} if out_specs is None else {"out_specs": out_specs}),
         scratch_shapes=list(scratch),
         cost_estimate=pl.CostEstimate(**{"flops": 0, "bytes_accessed": 0, "transcendentals": 0, **cost}),
     )
+
+    def run(*operands):
+        near = [
+            x if x.ndim == 1 or name == "load" else pltpu.with_memory_space_constraint(x, pltpu.VMEM)
+            for x in operands
+        ]
+        return kernel(*near)
+
+    return run
 
 
 def exchange(array, axes):
@@ -443,6 +514,7 @@
     azi, rad = lax.axis_size("azi"), lax.axis_size("rad")
     devices = azi * rad
     per = slab // azi
+    tiles = seg // LANES
     length = seg * azi
     nq = length // LANES
     local = kernel.shape[0]
@@ -450,24 +522,38 @@
     upper = modes // nq
     width = seg + LANES
     group = nz * per
-    base = -(-3 * group // SUB) * SUB
-    rows = base + SUB
+    stride = -(-3 * group // SUB) * SUB
+    rows = tiles * stride + PARTS * per * SUB + SUB
+    fast = min(4, azi)
+    slow = azi // fast
     both = ("rad", "azi")
     vmem, smem = pl.BlockSpec(memory_space=pltpu.VMEM), pl.BlockSpec(memory_space=pltpu.SMEM)
 
     fields = (density, radial_velocity, azimuthal_velocity)
-    tail = jnp.stack([f[:, slab - 2 :, :] for f in fields])
-    head = jnp.stack([f[:, :2, :] for f in fields])
+    anywhere = pl.BlockSpec(memory_space=pl.ANY)
+    edge = pltpu.VMEM((3, nz, 2, seg), F32)
+    *fields, tail, head = call(
+        load_kernel,
+        (*(pltpu.VMEM((nz, slab, seg), F32) for _ in range(3)), edge, edge),
+        in_specs=[anywhere] * 3,
+        scratch=(pltpu.SemaphoreType.DMA((3,)),),
+        name="load",
+        bytes_accessed=12 * nz * slab * seg,
+    )(*fields)
     low = lax.ppermute(tail, "rad", [(i, (i + 1) % rad) for i in range(rad)])
     high = lax.ppermute(head, "rad", [((i + 1) % rad, i) for i in range(rad)])
     bulk = call(
         functools.partial(hydro_kernel, per),
-        shape_of((azi, rows, seg), BF16),
+        shape_of((azi, rows, LANES), BF16),
+        out_specs=anywhere,
         scratch=(
             pltpu.VMEM((3, nz, slab + 4 * SUB, width), F32),
             pltpu.VMEM((3, nz, slab + 4 * SUB, width), F32),
-            pltpu.VMEM((azi, rows, seg), F32),
+            pltpu.VMEM((azi, rows, LANES), F32),
+            pltpu.VMEM((azi, rows, LANES), BF16),
+            pltpu.SemaphoreType.DMA((slab // SUB,)),
         ),
+        name="hydro",
         flops=100 * 3 * nz * slab * seg,
         bytes_accessed=24 * nz * slab * seg,
     )(*fields, low, high)
@@ -478,47 +564,72 @@
     circle = np.concatenate(cos_sin(k_id, k_id, nq), axis=1)
     twiddle = np.concatenate(cos_sin(l_id, k_id, length), axis=1)
     short = np.concatenate(cos_sin(np.arange(upper), l_id, LANES), axis=0)
-    side = pl.BlockSpec((azi, SUB, seg), lambda i: (0, base // SUB, 0))
     spectrum = call(
         functools.partial(forward_kernel, per, nz, modes),
-        shape_of((devices, 2 * per, nq), BF16),
-        in_specs=[smem, smem, side, vmem, vmem, vmem],
+        pltpu.VMEM((devices, 2 * per, nq), BF16),
+        in_specs=[smem, smem, vmem, vmem, vmem, vmem],
         scratch=(pltpu.VMEM((upper, 2 * per, nq), F32),),
-        grid=(1,),
+        name="forward",
         flops=100_000_000,
         bytes_accessed=1_000_000,
     )(cycle_shift, remainder, bulk, jnp.asarray(circle), jnp.asarray(twiddle), jnp.asarray(short))
     columns = exchange(spectrum, both)
-    total = devices * per
-    coupled = call(
+    blocks = call(
         functools.partial(couple_kernel, per, local),
-        shape_of((total, nq)),
+        tuple(pltpu.VMEM((azi * per, nq), F32) for _ in range(rad)),
         scratch=(pltpu.VMEM((devices, 2 * per, nq), F32),),
+        name="couple",
         flops=100_000_000,
         bytes_accessed=1_000_000,
     )(columns, kernel)
-    blocks = exchange(coupled, both)
+
+    def hop(buffers, axis, size, step):
+        around = range(lax.axis_size(axis))
+        return [buffers[0]] + [
+            lax.ppermute(
+                buffers[o],
+                axis,
+                [(i, i + ((i // step % size + o) % size - i // step % size) * step) for i in around],
+            )
+            for o in range(1, size)
+        ]
+
+    blocks = hop(blocks, "rad", rad, 1)
+    for size, middle, where, step, name in (
+        (fast, slow, lambda: lax.axis_index("azi") % fast, 1, "fast"),
+        (slow, fast * rad // fast, lambda: lax.axis_index("azi") // fast, fast, "slow"),
+    ):
+        lines = len(blocks) * blocks[0].shape[0] // size
+        middle = blocks[0].shape[0] // (size * per)
+        blocks = call(
+            functools.partial(route_kernel, size, middle, per, where),
+            tuple(pltpu.VMEM((lines, nq), F32) for _ in range(size)),
+            scratch=(pltpu.VMEM((size, lines, nq), F32),),
+            name="route_" + name,
+            bytes_accessed=100_000,
+        )(*blocks)
+        blocks = hop(blocks, "azi", size, step)
     j_of_block = np.arange(devices) * local // nq
     mixed = np.concatenate(cos_sin(j_of_block, l_id, LANES), axis=1)
     turn = np.concatenate(cos_sin(k_id, l_id, length), axis=1)
-    cosine, sine = cos_sin(k_id, k_id, nq)
-    across = np.concatenate([cosine, -sine], axis=1)
     potential = call(
-        functools.partial(inverse_kernel, per, local),
+        functools.partial(inverse_kernel, per, local, fast),
         shape_of((per, length)),
+        name="inverse",
         flops=100_000_000,
         bytes_accessed=1_000_000,
-    )(blocks, jnp.asarray(mixed), jnp.asarray(circle), jnp.asarray(turn), jnp.asarray(across))
+    )(*blocks, jnp.asarray(circle), jnp.asarray(turn), jnp.asarray(mixed))
 
     moved, top = call(
         functools.partial(advect_kernel, per, nz),
-        (shape_of((azi, 3 * group, seg), BF16), shape_of((SUB, LANES))),
+        (pltpu.VMEM((azi, 3 * group, seg), BF16), pltpu.VMEM((SUB, LANES), F32)),
         in_specs=[smem, smem, vmem],
         scratch=(
             pltpu.VMEM((3, nq, group, LANES), F32),
             pltpu.VMEM((3, nq, group, LANES), F32),
             pltpu.VMEM((3, azi, group, LANES), F32),
         ),
+        name="advect",
         flops=50 * 3 * nz * slab * seg,
         bytes_accessed=12 * nz * slab * seg,
     )(cycle_shift, remainder, bulk)
@@ -526,6 +637,7 @@
     results = call(
         functools.partial(settle_kernel, per),
         tuple(shape_of((nz, slab, seg)) for _ in range(3)),
+        name="settle",
         flops=20 * 3 * nz * slab * seg,
         bytes_accessed=18 * nz * slab * seg,
     )(moved, top)

time: 109 us -> 90 us (0.83)
  blocking collectives: 45.3 us -> 33.1 us
  starting transfers between devices: 10.1 us -> 20.6 us
  waiting for transfers between devices: 18.4 us -> 11.2 us
  Pallas kernels: 29.5 us -> 24 us
  local copies, waits for them, and re-layouts: 4.46 us -> 0.03 us
    all_to_all x2, waiting for transfers between devices: 17.1 us -> 0.01 us  [exchange(): return lax.all_to_all(array, axes, 0, 0, tiled=True)]
    all_to_all x2 -> x1, blocking collectives: 45.3 us -> 33.1 us  [exchange(): return lax.all_to_all(array, axes, 0, 0, tiled=True)]
    ppermute x0 -> x7, starting transfers between devices: none -> 10.3 us  [hop(): lax.ppermute(buffers[o], axis, [(i, i + ((i // step % size + o) % size -...]
    ppermute x0 -> x7, waiting for transfers between devices: none -> 9.95 us  [hop(): lax.ppermute(buffers[o], axis, [(i, i + ((i // step % size + o) % size -...]
    pallas_call x6 -> x9, Pallas kernels: 29.5 us -> 24 us  [run(): return kernel(*near)]
    unnamed x8 -> x10, local copies, waits for them, and re-layouts: 2.32 us -> 0.03 us
    another operation x2 -> x0, local copies, waits for them, and re-layouts: 2.14 us -> none  [body(): head = jnp.stack([f[:, :2, :] for f in fields])]
  transfers between devices with their start and end apart: 4 -> 11, of which waited for: 3 -> 7; matrix products, arithmetic and copies ran while one was open for 0% -> 0% of each run, Pallas kernels for 12% -> 13%
where the time goes in v3:
time: 90 us; the launch traced here: 89.6 us
  blocking collectives  33.1 us (37%)
  Pallas kernels  24 us (27%)
  starting transfers between devices  20.6 us (23%)
  waiting for transfers between devices  11.2 us (12%)
    all_to_all x1, blocking collectives, exchange(): return lax.all_to_all(array, axes, 0, 0, tiled=True)  33.1 us
    pallas_call x9, Pallas kernels, run(): return kernel(*near)  24 us
    ppermute x7, starting transfers between devices, hop(): lax.ppermute(buffers[o], axis, [(i, i + ((i // step % size + o) % size -...  10.3 us
    ppermute x7, waiting for transfers between devices, hop(): lax.ppermute(buffers[o], axis, [(i, i + ((i // step % size + o) % size -...  9.95 us
    all_to_all x2, starting transfers between devices, exchange(): return lax.all_to_all(array, axes, 0, 0, tiled=True)  9.66 us
  transfers between devices with their start and end apart: 11, of which 7 were waited for; matrix products, arithmetic and copies ran while one was open for 0% of the time, Pallas kernels for 13%

profile of v3, /device:TPU:0, one launch (start us, length us, event | category | flops | bytes accessed | tf_op | source)
XLA Modules:
  0.0 89.6 jit_solution(10867778856730274144)
XLA Ops:
  0.6 1.4 %shard_map.138 = (f32[4,32,1024]{2,1,0:T(8,128)S(1)}, f32[4,32,1024]{2,1,0:T(8,128)S(1)}, f32[4,32,1024]{2,1,0:T(8,128)S(1)}, f32[3,4,2,1024]{3,2,1,0:T(2,128)S(1)}, f32[3,4,2,1024]{3,2,1,0:T(2,128)S(1)}) custom-call(f32[4,32,1024]{2,1,0:T(8,128)} %rho.1, f32[4,32,1024]{2,1,0:T(8,128)} %ur.1, f32[4,32,1024]{2,1,0:T(8,128)} %up.1), custom_call_target="tpu_custom_call" | custom-call | bytes 1572864 | tf_op jit(solution)/shard_map/pallas_call | solution.py:499
  2.0 0.6 collective-permute-start
  2.6 0.1 collective-permute-start.1
  2.7 0.9 collective-permute-done.low
  3.5 0.4 collective-permute-done.1.high
  3.9 6.1 %shard_map.139 = bf16[16,232,128]{2,1,0:T(8,128)(2,1)} custom-call(f32[4,32,1024]{2,1,0:T(8,128)S(1)} %get-tuple-element.24.rho, f32[4,32,1024]{2,1,0:T(8,128)S(1)} %get-tuple-element.25.ur, f32[4,32,1024]{2,1,0:T(8,128)S(1)} %get-tuple-element.26.up, f32[3,4,2,1024]{3,2,1,0:T(2,128)S(1)} %collective-permute-done.low, ...), custom_call_target="tpu_custom_call" | custom-call | flops 39321600 | bytes 3145728 | tf_op jit(solution)/shard_map/pallas_call | solution.py:499
  10.0 0.0 copy-start.1
  10.0 0.0 copy-start.2
  10.0 0.0 copy-start.4
  10.0 33.1 %all_to_all.15.bulk.side = bf16[16,232,128]{2,1,0:T(8,128)(2,1)S(1)} all-to-all(bf16[16,232,128]{2,1,0:T(8,128)(2,1)} %shard_map.139), channel_id=1, replica_groups=mesh['rad'=2,'azi'=16] {'azi'}, dimensions={0} | all-to-all | bytes 1900544 | tf_op jit(solution)/shard_map/all_to_all | solution.py:505
  43.1 0.0 copy-done.1
  43.1 0.0 copy-done.2
  43.1 0.0 copy-done.4
  43.1 3.0 %shard_map.142 = bf16[32,4,128]{2,1,0:T(4,128)(2,1)} custom-call(s32[32]{0:T(128)} %shift.3, f32[32]{0:T(128)} %remainder.3, bf16[16,232,128]{2,1,0:T(8,128)(2,1)S(1)} %all_to_all.15.bulk.side, f32[128,256]{1,0:T(8,128)S(1)} %copy-done.2, f32[128,256]{1,0:T(8,128)S(1)} %copy-done.1, f32[32,128]{1,0:T(8,128)S(1)} %copy-done.4), custom_call_target="tpu_custom_call" | custom-call | flops 100000000 | bytes 1000000 | tf_op jit(solution)/shard_map/pallas_call | solution.py:499
  46.2 2.7 %all-to-all-start.2 = ((bf16[32,4,128]{2,1,0:T(4,128)(2,1)}), bf16[32,4,128]{2,1,0:T(4,128)(2,1)S(1)}, u32[]{:S(2)}, u32[]{:S(2)}) async-start(bf16[32,4,128]{2,1,0:T(4,128)(2,1)} %shard_map.142), calls=%async_computation.2 | async-start | bytes 65536 | tf_op jit(solution)/shard_map/all_to_all | solution.py:505
  48.8 8.7 %shard_map.140 = (bf16[16,24,1024]{2,1,0:T(8,128)(2,1)}, f32[8,128]{1,0:T(8,128)S(1)}) custom-call(s32[32]{0:T(128)} %shift.3, f32[32]{0:T(128)} %remainder.3, bf16[16,232,128]{2,1,0:T(8,128)(2,1)S(1)} %all_to_all.15.bulk.side), custom_call_target="tpu_custom_call" | custom-call | flops 19660800 | bytes 1572864 | tf_op jit(solution)/shard_map/pallas_call | solution.py:499
  57.5 0.0 copy-start
  57.5 0.0 all-to-all-done.2.columns
  57.5 7.0 %all-to-all-start.1 = ((bf16[16,24,1024]{2,1,0:T(8,128)(2,1)}), bf16[16,24,1024]{2,1,0:T(8,128)(2,1)S(1)}, u32[]{:S(2)}, u32[]{:S(2)}) async-start(bf16[16,24,1024]{2,1,0:T(8,128)(2,1)} %get-tuple-element.29), calls=%async_computation.1 | async-start | bytes 1572864 | tf_op jit(solution)/shard_map/all_to_all | solution.py:505
  64.5 0.0 copy-done
  64.5 0.7 shard_map.143
  65.2 0.1 collective-permute-start.2
  65.3 1.2 %collective-permute-done.2.rest_1_ = f32[32,128]{1,0:T(8,128)S(1)} collective-permute-done((f32[32,128]{1,0:T(8,128)S(1)}, f32[32,128]{1,0:T(8,128)S(1)}, u32[]{:S(2)}, u32[]{:S(2)}) %collective-permute-start.2) | collective-permute-done | bytes 16416 | tf_op jit(solution)/shard_map/ppermute | solution.py:589
  66.4 0.0 copy-start.3
  66.5 2.0 %collective-permute-start.3 = (f32[16,128]{1,0:T(8,128)S(1)}, f32[16,128]{1,0:T(8,128)S(1)}, u32[]{:S(2)}, u32[]{:S(2)}) collective-permute-start(f32[16,128]{1,0:T(8,128)S(1)} %get-tuple-element.37), channel_id=1, source_target_pairs={{0,1},{1,2},{2,3},{3,0},{4,5},{5,6},{6,7},{7,4},{8,9},{9,10},{10,1... | collective-permute-start | bytes 24584 | tf_op jit(solution)/shard_map/ppermute | solution.py:589
  68.5 1.5 %collective-permute-start.4 = (f32[16,128]{1,0:T(8,128)S(1)}, f32[16,128]{1,0:T(8,128)S(1)}, u32[]{:S(2)}, u32[]{:S(2)}) collective-permute-start(f32[16,128]{1,0:T(8,128)S(1)} %get-tuple-element.38), channel_id=1, source_target_pairs={{0,2},{1,3},{2,0},{3,1},{4,6},{5,7},{6,4},{7,5},{8,10},{9,11},{10,... | collective-permute-start | bytes 24584 | tf_op jit(solution)/shard_map/ppermute | solution.py:589
  69.9 1.5 %collective-permute-start.5 = (f32[16,128]{1,0:T(8,128)S(1)}, f32[16,128]{1,0:T(8,128)S(1)}, u32[]{:S(2)}, u32[]{:S(2)}) collective-permute-start(f32[16,128]{1,0:T(8,128)S(1)} %get-tuple-element.39), channel_id=1, source_target_pairs={{0,3},{1,0},{2,1},{3,2},{4,7},{5,4},{6,5},{7,6},{8,11},{9,8},{10,9... | collective-permute-start | bytes 24584 | tf_op jit(solution)/shard_map/ppermute | solution.py:589
  71.4 0.0 collective-permute-done.3.rest_1_
  71.4 0.8 collective-permute-done.4.rest_2_
  72.2 1.4 %collective-permute-done.5.rest_3_ = f32[16,128]{1,0:T(8,128)S(1)} collective-permute-done((f32[16,128]{1,0:T(8,128)S(1)}, f32[16,128]{1,0:T(8,128)S(1)}, u32[]{:S(2)}, u32[]{:S(2)}) %collective-permute-start.5) | collective-permute-done | bytes 8224 | tf_op jit(solution)/shard_map/ppermute | solution.py:589
  73.7 1.6 %collective-permute-start.6 = (f32[16,128]{1,0:T(8,128)S(1)}, f32[16,128]{1,0:T(8,128)S(1)}, u32[]{:S(2)}, u32[]{:S(2)}) collective-permute-start(f32[16,128]{1,0:T(8,128)S(1)} %get-tuple-element.41), channel_id=1, source_target_pairs={{0,4},{1,5},{2,6},{3,7},{4,8},{5,9},{6,10},{7,11},{8,12},{9,13},{1... | collective-permute-start | bytes 24584 | tf_op jit(solution)/shard_map/ppermute | solution.py:589
  75.2 2.3 %collective-permute-start.7 = (f32[16,128]{1,0:T(8,128)S(1)}, f32[16,128]{1,0:T(8,128)S(1)}, u32[]{:S(2)}, u32[]{:S(2)}) collective-permute-start(f32[16,128]{1,0:T(8,128)S(1)} %get-tuple-element.42), channel_id=1, source_target_pairs={{0,8},{1,9},{2,10},{3,11},{4,12},{5,13},{6,14},{7,15},{8,0},{9,1},... | collective-permute-start | bytes 24584 | tf_op jit(solution)/shard_map/ppermute | solution.py:589
  77.5 1.4 %collective-permute-start.8 = (f32[16,128]{1,0:T(8,128)S(1)}, f32[16,128]{1,0:T(8,128)S(1)}, u32[]{:S(2)}, u32[]{:S(2)}) collective-permute-start(f32[16,128]{1,0:T(8,128)S(1)} %get-tuple-element.43), channel_id=1, source_target_pairs={{0,12},{1,13},{2,14},{3,15},{4,0},{5,1},{6,2},{7,3},{8,4},{9,5},{1... | collective-permute-start | bytes 24584 | tf_op jit(solution)/shard_map/ppermute | solution.py:589
  78.9 3.1 %collective-permute-done.6.rest_1_ = f32[16,128]{1,0:T(8,128)S(1)} collective-permute-done((f32[16,128]{1,0:T(8,128)S(1)}, f32[16,128]{1,0:T(8,128)S(1)}, u32[]{:S(2)}, u32[]{:S(2)}) %collective-permute-start.6) | collective-permute-done | bytes 8224 | tf_op jit(solution)/shard_map/ppermute | solution.py:589
  82.1 3.4 %collective-permute-done.7.rest_2_ = f32[16,128]{1,0:T(8,128)S(1)} collective-permute-done((f32[16,128]{1,0:T(8,128)S(1)}, f32[16,128]{1,0:T(8,128)S(1)}, u32[]{:S(2)}, u32[]{:S(2)}) %collective-permute-start.7) | collective-permute-done | bytes 8224 | tf_op jit(solution)/shard_map/ppermute | solution.py:589
  85.5 0.0 collective-permute-done.8.rest_3_
  85.5 0.0 copy-done.3
  85.5 2.3 %shard_map.146 = f32[2,16384]{1,0:T(2,128)} custom-call(f32[16,128]{1,0:T(8,128)S(1)} %get-tuple-element.40.rest_0_, f32[16,128]{1,0:T(8,128)S(1)} %collective-permute-done.6.rest_1_, f32[16,128]{1,0:T(8,128)S(1)} %collective-permute-done.7.rest_2_, f32[16,128]{1,0:T(8,128)S(1)} %collective-permute-done.8.rest_3_, f32[128,256]{1,0:T(8,128)S(1)} %copy-done.2, ...), custom_call_target="tpu_custom_call" | custom-call | flops 100000000 | bytes 1000000 | tf_op jit(solution)/shard_map/pallas_call | solution.py:499
  87.8 0.0 all-to-all-done.1.bulk
  87.8 1.8 %shard_map.141 = (f32[4,32,1024]{2,1,0:T(8,128)}, f32[4,32,1024]{2,1,0:T(8,128)}, f32[4,32,1024]{2,1,0:T(8,128)}) custom-call(bf16[16,24,1024]{2,1,0:T(8,128)(2,1)S(1)} %all-to-all-done.1.bulk, f32[8,128]{1,0:T(8,128)S(1)} %get-tuple-element.30.top), custom_call_target="tpu_custom_call" | custom-call | flops 7864320 | bytes 2359296 | tf_op jit(solution)/shard_map/pallas_call | solution.py:499
  (2 shorter events, 0.1 us)
Async XLA Ops:
  2.0 1.5 %collective-permute-start = (f32[3,4,2,1024]{3,2,1,0:T(2,128)S(1)}, f32[3,4,2,1024]{3,2,1,0:T(2,128)S(1)}, u32[]{:S(2)}, u32[]{:S(2)}) collective-permute-start(f32[3,4,2,1024]{3,2,1,0:T(2,128)S(1)} %get-tuple-element.27), channel_id=1, source_target_pairs={{0,16},{16,0},{1,17},{17,1},{2,18},{18,2},{3,19},{19,3},{4,20},{20... | collective-permute-start | bytes 294920 | tf_op jit(solution)/shard_map/ppermute | solution.py:543
  2.6 1.3 %collective-permute-start.1 = (f32[3,4,2,1024]{3,2,1,0:T(2,128)S(1)}, f32[3,4,2,1024]{3,2,1,0:T(2,128)S(1)}, u32[]{:S(2)}, u32[]{:S(2)}) collective-permute-start(f32[3,4,2,1024]{3,2,1,0:T(2,128)S(1)} %get-tuple-element.28), channel_id=1, source_target_pairs={{16,0},{0,16},{17,1},{1,17},{18,2},{2,18},{19,3},{3,19},{20,4},{4,... | collective-permute-start | bytes 294920 | tf_op jit(solution)/shard_map/ppermute | solution.py:544
  10.0 33.2 %copy-start.1 = (f32[128,256]{1,0:T(8,128)S(1)}, f32[128,256]{1,0:T(8,128)}, u32[]{:S(2)}) copy-start(f32[128,256]{1,0:T(8,128)} %constant.9.clone.twiddle.rest_5_) | copy-start | bytes 393220
  10.0 33.2 %copy-start.2 = (f32[128,256]{1,0:T(8,128)S(1)}, f32[128,256]{1,0:T(8,128)}, u32[]{:S(2)}) copy-start(f32[128,256]{1,0:T(8,128)} %constant.8.clone.circle.rest_4_) | copy-start | bytes 393220
  10.0 33.1 %copy-start.4 = (f32[32,128]{1,0:T(8,128)S(1)}, f32[32,128]{1,0:T(8,128)}, u32[]{:S(2)}) copy-start(f32[32,128]{1,0:T(8,128)} %constant.10.clone.short) | copy-start | bytes 49156
  46.2 11.4 %all-to-all-start.2 = ((bf16[32,4,128]{2,1,0:T(4,128)(2,1)}), bf16[32,4,128]{2,1,0:T(4,128)(2,1)S(1)}, u32[]{:S(2)}, u32[]{:S(2)}) async-start(bf16[32,4,128]{2,1,0:T(4,128)(2,1)} %shard_map.142), calls=%async_computation.2 | async-start | bytes 65536 | tf_op jit(solution)/shard_map/all_to_all | solution.py:505
  57.5 7.0 %copy-start = (bf16[64,64,64]{2,1,0:T(8,128)(2,1)S(1)}, bf16[64,64,64]{2,1,0:T(8,128)(2,1)}, u32[]{:S(2)}) copy-start(bf16[64,64,64]{2,1,0:T(8,128)(2,1)} %kernel.1) | copy-start | bytes 1572868
  57.5 30.2 %all-to-all-start.1 = ((bf16[16,24,1024]{2,1,0:T(8,128)(2,1)}), bf16[16,24,1024]{2,1,0:T(8,128)(2,1)S(1)}, u32[]{:S(2)}, u32[]{:S(2)}) async-start(bf16[16,24,1024]{2,1,0:T(8,128)(2,1)} %get-tuple-element.29), calls=%async_computation.1 | async-start | bytes 1572864 | tf_op jit(solution)/shard_map/all_to_all | solution.py:505
  65.2 1.2 %collective-permute-start.2 = (f32[32,128]{1,0:T(8,128)S(1)}, f32[32,128]{1,0:T(8,128)S(1)}, u32[]{:S(2)}, u32[]{:S(2)}) collective-permute-start(f32[32,128]{1,0:T(8,128)S(1)} %get-tuple-element.35), channel_id=1, source_target_pairs={{0,16},{16,0},{1,17},{17,1},{2,18},{18,2},{3,19},{19,3},{4,20},{20... | collective-permute-start | bytes 49160 | tf_op jit(solution)/shard_map/ppermute | solution.py:589
  66.4 19.0 %copy-start.3 = (f32[32,256]{1,0:T(8,128)S(1)}, f32[32,256]{1,0:T(8,128)}, u32[]{:S(2)}) copy-start(f32[32,256]{1,0:T(8,128)} %constant.11.clone.rest_6_) | copy-start | bytes 98308
  66.5 4.9 %collective-permute-start.3 = (f32[16,128]{1,0:T(8,128)S(1)}, f32[16,128]{1,0:T(8,128)S(1)}, u32[]{:S(2)}, u32[]{:S(2)}) collective-permute-start(f32[16,128]{1,0:T(8,128)S(1)} %get-tuple-element.37), channel_id=1, source_target_pairs={{0,1},{1,2},{2,3},{3,0},{4,5},{5,6},{6,7},{7,4},{8,9},{9,10},{10,1... | collective-permute-start | bytes 24584 | tf_op jit(solution)/shard_map/ppermute | solution.py:589
  68.5 3.8 %collective-permute-start.4 = (f32[16,128]{1,0:T(8,128)S(1)}, f32[16,128]{1,0:T(8,128)S(1)}, u32[]{:S(2)}, u32[]{:S(2)}) collective-permute-start(f32[16,128]{1,0:T(8,128)S(1)} %get-tuple-element.38), channel_id=1, source_target_pairs={{0,2},{1,3},{2,0},{3,1},{4,6},{5,7},{6,4},{7,5},{8,10},{9,11},{10,... | collective-permute-start | bytes 24584 | tf_op jit(solution)/shard_map/ppermute | solution.py:589
  69.9 3.7 %collective-permute-start.5 = (f32[16,128]{1,0:T(8,128)S(1)}, f32[16,128]{1,0:T(8,128)S(1)}, u32[]{:S(2)}, u32[]{:S(2)}) collective-permute-start(f32[16,128]{1,0:T(8,128)S(1)} %get-tuple-element.39), channel_id=1, source_target_pairs={{0,3},{1,0},{2,1},{3,2},{4,7},{5,4},{6,5},{7,6},{8,11},{9,8},{10,9... | collective-permute-start | bytes 24584 | tf_op jit(solution)/shard_map/ppermute | solution.py:589
  73.7 8.4 %collective-permute-start.6 = (f32[16,128]{1,0:T(8,128)S(1)}, f32[16,128]{1,0:T(8,128)S(1)}, u32[]{:S(2)}, u32[]{:S(2)}) collective-permute-start(f32[16,128]{1,0:T(8,128)S(1)} %get-tuple-element.41), channel_id=1, source_target_pairs={{0,4},{1,5},{2,6},{3,7},{4,8},{5,9},{6,10},{7,11},{8,12},{9,13},{1... | collective-permute-start | bytes 24584 | tf_op jit(solution)/shard_map/ppermute | solution.py:589
  75.2 10.3 %collective-permute-start.7 = (f32[16,128]{1,0:T(8,128)S(1)}, f32[16,128]{1,0:T(8,128)S(1)}, u32[]{:S(2)}, u32[]{:S(2)}) collective-permute-start(f32[16,128]{1,0:T(8,128)S(1)} %get-tuple-element.42), channel_id=1, source_target_pairs={{0,8},{1,9},{2,10},{3,11},{4,12},{5,13},{6,14},{7,15},{8,0},{9,1},... | collective-permute-start | bytes 24584 | tf_op jit(solution)/shard_map/ppermute | solution.py:589
  77.5 8.0 %collective-permute-start.8 = (f32[16,128]{1,0:T(8,128)S(1)}, f32[16,128]{1,0:T(8,128)S(1)}, u32[]{:S(2)}, u32[]{:S(2)}) collective-permute-start(f32[16,128]{1,0:T(8,128)S(1)} %get-tuple-element.43), channel_id=1, source_target_pairs={{0,12},{1,13},{2,14},{3,15},{4,0},{5,1},{6,2},{7,3},{8,4},{9,5},{1... | collective-permute-start | bytes 24584 | tf_op jit(solution)/shard_map/ppermute | solution.py:589

commit v4 on v3

--- a/solution.py
+++ b/solution.py
@@ -45,16 +45,8 @@
     return lax.broadcasted_iota(jnp.int32, shape, 1)
 
 
-def parts_of(value):
-    high = value.astype(BF16).astype(F32)
-    return high, (value - high).astype(BF16).astype(F32)
-
-
-PARTS = 2
-
-
-def joined_parts(tile, per):
-    return tile + pltpu.roll(tile, tile.shape[0] - per, 0)
+def side_rows(per, tiles):
+    return -(-(per * tiles + per) // SUB) * SUB
 
 
 def load_kernel(rho, ur, up, rho_near, ur_near, up_near, tail, head, sems):
@@ -69,7 +61,7 @@
         head[c] = near[:, 0:2, :]
 
 
-def hydro_kernel(per, rho, ur, up, low, high, bulk, field, stage, block, narrow, sems):
+def hydro_kernel(per, rho, ur, up, low, high, bulk, surf, field, stage, block, narrow, sems):
     nz, slab, seg = rho.shape
     width = seg + LANES
     first = 2 * SUB
@@ -155,12 +147,9 @@
 
     largest = lax.fori_loop(2, last_tile, second_section, jnp.zeros((SUB, width), F32))
     peak = jnp.maximum(jnp.max(largest, keepdims=True), 1e-30)
-    peak = sum(parts_of(peak))
     scale = TOP / peak
     dests = SUB // per
     stride = -(-3 * nz * per // SUB) * SUB
-    base = tiles * stride
-    lines = base + PARTS * per * SUB
 
     def send(index):
         at = pl.ds(index * dests, dests)
@@ -185,18 +174,16 @@
                         ]
                 overflow = overflow + pltpu.roll(field[c, z, here, seg:width], 2 + 4 * plane, 1)
         overflow = jnp.where(lane_iota((SUB, LANES)) < LANES // 2, overflow, peak)
-        for part, (tall, over) in enumerate(zip(parts_of(column), parts_of(overflow))):
-            for d in range(dests):
-                dest = (tile - 2) * dests + d
-                for k in range(per):
-                    row = d * per + k
-                    at = base + (part * per + k) * SUB
-                    for b in range(tiles):
-                        block[dest, at + b : at + b + 1, :] = tall[
-                            row : row + 1, b * LANES : (b + 1) * LANES
-                        ]
-                    line = lines + part * per + k
-                    block[dest, line : line + 1, :] = over[row : row + 1, :]
+        for d in range(dests):
+            dest = (tile - 2) * dests + d
+            for k in range(per):
+                row = d * per + k
+                for b in range(tiles):
+                    surf[dest, k * tiles + b : k * tiles + b + 1, :] = column[
+                        row : row + 1, b * LANES : (b + 1) * LANES
+                    ]
+                line = per * tiles + k
+                surf[dest, line : line + 1, :] = overflow[row : row + 1, :]
         for d in range(dests):
             dest = (tile - 2) * dests + d
             narrow[dest] = block[dest].astype(BF16)
@@ -208,18 +195,17 @@
         send(index).wait()
 
 
-def advect_kernel(per, nz, shift, remainder, bulk, out, top, ring, tapped, over):
+def advect_kernel(per, nz, shift, remainder, bulk, sides, out, top, ring, tapped, over):
     sources = bulk.shape[0]
     count = ring.shape[1]
     tiles = count // sources
     group = nz * per
     stride = -(-3 * group // SUB) * SUB
-    lines = tiles * stride + PARTS * per * SUB
     me = lax.axis_index("azi")
 
     def widen(a, peak):
         whole_block = bulk[a].astype(F32)
-        packed = joined_parts(whole_block[lines : lines + SUB, :], per)[0:per, :]
+        packed = sides[a, per * tiles : per * tiles + per, :]
         mine = jnp.where(lane_iota((1, LANES)) >= LANES // 2, packed[0:1, :], 0.0)
         mine = jnp.max(mine, keepdims=True)
         unit = mine * (1.0 / TOP)
@@ -317,15 +303,20 @@
                 ref[z, a * per : (a + 1) * per, :] = value[plane * per : (plane + 1) * per, :]
 
 
-def forward_kernel(per, nz, modes, shift, remainder, side, circle, twiddle, short, out, rows_out):
-    sources = side.shape[0]
+def forward_kernel(per, nz, modes, fast, shift, remainder, circle, twiddle, short, *rest):
+    rad_count = lax.axis_size("rad")
+    hops, outs, (sides, rows_out) = rest[:fast], rest[fast:-2], rest[-2:]
+    azi = lax.axis_index("azi")
+    for o_fast, hop in enumerate(hops):
+        for o_slow in range(hop.shape[0]):
+            from_slow = lax.rem(azi // fast - o_slow + hop.shape[0], hop.shape[0])
+            from_fast = lax.rem(azi % fast - o_fast + fast, fast)
+            sides[from_slow * fast + from_fast] = hop[o_slow]
+    sources = sides.shape[0]
     nq = circle.shape[0]
     tiles = nq // sources
     length = nq * LANES
     upper = modes // nq
-    dests = out.shape[0]
-    base = tiles * (-(-3 * nz * per // SUB) * SUB)
-    lines = base + PARTS * per * SUB
     me = lax.axis_index("azi")
     lane = lane_iota((sources, LANES))
     q_id, a_id = row_iota((nq, sources)), lane_iota((nq, sources))
@@ -334,22 +325,11 @@
     mode = row_iota((upper, nq)) * nq + lane_iota((upper, nq))
     dot = functools.partial(jnp.dot, precision=EXACT, preferred_element_type=F32)
     for k in range(per):
-        folded = [
-            joined_parts(side[a, lines : lines + SUB, :].astype(F32), per)[k : k + 1, :]
-            for a in range(sources)
-        ]
-        packed = jnp.concatenate(folded, axis=0)
+        packed = sides[:, per * tiles + k, :]
         extra = jnp.zeros((sources, LANES), F32)
         for z in range(nz):
             extra = extra + pltpu.roll(packed, LANES - 2 - 4 * z, 1)
-        grid = []
-        for a in range(sources):
-            tile = jnp.zeros((SUB, LANES), F32)
-            for part in range(PARTS):
-                at = base + (part * per + k) * SUB
-                tile = tile + side[a, at : at + SUB, :].astype(F32)
-            grid.append(tile[0:tiles, :])
-        grid = jnp.concatenate(grid, axis=0)
+        grid = sides[:, k * tiles : (k + 1) * tiles, :].reshape(nq, LANES)
         grid = grid + dot(to_after, jnp.where(lane < 2, extra, 0.0))
         grid = grid + dot(to_before, jnp.where(lane >= LANES - 2, extra, 0.0))
         inner = dot(grid.T, circle[...])
@@ -377,9 +357,17 @@
             gain_sin = gain_sin + weight * jnp.sin(angle)
         rows_out[:, k, :] = real * gain_cos + imag * gain_sin
         rows_out[:, per + k, :] = imag * gain_cos - real * gain_sin
-    share = dests // upper
-    for d in range(dests):
-        out[d] = rows_out[d // share, 0 : 2 * per, :].astype(BF16)
+    share = rad_count * sources // upper
+    width = upper // rad_count
+    rad = lax.axis_index("rad")
+    slabs = [
+        jnp.concatenate(
+            [rows_out[i * width + a // share].astype(BF16).astype(F32) for a in range(sources)], axis=0
+        )
+        for i in range(rad_count)
+    ]
+    for offset, out in enumerate(outs):
+        out[...] = pick(slabs, lax.rem(rad + offset, rad_count))
 
 
 def pick(values, index):
@@ -405,19 +393,37 @@
         out[...] = pick(choices, lax.rem(index + offset, size))
 
 
-def couple_kernel(per, local, columns, kernel, *rest):
-    outs, lines = rest[:-1], rest[-1]
-    sources, _, nq = columns.shape
+def arrival_source(slow, fast, axis_iota):
+    rad_count = lax.axis_size("rad")
+    azi, rad = lax.axis_index("azi"), lax.axis_index("rad")
+    from_rad = lax.rem(rad - axis_iota % rad_count + rad_count, rad_count)
+    from_fast = lax.rem(azi % fast - axis_iota // rad_count % fast + fast, fast)
+    from_slow = lax.rem(azi // fast - axis_iota // (rad_count * fast) % slow + slow, slow)
+    return (from_rad * slow + from_slow) * fast + from_fast
+
+
+def couple_kernel(per, local, fast, slow, kernel, *rest):
+    columns, outs = rest[:slow], rest[slow:]
+    rad_count = lax.axis_size("rad")
+    sources = slow * fast * rad_count
+    nq = columns[0].shape[1]
     total = sources * per
     me = lax.axis_index("rad") * lax.axis_size("azi") + lax.axis_index("azi")
     offset = lax.rem(me * local, nq)
     row, col = row_iota((total, total)), lane_iota((total, total))
-    spread = (row == lax.rem(col, sources) * per + col // sources).astype(F32)
-    lines[...] = columns[...].astype(F32)
+    source = arrival_source(slow, fast, col % sources)
+    spread = (row == source * per + col // sources).astype(F32)
     lane = lane_iota((total, nq))
     sides = []
     for c in range(2):
-        stacked = jnp.concatenate([lines[:, c * per + k, :] for k in range(per)], axis=0)
+        stacked = jnp.concatenate(
+            [
+                ref[pl.ds(c * per + k, fast * rad_count, stride=2 * per), :]
+                for k in range(per)
+                for ref in columns
+            ],
+            axis=0,
+        )
         ordered = jnp.dot(spread, stacked, preferred_element_type=F32)
         sides.append(pltpu.roll(ordered, lax.rem(nq - offset + c * local, nq), 1))
     weights = jnp.where(lane < local, sides[0], sides[1]).astype(BF16)
@@ -444,12 +450,7 @@
     block_id = row_iota((count, nq))
     first = (block_id == 0) & (lane_iota((count, nq)) % local == 0)
     factor = jnp.where(first, 1.0, 2.0) / length
-    azi, rad = lax.axis_index("azi"), lax.axis_index("rad")
-    place = lane_iota((count, count))
-    from_rad = lax.rem(rad - place % rad_count + rad_count, rad_count)
-    from_fast = lax.rem(azi % fast - place // rad_count % fast + fast, fast)
-    from_slow = lax.rem(azi // fast - place // (rad_count * fast) + slow, slow)
-    source = (from_rad * slow + from_slow) * fast + from_fast
+    source = arrival_source(slow, fast, lane_iota((count, count)))
     order = (source == row_iota((count, count))).astype(F32)
     for k in range(per):
         picked = [
@@ -523,10 +524,10 @@
     width = seg + LANES
     group = nz * per
     stride = -(-3 * group // SUB) * SUB
-    rows = tiles * stride + PARTS * per * SUB + SUB
+    rows = tiles * stride
+    side = side_rows(per, tiles)
     fast = min(4, azi)
     slow = azi // fast
-    both = ("rad", "azi")
     vmem, smem = pl.BlockSpec(memory_space=pltpu.VMEM), pl.BlockSpec(memory_space=pltpu.SMEM)
 
     fields = (density, radial_velocity, azimuthal_velocity)
@@ -542,10 +543,10 @@
     )(*fields)
     low = lax.ppermute(tail, "rad", [(i, (i + 1) % rad) for i in range(rad)])
     high = lax.ppermute(head, "rad", [((i + 1) % rad, i) for i in range(rad)])
-    bulk = call(
+    bulk, surf = call(
         functools.partial(hydro_kernel, per),
-        shape_of((azi, rows, LANES), BF16),
-        out_specs=anywhere,
+        (shape_of((azi, rows, LANES), BF16), pltpu.VMEM((azi, side, LANES), F32)),
+        out_specs=(anywhere, vmem),
         scratch=(
             pltpu.VMEM((3, nz, slab + 4 * SUB, width), F32),
             pltpu.VMEM((3, nz, slab + 4 * SUB, width), F32),
@@ -558,31 +559,6 @@
         bytes_accessed=24 * nz * slab * seg,
     )(*fields, low, high)
 
-    bulk = exchange(bulk, "azi")
-
-    k_id, l_id = np.arange(nq), np.arange(LANES)
-    circle = np.concatenate(cos_sin(k_id, k_id, nq), axis=1)
-    twiddle = np.concatenate(cos_sin(l_id, k_id, length), axis=1)
-    short = np.concatenate(cos_sin(np.arange(upper), l_id, LANES), axis=0)
-    spectrum = call(
-        functools.partial(forward_kernel, per, nz, modes),
-        pltpu.VMEM((devices, 2 * per, nq), BF16),
-        in_specs=[smem, smem, vmem, vmem, vmem, vmem],
-        scratch=(pltpu.VMEM((upper, 2 * per, nq), F32),),
-        name="forward",
-        flops=100_000_000,
-        bytes_accessed=1_000_000,
-    )(cycle_shift, remainder, bulk, jnp.asarray(circle), jnp.asarray(twiddle), jnp.asarray(short))
-    columns = exchange(spectrum, both)
-    blocks = call(
-        functools.partial(couple_kernel, per, local),
-        tuple(pltpu.VMEM((azi * per, nq), F32) for _ in range(rad)),
-        scratch=(pltpu.VMEM((devices, 2 * per, nq), F32),),
-        name="couple",
-        flops=100_000_000,
-        bytes_accessed=1_000_000,
-    )(columns, kernel)
-
     def hop(buffers, axis, size, step):
         around = range(lax.axis_size(axis))
         return [buffers[0]] + [
@@ -594,21 +570,54 @@
             for o in range(1, size)
         ]
 
-    blocks = hop(blocks, "rad", rad, 1)
-    for size, middle, where, step, name in (
-        (fast, slow, lambda: lax.axis_index("azi") % fast, 1, "fast"),
-        (slow, fast * rad // fast, lambda: lax.axis_index("azi") // fast, fast, "slow"),
-    ):
-        lines = len(blocks) * blocks[0].shape[0] // size
-        middle = blocks[0].shape[0] // (size * per)
-        blocks = call(
-            functools.partial(route_kernel, size, middle, per, where),
-            tuple(pltpu.VMEM((lines, nq), F32) for _ in range(size)),
-            scratch=(pltpu.VMEM((size, lines, nq), F32),),
+    def route(buffers, size, inner, step, name):
+        count = buffers[0].shape[0]
+        lines = len(buffers) * count // size
+        where = lambda: lax.axis_index("azi") // step % size
+        buffers = call(
+            functools.partial(route_kernel, size, count // (size * inner), inner, where),
+            tuple(pltpu.VMEM((lines, LANES), F32) for _ in range(size)),
+            scratch=(pltpu.VMEM((size, lines, LANES), F32),),
             name="route_" + name,
             bytes_accessed=100_000,
-        )(*blocks)
-        blocks = hop(blocks, "azi", size, step)
+        )(*buffers)
+        return hop(buffers, "azi", size, step)
+
+    surf = [surf.reshape(azi * side, LANES)]
+    surf = route(surf, slow, fast * side, fast, "surf_slow")
+    bulk = exchange(bulk, "azi")
+    surf = route(surf, fast, side, 1, "surf_fast")
+    surf = [x.reshape(slow, side, LANES) for x in surf]
+
+    k_id, l_id = np.arange(nq), np.arange(LANES)
+    circle = np.concatenate(cos_sin(k_id, k_id, nq), axis=1)
+    twiddle = np.concatenate(cos_sin(l_id, k_id, length), axis=1)
+    short = np.concatenate(cos_sin(np.arange(upper), l_id, LANES), axis=0)
+    *spectrum, sides = call(
+        functools.partial(forward_kernel, per, nz, modes, fast),
+        (
+            *(pltpu.VMEM((azi * 2 * per, nq), F32) for _ in range(rad)),
+            pltpu.VMEM((azi, side, LANES), F32),
+        ),
+        in_specs=[smem, smem] + [vmem] * (3 + fast),
+        scratch=(pltpu.VMEM((upper, 2 * per, nq), F32),),
+        name="forward",
+        flops=100_000_000,
+        bytes_accessed=1_000_000,
+    )(cycle_shift, remainder, jnp.asarray(circle), jnp.asarray(twiddle), jnp.asarray(short), *surf)
+    columns = hop(spectrum, "rad", rad, 1)
+    columns = route(columns, fast, 2 * per, 1, "column_fast")
+    columns = route(columns, slow, 2 * per, fast, "column_slow")
+    blocks = call(
+        functools.partial(couple_kernel, per, local, fast, slow),
+        tuple(pltpu.VMEM((azi * per, nq), F32) for _ in range(rad)),
+        name="couple",
+        flops=100_000_000,
+        bytes_accessed=1_000_000,
+    )(kernel, *columns)
+    blocks = hop(blocks, "rad", rad, 1)
+    blocks = route(blocks, fast, per, 1, "block_fast")
+    blocks = route(blocks, slow, per, fast, "block_slow")
     j_of_block = np.arange(devices) * local // nq
     mixed = np.concatenate(cos_sin(j_of_block, l_id, LANES), axis=1)
     turn = np.concatenate(cos_sin(k_id, l_id, length), axis=1)
@@ -623,7 +632,7 @@
     moved, top = call(
         functools.partial(advect_kernel, per, nz),
         (pltpu.VMEM((azi, 3 * group, seg), BF16), pltpu.VMEM((SUB, LANES), F32)),
-        in_specs=[smem, smem, vmem],
+        in_specs=[smem, smem, vmem, vmem],
         scratch=(
             pltpu.VMEM((3, nq, group, LANES), F32),
             pltpu.VMEM((3, nq, group, LANES), F32),
@@ -632,7 +641,7 @@
         name="advect",
         flops=50 * 3 * nz * slab * seg,
         bytes_accessed=12 * nz * slab * seg,
-    )(cycle_shift, remainder, bulk)
+    )(cycle_shift, remainder, bulk, sides)
     moved = exchange(moved, "azi")
     results = call(
         functools.partial(settle_kernel, per),

time: 90 us -> 104 us (1.16)
  blocking collectives: 33.1 us -> 0 us
  waiting for transfers between devices: 11.2 us -> 36.9 us
  starting transfers between devices: 20.6 us -> 42.7 us
    all_to_all x1 -> x0, blocking collectives: 33.1 us -> none  [exchange(): return lax.all_to_all(array, axes, 0, 0, tiled=True)]
    ppermute x7 -> x20, waiting for transfers between devices: 9.95 us -> 35.6 us  [hop(): lax.ppermute(buffers[o], axis, [(i, i + ((i // step % size + o) % size -...]
    ppermute x7 -> x20, starting transfers between devices: 10.3 us -> 28.8 us  [hop(): lax.ppermute(buffers[o], axis, [(i, i + ((i // step % size + o) % size -...]
    all_to_all x2, starting transfers between devices: 9.66 us -> 13.3 us  [exchange(): return lax.all_to_all(array, axes, 0, 0, tiled=True)]
    pallas_call x9 -> x13, Pallas kernels: 24 us -> 23.4 us  [run(): return kernel(*near)]
  transfers between devices with their start and end apart: 11 -> 24, of which waited for: 7 -> 18; matrix products, arithmetic and copies ran while one was open for 0% -> 0% of each run, Pallas kernels for 13% -> 5%
where the time goes in v4:
time: 104 us
  starting transfers between devices  42.7 us (41%)
  waiting for transfers between devices  36.9 us (35%)
  Pallas kernels  23.4 us (22%)
    ppermute x20, waiting for transfers between devices, hop(): lax.ppermute(buffers[o], axis, [(i, i + ((i // step % size + o) % size -...  35.6 us
    ppermute x20, starting transfers between devices, hop(): lax.ppermute(buffers[o], axis, [(i, i + ((i // step % size + o) % size -...  28.8 us
    pallas_call x13, Pallas kernels, run(): return kernel(*near)  23.4 us
    all_to_all x2, starting transfers between devices, exchange(): return lax.all_to_all(array, axes, 0, 0, tiled=True)  13.3 us
  transfers between devices with their start and end apart: 24, of which 18 were waited for; matrix products, arithmetic and copies ran while one was open for 0% of the time, Pallas kernels for 5%

profile of v4, /device:TPU:0, one launch (start us, length us, event | category | flops | bytes accessed | tf_op | source)
XLA Modules:
  0.0 103.7 jit_solution(15576465522891494029)
XLA Ops:
  0.6 1.4 %shard_map.138 = (f32[4,32,1024]{2,1,0:T(8,128)S(1)}, f32[4,32,1024]{2,1,0:T(8,128)S(1)}, f32[4,32,1024]{2,1,0:T(8,128)S(1)}, f32[3,4,2,1024]{3,2,1,0:T(2,128)S(1)}, f32[3,4,2,1024]{3,2,1,0:T(2,128)S(1)}) custom-call(f32[4,32,1024]{2,1,0:T(8,128)} %rho.1, f32[4,32,1024]{2,1,0:T(8,128)} %ur.1, f32[4,32,1024]{2,1,0:T(8,128)} %up.1), custom_call_target="tpu_custom_call" | custom-call | bytes 1572864 | tf_op jit(solution)/shard_map/pallas_call | solution.py:500
  2.0 0.6 collective-permute-start
  2.6 0.1 collective-permute-start.1
  2.7 0.9 collective-permute-done.low
  3.5 0.4 collective-permute-done.1.high
  3.9 5.9 %shard_map.139 = (bf16[16,192,128]{2,1,0:T(8,128)(2,1)}, f32[16,24,128]{2,1,0:T(8,128)S(1)}) custom-call(f32[4,32,1024]{2,1,0:T(8,128)S(1)} %get-tuple-element.45.rho, f32[4,32,1024]{2,1,0:T(8,128)S(1)} %get-tuple-element.46.ur, f32[4,32,1024]{2,1,0:T(8,128)S(1)} %get-tuple-element.47.up, f32[3,4,2,1024]{3,2,1,0:T(2,128)S(1)} %collective-permute-done.low, ...), custom_call_target="tpu_custom_call" | custom-call | flops 39321600 | bytes 3145728 | tf_op jit(solution)/shard_map/pallas_call | solution.py:500
  9.8 8.0 %all-to-all-start = ((bf16[16,192,128]{2,1,0:T(8,128)(2,1)}), bf16[16,192,128]{2,1,0:T(8,128)(2,1)S(1)}, u32[]{:S(2)}, u32[]{:S(2)}) async-start(bf16[16,192,128]{2,1,0:T(8,128)(2,1)} %get-tuple-element.50), calls=%async_computation | async-start | bytes 1572864 | tf_op jit(solution)/shard_map/all_to_all | solution.py:506
  17.9 0.0 copy-start.2
  17.9 0.0 copy-start.1
  17.9 2.0 %collective-permute-start.2 = (f32[96,128]{1,0:T(8,128)S(1)}, f32[96,128]{1,0:T(8,128)S(1)}, u32[]{:S(2)}, u32[]{:S(2)}) collective-permute-start(f32[96,128]{1,0:T(8,128)S(1)} %get-tuple-element.53), channel_id=1, source_target_pairs={{0,4},{1,5},{2,6},{3,7},{4,8},{5,9},{6,10},{7,11},{8,12},{9,13},{1... | collective-permute-start | bytes 147464 | tf_op jit(solution)/shard_map/ppermute | solution.py:565
  19.9 2.4 %collective-permute-start.3 = (f32[96,128]{1,0:T(8,128)S(1)}, f32[96,128]{1,0:T(8,128)S(1)}, u32[]{:S(2)}, u32[]{:S(2)}) collective-permute-start(f32[96,128]{1,0:T(8,128)S(1)} %get-tuple-element.54), channel_id=1, source_target_pairs={{0,8},{1,9},{2,10},{3,11},{4,12},{5,13},{6,14},{7,15},{8,0},{9,1},... | collective-permute-start | bytes 147464 | tf_op jit(solution)/shard_map/ppermute | solution.py:565
  22.3 1.5 %collective-permute-start.4 = (f32[96,128]{1,0:T(8,128)S(1)}, f32[96,128]{1,0:T(8,128)S(1)}, u32[]{:S(2)}, u32[]{:S(2)}) collective-permute-start(f32[96,128]{1,0:T(8,128)S(1)} %get-tuple-element.55), channel_id=1, source_target_pairs={{0,12},{1,13},{2,14},{3,15},{4,0},{5,1},{6,2},{7,3},{8,4},{9,5},{1... | collective-permute-start | bytes 147464 | tf_op jit(solution)/shard_map/ppermute | solution.py:565
  23.7 13.4 %collective-permute-done.2.rest_1_ = f32[96,128]{1,0:T(8,128)S(1)} collective-permute-done((f32[96,128]{1,0:T(8,128)S(1)}, f32[96,128]{1,0:T(8,128)S(1)}, u32[]{:S(2)}, u32[]{:S(2)}) %collective-permute-start.2) | collective-permute-done | bytes 49184 | tf_op jit(solution)/shard_map/ppermute | solution.py:565
  37.1 5.0 %collective-permute-done.3.rest_2_ = f32[96,128]{1,0:T(8,128)S(1)} collective-permute-done((f32[96,128]{1,0:T(8,128)S(1)}, f32[96,128]{1,0:T(8,128)S(1)}, u32[]{:S(2)}, u32[]{:S(2)}) %collective-permute-start.3) | collective-permute-done | bytes 49184 | tf_op jit(solution)/shard_map/ppermute | solution.py:565
  42.1 0.0 collective-permute-done.4.rest_3_
  42.1 0.0 copy-start.4
  42.2 1.5 %collective-permute-start.5 = (f32[96,128]{1,0:T(8,128)S(1)}, f32[96,128]{1,0:T(8,128)S(1)}, u32[]{:S(2)}, u32[]{:S(2)}) collective-permute-start(f32[96,128]{1,0:T(8,128)S(1)} %get-tuple-element.57), channel_id=1, source_target_pairs={{0,1},{1,2},{2,3},{3,0},{4,5},{5,6},{6,7},{7,4},{8,9},{9,10},{10,1... | collective-permute-start | bytes 147464 | tf_op jit(solution)/shard_map/ppermute | solution.py:565
  43.7 1.5 %collective-permute-start.6 = (f32[96,128]{1,0:T(8,128)S(1)}, f32[96,128]{1,0:T(8,128)S(1)}, u32[]{:S(2)}, u32[]{:S(2)}) collective-permute-start(f32[96,128]{1,0:T(8,128)S(1)} %get-tuple-element.58), channel_id=1, source_target_pairs={{0,2},{1,3},{2,0},{3,1},{4,6},{5,7},{6,4},{7,5},{8,10},{9,11},{10,... | collective-permute-start | bytes 147464 | tf_op jit(solution)/shard_map/ppermute | solution.py:565
  45.2 1.5 %collective-permute-start.7 = (f32[96,128]{1,0:T(8,128)S(1)}, f32[96,128]{1,0:T(8,128)S(1)}, u32[]{:S(2)}, u32[]{:S(2)}) collective-permute-start(f32[96,128]{1,0:T(8,128)S(1)} %get-tuple-element.59), channel_id=1, source_target_pairs={{0,3},{1,0},{2,1},{3,2},{4,7},{5,4},{6,5},{7,6},{8,11},{9,8},{10,9... | collective-permute-start | bytes 147464 | tf_op jit(solution)/shard_map/ppermute | solution.py:565
  46.6 0.6 collective-permute-done.5
  47.2 0.6 collective-permute-done.6
  47.8 1.5 %collective-permute-done.7 = f32[96,128]{1,0:T(8,128)S(1)} collective-permute-done((f32[96,128]{1,0:T(8,128)S(1)}, f32[96,128]{1,0:T(8,128)S(1)}, u32[]{:S(2)}, u32[]{:S(2)}) %collective-permute-start.7) | collective-permute-done | bytes 49184 | tf_op jit(solution)/shard_map/ppermute | solution.py:565
  49.2 0.0 copy-done.2
  49.2 0.0 copy-done.1
  49.2 0.0 copy-done.4
  49.3 2.4 %shard_map.142 = (f32[64,128]{1,0:T(8,128)S(1)}, f32[64,128]{1,0:T(8,128)S(1)}, f32[16,24,128]{2,1,0:T(8,128)S(1)}) custom-call(s32[32]{0:T(128)} %shift.3, f32[32]{0:T(128)} %remainder.3, f32[128,256]{1,0:T(8,128)S(1)} %copy-done.2, f32[128,256]{1,0:T(8,128)S(1)} %copy-done.1, f32[32,128]{1,0:T(8,128)S(1)} %copy-done.4, f32[4,24,128]{2,1,0:T(8,128)S(1)} %bitcast.6, ...), custom_call_target="tpu_custom_call" | custom-call | flops 100000000 | bytes 1000000 | tf_op jit(solution)/shard_map/pallas_call | solution.py:500
  51.7 0.0 all-to-all-done.bulk
  51.7 8.7 %shard_map.143 = (bf16[16,24,1024]{2,1,0:T(8,128)(2,1)}, f32[8,128]{1,0:T(8,128)S(1)}) custom-call(s32[32]{0:T(128)} %shift.3, f32[32]{0:T(128)} %remainder.3, bf16[16,192,128]{2,1,0:T(8,128)(2,1)S(1)} %all-to-all-done.bulk, f32[16,24,128]{2,1,0:T(8,128)S(1)} %get-tuple-element.60.sides), custom_call_target="tpu_custom_call" | custom-call | flops 19660800 | bytes 1572864 | tf_op jit(solution)/shard_map/pallas_call | solution.py:500
  60.4 0.0 copy-start
  60.4 5.2 %all-to-all-start.1 = ((bf16[16,24,1024]{2,1,0:T(8,128)(2,1)}), bf16[16,24,1024]{2,1,0:T(8,128)(2,1)S(1)}, u32[]{:S(2)}, u32[]{:S(2)}) async-start(bf16[16,24,1024]{2,1,0:T(8,128)(2,1)} %get-tuple-element.61), calls=%async_computation.1 | async-start | bytes 1572864 | tf_op jit(solution)/shard_map/all_to_all | solution.py:506
  65.6 0.1 collective-permute-start.8
  65.7 1.2 %collective-permute-done.8.rest_1_ = f32[64,128]{1,0:T(8,128)S(1)} collective-permute-done((f32[64,128]{1,0:T(8,128)S(1)}, f32[64,128]{1,0:T(8,128)S(1)}, u32[]{:S(2)}, u32[]{:S(2)}) %collective-permute-start.8) | collective-permute-done | bytes 32800 | tf_op jit(solution)/shard_map/ppermute | solution.py:565
  66.9 1.9 %collective-permute-start.9 = (f32[32,128]{1,0:T(8,128)S(1)}, f32[32,128]{1,0:T(8,128)S(1)}, u32[]{:S(2)}, u32[]{:S(2)}) collective-permute-start(f32[32,128]{1,0:T(8,128)S(1)} %get-tuple-element.69), channel_id=1, source_target_pairs={{0,1},{1,2},{2,3},{3,0},{4,5},{5,6},{6,7},{7,4},{8,9},{9,10},{10,1... | collective-permute-start | bytes 49160 | tf_op jit(solution)/shard_map/ppermute | solution.py:565
  68.9 1.5 %collective-permute-start.10 = (f32[32,128]{1,0:T(8,128)S(1)}, f32[32,128]{1,0:T(8,128)S(1)}, u32[]{:S(2)}, u32[]{:S(2)}) collective-permute-start(f32[32,128]{1,0:T(8,128)S(1)} %get-tuple-element.70), channel_id=1, source_target_pairs={{0,2},{1,3},{2,0},{3,1},{4,6},{5,7},{6,4},{7,5},{8,10},{9,11},{10,... | collective-permute-start | bytes 49160 | tf_op jit(solution)/shard_map/ppermute | solution.py:565
  70.3 1.5 %collective-permute-start.11 = (f32[32,128]{1,0:T(8,128)S(1)}, f32[32,128]{1,0:T(8,128)S(1)}, u32[]{:S(2)}, u32[]{:S(2)}) collective-permute-start(f32[32,128]{1,0:T(8,128)S(1)} %get-tuple-element.71), channel_id=1, source_target_pairs={{0,3},{1,0},{2,1},{3,2},{4,7},{5,4},{6,5},{7,6},{8,11},{9,8},{10,9... | collective-permute-start | bytes 49160 | tf_op jit(solution)/shard_map/ppermute | solution.py:565
  71.8 2.1 %collective-permute-done.9.rest_1_ = f32[32,128]{1,0:T(8,128)S(1)} collective-permute-done((f32[32,128]{1,0:T(8,128)S(1)}, f32[32,128]{1,0:T(8,128)S(1)}, u32[]{:S(2)}, u32[]{:S(2)}) %collective-permute-start.9) | collective-permute-done | bytes 16416 | tf_op jit(solution)/shard_map/ppermute | solution.py:565
  73.9 0.0 collective-permute-done.10.rest_2_
  73.9 0.3 collective-permute-done.11.rest_3_
  74.2 1.6 %collective-permute-start.12 = (f32[32,128]{1,0:T(8,128)S(1)}, f32[32,128]{1,0:T(8,128)S(1)}, u32[]{:S(2)}, u32[]{:S(2)}) collective-permute-start(f32[32,128]{1,0:T(8,128)S(1)} %get-tuple-element.73), channel_id=1, source_target_pairs={{0,4},{1,5},{2,6},{3,7},{4,8},{5,9},{6,10},{7,11},{8,12},{9,13},{1... | collective-permute-start | bytes 49160 | tf_op jit(solution)/shard_map/ppermute | solution.py:565
  75.8 2.4 %collective-permute-start.13 = (f32[32,128]{1,0:T(8,128)S(1)}, f32[32,128]{1,0:T(8,128)S(1)}, u32[]{:S(2)}, u32[]{:S(2)}) collective-permute-start(f32[32,128]{1,0:T(8,128)S(1)} %get-tuple-element.74), channel_id=1, source_target_pairs={{0,8},{1,9},{2,10},{3,11},{4,12},{5,13},{6,14},{7,15},{8,0},{9,1},... | collective-permute-start | bytes 49160 | tf_op jit(solution)/shard_map/ppermute | solution.py:565
  78.2 1.3 %collective-permute-start.14 = (f32[32,128]{1,0:T(8,128)S(1)}, f32[32,128]{1,0:T(8,128)S(1)}, u32[]{:S(2)}, u32[]{:S(2)}) collective-permute-start(f32[32,128]{1,0:T(8,128)S(1)} %get-tuple-element.75), channel_id=1, source_target_pairs={{0,12},{1,13},{2,14},{3,15},{4,0},{5,1},{6,2},{7,3},{8,4},{9,5},{1... | collective-permute-start | bytes 49160 | tf_op jit(solution)/shard_map/ppermute | solution.py:565
  79.4 1.9 %collective-permute-done.12.rest_1_ = f32[32,128]{1,0:T(8,128)S(1)} collective-permute-done((f32[32,128]{1,0:T(8,128)S(1)}, f32[32,128]{1,0:T(8,128)S(1)}, u32[]{:S(2)}, u32[]{:S(2)}) %collective-permute-start.12) | collective-permute-done | bytes 16416 | tf_op jit(solution)/shard_map/ppermute | solution.py:565
  81.4 3.6 %collective-permute-done.13.rest_2_ = f32[32,128]{1,0:T(8,128)S(1)} collective-permute-done((f32[32,128]{1,0:T(8,128)S(1)}, f32[32,128]{1,0:T(8,128)S(1)}, u32[]{:S(2)}, u32[]{:S(2)}) %collective-permute-start.13) | collective-permute-done | bytes 16416 | tf_op jit(solution)/shard_map/ppermute | solution.py:565
  85.0 0.0 collective-permute-done.14.rest_3_
  85.0 0.0 copy-done
  85.0 0.6 shard_map.147
  85.6 0.1 collective-permute-start.15
  85.7 1.2 %collective-permute-done.15.rest_1_ = f32[32,128]{1,0:T(8,128)S(1)} collective-permute-done((f32[32,128]{1,0:T(8,128)S(1)}, f32[32,128]{1,0:T(8,128)S(1)}, u32[]{:S(2)}, u32[]{:S(2)}) %collective-permute-start.15) | collective-permute-done | bytes 16416 | tf_op jit(solution)/shard_map/ppermute | solution.py:565
  86.9 1.5 %collective-permute-start.16 = (f32[16,128]{1,0:T(8,128)S(1)}, f32[16,128]{1,0:T(8,128)S(1)}, u32[]{:S(2)}, u32[]{:S(2)}) collective-permute-start(f32[16,128]{1,0:T(8,128)S(1)} %get-tuple-element.79), channel_id=1, source_target_pairs={{0,1},{1,2},{2,3},{3,0},{4,5},{5,6},{6,7},{7,4},{8,9},{9,10},{10,1... | collective-permute-start | bytes 24584 | tf_op jit(solution)/shard_map/ppermute | solution.py:565
  88.4 1.5 %collective-permute-start.17 = (f32[16,128]{1,0:T(8,128)S(1)}, f32[16,128]{1,0:T(8,128)S(1)}, u32[]{:S(2)}, u32[]{:S(2)}) collective-permute-start(f32[16,128]{1,0:T(8,128)S(1)} %get-tuple-element.80), channel_id=1, source_target_pairs={{0,2},{1,3},{2,0},{3,1},{4,6},{5,7},{6,4},{7,5},{8,10},{9,11},{10,... | collective-permute-start | bytes 24584 | tf_op jit(solution)/shard_map/ppermute | solution.py:565
  89.9 1.5 %collective-permute-start.18 = (f32[16,128]{1,0:T(8,128)S(1)}, f32[16,128]{1,0:T(8,128)S(1)}, u32[]{:S(2)}, u32[]{:S(2)}) collective-permute-start(f32[16,128]{1,0:T(8,128)S(1)} %get-tuple-element.81), channel_id=1, source_target_pairs={{0,3},{1,0},{2,1},{3,2},{4,7},{5,4},{6,5},{7,6},{8,11},{9,8},{10,9... | collective-permute-start | bytes 24584 | tf_op jit(solution)/shard_map/ppermute | solution.py:565
  91.3 0.2 collective-permute-done.16.rest_1_
  91.5 0.6 collective-permute-done.17.rest_2_
  92.1 1.5 %collective-permute-done.18.rest_3_ = f32[16,128]{1,0:T(8,128)S(1)} collective-permute-done((f32[16,128]{1,0:T(8,128)S(1)}, f32[16,128]{1,0:T(8,128)S(1)}, u32[]{:S(2)}, u32[]{:S(2)}) %collective-permute-start.18) | collective-permute-done | bytes 8224 | tf_op jit(solution)/shard_map/ppermute | solution.py:565
  93.6 0.8 collective-permute-start.19
  94.3 1.5 %collective-permute-start.20 = (f32[16,128]{1,0:T(8,128)S(1)}, f32[16,128]{1,0:T(8,128)S(1)}, u32[]{:S(2)}, u32[]{:S(2)}) collective-permute-start(f32[16,128]{1,0:T(8,128)S(1)} %get-tuple-element.84), channel_id=1, source_target_pairs={{0,8},{1,9},{2,10},{3,11},{4,12},{5,13},{6,14},{7,15},{8,0},{9,1},... | collective-permute-start | bytes 24584 | tf_op jit(solution)/shard_map/ppermute | solution.py:565
  95.8 1.6 %collective-permute-start.21 = (f32[16,128]{1,0:T(8,128)S(1)}, f32[16,128]{1,0:T(8,128)S(1)}, u32[]{:S(2)}, u32[]{:S(2)}) collective-permute-start(f32[16,128]{1,0:T(8,128)S(1)} %get-tuple-element.85), channel_id=1, source_target_pairs={{0,12},{1,13},{2,14},{3,15},{4,0},{5,1},{6,2},{7,3},{8,4},{9,5},{1... | collective-permute-start | bytes 24584 | tf_op jit(solution)/shard_map/ppermute | solution.py:565
  97.4 1.6 %collective-permute-done.19.rest_1_ = f32[16,128]{1,0:T(8,128)S(1)} collective-permute-done((f32[16,128]{1,0:T(8,128)S(1)}, f32[16,128]{1,0:T(8,128)S(1)}, u32[]{:S(2)}, u32[]{:S(2)}) %collective-permute-start.19) | collective-permute-done | bytes 8224 | tf_op jit(solution)/shard_map/ppermute | solution.py:565
  99.1 0.0 collective-permute-done.20.rest_2_
  99.1 0.6 collective-permute-done.21.rest_3_
  99.6 0.0 copy-done.3
  99.6 2.3 %shard_map.150 = f32[2,16384]{1,0:T(2,128)} custom-call(f32[16,128]{1,0:T(8,128)S(1)} %get-tuple-element.82.rest_0_, f32[16,128]{1,0:T(8,128)S(1)} %collective-permute-done.19.rest_1_, f32[16,128]{1,0:T(8,128)S(1)} %collective-permute-done.20.rest_2_, f32[16,128]{1,0:T(8,128)S(1)} %collective-permute-done.21.rest_3_, f32[128,256]{1,0:T(8,128)S(1)} %copy-done.2, ...), custom_call_target="tpu_custom_call" | custom-call | flops 100000000 | bytes 1000000 | tf_op jit(solution)/shard_map/pallas_call | solution.py:500
  101.9 0.0 all-to-all-done.1.bulk
  101.9 1.8 %shard_map.144 = (f32[4,32,1024]{2,1,0:T(8,128)}, f32[4,32,1024]{2,1,0:T(8,128)}, f32[4,32,1024]{2,1,0:T(8,128)}) custom-call(bf16[16,24,1024]{2,1,0:T(8,128)(2,1)S(1)} %all-to-all-done.1.bulk, f32[8,128]{1,0:T(8,128)S(1)} %get-tuple-element.62.top), custom_call_target="tpu_custom_call" | custom-call | flops 7864320 | bytes 2359296 | tf_op jit(solution)/shard_map/pallas_call | solution.py:500
  (7 shorter events, 0.2 us)
Async XLA Ops:
  2.0 1.5 %collective-permute-start = (f32[3,4,2,1024]{3,2,1,0:T(2,128)S(1)}, f32[3,4,2,1024]{3,2,1,0:T(2,128)S(1)}, u32[]{:S(2)}, u32[]{:S(2)}) collective-permute-start(f32[3,4,2,1024]{3,2,1,0:T(2,128)S(1)} %get-tuple-element.48), channel_id=1, source_target_pairs={{0,16},{16,0},{1,17},{17,1},{2,18},{18,2},{3,19},{19,3},{4,20},{20... | collective-permute-start | bytes 294920 | tf_op jit(solution)/shard_map/ppermute | solution.py:544
  2.6 1.3 %collective-permute-start.1 = (f32[3,4,2,1024]{3,2,1,0:T(2,128)S(1)}, f32[3,4,2,1024]{3,2,1,0:T(2,128)S(1)}, u32[]{:S(2)}, u32[]{:S(2)}) collective-permute-start(f32[3,4,2,1024]{3,2,1,0:T(2,128)S(1)} %get-tuple-element.49), channel_id=1, source_target_pairs={{16,0},{0,16},{17,1},{1,17},{18,2},{2,18},{19,3},{3,19},{20,4},{4,... | collective-permute-start | bytes 294920 | tf_op jit(solution)/shard_map/ppermute | solution.py:545
  9.8 41.9 %all-to-all-start = ((bf16[16,192,128]{2,1,0:T(8,128)(2,1)}), bf16[16,192,128]{2,1,0:T(8,128)(2,1)S(1)}, u32[]{:S(2)}, u32[]{:S(2)}) async-start(bf16[16,192,128]{2,1,0:T(8,128)(2,1)} %get-tuple-element.50), calls=%async_computation | async-start | bytes 1572864 | tf_op jit(solution)/shard_map/all_to_all | solution.py:506
  17.9 31.4 %copy-start.2 = (f32[128,256]{1,0:T(8,128)S(1)}, f32[128,256]{1,0:T(8,128)}, u32[]{:S(2)}) copy-start(f32[128,256]{1,0:T(8,128)} %constant.8.clone.circle.rest_4_) | copy-start | bytes 393220
  17.9 31.3 %copy-start.1 = (f32[128,256]{1,0:T(8,128)S(1)}, f32[128,256]{1,0:T(8,128)}, u32[]{:S(2)}) copy-start(f32[128,256]{1,0:T(8,128)} %constant.9.clone.twiddle.rest_5_) | copy-start | bytes 393220
  17.9 19.2 %collective-permute-start.2 = (f32[96,128]{1,0:T(8,128)S(1)}, f32[96,128]{1,0:T(8,128)S(1)}, u32[]{:S(2)}, u32[]{:S(2)}) collective-permute-start(f32[96,128]{1,0:T(8,128)S(1)} %get-tuple-element.53), channel_id=1, source_target_pairs={{0,4},{1,5},{2,6},{3,7},{4,8},{5,9},{6,10},{7,11},{8,12},{9,13},{1... | collective-permute-start | bytes 147464 | tf_op jit(solution)/shard_map/ppermute | solution.py:565
  19.9 22.2 %collective-permute-start.3 = (f32[96,128]{1,0:T(8,128)S(1)}, f32[96,128]{1,0:T(8,128)S(1)}, u32[]{:S(2)}, u32[]{:S(2)}) collective-permute-start(f32[96,128]{1,0:T(8,128)S(1)} %get-tuple-element.54), channel_id=1, source_target_pairs={{0,8},{1,9},{2,10},{3,11},{4,12},{5,13},{6,14},{7,15},{8,0},{9,1},... | collective-permute-start | bytes 147464 | tf_op jit(solution)/shard_map/ppermute | solution.py:565
  22.3 19.8 %collective-permute-start.4 = (f32[96,128]{1,0:T(8,128)S(1)}, f32[96,128]{1,0:T(8,128)S(1)}, u32[]{:S(2)}, u32[]{:S(2)}) collective-permute-start(f32[96,128]{1,0:T(8,128)S(1)} %get-tuple-element.55), channel_id=1, source_target_pairs={{0,12},{1,13},{2,14},{3,15},{4,0},{5,1},{6,2},{7,3},{8,4},{9,5},{1... | collective-permute-start | bytes 147464 | tf_op jit(solution)/shard_map/ppermute | solution.py:565
  42.1 7.1 %copy-start.4 = (f32[32,128]{1,0:T(8,128)S(1)}, f32[32,128]{1,0:T(8,128)}, u32[]{:S(2)}) copy-start(f32[32,128]{1,0:T(8,128)} %constant.10.clone.short) | copy-start | bytes 49156
  42.2 5.0 %collective-permute-start.5 = (f32[96,128]{1,0:T(8,128)S(1)}, f32[96,128]{1,0:T(8,128)S(1)}, u32[]{:S(2)}, u32[]{:S(2)}) collective-permute-start(f32[96,128]{1,0:T(8,128)S(1)} %get-tuple-element.57), channel_id=1, source_target_pairs={{0,1},{1,2},{2,3},{3,0},{4,5},{5,6},{6,7},{7,4},{8,9},{9,10},{10,1... | collective-permute-start | bytes 147464 | tf_op jit(solution)/shard_map/ppermute | solution.py:565
  43.7 4.1 %collective-permute-start.6 = (f32[96,128]{1,0:T(8,128)S(1)}, f32[96,128]{1,0:T(8,128)S(1)}, u32[]{:S(2)}, u32[]{:S(2)}) collective-permute-start(f32[96,128]{1,0:T(8,128)S(1)} %get-tuple-element.58), channel_id=1, source_target_pairs={{0,2},{1,3},{2,0},{3,1},{4,6},{5,7},{6,4},{7,5},{8,10},{9,11},{10,... | collective-permute-start | bytes 147464 | tf_op jit(solution)/shard_map/ppermute | solution.py:565
  45.2 4.1 %collective-permute-start.7 = (f32[96,128]{1,0:T(8,128)S(1)}, f32[96,128]{1,0:T(8,128)S(1)}, u32[]{:S(2)}, u32[]{:S(2)}) collective-permute-start(f32[96,128]{1,0:T(8,128)S(1)} %get-tuple-element.59), channel_id=1, source_target_pairs={{0,3},{1,0},{2,1},{3,2},{4,7},{5,4},{6,5},{7,6},{8,11},{9,8},{10,9... | collective-permute-start | bytes 147464 | tf_op jit(solution)/shard_map/ppermute | solution.py:565
  60.4 24.6 %copy-start = (bf16[64,64,64]{2,1,0:T(8,128)(2,1)S(1)}, bf16[64,64,64]{2,1,0:T(8,128)(2,1)}, u32[]{:S(2)}) copy-start(bf16[64,64,64]{2,1,0:T(8,128)(2,1)} %kernel.1) | copy-start | bytes 1572868
  60.4 41.5 %all-to-all-start.1 = ((bf16[16,24,1024]{2,1,0:T(8,128)(2,1)}), bf16[16,24,1024]{2,1,0:T(8,128)(2,1)S(1)}, u32[]{:S(2)}, u32[]{:S(2)}) async-start(bf16[16,24,1024]{2,1,0:T(8,128)(2,1)} %get-tuple-element.61), calls=%async_computation.1 | async-start | bytes 1572864 | tf_op jit(solution)/shard_map/all_to_all | solution.py:506
  65.6 1.3 %collective-permute-start.8 = (f32[64,128]{1,0:T(8,128)S(1)}, f32[64,128]{1,0:T(8,128)S(1)}, u32[]{:S(2)}, u32[]{:S(2)}) collective-permute-start(f32[64,128]{1,0:T(8,128)S(1)} %get-tuple-element.67), channel_id=1, source_target_pairs={{0,16},{16,0},{1,17},{17,1},{2,18},{18,2},{3,19},{19,3},{4,20},{20... | collective-permute-start | bytes 98312 | tf_op jit(solution)/shard_map/ppermute | solution.py:565
  66.9 6.9 %collective-permute-start.9 = (f32[32,128]{1,0:T(8,128)S(1)}, f32[32,128]{1,0:T(8,128)S(1)}, u32[]{:S(2)}, u32[]{:S(2)}) collective-permute-start(f32[32,128]{1,0:T(8,128)S(1)} %get-tuple-element.69), channel_id=1, source_target_pairs={{0,1},{1,2},{2,3},{3,0},{4,5},{5,6},{6,7},{7,4},{8,9},{9,10},{10,1... | collective-permute-start | bytes 49160 | tf_op jit(solution)/shard_map/ppermute | solution.py:565
  68.9 5.0 %collective-permute-start.10 = (f32[32,128]{1,0:T(8,128)S(1)}, f32[32,128]{1,0:T(8,128)S(1)}, u32[]{:S(2)}, u32[]{:S(2)}) collective-permute-start(f32[32,128]{1,0:T(8,128)S(1)} %get-tuple-element.70), channel_id=1, source_target_pairs={{0,2},{1,3},{2,0},{3,1},{4,6},{5,7},{6,4},{7,5},{8,10},{9,11},{10,... | collective-permute-start | bytes 49160 | tf_op jit(solution)/shard_map/ppermute | solution.py:565
  70.3 3.8 %collective-permute-start.11 = (f32[32,128]{1,0:T(8,128)S(1)}, f32[32,128]{1,0:T(8,128)S(1)}, u32[]{:S(2)}, u32[]{:S(2)}) collective-permute-start(f32[32,128]{1,0:T(8,128)S(1)} %get-tuple-element.71), channel_id=1, source_target_pairs={{0,3},{1,0},{2,1},{3,2},{4,7},{5,4},{6,5},{7,6},{8,11},{9,8},{10,9... | collective-permute-start | bytes 49160 | tf_op jit(solution)/shard_map/ppermute | solution.py:565
  74.2 7.2 %collective-permute-start.12 = (f32[32,128]{1,0:T(8,128)S(1)}, f32[32,128]{1,0:T(8,128)S(1)}, u32[]{:S(2)}, u32[]{:S(2)}) collective-permute-start(f32[32,128]{1,0:T(8,128)S(1)} %get-tuple-element.73), channel_id=1, source_target_pairs={{0,4},{1,5},{2,6},{3,7},{4,8},{5,9},{6,10},{7,11},{8,12},{9,13},{1... | collective-permute-start | bytes 49160 | tf_op jit(solution)/shard_map/ppermute | solution.py:565
  75.8 9.2 %collective-permute-start.13 = (f32[32,128]{1,0:T(8,128)S(1)}, f32[32,128]{1,0:T(8,128)S(1)}, u32[]{:S(2)}, u32[]{:S(2)}) collective-permute-start(f32[32,128]{1,0:T(8,128)S(1)} %get-tuple-element.74), channel_id=1, source_target_pairs={{0,8},{1,9},{2,10},{3,11},{4,12},{5,13},{6,14},{7,15},{8,0},{9,1},... | collective-permute-start | bytes 49160 | tf_op jit(solution)/shard_map/ppermute | solution.py:565
  78.2 6.8 %collective-permute-start.14 = (f32[32,128]{1,0:T(8,128)S(1)}, f32[32,128]{1,0:T(8,128)S(1)}, u32[]{:S(2)}, u32[]{:S(2)}) collective-permute-start(f32[32,128]{1,0:T(8,128)S(1)} %get-tuple-element.75), channel_id=1, source_target_pairs={{0,12},{1,13},{2,14},{3,15},{4,0},{5,1},{6,2},{7,3},{8,4},{9,5},{1... | collective-permute-start | bytes 49160 | tf_op jit(solution)/shard_map/ppermute | solution.py:565
  85.6 1.2 %collective-permute-start.15 = (f32[32,128]{1,0:T(8,128)S(1)}, f32[32,128]{1,0:T(8,128)S(1)}, u32[]{:S(2)}, u32[]{:S(2)}) collective-permute-start(f32[32,128]{1,0:T(8,128)S(1)} %get-tuple-element.77), channel_id=1, source_target_pairs={{0,16},{16,0},{1,17},{17,1},{2,18},{18,2},{3,19},{19,3},{4,20},{20... | collective-permute-start | bytes 49160 | tf_op jit(solution)/shard_map/ppermute | solution.py:565
  86.9 12.8 %copy-start.3 = (f32[32,256]{1,0:T(8,128)S(1)}, f32[32,256]{1,0:T(8,128)}, u32[]{:S(2)}) copy-start(f32[32,256]{1,0:T(8,128)} %constant.11.clone.rest_6_) | copy-start | bytes 98308
  86.9 4.6 %collective-permute-start.16 = (f32[16,128]{1,0:T(8,128)S(1)}, f32[16,128]{1,0:T(8,128)S(1)}, u32[]{:S(2)}, u32[]{:S(2)}) collective-permute-start(f32[16,128]{1,0:T(8,128)S(1)} %get-tuple-element.79), channel_id=1, source_target_pairs={{0,1},{1,2},{2,3},{3,0},{4,5},{5,6},{6,7},{7,4},{8,9},{9,10},{10,1... | collective-permute-start | bytes 24584 | tf_op jit(solution)/shard_map/ppermute | solution.py:565
  88.4 3.7 %collective-permute-start.17 = (f32[16,128]{1,0:T(8,128)S(1)}, f32[16,128]{1,0:T(8,128)S(1)}, u32[]{:S(2)}, u32[]{:S(2)}) collective-permute-start(f32[16,128]{1,0:T(8,128)S(1)} %get-tuple-element.80), channel_id=1, source_target_pairs={{0,2},{1,3},{2,0},{3,1},{4,6},{5,7},{6,4},{7,5},{8,10},{9,11},{10,... | collective-permute-start | bytes 24584 | tf_op jit(solution)/shard_map/ppermute | solution.py:565
  89.9 3.7 %collective-permute-start.18 = (f32[16,128]{1,0:T(8,128)S(1)}, f32[16,128]{1,0:T(8,128)S(1)}, u32[]{:S(2)}, u32[]{:S(2)}) collective-permute-start(f32[16,128]{1,0:T(8,128)S(1)} %get-tuple-element.81), channel_id=1, source_target_pairs={{0,3},{1,0},{2,1},{3,2},{4,7},{5,4},{6,5},{7,6},{8,11},{9,8},{10,9... | collective-permute-start | bytes 24584 | tf_op jit(solution)/shard_map/ppermute | solution.py:565
  93.6 5.5 %collective-permute-start.19 = (f32[16,128]{1,0:T(8,128)S(1)}, f32[16,128]{1,0:T(8,128)S(1)}, u32[]{:S(2)}, u32[]{:S(2)}) collective-permute-start(f32[16,128]{1,0:T(8,128)S(1)} %get-tuple-element.83), channel_id=1, source_target_pairs={{0,4},{1,5},{2,6},{3,7},{4,8},{5,9},{6,10},{7,11},{8,12},{9,13},{1... | collective-permute-start | bytes 24584 | tf_op jit(solution)/shard_map/ppermute | solution.py:565
  94.3 4.7 %collective-permute-start.20 = (f32[16,128]{1,0:T(8,128)S(1)}, f32[16,128]{1,0:T(8,128)S(1)}, u32[]{:S(2)}, u32[]{:S(2)}) collective-permute-start(f32[16,128]{1,0:T(8,128)S(1)} %get-tuple-element.84), channel_id=1, source_target_pairs={{0,8},{1,9},{2,10},{3,11},{4,12},{5,13},{6,14},{7,15},{8,0},{9,1},... | collective-permute-start | bytes 24584 | tf_op jit(solution)/shard_map/ppermute | solution.py:565
  95.8 3.8 %collective-permute-start.21 = (f32[16,128]{1,0:T(8,128)S(1)}, f32[16,128]{1,0:T(8,128)S(1)}, u32[]{:S(2)}, u32[]{:S(2)}) collective-permute-start(f32[16,128]{1,0:T(8,128)S(1)} %get-tuple-element.85), channel_id=1, source_target_pairs={{0,12},{1,13},{2,14},{3,15},{4,0},{5,1},{6,2},{7,3},{8,4},{9,5},{1... | collective-permute-start | bytes 24584 | tf_op jit(solution)/shard_map/ppermute | solution.py:565

commit v5 on v4

--- a/solution.py
+++ b/solution.py
@@ -32,9 +32,16 @@
 
 
 def decode(code, scale):
-    size = jnp.abs(code)
-    root = jnp.exp2(jnp.log2(jnp.maximum(size, 1e-37)) * (1.0 / POWER)) * scale
-    return jnp.where(size < 2e-38, 0.0, jnp.where(code < 0.0, -root, root))
+    root = lax.exp2(lax.log(jnp.abs(code)) * (1.0 / (POWER * math.log(2.0)))) * scale
+    return jnp.where(code < 0.0, -root, root)
+
+
+def sent_to(place, offset, size, ring):
+    return (place + offset) % size if ring else place ^ offset
+
+
+def came_from(place, offset, size, ring):
+    return (place - offset + size) % size if ring else place ^ offset
 
 
 def row_iota(shape):
@@ -195,7 +202,16 @@
         send(index).wait()
 
 
-def advect_kernel(per, nz, shift, remainder, bulk, sides, out, top, ring, tapped, over):
+def advect_kernel(
+    per, nz, far_shift, far_remainder, bulk, sides, out, top,
+    ring, tapped, over, codes, shift, remainder, scalar_sems, sems,
+):
+    scalars = [
+        pltpu.make_async_copy(far, near, scalar_sems.at[i])
+        for i, (far, near) in enumerate(((far_shift, shift), (far_remainder, remainder)))
+    ]
+    for copy in scalars:
+        copy.start()
     sources = bulk.shape[0]
     count = ring.shape[1]
     tiles = count // sources
@@ -219,7 +235,7 @@
                 over[c, a, z * per : (z + 1) * per, :] = turned
         return jnp.maximum(peak, mine)
 
-    peak = lax.fori_loop(0, sources, widen, jnp.zeros((1, 1), F32))
+    peak = lax.fori_loop(0, sources, widen, jnp.zeros((1, 1), F32), unroll=2)
     top[...] = jnp.broadcast_to(peak, top.shape)
     lane = lane_iota((group, LANES))
     cycle = row_iota((group, LANES)) % per
@@ -234,6 +250,8 @@
         return carry
 
     lax.fori_loop(0, sources, spill, 0, unroll=4)
+    for copy in scalars:
+        copy.wait()
     x = jnp.zeros((group, LANES), F32)
     whole, part = [], []
     for k in range(per):
@@ -263,8 +281,11 @@
                 )
         return carry
 
-    lax.fori_loop(0, sources, tap, 0)
+    lax.fori_loop(0, sources, tap, 0, unroll=2)
     scale = (TOP / GAIN) / peak
+
+    def send(dest):
+        return pltpu.make_async_copy(codes.at[dest], out.at[dest], sems.at[dest])
 
     def turned_tile(c, k, t):
         source = lax.rem(t - whole[k] + 2 * count, count)
@@ -284,90 +305,113 @@
                     carry[c * per + k] = now
                 pieces[c][b] = encode(joined, scale)
         columns = [jnp.concatenate([pieces[c][b] for b in range(tiles)], axis=1) for c in range(3)]
-        out[dest] = jnp.concatenate(columns, axis=0).astype(BF16)
+        codes[dest] = jnp.concatenate(columns, axis=0).astype(BF16)
+        send(dest).start()
         return tuple(carry)
 
     start = tuple(turned_tile(c, k, -1) for c in range(3) for k in range(per))
-    lax.fori_loop(0, sources, turn, start)
-
-
-def settle_kernel(per, bulk, top, rho, ur, up):
+    lax.fori_loop(0, sources, turn, start, unroll=2)
+    for dest in range(sources):
+        send(dest).wait()
+
+
+def settle_kernel(per, bulk, top, rho, ur, up, near, sems):
     nz = rho.shape[0]
     sources, _, seg = bulk.shape
+    group = nz * per
     unit = jnp.concatenate([top[0:1, :] * (GAIN / TOP)] * (seg // LANES), axis=1)
-    for a in range(sources):
-        value = decode(bulk[a].astype(F32), unit)
-        for c, ref in enumerate((rho, ur, up)):
+    copies = [
+        pltpu.make_async_copy(near.at[c], far, sems.at[c]) for c, far in enumerate((rho, ur, up))
+    ]
+    for c in range(3):
+        for a in range(sources):
+            value = decode(bulk[a, c * group : (c + 1) * group, :].astype(F32), unit)
             for z in range(nz):
-                plane = c * nz + z
-                ref[z, a * per : (a + 1) * per, :] = value[plane * per : (plane + 1) * per, :]
-
-
-def forward_kernel(per, nz, modes, fast, shift, remainder, circle, twiddle, short, *rest):
+                near[c, z, a * per : (a + 1) * per, :] = value[z * per : (z + 1) * per, :]
+        copies[c].start()
+    for copy in copies:
+        copy.wait()
+
+
+def forward_kernel(per, nz, modes, fast, far_shift, far_remainder, circle, twiddle, short, steps, *rest):
     rad_count = lax.axis_size("rad")
-    hops, outs, (sides, rows_out) = rest[:fast], rest[fast:-2], rest[-2:]
+    hops, (out, sides, rows_out, shift, remainder, scalar_sems) = rest[:fast], rest[fast:]
+    scalars = [
+        pltpu.make_async_copy(far, near, scalar_sems.at[i])
+        for i, (far, near) in enumerate(((far_shift, shift), (far_remainder, remainder)))
+    ]
+    for copy in scalars:
+        copy.start()
+    me = lax.axis_index("azi")
     azi = lax.axis_index("azi")
     for o_fast, hop in enumerate(hops):
         for o_slow in range(hop.shape[0]):
-            from_slow = lax.rem(azi // fast - o_slow + hop.shape[0], hop.shape[0])
-            from_fast = lax.rem(azi % fast - o_fast + fast, fast)
+            from_slow = came_from(azi // fast, o_slow, hop.shape[0], True)
+            from_fast = came_from(azi % fast, o_fast, fast, False)
             sides[from_slow * fast + from_fast] = hop[o_slow]
     sources = sides.shape[0]
     nq = circle.shape[0]
     tiles = nq // sources
     length = nq * LANES
     upper = modes // nq
-    me = lax.axis_index("azi")
     lane = lane_iota((sources, LANES))
-    q_id, a_id = row_iota((nq, sources)), lane_iota((nq, sources))
-    to_after = (q_id == lax.rem((a_id + 1) * tiles, nq)).astype(F32)
-    to_before = (q_id == lax.rem(a_id * tiles + nq - 1, nq)).astype(F32)
-    mode = row_iota((upper, nq)) * nq + lane_iota((upper, nq))
+    q_id, a_id = row_iota((nq, 2 * sources)), lane_iota((nq, 2 * sources))
+    after = lax.rem((a_id + 1) * tiles, nq)
+    before = lax.rem((a_id - sources) * tiles + nq - 1, nq)
+    target = (q_id == jnp.where(a_id < sources, after, before)).astype(F32)
     dot = functools.partial(jnp.dot, precision=EXACT, preferred_element_type=F32)
+    spilled = []
     for k in range(per):
         packed = sides[:, per * tiles + k, :]
         extra = jnp.zeros((sources, LANES), F32)
         for z in range(nz):
             extra = extra + pltpu.roll(packed, LANES - 2 - 4 * z, 1)
+        halves = (jnp.where(lane < 2, extra, 0.0), jnp.where(lane >= LANES - 2, extra, 0.0))
+        spilled.append(jnp.concatenate(halves, axis=0))
+    spilled = dot(target, jnp.concatenate(spilled, axis=1))
+    grids = []
+    for k in range(per):
         grid = sides[:, k * tiles : (k + 1) * tiles, :].reshape(nq, LANES)
-        grid = grid + dot(to_after, jnp.where(lane < 2, extra, 0.0))
-        grid = grid + dot(to_before, jnp.where(lane >= LANES - 2, extra, 0.0))
-        inner = dot(grid.T, circle[...])
-        cos_part, sin_part = inner[:, :nq], inner[:, nq:]
-        turn_cos, turn_sin = twiddle[:, :nq], twiddle[:, nq:]
-        real = cos_part * turn_cos - sin_part * turn_sin
-        imag = -(sin_part * turn_cos + cos_part * turn_sin)
-        outer = dot(short[...], jnp.concatenate([real, imag], axis=1))
-        real = outer[:upper, :nq] + outer[upper:, nq:]
-        imag = outer[:upper, nq:] - outer[upper:, :nq]
-        amount = shift[me * per + k]
+        grids.append((grid + spilled[:, k * LANES : (k + 1) * LANES]).T)
+    inner = dot(jnp.concatenate(grids, axis=0), circle[...])
+    turn_cos, turn_sin = twiddle[:, :nq], twiddle[:, nq:]
+    turned = []
+    for k in range(per):
+        cos_part = inner[k * LANES : (k + 1) * LANES, :nq]
+        sin_part = inner[k * LANES : (k + 1) * LANES, nq:]
+        turned.append(cos_part * turn_cos - sin_part * turn_sin)
+        turned.append(-(sin_part * turn_cos + cos_part * turn_sin))
+    outer = dot(short[...], jnp.concatenate(turned, axis=1))
+    for copy in scalars:
+        copy.wait()
+    mode = row_iota((upper, nq)) * nq + lane_iota((upper, nq))
+    cos_one, sin_one = steps[0:upper, :nq], steps[0:upper, nq:]
+    cos_two, sin_two = steps[upper:, :nq], steps[upper:, nq:]
+    for k in range(per):
+        at = 2 * k * nq
+        real = outer[:upper, at : at + nq] + outer[upper:, at + nq : at + 2 * nq]
+        imag = outer[:upper, at + nq : at + 2 * nq] - outer[upper:, at : at + nq]
         x = jnp.full((upper, nq), -remainder[me * per + k], F32)
-        weights = (
-            (-1, x * (x + 1.0) * (x + 2.0) / 6.0),
-            (0, -(x - 1.0) * (x + 1.0) * (x + 2.0) / 2.0),
-            (1, (x - 1.0) * x * (x + 2.0) / 2.0),
-            (2, -(x - 1.0) * x * (x + 1.0) / 6.0),
-        )
-        gain_cos = jnp.zeros((upper, nq), F32)
-        gain_sin = jnp.zeros((upper, nq), F32)
-        for offset, weight in weights:
-            steps = lax.rem(mode * (amount + offset + length), length)
-            angle = steps.astype(F32) * (2.0 * math.pi / length)
-            gain_cos = gain_cos + weight * jnp.cos(angle)
-            gain_sin = gain_sin + weight * jnp.sin(angle)
+        w_next = x * (x + 1.0) * (x + 2.0) / 6.0
+        w_here = -(x - 1.0) * (x + 1.0) * (x + 2.0) / 2.0
+        w_prev = (x - 1.0) * x * (x + 2.0) / 2.0
+        w_prev_two = -(x - 1.0) * x * (x + 1.0) / 6.0
+        tap_cos = w_here + (w_next + w_prev) * cos_one + w_prev_two * cos_two
+        tap_sin = (w_prev - w_next) * sin_one + w_prev_two * sin_two
+        phase = lax.rem(mode * shift[me * per + k], length)
+        phase = jnp.where(phase > length // 2, phase - length, phase)
+        angle = phase.astype(F32) * (2.0 * math.pi / length)
+        spin_cos, spin_sin = jnp.cos(angle), jnp.sin(angle)
+        gain_cos = tap_cos * spin_cos - tap_sin * spin_sin
+        gain_sin = tap_sin * spin_cos + tap_cos * spin_sin
         rows_out[:, k, :] = real * gain_cos + imag * gain_sin
         rows_out[:, per + k, :] = imag * gain_cos - real * gain_sin
     share = rad_count * sources // upper
-    width = upper // rad_count
-    rad = lax.axis_index("rad")
-    slabs = [
-        jnp.concatenate(
-            [rows_out[i * width + a // share].astype(BF16).astype(F32) for a in range(sources)], axis=0
-        )
-        for i in range(rad_count)
-    ]
-    for offset, out in enumerate(outs):
-        out[...] = pick(slabs, lax.rem(rad + offset, rad_count))
+    for rad in range(rad_count):
+        for a in range(sources):
+            at = (a * rad_count + rad) * 2 * per
+            value = rows_out[(rad * sources + a) // share]
+            out[at : at + 2 * per, :] = value.astype(BF16).astype(F32)
 
 
 def pick(values, index):
@@ -377,7 +421,7 @@
     return chosen
 
 
-def route_kernel(size, middle, inner, where, *rest):
+def route_kernel(size, middle, inner, where, ring, *rest):
     count = (len(rest) - 1 - size)
     sources, outs, sorted_rows = rest[:count], rest[count:-1], rest[-1]
     for i, source in enumerate(sources):
@@ -390,35 +434,54 @@
     choices = [sorted_rows[dest] for dest in range(size)]
     index = where()
     for offset, out in enumerate(outs):
-        out[...] = pick(choices, lax.rem(index + offset, size))
+        out[...] = pick(choices, sent_to(index, offset, size, ring))
+
+
+def halve_kernel(inner, *rest):
+    rad_count = lax.axis_size("rad")
+    outs, sorted_rows = rest[-1 - rad_count : -1], rest[-1]
+    to = 0
+    for source in rest[: -1 - rad_count]:
+        value = source[...]
+        for m in range(value.shape[0] // (rad_count * inner)):
+            for rad in range(rad_count):
+                at = (m * rad_count + rad) * inner
+                sorted_rows[rad, to : to + inner, :] = value[at : at + inner, :]
+            to += inner
+    choices = [sorted_rows[rad] for rad in range(rad_count)]
+    for offset, out in enumerate(outs):
+        out[...] = pick(choices, sent_to(lax.axis_index("rad"), offset, rad_count, False))
 
 
 def arrival_source(slow, fast, axis_iota):
     rad_count = lax.axis_size("rad")
     azi, rad = lax.axis_index("azi"), lax.axis_index("rad")
-    from_rad = lax.rem(rad - axis_iota % rad_count + rad_count, rad_count)
-    from_fast = lax.rem(azi % fast - axis_iota // rad_count % fast + fast, fast)
-    from_slow = lax.rem(azi // fast - axis_iota // (rad_count * fast) % slow + slow, slow)
+    from_rad = came_from(rad, axis_iota % rad_count, rad_count, False)
+    from_fast = came_from(azi % fast, axis_iota // rad_count % fast, fast, False)
+    from_slow = came_from(azi // fast, axis_iota // (rad_count * fast) % slow, slow, True)
     return (from_rad * slow + from_slow) * fast + from_fast
 
 
 def couple_kernel(per, local, fast, slow, kernel, *rest):
-    columns, outs = rest[:slow], rest[slow:]
     rad_count = lax.axis_size("rad")
+    columns, outs = rest[:rad_count], rest[rad_count:]
     sources = slow * fast * rad_count
     nq = columns[0].shape[1]
     total = sources * per
     me = lax.axis_index("rad") * lax.axis_size("azi") + lax.axis_index("azi")
     offset = lax.rem(me * local, nq)
     row, col = row_iota((total, total)), lane_iota((total, total))
-    source = arrival_source(slow, fast, col % sources)
+    place = col % sources
+    azi_count = slow * fast
+    place = place % azi_count * rad_count + place // azi_count
+    source = arrival_source(slow, fast, place)
     spread = (row == source * per + col // sources).astype(F32)
     lane = lane_iota((total, nq))
     sides = []
     for c in range(2):
         stacked = jnp.concatenate(
             [
-                ref[pl.ds(c * per + k, fast * rad_count, stride=2 * per), :]
+                ref[pl.ds(c * per + k, slow * fast, stride=2 * per), :]
                 for k in range(per)
                 for ref in columns
             ],
@@ -435,7 +498,7 @@
     share = total // len(outs)
     slabs = [result[i * share : (i + 1) * share, :] for i in range(len(outs))]
     for offset, out in enumerate(outs):
-        out[...] = pick(slabs, lax.rem(rad + offset, len(outs)))
+        out[...] = pick(slabs, sent_to(rad, offset, len(outs), False))
 
 
 def inverse_kernel(per, local, fast, *rest):
@@ -452,28 +515,37 @@
     factor = jnp.where(first, 1.0, 2.0) / length
     source = arrival_source(slow, fast, lane_iota((count, count)))
     order = (source == row_iota((count, count))).astype(F32)
+    picked = []
     for k in range(per):
-        picked = [
+        rows = [
             ref[pl.ds(k, fast * rad_count, stride=per), :] if per > 1 else ref[...] for ref in blocks
         ]
-        values = dot(order, jnp.concatenate(picked, axis=0))
-        values = values * factor
+        picked.append(jnp.concatenate(rows, axis=0))
+    values = dot(order, jnp.concatenate(picked, axis=1)) * jnp.concatenate([factor] * per, axis=1)
+    tables = mixed[...]
+    own = row_iota(tables.shape) % share
+    tables = jnp.concatenate([jnp.where(own == h, tables, 0.0) for h in range(share)], axis=1)
+    mid = dot(values.T, tables)
+    turn_cos, turn_sin = twiddle[:, :LANES], twiddle[:, LANES:]
+    turned = []
+    for k in range(per):
         real, imag = [], []
         for h in range(share):
-            chosen = jnp.where(block_id % share == h, values, 0.0)
-            mid = dot(chosen.T, mixed[...])
-            top, bottom = mid[0:local, :], mid[local : 2 * local, :]
+            at = 2 * LANES * h
+            top = mid[k * nq : k * nq + local, at : at + 2 * LANES]
+            bottom = mid[k * nq + local : k * nq + 2 * local, at : at + 2 * LANES]
             real.append(top[:, :LANES] - bottom[:, LANES:])
             imag.append(top[:, LANES:] + bottom[:, :LANES])
         real = jnp.concatenate(real, axis=0)
         imag = jnp.concatenate(imag, axis=0)
-        turn_cos, turn_sin = twiddle[:, :LANES], twiddle[:, LANES:]
-        turned = jnp.concatenate(
-            [real * turn_cos - imag * turn_sin, -(real * turn_sin + imag * turn_cos)], axis=0
-        )
-        wave = dot(circle[...], turned)
+        pair = [real * turn_cos - imag * turn_sin, -(real * turn_sin + imag * turn_cos)]
+        turned.append(jnp.concatenate(pair, axis=0))
+    wave = dot(circle[...], jnp.concatenate(turned, axis=1))
+    for k in range(per):
         for q in range(nq):
-            out[k : k + 1, q * LANES : (q + 1) * LANES] = wave[q : q + 1, :]
+            out[k : k + 1, q * LANES : (q + 1) * LANES] = wave[
+                q : q + 1, k * LANES : (k + 1) * LANES
+            ]
 
 
 def cos_sin(rows, columns, length):
@@ -559,32 +631,31 @@
         bytes_accessed=24 * nz * slab * seg,
     )(*fields, low, high)
 
-    def hop(buffers, axis, size, step):
+    def hop(buffers, axis, size, step, ring=False):
         around = range(lax.axis_size(axis))
         return [buffers[0]] + [
-            lax.ppermute(
-                buffers[o],
-                axis,
-                [(i, i + ((i // step % size + o) % size - i // step % size) * step) for i in around],
-            )
+            lax.ppermute(buffers[o], axis, [
+                (i, i + (sent_to(i // step % size, o, size, ring) - i // step % size) * step)
+                for i in around
+            ])
             for o in range(1, size)
         ]
 
-    def route(buffers, size, inner, step, name):
+    def route(buffers, size, inner, step, name, ring=False):
         count = buffers[0].shape[0]
         lines = len(buffers) * count // size
         where = lambda: lax.axis_index("azi") // step % size
         buffers = call(
-            functools.partial(route_kernel, size, count // (size * inner), inner, where),
+            functools.partial(route_kernel, size, count // (size * inner), inner, where, ring),
             tuple(pltpu.VMEM((lines, LANES), F32) for _ in range(size)),
             scratch=(pltpu.VMEM((size, lines, LANES), F32),),
             name="route_" + name,
             bytes_accessed=100_000,
         )(*buffers)
-        return hop(buffers, "azi", size, step)
+        return hop(buffers, "azi", size, step, ring)
 
     surf = [surf.reshape(azi * side, LANES)]
-    surf = route(surf, slow, fast * side, fast, "surf_slow")
+    surf = route(surf, slow, fast * side, fast, "surf_slow", ring=True)
     bulk = exchange(bulk, "azi")
     surf = route(surf, fast, side, 1, "surf_fast")
     surf = [x.reshape(slow, side, LANES) for x in surf]
@@ -593,21 +664,36 @@
     circle = np.concatenate(cos_sin(k_id, k_id, nq), axis=1)
     twiddle = np.concatenate(cos_sin(l_id, k_id, length), axis=1)
     short = np.concatenate(cos_sin(np.arange(upper), l_id, LANES), axis=0)
-    *spectrum, sides = call(
+    m_id = np.arange(modes)
+    steps = [np.concatenate([t.reshape(upper, nq) for t in cos_sin(m_id, [n], length)], 1) for n in (1, 2)]
+    steps = np.concatenate(steps, axis=0)
+    spectrum, sides = call(
         functools.partial(forward_kernel, per, nz, modes, fast),
         (
-            *(pltpu.VMEM((azi * 2 * per, nq), F32) for _ in range(rad)),
+            pltpu.VMEM((devices * 2 * per, nq), F32),
             pltpu.VMEM((azi, side, LANES), F32),
         ),
-        in_specs=[smem, smem] + [vmem] * (3 + fast),
-        scratch=(pltpu.VMEM((upper, 2 * per, nq), F32),),
+        in_specs=[anywhere] * 2 + [vmem] * (4 + fast),
+        scratch=(
+            pltpu.VMEM((upper, 2 * per, nq), F32),
+            pltpu.SMEM((slab,), jnp.int32),
+            pltpu.SMEM((slab,), F32),
+            pltpu.SemaphoreType.DMA((2,)),
+        ),
         name="forward",
         flops=100_000_000,
         bytes_accessed=1_000_000,
-    )(cycle_shift, remainder, jnp.asarray(circle), jnp.asarray(twiddle), jnp.asarray(short), *surf)
-    columns = hop(spectrum, "rad", rad, 1)
-    columns = route(columns, fast, 2 * per, 1, "column_fast")
-    columns = route(columns, slow, 2 * per, fast, "column_slow")
+    )(cycle_shift, remainder, jnp.asarray(circle), jnp.asarray(twiddle), jnp.asarray(short), jnp.asarray(steps), *surf)
+    columns = route([spectrum], fast, rad * 2 * per, 1, "column_fast")
+    columns = route(columns, slow, rad * 2 * per, fast, "column_slow", ring=True)
+    columns = call(
+        functools.partial(halve_kernel, 2 * per),
+        tuple(pltpu.VMEM((azi * 2 * per, nq), F32) for _ in range(rad)),
+        scratch=(pltpu.VMEM((rad, azi * 2 * per, nq), F32),),
+        name="route_column_rad",
+        bytes_accessed=100_000,
+    )(*columns)
+    columns = hop(columns, "rad", rad, 1)
     blocks = call(
         functools.partial(couple_kernel, per, local, fast, slow),
         tuple(pltpu.VMEM((azi * per, nq), F32) for _ in range(rad)),
@@ -617,7 +703,7 @@
     )(kernel, *columns)
     blocks = hop(blocks, "rad", rad, 1)
     blocks = route(blocks, fast, per, 1, "block_fast")
-    blocks = route(blocks, slow, per, fast, "block_slow")
+    blocks = route(blocks, slow, per, fast, "block_slow", ring=True)
     j_of_block = np.arange(devices) * local // nq
     mixed = np.concatenate(cos_sin(j_of_block, l_id, LANES), axis=1)
     turn = np.concatenate(cos_sin(k_id, l_id, length), axis=1)
@@ -631,12 +717,18 @@
 
     moved, top = call(
         functools.partial(advect_kernel, per, nz),
-        (pltpu.VMEM((azi, 3 * group, seg), BF16), pltpu.VMEM((SUB, LANES), F32)),
-        in_specs=[smem, smem, vmem, vmem],
+        (shape_of((azi, 3 * group, seg), BF16), pltpu.VMEM((SUB, LANES), F32)),
+        in_specs=[anywhere, anywhere, vmem, vmem],
+        out_specs=(anywhere, vmem),
         scratch=(
             pltpu.VMEM((3, nq, group, LANES), F32),
             pltpu.VMEM((3, nq, group, LANES), F32),
             pltpu.VMEM((3, azi, group, LANES), F32),
+            pltpu.VMEM((azi, 3 * group, seg), BF16),
+            pltpu.SMEM((slab,), jnp.int32),
+            pltpu.SMEM((slab,), F32),
+            pltpu.SemaphoreType.DMA((2,)),
+            pltpu.SemaphoreType.DMA((azi,)),
         ),
         name="advect",
         flops=50 * 3 * nz * slab * seg,
@@ -646,6 +738,8 @@
     results = call(
         functools.partial(settle_kernel, per),
         tuple(shape_of((nz, slab, seg)) for _ in range(3)),
+        out_specs=(anywhere,) * 3,
+        scratch=(pltpu.VMEM((3, nz, slab, seg), F32), pltpu.SemaphoreType.DMA((3,))),
         name="settle",
         flops=20 * 3 * nz * slab * seg,
         bytes_accessed=18 * nz * slab * seg,

time: 104 us -> 102 us (0.981)
  waiting for transfers between devices: 36.9 us -> 42.9 us
  starting transfers between devices: 42.7 us -> 38.4 us
  Pallas kernels: 23.4 us -> 19.3 us
    ppermute x20, waiting for transfers between devices: 35.6 us -> 41.7 us  [hop(): lax.ppermute(buffers[o], axis, [(i, i + (sent_to(i // step % size, o, siz...]
    pallas_call x13 -> x14, Pallas kernels: 23.4 us -> 19.3 us  [run(): return kernel(*near)]
    ppermute x20, starting transfers between devices: 28.8 us -> 26 us  [hop(): lax.ppermute(buffers[o], axis, [(i, i + (sent_to(i // step % size, o, siz...]
    all_to_all x2, starting transfers between devices: 13.3 us -> 11.8 us  [exchange(): return lax.all_to_all(array, axes, 0, 0, tiled=True)]
  transfers between devices with their start and end apart: 24 -> 24, of which waited for: 18 -> 19; matrix products, arithmetic and copies ran while one was open for 0% -> 0% of each run, Pallas kernels for 5% -> 5%
where the time goes in v5:
time: 102 us; the launch traced here: 101 us
  waiting for transfers between devices  42.9 us (42%)
  starting transfers between devices  38.4 us (38%)
  Pallas kernels  19.3 us (19%)
    ppermute x20, waiting for transfers between devices, hop(): lax.ppermute(buffers[o], axis, [(i, i + (sent_to(i // step % size, o, siz...  41.7 us
    ppermute x20, starting transfers between devices, hop(): lax.ppermute(buffers[o], axis, [(i, i + (sent_to(i // step % size, o, siz...  26 us
    pallas_call x14, Pallas kernels, run(): return kernel(*near)  19.3 us
    all_to_all x2, starting transfers between devices, exchange(): return lax.all_to_all(array, axes, 0, 0, tiled=True)  11.8 us
  transfers between devices with their start and end apart: 24, of which 19 were waited for; matrix products, arithmetic and copies ran while one was open for 0% of the time, Pallas kernels for 5%

profile of v5, /device:TPU:0, one launch (start us, length us, event | category | flops | bytes accessed | tf_op | source)
XLA Modules:
  0.0 101.4 jit_solution(10355365982856264131)
XLA Ops:
  0.6 1.4 %shard_map.147 = (f32[4,32,1024]{2,1,0:T(8,128)S(1)}, f32[4,32,1024]{2,1,0:T(8,128)S(1)}, f32[4,32,1024]{2,1,0:T(8,128)S(1)}, f32[3,4,2,1024]{3,2,1,0:T(2,128)S(1)}, f32[3,4,2,1024]{3,2,1,0:T(2,128)S(1)}) custom-call(f32[4,32,1024]{2,1,0:T(8,128)} %rho.1, f32[4,32,1024]{2,1,0:T(8,128)} %ur.1, f32[4,32,1024]{2,1,0:T(8,128)} %up.1), custom_call_target="tpu_custom_call" | custom-call | bytes 1572864 | tf_op jit(solution)/shard_map/pallas_call | solution.py:572
  2.0 0.6 collective-permute-start
  2.6 0.1 collective-permute-start.1
  2.7 0.9 collective-permute-done.low
  3.5 0.4 collective-permute-done.1.high
  3.9 6.0 %shard_map.148 = (bf16[16,192,128]{2,1,0:T(8,128)(2,1)}, f32[16,24,128]{2,1,0:T(8,128)S(1)}) custom-call(f32[4,32,1024]{2,1,0:T(8,128)S(1)} %get-tuple-element.46.rho, f32[4,32,1024]{2,1,0:T(8,128)S(1)} %get-tuple-element.47.ur, f32[4,32,1024]{2,1,0:T(8,128)S(1)} %get-tuple-element.48.up, f32[3,4,2,1024]{3,2,1,0:T(2,128)S(1)} %collective-permute-done.low, ...), custom_call_target="tpu_custom_call" | custom-call | flops 39321600 | bytes 3145728 | tf_op jit(solution)/shard_map/pallas_call | solution.py:572
  9.9 8.0 %all-to-all-start = ((bf16[16,192,128]{2,1,0:T(8,128)(2,1)}), bf16[16,192,128]{2,1,0:T(8,128)(2,1)S(1)}, u32[]{:S(2)}, u32[]{:S(2)}) async-start(bf16[16,192,128]{2,1,0:T(8,128)(2,1)} %get-tuple-element.51), calls=%async_computation | async-start | bytes 1572864 | tf_op jit(solution)/shard_map/all_to_all | solution.py:578
  17.9 0.0 copy-start.2
  17.9 0.1 shard_map.149
  18.0 0.0 copy-start.1
  18.0 2.0 %collective-permute-start.2 = (f32[96,128]{1,0:T(8,128)S(1)}, f32[96,128]{1,0:T(8,128)S(1)}, u32[]{:S(2)}, u32[]{:S(2)}) collective-permute-start(f32[96,128]{1,0:T(8,128)S(1)} %get-tuple-element.54), channel_id=1, source_target_pairs={{0,4},{1,5},{2,6},{3,7},{4,8},{5,9},{6,10},{7,11},{8,12},{9,13},{1... | collective-permute-start | bytes 147464 | tf_op jit(solution)/shard_map/ppermute | solution.py:637
  20.0 2.4 %collective-permute-start.3 = (f32[96,128]{1,0:T(8,128)S(1)}, f32[96,128]{1,0:T(8,128)S(1)}, u32[]{:S(2)}, u32[]{:S(2)}) collective-permute-start(f32[96,128]{1,0:T(8,128)S(1)} %get-tuple-element.55), channel_id=1, source_target_pairs={{0,8},{1,9},{2,10},{3,11},{4,12},{5,13},{6,14},{7,15},{8,0},{9,1},... | collective-permute-start | bytes 147464 | tf_op jit(solution)/shard_map/ppermute | solution.py:637
  22.3 1.5 %collective-permute-start.4 = (f32[96,128]{1,0:T(8,128)S(1)}, f32[96,128]{1,0:T(8,128)S(1)}, u32[]{:S(2)}, u32[]{:S(2)}) collective-permute-start(f32[96,128]{1,0:T(8,128)S(1)} %get-tuple-element.56), channel_id=1, source_target_pairs={{0,12},{1,13},{2,14},{3,15},{4,0},{5,1},{6,2},{7,3},{8,4},{9,5},{1... | collective-permute-start | bytes 147464 | tf_op jit(solution)/shard_map/ppermute | solution.py:637
  23.8 13.4 %collective-permute-done.2.rest_1_ = f32[96,128]{1,0:T(8,128)S(1)} collective-permute-done((f32[96,128]{1,0:T(8,128)S(1)}, f32[96,128]{1,0:T(8,128)S(1)}, u32[]{:S(2)}, u32[]{:S(2)}) %collective-permute-start.2) | collective-permute-done | bytes 49184 | tf_op jit(solution)/shard_map/ppermute | solution.py:637
  37.2 5.0 %collective-permute-done.3.rest_2_ = f32[96,128]{1,0:T(8,128)S(1)} collective-permute-done((f32[96,128]{1,0:T(8,128)S(1)}, f32[96,128]{1,0:T(8,128)S(1)}, u32[]{:S(2)}, u32[]{:S(2)}) %collective-permute-start.3) | collective-permute-done | bytes 49184 | tf_op jit(solution)/shard_map/ppermute | solution.py:637
  42.2 0.0 collective-permute-done.4.rest_3_
  42.2 1.5 %collective-permute-start.5 = (f32[96,128]{1,0:T(8,128)S(1)}, f32[96,128]{1,0:T(8,128)S(1)}, u32[]{:S(2)}, u32[]{:S(2)}) collective-permute-start(f32[96,128]{1,0:T(8,128)S(1)} %get-tuple-element.58), channel_id=1, source_target_pairs={{0,1},{1,0},{2,3},{3,2},{4,5},{5,4},{6,7},{7,6},{8,9},{9,8},{10,11... | collective-permute-start | bytes 147464 | tf_op jit(solution)/shard_map/ppermute | solution.py:637
  43.7 1.5 %collective-permute-start.6 = (f32[96,128]{1,0:T(8,128)S(1)}, f32[96,128]{1,0:T(8,128)S(1)}, u32[]{:S(2)}, u32[]{:S(2)}) collective-permute-start(f32[96,128]{1,0:T(8,128)S(1)} %get-tuple-element.59), channel_id=1, source_target_pairs={{0,2},{1,3},{2,0},{3,1},{4,6},{5,7},{6,4},{7,5},{8,10},{9,11},{10,... | collective-permute-start | bytes 147464 | tf_op jit(solution)/shard_map/ppermute | solution.py:637
  45.2 0.6 collective-permute-start.7
  45.8 0.9 collective-permute-done.5
  46.7 1.2 %collective-permute-done.6 = f32[96,128]{1,0:T(8,128)S(1)} collective-permute-done((f32[96,128]{1,0:T(8,128)S(1)}, f32[96,128]{1,0:T(8,128)S(1)}, u32[]{:S(2)}, u32[]{:S(2)}) %collective-permute-start.6) | collective-permute-done | bytes 49184 | tf_op jit(solution)/shard_map/ppermute | solution.py:637
  47.9 2.3 %collective-permute-done.7 = f32[96,128]{1,0:T(8,128)S(1)} collective-permute-done((f32[96,128]{1,0:T(8,128)S(1)}, f32[96,128]{1,0:T(8,128)S(1)}, u32[]{:S(2)}, u32[]{:S(2)}) %collective-permute-start.7) | collective-permute-done | bytes 49184 | tf_op jit(solution)/shard_map/ppermute | solution.py:637
  50.2 0.0 copy-done.2
  50.2 0.0 copy-done.1
  50.2 0.0 copy-done.4
  50.2 0.0 copy-done.5
  50.2 1.8 %shard_map.151 = (f32[128,128]{1,0:T(8,128)S(1)}, f32[16,24,128]{2,1,0:T(8,128)S(1)}) custom-call(s32[32]{0:T(128)} %far_shift.3, f32[32]{0:T(128)} %far_remainder.3, f32[128,256]{1,0:T(8,128)S(1)} %copy-done.2, f32[128,256]{1,0:T(8,128)S(1)} %copy-done.1, f32[32,128]{1,0:T(8,128)S(1)} %copy-done.5, f32[32,256]{1,0:T(8,128)S(1)} %copy-done.4, ...), custom_call_target="tpu_custom_call" | custom-call | flops 100000000 | bytes 1000000 | tf_op jit(solution)/shard_map/pallas_call | solution.py:572
  52.0 0.0 all-to-all-done.bulk
  52.0 5.8 %shard_map.152 = (bf16[16,24,1024]{2,1,0:T(8,128)(2,1)}, f32[8,128]{1,0:T(8,128)S(1)}) custom-call(s32[32]{0:T(128)} %far_shift.3, f32[32]{0:T(128)} %far_remainder.3, bf16[16,192,128]{2,1,0:T(8,128)(2,1)S(1)} %all-to-all-done.bulk, f32[16,24,128]{2,1,0:T(8,128)S(1)} %get-tuple-element.61.sides), custom_call_target="tpu_custom_call" | custom-call | flops 19660800 | bytes 1572864 | tf_op jit(solution)/shard_map/pallas_call | solution.py:572
  57.8 0.0 copy-start
  57.8 3.8 %all-to-all-start.1 = ((bf16[16,24,1024]{2,1,0:T(8,128)(2,1)}), bf16[16,24,1024]{2,1,0:T(8,128)(2,1)S(1)}, u32[]{:S(2)}, u32[]{:S(2)}) async-start(bf16[16,24,1024]{2,1,0:T(8,128)(2,1)} %get-tuple-element.62), calls=%async_computation.1 | async-start | bytes 1572864 | tf_op jit(solution)/shard_map/all_to_all | solution.py:578
  61.6 1.9 %collective-permute-start.8 = (f32[32,128]{1,0:T(8,128)S(1)}, f32[32,128]{1,0:T(8,128)S(1)}, u32[]{:S(2)}, u32[]{:S(2)}) collective-permute-start(f32[32,128]{1,0:T(8,128)S(1)} %get-tuple-element.69), channel_id=1, source_target_pairs={{0,1},{1,0},{2,3},{3,2},{4,5},{5,4},{6,7},{7,6},{8,9},{9,8},{10,11... | collective-permute-start | bytes 49160 | tf_op jit(solution)/shard_map/ppermute | solution.py:637
  63.5 1.5 %collective-permute-start.9 = (f32[32,128]{1,0:T(8,128)S(1)}, f32[32,128]{1,0:T(8,128)S(1)}, u32[]{:S(2)}, u32[]{:S(2)}) collective-permute-start(f32[32,128]{1,0:T(8,128)S(1)} %get-tuple-element.70), channel_id=1, source_target_pairs={{0,2},{1,3},{2,0},{3,1},{4,6},{5,7},{6,4},{7,5},{8,10},{9,11},{10,... | collective-permute-start | bytes 49160 | tf_op jit(solution)/shard_map/ppermute | solution.py:637
  65.0 0.2 collective-permute-start.10
  65.2 1.6 %collective-permute-done.8.rest_1_ = f32[32,128]{1,0:T(8,128)S(1)} collective-permute-done((f32[32,128]{1,0:T(8,128)S(1)}, f32[32,128]{1,0:T(8,128)S(1)}, u32[]{:S(2)}, u32[]{:S(2)}) %collective-permute-start.8) | collective-permute-done | bytes 16416 | tf_op jit(solution)/shard_map/ppermute | solution.py:637
  66.8 1.3 %collective-permute-done.9.rest_2_ = f32[32,128]{1,0:T(8,128)S(1)} collective-permute-done((f32[32,128]{1,0:T(8,128)S(1)}, f32[32,128]{1,0:T(8,128)S(1)}, u32[]{:S(2)}, u32[]{:S(2)}) %collective-permute-start.9) | collective-permute-done | bytes 16416 | tf_op jit(solution)/shard_map/ppermute | solution.py:637
  68.1 1.7 %collective-permute-done.10.rest_3_ = f32[32,128]{1,0:T(8,128)S(1)} collective-permute-done((f32[32,128]{1,0:T(8,128)S(1)}, f32[32,128]{1,0:T(8,128)S(1)}, u32[]{:S(2)}, u32[]{:S(2)}) %collective-permute-start.10) | collective-permute-done | bytes 16416 | tf_op jit(solution)/shard_map/ppermute | solution.py:637
  69.8 1.5 %collective-permute-start.11 = (f32[32,128]{1,0:T(8,128)S(1)}, f32[32,128]{1,0:T(8,128)S(1)}, u32[]{:S(2)}, u32[]{:S(2)}) collective-permute-start(f32[32,128]{1,0:T(8,128)S(1)} %get-tuple-element.73), channel_id=1, source_target_pairs={{0,4},{1,5},{2,6},{3,7},{4,8},{5,9},{6,10},{7,11},{8,12},{9,13},{1... | collective-permute-start | bytes 49160 | tf_op jit(solution)/shard_map/ppermute | solution.py:637
  71.4 2.4 %collective-permute-start.12 = (f32[32,128]{1,0:T(8,128)S(1)}, f32[32,128]{1,0:T(8,128)S(1)}, u32[]{:S(2)}, u32[]{:S(2)}) collective-permute-start(f32[32,128]{1,0:T(8,128)S(1)} %get-tuple-element.74), channel_id=1, source_target_pairs={{0,8},{1,9},{2,10},{3,11},{4,12},{5,13},{6,14},{7,15},{8,0},{9,1},... | collective-permute-start | bytes 49160 | tf_op jit(solution)/shard_map/ppermute | solution.py:637
  73.8 1.4 %collective-permute-start.13 = (f32[32,128]{1,0:T(8,128)S(1)}, f32[32,128]{1,0:T(8,128)S(1)}, u32[]{:S(2)}, u32[]{:S(2)}) collective-permute-start(f32[32,128]{1,0:T(8,128)S(1)} %get-tuple-element.75), channel_id=1, source_target_pairs={{0,12},{1,13},{2,14},{3,15},{4,0},{5,1},{6,2},{7,3},{8,4},{9,5},{1... | collective-permute-start | bytes 49160 | tf_op jit(solution)/shard_map/ppermute | solution.py:637
  75.1 2.3 %collective-permute-done.11.rest_1_ = f32[32,128]{1,0:T(8,128)S(1)} collective-permute-done((f32[32,128]{1,0:T(8,128)S(1)}, f32[32,128]{1,0:T(8,128)S(1)}, u32[]{:S(2)}, u32[]{:S(2)}) %collective-permute-start.11) | collective-permute-done | bytes 16416 | tf_op jit(solution)/shard_map/ppermute | solution.py:637
  77.4 3.6 %collective-permute-done.12.rest_2_ = f32[32,128]{1,0:T(8,128)S(1)} collective-permute-done((f32[32,128]{1,0:T(8,128)S(1)}, f32[32,128]{1,0:T(8,128)S(1)}, u32[]{:S(2)}, u32[]{:S(2)}) %collective-permute-start.12) | collective-permute-done | bytes 16416 | tf_op jit(solution)/shard_map/ppermute | solution.py:637
  81.0 0.0 collective-permute-done.13.rest_3_
  81.1 0.1 collective-permute-start.14
  81.2 1.2 %collective-permute-done.14.rest_1_ = f32[64,128]{1,0:T(8,128)S(1)} collective-permute-done((f32[64,128]{1,0:T(8,128)S(1)}, f32[64,128]{1,0:T(8,128)S(1)}, u32[]{:S(2)}, u32[]{:S(2)}) %collective-permute-start.14) | collective-permute-done | bytes 32800 | tf_op jit(solution)/shard_map/ppermute | solution.py:637
  82.4 0.0 copy-done
  82.4 0.6 shard_map.157
  83.0 0.2 collective-permute-start.15
  83.2 1.0 collective-permute-done.15.rest_1_
  84.3 1.5 %collective-permute-start.16 = (f32[16,128]{1,0:T(8,128)S(1)}, f32[16,128]{1,0:T(8,128)S(1)}, u32[]{:S(2)}, u32[]{:S(2)}) collective-permute-start(f32[16,128]{1,0:T(8,128)S(1)} %get-tuple-element.81), channel_id=1, source_target_pairs={{0,1},{1,0},{2,3},{3,2},{4,5},{5,4},{6,7},{7,6},{8,9},{9,8},{10,11... | collective-permute-start | bytes 24584 | tf_op jit(solution)/shard_map/ppermute | solution.py:637
  85.8 1.5 %collective-permute-start.17 = (f32[16,128]{1,0:T(8,128)S(1)}, f32[16,128]{1,0:T(8,128)S(1)}, u32[]{:S(2)}, u32[]{:S(2)}) collective-permute-start(f32[16,128]{1,0:T(8,128)S(1)} %get-tuple-element.82), channel_id=1, source_target_pairs={{0,2},{1,3},{2,0},{3,1},{4,6},{5,7},{6,4},{7,5},{8,10},{9,11},{10,... | collective-permute-start | bytes 24584 | tf_op jit(solution)/shard_map/ppermute | solution.py:637
  87.3 0.6 collective-permute-start.18
  87.8 0.2 collective-permute-done.16.rest_1_
  88.0 1.5 %collective-permute-done.17.rest_2_ = f32[16,128]{1,0:T(8,128)S(1)} collective-permute-done((f32[16,128]{1,0:T(8,128)S(1)}, f32[16,128]{1,0:T(8,128)S(1)}, u32[]{:S(2)}, u32[]{:S(2)}) %collective-permute-start.17) | collective-permute-done | bytes 8224 | tf_op jit(solution)/shard_map/ppermute | solution.py:637
  89.5 2.4 %collective-permute-done.18.rest_3_ = f32[16,128]{1,0:T(8,128)S(1)} collective-permute-done((f32[16,128]{1,0:T(8,128)S(1)}, f32[16,128]{1,0:T(8,128)S(1)}, u32[]{:S(2)}, u32[]{:S(2)}) %collective-permute-start.18) | collective-permute-done | bytes 8224 | tf_op jit(solution)/shard_map/ppermute | solution.py:637
  91.9 0.8 collective-permute-start.19
  92.7 1.5 %collective-permute-start.20 = (f32[16,128]{1,0:T(8,128)S(1)}, f32[16,128]{1,0:T(8,128)S(1)}, u32[]{:S(2)}, u32[]{:S(2)}) collective-permute-start(f32[16,128]{1,0:T(8,128)S(1)} %get-tuple-element.86), channel_id=1, source_target_pairs={{0,8},{1,9},{2,10},{3,11},{4,12},{5,13},{6,14},{7,15},{8,0},{9,1},... | collective-permute-start | bytes 24584 | tf_op jit(solution)/shard_map/ppermute | solution.py:637
  94.2 1.6 %collective-permute-start.21 = (f32[16,128]{1,0:T(8,128)S(1)}, f32[16,128]{1,0:T(8,128)S(1)}, u32[]{:S(2)}, u32[]{:S(2)}) collective-permute-start(f32[16,128]{1,0:T(8,128)S(1)} %get-tuple-element.87), channel_id=1, source_target_pairs={{0,12},{1,13},{2,14},{3,15},{4,0},{5,1},{6,2},{7,3},{8,4},{9,5},{1... | collective-permute-start | bytes 24584 | tf_op jit(solution)/shard_map/ppermute | solution.py:637
  95.8 1.6 %collective-permute-done.19.rest_1_ = f32[16,128]{1,0:T(8,128)S(1)} collective-permute-done((f32[16,128]{1,0:T(8,128)S(1)}, f32[16,128]{1,0:T(8,128)S(1)}, u32[]{:S(2)}, u32[]{:S(2)}) %collective-permute-start.19) | collective-permute-done | bytes 8224 | tf_op jit(solution)/shard_map/ppermute | solution.py:637
  97.4 0.0 collective-permute-done.20.rest_2_
  97.4 0.6 collective-permute-done.21.rest_3_
  97.9 1.9 %shard_map.160 = f32[2,16384]{1,0:T(2,128)} custom-call(f32[16,128]{1,0:T(8,128)S(1)} %get-tuple-element.84.rest_0_, f32[16,128]{1,0:T(8,128)S(1)} %collective-permute-done.19.rest_1_, f32[16,128]{1,0:T(8,128)S(1)} %collective-permute-done.20.rest_2_, f32[16,128]{1,0:T(8,128)S(1)} %collective-permute-done.21.rest_3_, f32[128,256]{1,0:T(8,128)S(1)} %copy-done.2, ...), custom_call_target="tpu_custom_call" | custom-call | flops 100000000 | bytes 1000000 | tf_op jit(solution)/shard_map/pallas_call | solution.py:572
  99.9 0.0 all-to-all-done.1.bulk
  99.9 1.6 %shard_map.153 = (f32[4,32,1024]{2,1,0:T(8,128)}, f32[4,32,1024]{2,1,0:T(8,128)}, f32[4,32,1024]{2,1,0:T(8,128)}) custom-call(bf16[16,24,1024]{2,1,0:T(8,128)(2,1)S(1)} %all-to-all-done.1.bulk, f32[8,128]{1,0:T(8,128)S(1)} %get-tuple-element.63.top), custom_call_target="tpu_custom_call" | custom-call | flops 7864320 | bytes 2359296 | tf_op jit(solution)/shard_map/pallas_call | solution.py:572
  (10 shorter events, 0.2 us)
Async XLA Ops:
  2.0 1.5 %collective-permute-start = (f32[3,4,2,1024]{3,2,1,0:T(2,128)S(1)}, f32[3,4,2,1024]{3,2,1,0:T(2,128)S(1)}, u32[]{:S(2)}, u32[]{:S(2)}) collective-permute-start(f32[3,4,2,1024]{3,2,1,0:T(2,128)S(1)} %get-tuple-element.49), channel_id=1, source_target_pairs={{0,16},{16,0},{1,17},{17,1},{2,18},{18,2},{3,19},{19,3},{4,20},{20... | collective-permute-start | bytes 294920 | tf_op jit(solution)/shard_map/ppermute | solution.py:616
  2.6 1.3 %collective-permute-start.1 = (f32[3,4,2,1024]{3,2,1,0:T(2,128)S(1)}, f32[3,4,2,1024]{3,2,1,0:T(2,128)S(1)}, u32[]{:S(2)}, u32[]{:S(2)}) collective-permute-start(f32[3,4,2,1024]{3,2,1,0:T(2,128)S(1)} %get-tuple-element.50), channel_id=1, source_target_pairs={{16,0},{0,16},{17,1},{1,17},{18,2},{2,18},{19,3},{3,19},{20,4},{4,... | collective-permute-start | bytes 294920 | tf_op jit(solution)/shard_map/ppermute | solution.py:617
  9.9 42.2 %all-to-all-start = ((bf16[16,192,128]{2,1,0:T(8,128)(2,1)}), bf16[16,192,128]{2,1,0:T(8,128)(2,1)S(1)}, u32[]{:S(2)}, u32[]{:S(2)}) async-start(bf16[16,192,128]{2,1,0:T(8,128)(2,1)} %get-tuple-element.51), calls=%async_computation | async-start | bytes 1572864 | tf_op jit(solution)/shard_map/all_to_all | solution.py:578
  17.9 32.3 %copy-start.2 = (f32[128,256]{1,0:T(8,128)S(1)}, f32[128,256]{1,0:T(8,128)}, u32[]{:S(2)}) copy-start(f32[128,256]{1,0:T(8,128)} %constant.10.clone.circle.rest_4_) | copy-start | bytes 393220
  18.0 32.2 %copy-start.1 = (f32[128,256]{1,0:T(8,128)S(1)}, f32[128,256]{1,0:T(8,128)}, u32[]{:S(2)}) copy-start(f32[128,256]{1,0:T(8,128)} %constant.11.clone.twiddle.rest_5_) | copy-start | bytes 393220
  18.0 19.2 %collective-permute-start.2 = (f32[96,128]{1,0:T(8,128)S(1)}, f32[96,128]{1,0:T(8,128)S(1)}, u32[]{:S(2)}, u32[]{:S(2)}) collective-permute-start(f32[96,128]{1,0:T(8,128)S(1)} %get-tuple-element.54), channel_id=1, source_target_pairs={{0,4},{1,5},{2,6},{3,7},{4,8},{5,9},{6,10},{7,11},{8,12},{9,13},{1... | collective-permute-start | bytes 147464 | tf_op jit(solution)/shard_map/ppermute | solution.py:637
  20.0 22.2 %collective-permute-start.3 = (f32[96,128]{1,0:T(8,128)S(1)}, f32[96,128]{1,0:T(8,128)S(1)}, u32[]{:S(2)}, u32[]{:S(2)}) collective-permute-start(f32[96,128]{1,0:T(8,128)S(1)} %get-tuple-element.55), channel_id=1, source_target_pairs={{0,8},{1,9},{2,10},{3,11},{4,12},{5,13},{6,14},{7,15},{8,0},{9,1},... | collective-permute-start | bytes 147464 | tf_op jit(solution)/shard_map/ppermute | solution.py:637
  22.3 19.8 %collective-permute-start.4 = (f32[96,128]{1,0:T(8,128)S(1)}, f32[96,128]{1,0:T(8,128)S(1)}, u32[]{:S(2)}, u32[]{:S(2)}) collective-permute-start(f32[96,128]{1,0:T(8,128)S(1)} %get-tuple-element.56), channel_id=1, source_target_pairs={{0,12},{1,13},{2,14},{3,15},{4,0},{5,1},{6,2},{7,3},{8,4},{9,5},{1... | collective-permute-start | bytes 147464 | tf_op jit(solution)/shard_map/ppermute | solution.py:637
  42.2 8.0 %copy-start.4 = (f32[32,256]{1,0:T(8,128)S(1)}, f32[32,256]{1,0:T(8,128)}, u32[]{:S(2)}) copy-start(f32[32,256]{1,0:T(8,128)} %constant.13.clone.steps) | copy-start | bytes 98308
  42.2 8.0 %copy-start.5 = (f32[32,128]{1,0:T(8,128)S(1)}, f32[32,128]{1,0:T(8,128)}, u32[]{:S(2)}) copy-start(f32[32,128]{1,0:T(8,128)} %constant.12.clone.short) | copy-start | bytes 49156
  42.2 4.5 %collective-permute-start.5 = (f32[96,128]{1,0:T(8,128)S(1)}, f32[96,128]{1,0:T(8,128)S(1)}, u32[]{:S(2)}, u32[]{:S(2)}) collective-permute-start(f32[96,128]{1,0:T(8,128)S(1)} %get-tuple-element.58), channel_id=1, source_target_pairs={{0,1},{1,0},{2,3},{3,2},{4,5},{5,4},{6,7},{7,6},{8,9},{9,8},{10,11... | collective-permute-start | bytes 147464 | tf_op jit(solution)/shard_map/ppermute | solution.py:637
  43.7 4.1 %collective-permute-start.6 = (f32[96,128]{1,0:T(8,128)S(1)}, f32[96,128]{1,0:T(8,128)S(1)}, u32[]{:S(2)}, u32[]{:S(2)}) collective-permute-start(f32[96,128]{1,0:T(8,128)S(1)} %get-tuple-element.59), channel_id=1, source_target_pairs={{0,2},{1,3},{2,0},{3,1},{4,6},{5,7},{6,4},{7,5},{8,10},{9,11},{10,... | collective-permute-start | bytes 147464 | tf_op jit(solution)/shard_map/ppermute | solution.py:637
  45.2 5.0 %collective-permute-start.7 = (f32[96,128]{1,0:T(8,128)S(1)}, f32[96,128]{1,0:T(8,128)S(1)}, u32[]{:S(2)}, u32[]{:S(2)}) collective-permute-start(f32[96,128]{1,0:T(8,128)S(1)} %get-tuple-element.60), channel_id=1, source_target_pairs={{0,3},{1,2},{2,1},{3,0},{4,7},{5,6},{6,5},{7,4},{8,11},{9,10},{10,... | collective-permute-start | bytes 147464 | tf_op jit(solution)/shard_map/ppermute | solution.py:637
  57.8 24.5 %copy-start = (bf16[64,64,64]{2,1,0:T(8,128)(2,1)S(1)}, bf16[64,64,64]{2,1,0:T(8,128)(2,1)}, u32[]{:S(2)}) copy-start(bf16[64,64,64]{2,1,0:T(8,128)(2,1)} %kernel.1) | copy-start | bytes 1572868
  57.8 42.0 %all-to-all-start.1 = ((bf16[16,24,1024]{2,1,0:T(8,128)(2,1)}), bf16[16,24,1024]{2,1,0:T(8,128)(2,1)S(1)}, u32[]{:S(2)}, u32[]{:S(2)}) async-start(bf16[16,24,1024]{2,1,0:T(8,128)(2,1)} %get-tuple-element.62), calls=%async_computation.1 | async-start | bytes 1572864 | tf_op jit(solution)/shard_map/all_to_all | solution.py:578
  61.6 5.1 %collective-permute-start.8 = (f32[32,128]{1,0:T(8,128)S(1)}, f32[32,128]{1,0:T(8,128)S(1)}, u32[]{:S(2)}, u32[]{:S(2)}) collective-permute-start(f32[32,128]{1,0:T(8,128)S(1)} %get-tuple-element.69), channel_id=1, source_target_pairs={{0,1},{1,0},{2,3},{3,2},{4,5},{5,4},{6,7},{7,6},{8,9},{9,8},{10,11... | collective-permute-start | bytes 49160 | tf_op jit(solution)/shard_map/ppermute | solution.py:637
  63.5 4.6 %collective-permute-start.9 = (f32[32,128]{1,0:T(8,128)S(1)}, f32[32,128]{1,0:T(8,128)S(1)}, u32[]{:S(2)}, u32[]{:S(2)}) collective-permute-start(f32[32,128]{1,0:T(8,128)S(1)} %get-tuple-element.70), channel_id=1, source_target_pairs={{0,2},{1,3},{2,0},{3,1},{4,6},{5,7},{6,4},{7,5},{8,10},{9,11},{10,... | collective-permute-start | bytes 49160 | tf_op jit(solution)/shard_map/ppermute | solution.py:637
  65.0 4.8 %collective-permute-start.10 = (f32[32,128]{1,0:T(8,128)S(1)}, f32[32,128]{1,0:T(8,128)S(1)}, u32[]{:S(2)}, u32[]{:S(2)}) collective-permute-start(f32[32,128]{1,0:T(8,128)S(1)} %get-tuple-element.71), channel_id=1, source_target_pairs={{0,3},{1,2},{2,1},{3,0},{4,7},{5,6},{6,5},{7,4},{8,11},{9,10},{10,... | collective-permute-start | bytes 49160 | tf_op jit(solution)/shard_map/ppermute | solution.py:637
  69.8 7.6 %collective-permute-start.11 = (f32[32,128]{1,0:T(8,128)S(1)}, f32[32,128]{1,0:T(8,128)S(1)}, u32[]{:S(2)}, u32[]{:S(2)}) collective-permute-start(f32[32,128]{1,0:T(8,128)S(1)} %get-tuple-element.73), channel_id=1, source_target_pairs={{0,4},{1,5},{2,6},{3,7},{4,8},{5,9},{6,10},{7,11},{8,12},{9,13},{1... | collective-permute-start | bytes 49160 | tf_op jit(solution)/shard_map/ppermute | solution.py:637
  71.4 9.7 %collective-permute-start.12 = (f32[32,128]{1,0:T(8,128)S(1)}, f32[32,128]{1,0:T(8,128)S(1)}, u32[]{:S(2)}, u32[]{:S(2)}) collective-permute-start(f32[32,128]{1,0:T(8,128)S(1)} %get-tuple-element.74), channel_id=1, source_target_pairs={{0,8},{1,9},{2,10},{3,11},{4,12},{5,13},{6,14},{7,15},{8,0},{9,1},... | collective-permute-start | bytes 49160 | tf_op jit(solution)/shard_map/ppermute | solution.py:637
  73.8 7.3 %collective-permute-start.13 = (f32[32,128]{1,0:T(8,128)S(1)}, f32[32,128]{1,0:T(8,128)S(1)}, u32[]{:S(2)}, u32[]{:S(2)}) collective-permute-start(f32[32,128]{1,0:T(8,128)S(1)} %get-tuple-element.75), channel_id=1, source_target_pairs={{0,12},{1,13},{2,14},{3,15},{4,0},{5,1},{6,2},{7,3},{8,4},{9,5},{1... | collective-permute-start | bytes 49160 | tf_op jit(solution)/shard_map/ppermute | solution.py:637
  81.1 1.3 %collective-permute-start.14 = (f32[64,128]{1,0:T(8,128)S(1)}, f32[64,128]{1,0:T(8,128)S(1)}, u32[]{:S(2)}, u32[]{:S(2)}) collective-permute-start(f32[64,128]{1,0:T(8,128)S(1)} %get-tuple-element.77), channel_id=1, source_target_pairs={{0,16},{16,0},{1,17},{17,1},{2,18},{18,2},{3,19},{19,3},{4,20},{20... | collective-permute-start | bytes 98312 | tf_op jit(solution)/shard_map/ppermute | solution.py:637
  83.0 1.2 %collective-permute-start.15 = (f32[32,128]{1,0:T(8,128)S(1)}, f32[32,128]{1,0:T(8,128)S(1)}, u32[]{:S(2)}, u32[]{:S(2)}) collective-permute-start(f32[32,128]{1,0:T(8,128)S(1)} %get-tuple-element.79), channel_id=1, source_target_pairs={{0,16},{16,0},{1,17},{17,1},{2,18},{18,2},{3,19},{19,3},{4,20},{20... | collective-permute-start | bytes 49160 | tf_op jit(solution)/shard_map/ppermute | solution.py:637
  84.3 13.7 %copy-start.3 = (f32[32,256]{1,0:T(8,128)S(1)}, f32[32,256]{1,0:T(8,128)}, u32[]{:S(2)}) copy-start(f32[32,256]{1,0:T(8,128)} %constant.14.clone.rest_6_) | copy-start | bytes 98308
  84.3 3.7 %collective-permute-start.16 = (f32[16,128]{1,0:T(8,128)S(1)}, f32[16,128]{1,0:T(8,128)S(1)}, u32[]{:S(2)}, u32[]{:S(2)}) collective-permute-start(f32[16,128]{1,0:T(8,128)S(1)} %get-tuple-element.81), channel_id=1, source_target_pairs={{0,1},{1,0},{2,3},{3,2},{4,5},{5,4},{6,7},{7,6},{8,9},{9,8},{10,11... | collective-permute-start | bytes 24584 | tf_op jit(solution)/shard_map/ppermute | solution.py:637
  85.8 3.7 %collective-permute-start.17 = (f32[16,128]{1,0:T(8,128)S(1)}, f32[16,128]{1,0:T(8,128)S(1)}, u32[]{:S(2)}, u32[]{:S(2)}) collective-permute-start(f32[16,128]{1,0:T(8,128)S(1)} %get-tuple-element.82), channel_id=1, source_target_pairs={{0,2},{1,3},{2,0},{3,1},{4,6},{5,7},{6,4},{7,5},{8,10},{9,11},{10,... | collective-permute-start | bytes 24584 | tf_op jit(solution)/shard_map/ppermute | solution.py:637
  87.3 4.5 %collective-permute-start.18 = (f32[16,128]{1,0:T(8,128)S(1)}, f32[16,128]{1,0:T(8,128)S(1)}, u32[]{:S(2)}, u32[]{:S(2)}) collective-permute-start(f32[16,128]{1,0:T(8,128)S(1)} %get-tuple-element.83), channel_id=1, source_target_pairs={{0,3},{1,2},{2,1},{3,0},{4,7},{5,6},{6,5},{7,4},{8,11},{9,10},{10,... | collective-permute-start | bytes 24584 | tf_op jit(solution)/shard_map/ppermute | solution.py:637
  91.9 5.5 %collective-permute-start.19 = (f32[16,128]{1,0:T(8,128)S(1)}, f32[16,128]{1,0:T(8,128)S(1)}, u32[]{:S(2)}, u32[]{:S(2)}) collective-permute-start(f32[16,128]{1,0:T(8,128)S(1)} %get-tuple-element.85), channel_id=1, source_target_pairs={{0,4},{1,5},{2,6},{3,7},{4,8},{5,9},{6,10},{7,11},{8,12},{9,13},{1... | collective-permute-start | bytes 24584 | tf_op jit(solution)/shard_map/ppermute | solution.py:637
  92.7 4.7 %collective-permute-start.20 = (f32[16,128]{1,0:T(8,128)S(1)}, f32[16,128]{1,0:T(8,128)S(1)}, u32[]{:S(2)}, u32[]{:S(2)}) collective-permute-start(f32[16,128]{1,0:T(8,128)S(1)} %get-tuple-element.86), channel_id=1, source_target_pairs={{0,8},{1,9},{2,10},{3,11},{4,12},{5,13},{6,14},{7,15},{8,0},{9,1},... | collective-permute-start | bytes 24584 | tf_op jit(solution)/shard_map/ppermute | solution.py:637
  94.2 3.8 %collective-permute-start.21 = (f32[16,128]{1,0:T(8,128)S(1)}, f32[16,128]{1,0:T(8,128)S(1)}, u32[]{:S(2)}, u32[]{:S(2)}) collective-permute-start(f32[16,128]{1,0:T(8,128)S(1)} %get-tuple-element.87), channel_id=1, source_target_pairs={{0,12},{1,13},{2,14},{3,15},{4,0},{5,1},{6,2},{7,3},{8,4},{9,5},{1... | collective-permute-start | bytes 24584 | tf_op jit(solution)/shard_map/ppermute | solution.py:637

commit v6 on v5

--- a/solution.py
+++ b/solution.py
@@ -13,6 +13,7 @@
 RADIAL_COURANT = 0.3
 VISCOSITY = 0.08
 LANES = 128
+VMEM_BYTES = 67_043_328
 SUB = 8
 EXACT = lax.Precision.HIGHEST
 F32 = jnp.float32
@@ -56,103 +57,131 @@
     return -(-(per * tiles + per) // SUB) * SUB
 
 
-def load_kernel(rho, ur, up, rho_near, ur_near, up_near, tail, head, sems):
+def edges_kernel(rho, ur, up, tail, head, last, first, sems):
     slab = rho.shape[1]
-    pairs = ((rho, rho_near), (ur, ur_near), (up, up_near))
-    copies = [pltpu.make_async_copy(far, near, sems.at[c]) for c, (far, near) in enumerate(pairs)]
+    copies = []
+    for c, far in enumerate((rho, ur, up)):
+        ends = (far.at[:, pl.ds(slab - SUB, SUB), :], last.at[c]), (far.at[:, pl.ds(0, SUB), :], first.at[c])
+        copies += [pltpu.make_async_copy(*end, sems.at[2 * c + i]) for i, end in enumerate(ends)]
     for copy in copies:
         copy.start()
-    for c, (_, near) in enumerate(pairs):
-        copies[c].wait()
-        tail[c] = near[:, slab - 2 :, :]
-        head[c] = near[:, 0:2, :]
-
-
-def hydro_kernel(per, rho, ur, up, low, high, bulk, surf, field, stage, block, narrow, sems):
+    for c in range(3):
+        copies[2 * c].wait()
+        tail[c] = last[c, :, SUB - 2 :, :]
+        copies[2 * c + 1].wait()
+        head[c] = first[c, :, 0:2, :]
+
+
+def advance(ref, tile, z, slab, scale):
+    _, nz, lines, width = ref.shape
+    count = lines // SUB
+    sub = row_iota((SUB, width))
+    near_rows = row_iota((SUB, LANES))
+    cycle = tile * SUB + near_rows
+    cycle = jnp.where((tile == count - 1) & (near_rows >= SUB // 2), near_rows - SUB, cycle)
+    cycle = lax.axis_index("rad") * slab + cycle
+    radius = 1.0 + 4.0 * (cycle.astype(F32) + 0.5) / (slab * lax.axis_size("rad"))
+    power = 1.0 / (radius * jnp.sqrt(radius))
+    wide = lambda x: jnp.concatenate([x] * (width // LANES), axis=1)
+    courant = wide((0.5 * scale) * (0.3 / radius))
+    coriolis, epicycle = wide((0.2 * scale) * power), wide((0.05 * scale) * power)
+    rows = lambda t: pl.ds(pl.multiple_of(t * SUB, SUB), SUB)
+    here, before, after = rows(tile), rows(lax.rem(tile + count - 1, count)), rows(lax.rem(tile + 1, count))
+    z_up, z_down = min(z + 1, nz - 1), max(z - 1, 0)
+    center, base, rad_diff, azi_diff = [], [], [], []
+    for c in range(3):
+        cur = ref[c, z, here, :]
+        inward = pltpu.roll(jnp.where(sub == SUB - 1, ref[c, z, before, :], cur), 1, 0)
+        outward = pltpu.roll(jnp.where(sub == 0, ref[c, z, after, :], cur), SUB - 1, 0)
+        ahead = pltpu.roll(cur, width - 1, 1)
+        behind = pltpu.roll(cur, 1, 1)
+        near = ref[c, z_up, here, :] + ref[c, z_down, here, :] + inward + outward + ahead + behind
+        base.append((scale * VISCOSITY) * near + (scale * (1.0 - 6.0 * VISCOSITY)) * cur)
+        rad_diff.append(outward - inward)
+        azi_diff.append(ahead - behind)
+        center.append(cur)
+    half = 0.5 * scale * RADIAL_COURANT
+    return (
+        base[0] - (half * rad_diff[1] + courant * azi_diff[2]),
+        base[1] + coriolis * center[2] - half * rad_diff[0],
+        base[2] - epicycle * center[1] - courant * azi_diff[0],
+    )
+
+
+def store_section(field, stage, slab, tile):
+    for z in range(field.shape[1]):
+        for c, value in enumerate(advance(field, tile, z, slab, 1.0)):
+            stage[c, z, pl.ds(pl.multiple_of(tile * SUB, SUB), SUB), :] = value
+
+
+def interior_kernel(rho, ur, up, field, stage, sems):
     nz, slab, seg = rho.shape
-    width = seg + LANES
-    first = 2 * SUB
-    last_tile = slab // SUB + 2
+    copies = [
+        pltpu.make_async_copy(far, field.at[c, :, pl.ds(0, slab), pl.ds(0, seg)], sems.at[c])
+        for c, far in enumerate((rho, ur, up))
+    ]
+    for copy in copies:
+        copy.start()
+    lines, width = field.shape[2:]
+    for c in range(3):
+        for z in range(nz):
+            field[c, z, :, seg:width] = jnp.zeros((lines, width - seg), F32)
+    for copy in copies:
+        copy.wait()
+
+    def section(tile, carry):
+        store_section(field, stage, slab, tile)
+        return carry
+
+    lax.fori_loop(1, slab // SUB - 1, section, 0)
+
+
+def hydro_kernel(
+    per, seg, field_in, stage_in, low, high, bulk, surf, field, stage, block, narrow, sems
+):
+    _, nz, lines, width = field.shape
+    slab = lines - SUB
+    last = slab // SUB
     tiles = seg // LANES
     rad = lax.axis_index("rad")
     rad_count = lax.axis_size("rad")
-    total = slab * rad_count
-    for c, ref in enumerate((rho, ur, up)):
+    for c in range(3):
         for z in range(nz):
-            field[c, z, SUB : slab + 3 * SUB, seg:width] = jnp.zeros((slab + 2 * SUB, LANES), F32)
-            field[c, z, first : first + slab, 0:seg] = ref[z]
-            inner = jnp.broadcast_to(ref[z, 0:1, :], (2, seg))
-            outer = jnp.broadcast_to(ref[z, slab - 1 : slab, :], (2, seg))
-            field[c, z, first - 2 : first, 0:seg] = jnp.where(rad == 0, inner, low[c, z])
-            field[c, z, first + slab : first + slab + 2, 0:seg] = jnp.where(
-                rad == rad_count - 1, outer, high[c, z]
-            )
-    sub = row_iota((SUB, width))
-
-    def rates_at(ref, tile, z):
-        cycle = rad * slab - first + tile * SUB + row_iota((SUB, LANES))
-        radius = 1.0 + 4.0 * (cycle.astype(F32) + 0.5) / total
-        power = 1.0 / (radius * jnp.sqrt(radius))
-        wide = lambda x: jnp.concatenate([x] * (width // LANES), axis=1)
-        courant = wide(0.5 * (0.3 / radius))
-        coriolis, epicycle = wide(0.2 * power), wide(0.05 * power)
-        here = pl.ds(pl.multiple_of(tile * SUB, SUB), SUB)
-        before = pl.ds(pl.multiple_of((tile - 1) * SUB, SUB), SUB)
-        after = pl.ds(pl.multiple_of((tile + 1) * SUB, SUB), SUB)
-        z_up, z_down = min(z + 1, nz - 1), max(z - 1, 0)
-        center, rad_diff, azi_diff, spread = [], [], [], []
-        for c in range(3):
-            cur = ref[c, z, here, :]
-            inward = pltpu.roll(jnp.where(sub == SUB - 1, ref[c, z, before, :], cur), 1, 0)
-            outward = pltpu.roll(jnp.where(sub == 0, ref[c, z, after, :], cur), SUB - 1, 0)
-            ahead = pltpu.roll(cur, width - 1, 1)
-            behind = pltpu.roll(cur, 1, 1)
-            near = ref[c, z_up, here, :] + ref[c, z_down, here, :] + inward + outward + ahead + behind
-            spread.append(VISCOSITY * near - (6.0 * VISCOSITY) * cur)
-            rad_diff.append(outward - inward)
-            azi_diff.append(ahead - behind)
-            center.append(cur)
-        half = 0.5 * RADIAL_COURANT
-        return center, (
-            spread[0] - (half * rad_diff[1] + courant * azi_diff[2]),
-            coriolis * center[2] - half * rad_diff[0] + spread[1],
-            spread[2] - epicycle * center[1] - courant * azi_diff[0],
-        )
-
-    def first_section(tile, carry):
-        for z in range(nz):
-            center, change = rates_at(field, tile, z)
-            for c in range(3):
-                stage[c, z, pl.ds(pl.multiple_of(tile * SUB, SUB), SUB), :] = center[c] + change[c]
+            inner = jnp.broadcast_to(field[c, z, 0:1, 0:seg], (2, seg))
+            outer = jnp.broadcast_to(field[c, z, slab - 1 : slab, 0:seg], (2, seg))
+            outward = jnp.where(rad == rad_count - 1, outer, high[c, z])
+            inward = jnp.where(rad == 0, inner, low[c, z])
+            between = jnp.zeros((SUB - 4, seg), F32)
+            field[c, z, slab:lines, 0:seg] = jnp.concatenate([outward, between, inward], axis=0)
+
+    def section(index, carry):
+        store_section(field, stage, slab, lax.rem(index + last - 1, last + 1))
         return carry
 
-    lax.fori_loop(1, last_tile + 1, first_section, 0)
+    lax.fori_loop(0, 3, section, 0)
 
     @pl.when(rad == 0)
     def _():
         for c in range(3):
             for z in range(nz):
-                stage[c, z, first - 1 : first, :] = stage[c, z, first : first + 1, :]
+                stage[c, z, lines - 1 : lines, :] = stage[c, z, 0:1, :]
 
     @pl.when(rad == rad_count - 1)
     def _():
         for c in range(3):
             for z in range(nz):
-                stage[c, z, first + slab : first + slab + 1, :] = stage[
-                    c, z, first + slab - 1 : first + slab, :
-                ]
+                stage[c, z, slab : slab + 1, :] = stage[c, z, slab - 1 : slab, :]
 
     def second_section(tile, largest):
         here = pl.ds(pl.multiple_of(tile * SUB, SUB), SUB)
         for z in range(nz):
-            center, change = rates_at(stage, tile, z)
-            for c in range(3):
-                value = 0.5 * field[c, z, here, :] + 0.5 * (center[c] + change[c])
+            for c, value in enumerate(advance(stage, tile, z, slab, 0.5)):
+                value = 0.5 * field[c, z, here, :] + value
                 field[c, z, here, :] = value
                 largest = jnp.maximum(largest, jnp.abs(value))
         return largest
 
-    largest = lax.fori_loop(2, last_tile, second_section, jnp.zeros((SUB, width), F32))
+    largest = lax.fori_loop(0, last, second_section, jnp.zeros((SUB, width), F32))
     peak = jnp.maximum(jnp.max(largest, keepdims=True), 1e-30)
     scale = TOP / peak
     dests = SUB // per
@@ -176,13 +205,13 @@
                 for d in range(dests):
                     for b in range(tiles):
                         line = b * stride + plane * per
-                        block[(tile - 2) * dests + d, line : line + per, :] = code[
+                        block[tile * dests + d, line : line + per, :] = code[
                             d * per : (d + 1) * per, b * LANES : (b + 1) * LANES
                         ]
                 overflow = overflow + pltpu.roll(field[c, z, here, seg:width], 2 + 4 * plane, 1)
         overflow = jnp.where(lane_iota((SUB, LANES)) < LANES // 2, overflow, peak)
         for d in range(dests):
-            dest = (tile - 2) * dests + d
+            dest = tile * dests + d
             for k in range(per):
                 row = d * per + k
                 for b in range(tiles):
@@ -192,13 +221,13 @@
                 line = per * tiles + k
                 surf[dest, line : line + 1, :] = overflow[row : row + 1, :]
         for d in range(dests):
-            dest = (tile - 2) * dests + d
+            dest = tile * dests + d
             narrow[dest] = block[dest].astype(BF16)
-        send(tile - 2).start()
+        send(tile).start()
         return carry
 
-    lax.fori_loop(2, last_tile, pack, 0)
-    for index in range(slab // SUB):
+    lax.fori_loop(0, last, pack, 0)
+    for index in range(last):
         send(index).wait()
 
 
@@ -554,20 +583,26 @@
     return np.cos(angle).astype(np.float32), np.sin(angle).astype(np.float32)
 
 
-def call(body, out_shape, in_specs=None, out_specs=None, scratch=(), name=None, **cost):
+def call(body, out_shape, in_specs=None, out_specs=None, scratch=(), name=None, aliases=None, room=40 * 2**20, **cost):
     kernel = pl.pallas_call(
         body,
         out_shape=out_shape,
         **({} if in_specs is None else {"in_specs": in_specs}),
         **({} if out_specs is None else {"out_specs": out_specs}),
         scratch_shapes=list(scratch),
+        input_output_aliases=aliases or {},
+        compiler_params=pltpu.CompilerParams(vmem_limit_bytes=VMEM_BYTES - room),
         cost_estimate=pl.CostEstimate(**{"flops": 0, "bytes_accessed": 0, "transcendentals": 0, **cost}),
     )
 
     def run(*operands):
+        places = [
+            None if x.ndim == 1 else pltpu.HBM if name in ("edges", "interior") else pltpu.VMEM
+            for x in operands
+        ]
         near = [
-            x if x.ndim == 1 or name == "load" else pltpu.with_memory_space_constraint(x, pltpu.VMEM)
-            for x in operands
+            x if place is None else pltpu.with_memory_space_constraint(x, place)
+            for x, place in zip(operands, places)
         ]
         return kernel(*near)
 
@@ -604,24 +639,37 @@
 
     fields = (density, radial_velocity, azimuthal_velocity)
     anywhere = pl.BlockSpec(memory_space=pl.ANY)
+    far = pl.BlockSpec(memory_space=pltpu.HBM)
     edge = pltpu.VMEM((3, nz, 2, seg), F32)
-    *fields, tail, head = call(
-        load_kernel,
-        (*(pltpu.VMEM((nz, slab, seg), F32) for _ in range(3)), edge, edge),
-        in_specs=[anywhere] * 3,
-        scratch=(pltpu.SemaphoreType.DMA((3,)),),
-        name="load",
-        bytes_accessed=12 * nz * slab * seg,
+    tail, head = call(
+        edges_kernel,
+        (edge, edge),
+        in_specs=[far] * 3,
+        scratch=(
+            pltpu.VMEM((3, nz, SUB, seg), F32),
+            pltpu.VMEM((3, nz, SUB, seg), F32),
+            pltpu.SemaphoreType.DMA((6,)),
+        ),
+        name="edges",
+        bytes_accessed=24 * nz * SUB * seg,
     )(*fields)
     low = lax.ppermute(tail, "rad", [(i, (i + 1) % rad) for i in range(rad)])
     high = lax.ppermute(head, "rad", [((i + 1) % rad, i) for i in range(rad)])
-    bulk, surf = call(
-        functools.partial(hydro_kernel, per),
-        (shape_of((azi, rows, LANES), BF16), pltpu.VMEM((azi, side, LANES), F32)),
-        out_specs=(anywhere, vmem),
+    padded = pltpu.VMEM((3, nz, slab + SUB, width), F32)
+    field, stage = call(
+        interior_kernel,
+        (padded, padded),
+        in_specs=[far] * 3,
+        scratch=(pltpu.SemaphoreType.DMA((3,)),),
+        name="interior",
+        bytes_accessed=12 * nz * slab * seg,
+    )(*fields)
+    bulk, surf, *_ = call(
+        functools.partial(hydro_kernel, per, seg),
+        (pltpu.HBM((azi, rows, LANES), BF16), pltpu.VMEM((azi, side, LANES), F32), padded, padded),
+        out_specs=(far, vmem, vmem, vmem),
+        aliases={0: 2, 1: 3},
         scratch=(
-            pltpu.VMEM((3, nz, slab + 4 * SUB, width), F32),
-            pltpu.VMEM((3, nz, slab + 4 * SUB, width), F32),
             pltpu.VMEM((azi, rows, LANES), F32),
             pltpu.VMEM((azi, rows, LANES), BF16),
             pltpu.SemaphoreType.DMA((slab // SUB,)),
@@ -629,7 +677,7 @@
         name="hydro",
         flops=100 * 3 * nz * slab * seg,
         bytes_accessed=24 * nz * slab * seg,
-    )(*fields, low, high)
+    )(field, stage, low, high)
 
     def hop(buffers, axis, size, step, ring=False):
         around = range(lax.axis_size(axis))
@@ -717,9 +765,9 @@
 
     moved, top = call(
         functools.partial(advect_kernel, per, nz),
-        (shape_of((azi, 3 * group, seg), BF16), pltpu.VMEM((SUB, LANES), F32)),
+        (pltpu.HBM((azi, 3 * group, seg), BF16), pltpu.VMEM((SUB, LANES), F32)),
         in_specs=[anywhere, anywhere, vmem, vmem],
-        out_specs=(anywhere, vmem),
+        out_specs=(far, vmem),
         scratch=(
             pltpu.VMEM((3, nq, group, LANES), F32),
             pltpu.VMEM((3, nq, group, LANES), F32),
@@ -737,8 +785,8 @@
     moved = exchange(moved, "azi")
     results = call(
         functools.partial(settle_kernel, per),
-        tuple(shape_of((nz, slab, seg)) for _ in range(3)),
-        out_specs=(anywhere,) * 3,
+        tuple(pltpu.HBM((nz, slab, seg), F32) for _ in range(3)),
+        out_specs=(far,) * 3,
         scratch=(pltpu.VMEM((3, nz, slab, seg), F32), pltpu.SemaphoreType.DMA((3,))),
         name="settle",
         flops=20 * 3 * nz * slab * seg,

time: 102 us -> 101 us (level)
  waiting for transfers between devices: 42.9 us -> 41.5 us
    pallas_call x14 -> x15, Pallas kernels: 19.3 us -> 19.4 us  [run(): return kernel(*near)]
  transfers between devices with their start and end apart: 24 -> 24, of which waited for: 19 -> 17; matrix products, arithmetic and copies ran while one was open for 0% -> 0% of each run, Pallas kernels for 5% -> 6%
where the time goes in v6:
time: 101 us; the launch traced here: 100 us
  waiting for transfers between devices  41.5 us (41%)
  starting transfers between devices  38.5 us (38%)
  Pallas kernels  19.4 us (19%)
    ppermute x20, waiting for transfers between devices, hop(): lax.ppermute(buffers[o], axis, [(i, i + (sent_to(i // step % size, o, siz...  41.5 us
    ppermute x20, starting transfers between devices, hop(): lax.ppermute(buffers[o], axis, [(i, i + (sent_to(i // step % size, o, siz...  25.9 us
    pallas_call x15, Pallas kernels, run(): return kernel(*near)  19.4 us
    all_to_all x2, starting transfers between devices, exchange(): return lax.all_to_all(array, axes, 0, 0, tiled=True)  11.9 us
  transfers between devices with their start and end apart: 24, of which 17 were waited for; matrix products, arithmetic and copies ran while one was open for 0% of the time, Pallas kernels for 6%

profile of v6, /device:TPU:0, one launch (start us, length us, event | category | flops | bytes accessed | tf_op | source)
XLA Modules:
  0.0 100.3 jit_solution(16139405789423926868)
XLA Ops:
  0.6 1.3 %shard_map.148 = (f32[3,4,2,1024]{3,2,1,0:T(2,128)S(1)}, f32[3,4,2,1024]{3,2,1,0:T(2,128)S(1)}) custom-call(f32[4,32,1024]{2,1,0:T(8,128)} %rho.3, f32[4,32,1024]{2,1,0:T(8,128)} %ur.3, f32[4,32,1024]{2,1,0:T(8,128)} %up.3), custom_call_target="tpu_custom_call" | custom-call | bytes 786432 | tf_op jit(solution)/shard_map/pallas_call | solution.py:607
  1.9 0.6 collective-permute-start
  2.5 0.1 collective-permute-start.1
  2.5 2.1 %shard_map.147 = (f32[3,4,40,1152]{3,2,1,0:T(8,128)S(1)}, f32[3,4,40,1152]{3,2,1,0:T(8,128)S(1)}) custom-call(f32[4,32,1024]{2,1,0:T(8,128)} %rho.3, f32[4,32,1024]{2,1,0:T(8,128)} %ur.3, f32[4,32,1024]{2,1,0:T(8,128)} %up.3), custom_call_target="tpu_custom_call" | custom-call | bytes 1572864 | tf_op jit(solution)/shard_map/pallas_call | solution.py:607
  4.7 0.0 collective-permute-done.low
  4.7 0.0 collective-permute-done.1.high
  4.7 0.0 copy-start.1
  4.7 0.0 copy-start.2
  4.7 0.0 copy-start.4
  4.7 0.0 copy-start.5
  4.7 0.0 copy-start.6
  4.8 0.0 copy-start.7
  4.8 4.4 %shard_map.149 = (bf16[16,192,128]{2,1,0:T(8,128)(2,1)}, f32[16,24,128]{2,1,0:T(8,128)S(1)}, f32[3,4,40,1152]{3,2,1,0:T(8,128)S(1)}, f32[3,4,40,1152]{3,2,1,0:T(8,128)S(1)}) custom-call(f32[3,4,40,1152]{3,2,1,0:T(8,128)S(1)} %get-tuple-element.45.field_in, ...), custom_call_target="tpu_custom_call", output_to_operand_aliasing={{2}: (0, {}), {3}: (1, {})} | custom-call | flops 39321600 | bytes 3145728 | tf_op jit(solution)/shard_map/pallas_call | solution.py:607
  9.2 8.3 %all-to-all-start = ((bf16[16,192,128]{2,1,0:T(8,128)(2,1)}), bf16[16,192,128]{2,1,0:T(8,128)(2,1)S(1)}, u32[]{:S(2)}, u32[]{:S(2)}) async-start(bf16[16,192,128]{2,1,0:T(8,128)(2,1)} %get-tuple-element.49), calls=%async_computation | async-start | bytes 1572864 | tf_op jit(solution)/shard_map/all_to_all | solution.py:613
  17.5 0.0 copy-start
  17.5 0.1 shard_map.150
  17.6 2.0 %collective-permute-start.2 = (f32[96,128]{1,0:T(8,128)S(1)}, f32[96,128]{1,0:T(8,128)S(1)}, u32[]{:S(2)}, u32[]{:S(2)}) collective-permute-start(f32[96,128]{1,0:T(8,128)S(1)} %get-tuple-element.52), channel_id=1, source_target_pairs={{0,4},{1,5},{2,6},{3,7},{4,8},{5,9},{6,10},{7,11},{8,12},{9,13},{1... | collective-permute-start | bytes 147464 | tf_op jit(solution)/shard_map/ppermute | solution.py:685
  19.6 2.4 %collective-permute-start.3 = (f32[96,128]{1,0:T(8,128)S(1)}, f32[96,128]{1,0:T(8,128)S(1)}, u32[]{:S(2)}, u32[]{:S(2)}) collective-permute-start(f32[96,128]{1,0:T(8,128)S(1)} %get-tuple-element.53), channel_id=1, source_target_pairs={{0,8},{1,9},{2,10},{3,11},{4,12},{5,13},{6,14},{7,15},{8,0},{9,1},... | collective-permute-start | bytes 147464 | tf_op jit(solution)/shard_map/ppermute | solution.py:685
  21.9 1.5 %collective-permute-start.4 = (f32[96,128]{1,0:T(8,128)S(1)}, f32[96,128]{1,0:T(8,128)S(1)}, u32[]{:S(2)}, u32[]{:S(2)}) collective-permute-start(f32[96,128]{1,0:T(8,128)S(1)} %get-tuple-element.54), channel_id=1, source_target_pairs={{0,12},{1,13},{2,14},{3,15},{4,0},{5,1},{6,2},{7,3},{8,4},{9,5},{1... | collective-permute-start | bytes 147464 | tf_op jit(solution)/shard_map/ppermute | solution.py:685
  23.4 13.3 %collective-permute-done.2.rest_1_ = f32[96,128]{1,0:T(8,128)S(1)} collective-permute-done((f32[96,128]{1,0:T(8,128)S(1)}, f32[96,128]{1,0:T(8,128)S(1)}, u32[]{:S(2)}, u32[]{:S(2)}) %collective-permute-start.2) | collective-permute-done | bytes 49184 | tf_op jit(solution)/shard_map/ppermute | solution.py:685
  36.7 4.8 %collective-permute-done.3.rest_2_ = f32[96,128]{1,0:T(8,128)S(1)} collective-permute-done((f32[96,128]{1,0:T(8,128)S(1)}, f32[96,128]{1,0:T(8,128)S(1)}, u32[]{:S(2)}, u32[]{:S(2)}) %collective-permute-start.3) | collective-permute-done | bytes 49184 | tf_op jit(solution)/shard_map/ppermute | solution.py:685
  41.5 0.0 collective-permute-done.4.rest_3_
  41.5 1.5 %collective-permute-start.5 = (f32[96,128]{1,0:T(8,128)S(1)}, f32[96,128]{1,0:T(8,128)S(1)}, u32[]{:S(2)}, u32[]{:S(2)}) collective-permute-start(f32[96,128]{1,0:T(8,128)S(1)} %get-tuple-element.56), channel_id=1, source_target_pairs={{0,1},{1,0},{2,3},{3,2},{4,5},{5,4},{6,7},{7,6},{8,9},{9,8},{10,11... | collective-permute-start | bytes 147464 | tf_op jit(solution)/shard_map/ppermute | solution.py:685
  43.1 1.5 %collective-permute-start.6 = (f32[96,128]{1,0:T(8,128)S(1)}, f32[96,128]{1,0:T(8,128)S(1)}, u32[]{:S(2)}, u32[]{:S(2)}) collective-permute-start(f32[96,128]{1,0:T(8,128)S(1)} %get-tuple-element.57), channel_id=1, source_target_pairs={{0,2},{1,3},{2,0},{3,1},{4,6},{5,7},{6,4},{7,5},{8,10},{9,11},{10,... | collective-permute-start | bytes 147464 | tf_op jit(solution)/shard_map/ppermute | solution.py:685
  44.5 0.6 collective-permute-start.7
  45.1 0.8 collective-permute-done.5
  45.9 1.2 %collective-permute-done.6 = f32[96,128]{1,0:T(8,128)S(1)} collective-permute-done((f32[96,128]{1,0:T(8,128)S(1)}, f32[96,128]{1,0:T(8,128)S(1)}, u32[]{:S(2)}, u32[]{:S(2)}) %collective-permute-start.6) | collective-permute-done | bytes 49184 | tf_op jit(solution)/shard_map/ppermute | solution.py:685
  47.2 2.4 %collective-permute-done.7 = f32[96,128]{1,0:T(8,128)S(1)} collective-permute-done((f32[96,128]{1,0:T(8,128)S(1)}, f32[96,128]{1,0:T(8,128)S(1)}, u32[]{:S(2)}, u32[]{:S(2)}) %collective-permute-start.7) | collective-permute-done | bytes 49184 | tf_op jit(solution)/shard_map/ppermute | solution.py:685
  49.6 0.0 copy-start.3
  49.6 1.5 %shard_map.152 = (f32[128,128]{1,0:T(8,128)S(1)}, f32[16,24,128]{2,1,0:T(8,128)S(1)}) custom-call(s32[32]{0:T(128)S(1)} %copy-done.6, f32[32]{0:T(128)S(1)} %copy-done.7, f32[128,256]{1,0:T(8,128)S(1)} %copy-done.2, f32[128,256]{1,0:T(8,128)S(1)} %copy-done.1, f32[32,128]{1,0:T(8,128)S(1)} %copy-done.5, f32[32,256]{1,0:T(8,128)S(1)} %copy-done.4, ...), custom_call_target="tpu_custom_call" | custom-call | flops 100000000 | bytes 1000000 | tf_op jit(solution)/shard_map/pallas_call | solution.py:607
  51.1 0.0 all-to-all-done.bulk
  51.1 5.8 %shard_map.153 = (bf16[16,24,1024]{2,1,0:T(8,128)(2,1)}, f32[8,128]{1,0:T(8,128)S(1)}) custom-call(s32[32]{0:T(128)S(1)} %copy-done.6, f32[32]{0:T(128)S(1)} %copy-done.7, bf16[16,192,128]{2,1,0:T(8,128)(2,1)S(1)} %all-to-all-done.bulk, f32[16,24,128]{2,1,0:T(8,128)S(1)} %get-tuple-element.59.sides), custom_call_target="tpu_custom_call" | custom-call | flops 19660800 | bytes 1572864 | tf_op jit(solution)/shard_map/pallas_call | solution.py:607
  56.9 3.6 %all-to-all-start.1 = ((bf16[16,24,1024]{2,1,0:T(8,128)(2,1)}), bf16[16,24,1024]{2,1,0:T(8,128)(2,1)S(1)}, u32[]{:S(2)}, u32[]{:S(2)}) async-start(bf16[16,24,1024]{2,1,0:T(8,128)(2,1)} %get-tuple-element.60), calls=%async_computation.1 | async-start | bytes 1572864 | tf_op jit(solution)/shard_map/all_to_all | solution.py:613
  60.5 1.9 %collective-permute-start.8 = (f32[32,128]{1,0:T(8,128)S(1)}, f32[32,128]{1,0:T(8,128)S(1)}, u32[]{:S(2)}, u32[]{:S(2)}) collective-permute-start(f32[32,128]{1,0:T(8,128)S(1)} %get-tuple-element.67), channel_id=1, source_target_pairs={{0,1},{1,0},{2,3},{3,2},{4,5},{5,4},{6,7},{7,6},{8,9},{9,8},{10,11... | collective-permute-start | bytes 49160 | tf_op jit(solution)/shard_map/ppermute | solution.py:685
  62.4 1.5 %collective-permute-start.9 = (f32[32,128]{1,0:T(8,128)S(1)}, f32[32,128]{1,0:T(8,128)S(1)}, u32[]{:S(2)}, u32[]{:S(2)}) collective-permute-start(f32[32,128]{1,0:T(8,128)S(1)} %get-tuple-element.68), channel_id=1, source_target_pairs={{0,2},{1,3},{2,0},{3,1},{4,6},{5,7},{6,4},{7,5},{8,10},{9,11},{10,... | collective-permute-start | bytes 49160 | tf_op jit(solution)/shard_map/ppermute | solution.py:685
  63.9 0.2 collective-permute-start.10
  64.1 1.6 %collective-permute-done.8.rest_1_ = f32[32,128]{1,0:T(8,128)S(1)} collective-permute-done((f32[32,128]{1,0:T(8,128)S(1)}, f32[32,128]{1,0:T(8,128)S(1)}, u32[]{:S(2)}, u32[]{:S(2)}) %collective-permute-start.8) | collective-permute-done | bytes 16416 | tf_op jit(solution)/shard_map/ppermute | solution.py:685
  65.7 1.3 %collective-permute-done.9.rest_2_ = f32[32,128]{1,0:T(8,128)S(1)} collective-permute-done((f32[32,128]{1,0:T(8,128)S(1)}, f32[32,128]{1,0:T(8,128)S(1)}, u32[]{:S(2)}, u32[]{:S(2)}) %collective-permute-start.9) | collective-permute-done | bytes 16416 | tf_op jit(solution)/shard_map/ppermute | solution.py:685
  67.0 1.7 %collective-permute-done.10.rest_3_ = f32[32,128]{1,0:T(8,128)S(1)} collective-permute-done((f32[32,128]{1,0:T(8,128)S(1)}, f32[32,128]{1,0:T(8,128)S(1)}, u32[]{:S(2)}, u32[]{:S(2)}) %collective-permute-start.10) | collective-permute-done | bytes 16416 | tf_op jit(solution)/shard_map/ppermute | solution.py:685
  68.7 1.5 %collective-permute-start.11 = (f32[32,128]{1,0:T(8,128)S(1)}, f32[32,128]{1,0:T(8,128)S(1)}, u32[]{:S(2)}, u32[]{:S(2)}) collective-permute-start(f32[32,128]{1,0:T(8,128)S(1)} %get-tuple-element.71), channel_id=1, source_target_pairs={{0,4},{1,5},{2,6},{3,7},{4,8},{5,9},{6,10},{7,11},{8,12},{9,13},{1... | collective-permute-start | bytes 49160 | tf_op jit(solution)/shard_map/ppermute | solution.py:685
  70.2 2.4 %collective-permute-start.12 = (f32[32,128]{1,0:T(8,128)S(1)}, f32[32,128]{1,0:T(8,128)S(1)}, u32[]{:S(2)}, u32[]{:S(2)}) collective-permute-start(f32[32,128]{1,0:T(8,128)S(1)} %get-tuple-element.72), channel_id=1, source_target_pairs={{0,8},{1,9},{2,10},{3,11},{4,12},{5,13},{6,14},{7,15},{8,0},{9,1},... | collective-permute-start | bytes 49160 | tf_op jit(solution)/shard_map/ppermute | solution.py:685
  72.7 1.4 %collective-permute-start.13 = (f32[32,128]{1,0:T(8,128)S(1)}, f32[32,128]{1,0:T(8,128)S(1)}, u32[]{:S(2)}, u32[]{:S(2)}) collective-permute-start(f32[32,128]{1,0:T(8,128)S(1)} %get-tuple-element.73), channel_id=1, source_target_pairs={{0,12},{1,13},{2,14},{3,15},{4,0},{5,1},{6,2},{7,3},{8,4},{9,5},{1... | collective-permute-start | bytes 49160 | tf_op jit(solution)/shard_map/ppermute | solution.py:685
  74.0 2.3 %collective-permute-done.11.rest_1_ = f32[32,128]{1,0:T(8,128)S(1)} collective-permute-done((f32[32,128]{1,0:T(8,128)S(1)}, f32[32,128]{1,0:T(8,128)S(1)}, u32[]{:S(2)}, u32[]{:S(2)}) %collective-permute-start.11) | collective-permute-done | bytes 16416 | tf_op jit(solution)/shard_map/ppermute | solution.py:685
  76.3 3.6 %collective-permute-done.12.rest_2_ = f32[32,128]{1,0:T(8,128)S(1)} collective-permute-done((f32[32,128]{1,0:T(8,128)S(1)}, f32[32,128]{1,0:T(8,128)S(1)}, u32[]{:S(2)}, u32[]{:S(2)}) %collective-permute-start.12) | collective-permute-done | bytes 16416 | tf_op jit(solution)/shard_map/ppermute | solution.py:685
  79.9 0.0 collective-permute-done.13.rest_3_
  80.0 0.1 collective-permute-start.14
  80.0 1.2 %collective-permute-done.14.rest_1_ = f32[64,128]{1,0:T(8,128)S(1)} collective-permute-done((f32[64,128]{1,0:T(8,128)S(1)}, f32[64,128]{1,0:T(8,128)S(1)}, u32[]{:S(2)}, u32[]{:S(2)}) %collective-permute-start.14) | collective-permute-done | bytes 32800 | tf_op jit(solution)/shard_map/ppermute | solution.py:685
  81.2 0.6 shard_map.158
  81.9 0.2 collective-permute-start.15
  82.1 1.0 %collective-permute-done.15.rest_1_ = f32[32,128]{1,0:T(8,128)S(1)} collective-permute-done((f32[32,128]{1,0:T(8,128)S(1)}, f32[32,128]{1,0:T(8,128)S(1)}, u32[]{:S(2)}, u32[]{:S(2)}) %collective-permute-start.15) | collective-permute-done | bytes 16416 | tf_op jit(solution)/shard_map/ppermute | solution.py:685
  83.2 1.5 %collective-permute-start.16 = (f32[16,128]{1,0:T(8,128)S(1)}, f32[16,128]{1,0:T(8,128)S(1)}, u32[]{:S(2)}, u32[]{:S(2)}) collective-permute-start(f32[16,128]{1,0:T(8,128)S(1)} %get-tuple-element.79), channel_id=1, source_target_pairs={{0,1},{1,0},{2,3},{3,2},{4,5},{5,4},{6,7},{7,6},{8,9},{9,8},{10,11... | collective-permute-start | bytes 24584 | tf_op jit(solution)/shard_map/ppermute | solution.py:685
  84.7 1.5 %collective-permute-start.17 = (f32[16,128]{1,0:T(8,128)S(1)}, f32[16,128]{1,0:T(8,128)S(1)}, u32[]{:S(2)}, u32[]{:S(2)}) collective-permute-start(f32[16,128]{1,0:T(8,128)S(1)} %get-tuple-element.80), channel_id=1, source_target_pairs={{0,2},{1,3},{2,0},{3,1},{4,6},{5,7},{6,4},{7,5},{8,10},{9,11},{10,... | collective-permute-start | bytes 24584 | tf_op jit(solution)/shard_map/ppermute | solution.py:685
  86.2 0.6 collective-permute-start.18
  86.7 0.2 collective-permute-done.16.rest_1_
  86.9 1.5 %collective-permute-done.17.rest_2_ = f32[16,128]{1,0:T(8,128)S(1)} collective-permute-done((f32[16,128]{1,0:T(8,128)S(1)}, f32[16,128]{1,0:T(8,128)S(1)}, u32[]{:S(2)}, u32[]{:S(2)}) %collective-permute-start.17) | collective-permute-done | bytes 8224 | tf_op jit(solution)/shard_map/ppermute | solution.py:685
  88.3 2.4 %collective-permute-done.18.rest_3_ = f32[16,128]{1,0:T(8,128)S(1)} collective-permute-done((f32[16,128]{1,0:T(8,128)S(1)}, f32[16,128]{1,0:T(8,128)S(1)}, u32[]{:S(2)}, u32[]{:S(2)}) %collective-permute-start.18) | collective-permute-done | bytes 8224 | tf_op jit(solution)/shard_map/ppermute | solution.py:685
  90.8 0.8 collective-permute-start.19
  91.5 1.5 %collective-permute-start.20 = (f32[16,128]{1,0:T(8,128)S(1)}, f32[16,128]{1,0:T(8,128)S(1)}, u32[]{:S(2)}, u32[]{:S(2)}) collective-permute-start(f32[16,128]{1,0:T(8,128)S(1)} %get-tuple-element.84), channel_id=1, source_target_pairs={{0,8},{1,9},{2,10},{3,11},{4,12},{5,13},{6,14},{7,15},{8,0},{9,1},... | collective-permute-start | bytes 24584 | tf_op jit(solution)/shard_map/ppermute | solution.py:685
  93.0 1.6 %collective-permute-start.21 = (f32[16,128]{1,0:T(8,128)S(1)}, f32[16,128]{1,0:T(8,128)S(1)}, u32[]{:S(2)}, u32[]{:S(2)}) collective-permute-start(f32[16,128]{1,0:T(8,128)S(1)} %get-tuple-element.85), channel_id=1, source_target_pairs={{0,12},{1,13},{2,14},{3,15},{4,0},{5,1},{6,2},{7,3},{8,4},{9,5},{1... | collective-permute-start | bytes 24584 | tf_op jit(solution)/shard_map/ppermute | solution.py:685
  94.6 1.6 %collective-permute-done.19.rest_1_ = f32[16,128]{1,0:T(8,128)S(1)} collective-permute-done((f32[16,128]{1,0:T(8,128)S(1)}, f32[16,128]{1,0:T(8,128)S(1)}, u32[]{:S(2)}, u32[]{:S(2)}) %collective-permute-start.19) | collective-permute-done | bytes 8224 | tf_op jit(solution)/shard_map/ppermute | solution.py:685
  96.3 0.6 collective-permute-done.21.rest_3_
  96.8 1.9 %shard_map.161 = f32[2,16384]{1,0:T(2,128)} custom-call(f32[16,128]{1,0:T(8,128)S(1)} %get-tuple-element.82.rest_0_, f32[16,128]{1,0:T(8,128)S(1)} %collective-permute-done.19.rest_1_, f32[16,128]{1,0:T(8,128)S(1)} %collective-permute-done.20.rest_2_, f32[16,128]{1,0:T(8,128)S(1)} %collective-permute-done.21.rest_3_, f32[128,256]{1,0:T(8,128)S(1)} %copy-done.2, ...), custom_call_target="tpu_custom_call" | custom-call | flops 100000000 | bytes 1000000 | tf_op jit(solution)/shard_map/pallas_call | solution.py:607
  98.7 0.0 all-to-all-done.1.bulk
  98.7 1.6 %shard_map.154 = (f32[4,32,1024]{2,1,0:T(8,128)}, f32[4,32,1024]{2,1,0:T(8,128)}, f32[4,32,1024]{2,1,0:T(8,128)}) custom-call(bf16[16,24,1024]{2,1,0:T(8,128)(2,1)S(1)} %all-to-all-done.1.bulk, f32[8,128]{1,0:T(8,128)S(1)} %get-tuple-element.61.top), custom_call_target="tpu_custom_call" | custom-call | flops 7864320 | bytes 2359296 | tf_op jit(solution)/shard_map/pallas_call | solution.py:607
  (15 shorter events, 0.2 us)
Async XLA Ops:
  1.9 2.8 %collective-permute-start = (f32[3,4,2,1024]{3,2,1,0:T(2,128)S(1)}, f32[3,4,2,1024]{3,2,1,0:T(2,128)S(1)}, u32[]{:S(2)}, u32[]{:S(2)}) collective-permute-start(f32[3,4,2,1024]{3,2,1,0:T(2,128)S(1)} %get-tuple-element.47), channel_id=1, source_target_pairs={{0,16},{16,0},{1,17},{17,1},{2,18},{18,2},{3,19},{19,3},{4,20},{20... | collective-permute-start | bytes 294920 | tf_op jit(solution)/shard_map/ppermute | solution.py:656
  2.5 2.2 %collective-permute-start.1 = (f32[3,4,2,1024]{3,2,1,0:T(2,128)S(1)}, f32[3,4,2,1024]{3,2,1,0:T(2,128)S(1)}, u32[]{:S(2)}, u32[]{:S(2)}) collective-permute-start(f32[3,4,2,1024]{3,2,1,0:T(2,128)S(1)} %get-tuple-element.48), channel_id=1, source_target_pairs={{16,0},{0,16},{17,1},{1,17},{18,2},{2,18},{19,3},{3,19},{20,4},{4,... | collective-permute-start | bytes 294920 | tf_op jit(solution)/shard_map/ppermute | solution.py:657
  4.7 44.8 %copy-start.1 = (f32[128,256]{1,0:T(8,128)S(1)}, f32[128,256]{1,0:T(8,128)}, u32[]{:S(2)}) copy-start(f32[128,256]{1,0:T(8,128)} %constant.11.clone.twiddle.rest_5_) | copy-start | bytes 393220
  4.7 44.8 %copy-start.2 = (f32[128,256]{1,0:T(8,128)S(1)}, f32[128,256]{1,0:T(8,128)}, u32[]{:S(2)}) copy-start(f32[128,256]{1,0:T(8,128)} %constant.10.clone.circle.rest_4_) | copy-start | bytes 393220
  4.7 44.8 %copy-start.4 = (f32[32,256]{1,0:T(8,128)S(1)}, f32[32,256]{1,0:T(8,128)}, u32[]{:S(2)}) copy-start(f32[32,256]{1,0:T(8,128)} %constant.13.clone.steps) | copy-start | bytes 98308
  4.7 44.8 %copy-start.5 = (f32[32,128]{1,0:T(8,128)S(1)}, f32[32,128]{1,0:T(8,128)}, u32[]{:S(2)}) copy-start(f32[32,128]{1,0:T(8,128)} %constant.12.clone.short) | copy-start | bytes 49156
  4.7 44.8 %copy-start.6 = (s32[32]{0:T(128)S(1)}, s32[32]{0:T(128)}, u32[]{:S(2)}) copy-start(s32[32]{0:T(128)} %far_shift.3) | copy-start | bytes 388
  4.8 44.8 %copy-start.7 = (f32[32]{0:T(128)S(1)}, f32[32]{0:T(128)}, u32[]{:S(2)}) copy-start(f32[32]{0:T(128)} %far_remainder.3) | copy-start | bytes 388
  9.2 41.9 %all-to-all-start = ((bf16[16,192,128]{2,1,0:T(8,128)(2,1)}), bf16[16,192,128]{2,1,0:T(8,128)(2,1)S(1)}, u32[]{:S(2)}, u32[]{:S(2)}) async-start(bf16[16,192,128]{2,1,0:T(8,128)(2,1)} %get-tuple-element.49), calls=%async_computation | async-start | bytes 1572864 | tf_op jit(solution)/shard_map/all_to_all | solution.py:613
  17.5 63.7 %copy-start = (bf16[64,64,64]{2,1,0:T(8,128)(2,1)S(1)}, bf16[64,64,64]{2,1,0:T(8,128)(2,1)}, u32[]{:S(2)}) copy-start(bf16[64,64,64]{2,1,0:T(8,128)(2,1)} %kernel.1) | copy-start | bytes 1572868
  17.6 19.1 %collective-permute-start.2 = (f32[96,128]{1,0:T(8,128)S(1)}, f32[96,128]{1,0:T(8,128)S(1)}, u32[]{:S(2)}, u32[]{:S(2)}) collective-permute-start(f32[96,128]{1,0:T(8,128)S(1)} %get-tuple-element.52), channel_id=1, source_target_pairs={{0,4},{1,5},{2,6},{3,7},{4,8},{5,9},{6,10},{7,11},{8,12},{9,13},{1... | collective-permute-start | bytes 147464 | tf_op jit(solution)/shard_map/ppermute | solution.py:685
  19.6 21.9 %collective-permute-start.3 = (f32[96,128]{1,0:T(8,128)S(1)}, f32[96,128]{1,0:T(8,128)S(1)}, u32[]{:S(2)}, u32[]{:S(2)}) collective-permute-start(f32[96,128]{1,0:T(8,128)S(1)} %get-tuple-element.53), channel_id=1, source_target_pairs={{0,8},{1,9},{2,10},{3,11},{4,12},{5,13},{6,14},{7,15},{8,0},{9,1},... | collective-permute-start | bytes 147464 | tf_op jit(solution)/shard_map/ppermute | solution.py:685
  21.9 19.6 %collective-permute-start.4 = (f32[96,128]{1,0:T(8,128)S(1)}, f32[96,128]{1,0:T(8,128)S(1)}, u32[]{:S(2)}, u32[]{:S(2)}) collective-permute-start(f32[96,128]{1,0:T(8,128)S(1)} %get-tuple-element.54), channel_id=1, source_target_pairs={{0,12},{1,13},{2,14},{3,15},{4,0},{5,1},{6,2},{7,3},{8,4},{9,5},{1... | collective-permute-start | bytes 147464 | tf_op jit(solution)/shard_map/ppermute | solution.py:685
  41.5 4.4 %collective-permute-start.5 = (f32[96,128]{1,0:T(8,128)S(1)}, f32[96,128]{1,0:T(8,128)S(1)}, u32[]{:S(2)}, u32[]{:S(2)}) collective-permute-start(f32[96,128]{1,0:T(8,128)S(1)} %get-tuple-element.56), channel_id=1, source_target_pairs={{0,1},{1,0},{2,3},{3,2},{4,5},{5,4},{6,7},{7,6},{8,9},{9,8},{10,11... | collective-permute-start | bytes 147464 | tf_op jit(solution)/shard_map/ppermute | solution.py:685
  43.1 4.1 %collective-permute-start.6 = (f32[96,128]{1,0:T(8,128)S(1)}, f32[96,128]{1,0:T(8,128)S(1)}, u32[]{:S(2)}, u32[]{:S(2)}) collective-permute-start(f32[96,128]{1,0:T(8,128)S(1)} %get-tuple-element.57), channel_id=1, source_target_pairs={{0,2},{1,3},{2,0},{3,1},{4,6},{5,7},{6,4},{7,5},{8,10},{9,11},{10,... | collective-permute-start | bytes 147464 | tf_op jit(solution)/shard_map/ppermute | solution.py:685
  44.5 5.0 %collective-permute-start.7 = (f32[96,128]{1,0:T(8,128)S(1)}, f32[96,128]{1,0:T(8,128)S(1)}, u32[]{:S(2)}, u32[]{:S(2)}) collective-permute-start(f32[96,128]{1,0:T(8,128)S(1)} %get-tuple-element.58), channel_id=1, source_target_pairs={{0,3},{1,2},{2,1},{3,0},{4,7},{5,6},{6,5},{7,4},{8,11},{9,10},{10,... | collective-permute-start | bytes 147464 | tf_op jit(solution)/shard_map/ppermute | solution.py:685
  49.6 47.3 %copy-start.3 = (f32[32,256]{1,0:T(8,128)S(1)}, f32[32,256]{1,0:T(8,128)}, u32[]{:S(2)}) copy-start(f32[32,256]{1,0:T(8,128)} %constant.14.clone.rest_6_) | copy-start | bytes 98308
  56.9 41.9 %all-to-all-start.1 = ((bf16[16,24,1024]{2,1,0:T(8,128)(2,1)}), bf16[16,24,1024]{2,1,0:T(8,128)(2,1)S(1)}, u32[]{:S(2)}, u32[]{:S(2)}) async-start(bf16[16,24,1024]{2,1,0:T(8,128)(2,1)} %get-tuple-element.60), calls=%async_computation.1 | async-start | bytes 1572864 | tf_op jit(solution)/shard_map/all_to_all | solution.py:613
  60.5 5.1 %collective-permute-start.8 = (f32[32,128]{1,0:T(8,128)S(1)}, f32[32,128]{1,0:T(8,128)S(1)}, u32[]{:S(2)}, u32[]{:S(2)}) collective-permute-start(f32[32,128]{1,0:T(8,128)S(1)} %get-tuple-element.67), channel_id=1, source_target_pairs={{0,1},{1,0},{2,3},{3,2},{4,5},{5,4},{6,7},{7,6},{8,9},{9,8},{10,11... | collective-permute-start | bytes 49160 | tf_op jit(solution)/shard_map/ppermute | solution.py:685
  62.4 4.6 %collective-permute-start.9 = (f32[32,128]{1,0:T(8,128)S(1)}, f32[32,128]{1,0:T(8,128)S(1)}, u32[]{:S(2)}, u32[]{:S(2)}) collective-permute-start(f32[32,128]{1,0:T(8,128)S(1)} %get-tuple-element.68), channel_id=1, source_target_pairs={{0,2},{1,3},{2,0},{3,1},{4,6},{5,7},{6,4},{7,5},{8,10},{9,11},{10,... | collective-permute-start | bytes 49160 | tf_op jit(solution)/shard_map/ppermute | solution.py:685
  63.9 4.8 %collective-permute-start.10 = (f32[32,128]{1,0:T(8,128)S(1)}, f32[32,128]{1,0:T(8,128)S(1)}, u32[]{:S(2)}, u32[]{:S(2)}) collective-permute-start(f32[32,128]{1,0:T(8,128)S(1)} %get-tuple-element.69), channel_id=1, source_target_pairs={{0,3},{1,2},{2,1},{3,0},{4,7},{5,6},{6,5},{7,4},{8,11},{9,10},{10,... | collective-permute-start | bytes 49160 | tf_op jit(solution)/shard_map/ppermute | solution.py:685
  68.7 7.6 %collective-permute-start.11 = (f32[32,128]{1,0:T(8,128)S(1)}, f32[32,128]{1,0:T(8,128)S(1)}, u32[]{:S(2)}, u32[]{:S(2)}) collective-permute-start(f32[32,128]{1,0:T(8,128)S(1)} %get-tuple-element.71), channel_id=1, source_target_pairs={{0,4},{1,5},{2,6},{3,7},{4,8},{5,9},{6,10},{7,11},{8,12},{9,13},{1... | collective-permute-start | bytes 49160 | tf_op jit(solution)/shard_map/ppermute | solution.py:685
  70.2 9.7 %collective-permute-start.12 = (f32[32,128]{1,0:T(8,128)S(1)}, f32[32,128]{1,0:T(8,128)S(1)}, u32[]{:S(2)}, u32[]{:S(2)}) collective-permute-start(f32[32,128]{1,0:T(8,128)S(1)} %get-tuple-element.72), channel_id=1, source_target_pairs={{0,8},{1,9},{2,10},{3,11},{4,12},{5,13},{6,14},{7,15},{8,0},{9,1},... | collective-permute-start | bytes 49160 | tf_op jit(solution)/shard_map/ppermute | solution.py:685
  72.7 7.3 %collective-permute-start.13 = (f32[32,128]{1,0:T(8,128)S(1)}, f32[32,128]{1,0:T(8,128)S(1)}, u32[]{:S(2)}, u32[]{:S(2)}) collective-permute-start(f32[32,128]{1,0:T(8,128)S(1)} %get-tuple-element.73), channel_id=1, source_target_pairs={{0,12},{1,13},{2,14},{3,15},{4,0},{5,1},{6,2},{7,3},{8,4},{9,5},{1... | collective-permute-start | bytes 49160 | tf_op jit(solution)/shard_map/ppermute | solution.py:685
  80.0 1.3 %collective-permute-start.14 = (f32[64,128]{1,0:T(8,128)S(1)}, f32[64,128]{1,0:T(8,128)S(1)}, u32[]{:S(2)}, u32[]{:S(2)}) collective-permute-start(f32[64,128]{1,0:T(8,128)S(1)} %get-tuple-element.75), channel_id=1, source_target_pairs={{0,16},{16,0},{1,17},{17,1},{2,18},{18,2},{3,19},{19,3},{4,20},{20... | collective-permute-start | bytes 98312 | tf_op jit(solution)/shard_map/ppermute | solution.py:685
  81.9 1.2 %collective-permute-start.15 = (f32[32,128]{1,0:T(8,128)S(1)}, f32[32,128]{1,0:T(8,128)S(1)}, u32[]{:S(2)}, u32[]{:S(2)}) collective-permute-start(f32[32,128]{1,0:T(8,128)S(1)} %get-tuple-element.77), channel_id=1, source_target_pairs={{0,16},{16,0},{1,17},{17,1},{2,18},{18,2},{3,19},{19,3},{4,20},{20... | collective-permute-start | bytes 49160 | tf_op jit(solution)/shard_map/ppermute | solution.py:685
  83.2 3.7 %collective-permute-start.16 = (f32[16,128]{1,0:T(8,128)S(1)}, f32[16,128]{1,0:T(8,128)S(1)}, u32[]{:S(2)}, u32[]{:S(2)}) collective-permute-start(f32[16,128]{1,0:T(8,128)S(1)} %get-tuple-element.79), channel_id=1, source_target_pairs={{0,1},{1,0},{2,3},{3,2},{4,5},{5,4},{6,7},{7,6},{8,9},{9,8},{10,11... | collective-permute-start | bytes 24584 | tf_op jit(solution)/shard_map/ppermute | solution.py:685
  84.7 3.7 %collective-permute-start.17 = (f32[16,128]{1,0:T(8,128)S(1)}, f32[16,128]{1,0:T(8,128)S(1)}, u32[]{:S(2)}, u32[]{:S(2)}) collective-permute-start(f32[16,128]{1,0:T(8,128)S(1)} %get-tuple-element.80), channel_id=1, source_target_pairs={{0,2},{1,3},{2,0},{3,1},{4,6},{5,7},{6,4},{7,5},{8,10},{9,11},{10,... | collective-permute-start | bytes 24584 | tf_op jit(solution)/shard_map/ppermute | solution.py:685
  86.2 4.5 %collective-permute-start.18 = (f32[16,128]{1,0:T(8,128)S(1)}, f32[16,128]{1,0:T(8,128)S(1)}, u32[]{:S(2)}, u32[]{:S(2)}) collective-permute-start(f32[16,128]{1,0:T(8,128)S(1)} %get-tuple-element.81), channel_id=1, source_target_pairs={{0,3},{1,2},{2,1},{3,0},{4,7},{5,6},{6,5},{7,4},{8,11},{9,10},{10,... | collective-permute-start | bytes 24584 | tf_op jit(solution)/shard_map/ppermute | solution.py:685
  90.8 5.5 %collective-permute-start.19 = (f32[16,128]{1,0:T(8,128)S(1)}, f32[16,128]{1,0:T(8,128)S(1)}, u32[]{:S(2)}, u32[]{:S(2)}) collective-permute-start(f32[16,128]{1,0:T(8,128)S(1)} %get-tuple-element.83), channel_id=1, source_target_pairs={{0,4},{1,5},{2,6},{3,7},{4,8},{5,9},{6,10},{7,11},{8,12},{9,13},{1... | collective-permute-start | bytes 24584 | tf_op jit(solution)/shard_map/ppermute | solution.py:685
  91.5 4.7 %collective-permute-start.20 = (f32[16,128]{1,0:T(8,128)S(1)}, f32[16,128]{1,0:T(8,128)S(1)}, u32[]{:S(2)}, u32[]{:S(2)}) collective-permute-start(f32[16,128]{1,0:T(8,128)S(1)} %get-tuple-element.84), channel_id=1, source_target_pairs={{0,8},{1,9},{2,10},{3,11},{4,12},{5,13},{6,14},{7,15},{8,0},{9,1},... | collective-permute-start | bytes 24584 | tf_op jit(solution)/shard_map/ppermute | solution.py:685
  93.0 3.8 %collective-permute-start.21 = (f32[16,128]{1,0:T(8,128)S(1)}, f32[16,128]{1,0:T(8,128)S(1)}, u32[]{:S(2)}, u32[]{:S(2)}) collective-permute-start(f32[16,128]{1,0:T(8,128)S(1)} %get-tuple-element.85), channel_id=1, source_target_pairs={{0,12},{1,13},{2,14},{3,15},{4,0},{5,1},{6,2},{7,3},{8,4},{9,5},{1... | collective-permute-start | bytes 24584 | tf_op jit(solution)/shard_map/ppermute | solution.py:685

commit v7 on v6

--- a/solution.py
+++ b/solution.py
@@ -19,8 +19,8 @@
 F32 = jnp.float32
 BF16 = jnp.bfloat16
 
-POWER = 12
-TOP = 2.0**10.5
+POWER = 13
+TOP = 2.0**9.69
 GAIN = 1.25
 
 
@@ -28,8 +28,7 @@
     scaled = value * scale
     second = scaled * scaled
     fourth = second * second
-    size = fourth * fourth * fourth
-    return jnp.where(scaled < 0.0, -size, size)
+    return (fourth * fourth) * (fourth * scaled)
 
 
 def decode(code, scale):
@@ -342,24 +341,6 @@
     lax.fori_loop(0, sources, turn, start, unroll=2)
     for dest in range(sources):
         send(dest).wait()
-
-
-def settle_kernel(per, bulk, top, rho, ur, up, near, sems):
-    nz = rho.shape[0]
-    sources, _, seg = bulk.shape
-    group = nz * per
-    unit = jnp.concatenate([top[0:1, :] * (GAIN / TOP)] * (seg // LANES), axis=1)
-    copies = [
-        pltpu.make_async_copy(near.at[c], far, sems.at[c]) for c, far in enumerate((rho, ur, up))
-    ]
-    for c in range(3):
-        for a in range(sources):
-            value = decode(bulk[a, c * group : (c + 1) * group, :].astype(F32), unit)
-            for z in range(nz):
-                near[c, z, a * per : (a + 1) * per, :] = value[z * per : (z + 1) * per, :]
-        copies[c].start()
-    for copy in copies:
-        copy.wait()
 
 
 def forward_kernel(per, nz, modes, fast, far_shift, far_remainder, circle, twiddle, short, steps, *rest):
@@ -491,9 +472,9 @@
     return (from_rad * slow + from_slow) * fast + from_fast
 
 
-def couple_kernel(per, local, fast, slow, kernel, *rest):
+def couple_kernel(per, local, fast, slow, kernel, mixed, *rest):
     rad_count = lax.axis_size("rad")
-    columns, outs = rest[:rad_count], rest[rad_count:]
+    columns, outs, (tables, factor) = rest[:rad_count], rest[rad_count:-2], rest[-2:]
     sources = slow * fast * rad_count
     nq = columns[0].shape[1]
     total = sources * per
@@ -528,48 +509,77 @@
     slabs = [result[i * share : (i + 1) * share, :] for i in range(len(outs))]
     for offset, out in enumerate(outs):
         out[...] = pick(slabs, sent_to(rad, offset, len(outs), False))
-
-
-def inverse_kernel(per, local, fast, *rest):
-    blocks, (circle, twiddle, mixed, out) = rest[:-4], rest[-4:]
+    share = nq // local
+    source = arrival_source(slow, fast, row_iota((sources, sources)))
+    order = (source == lane_iota((sources, sources))).astype(F32)
+    ordered = jnp.dot(order, mixed[...], precision=EXACT, preferred_element_type=F32)
+    own = arrival_source(slow, fast, row_iota(ordered.shape)) % share
+    tables[...] = jnp.concatenate([jnp.where(own == h, ordered, 0.0) for h in range(share)], axis=1)
+    source = arrival_source(slow, fast, row_iota((sources, nq)))
+    constant = (source == 0) & (lane_iota((sources, nq)) % local == 0)
+    factor[...] = jnp.where(constant, 1.0, 2.0) / (nq * LANES)
+
+
+def three_pass_dot(left, right):
+    dot = functools.partial(jnp.dot, preferred_element_type=F32)
+    left_high, right_high = left.astype(BF16), right.astype(BF16)
+    left_low = (left - left_high.astype(F32)).astype(BF16)
+    right_low = (right - right_high.astype(F32)).astype(BF16)
+    return dot(left_high, right_high) + (dot(left_low, right_high) + dot(left_high, right_low))
+
+
+def settle_kernel(per, bulk, top, rho, ur, up, near, sems):
+    nz = rho.shape[0]
+    sources, _, seg = bulk.shape
+    group = nz * per
+    unit = jnp.concatenate([top[0:1, :] * (GAIN / TOP)] * (seg // LANES), axis=1)
+    half = sources // 2 * per
+    copies = [
+        pltpu.make_async_copy(
+            near.at[c, :, pl.ds(i * half, half), :], far.at[:, pl.ds(i * half, half), :], sems.at[2 * c + i]
+        )
+        for c, far in enumerate((rho, ur, up))
+        for i in range(2)
+    ]
+    for c in range(3):
+        for a in range(sources):
+            value = decode(bulk[a, c * group : (c + 1) * group, :].astype(F32), unit)
+            for z in range(nz):
+                near[c, z, a * per : (a + 1) * per, :] = value[z * per : (z + 1) * per, :]
+            if (a + 1) * per % half == 0:
+                copies[2 * c + a * per // half].start()
+    for copy in copies:
+        copy.wait()
+
+
+def inverse_kernel(per, local, circle, twiddle, tables, factor, *rest):
+    blocks, out = rest[:-1], rest[-1]
     slow = len(blocks)
     nq = circle.shape[0]
-    length = nq * LANES
     share = nq // local
-    rad_count = lax.axis_size("rad")
-    count = slow * fast * rad_count
-    dot = functools.partial(jnp.dot, precision=EXACT, preferred_element_type=F32)
-    block_id = row_iota((count, nq))
-    first = (block_id == 0) & (lane_iota((count, nq)) % local == 0)
-    factor = jnp.where(first, 1.0, 2.0) / length
-    source = arrival_source(slow, fast, lane_iota((count, count)))
-    order = (source == row_iota((count, count))).astype(F32)
+    count = tables.shape[0]
     picked = []
     for k in range(per):
         rows = [
-            ref[pl.ds(k, fast * rad_count, stride=per), :] if per > 1 else ref[...] for ref in blocks
+            ref[pl.ds(k, count // slow, stride=per), :] if per > 1 else ref[...] for ref in blocks
         ]
-        picked.append(jnp.concatenate(rows, axis=0))
-    values = dot(order, jnp.concatenate(picked, axis=1)) * jnp.concatenate([factor] * per, axis=1)
-    tables = mixed[...]
-    own = row_iota(tables.shape) % share
-    tables = jnp.concatenate([jnp.where(own == h, tables, 0.0) for h in range(share)], axis=1)
-    mid = dot(values.T, tables)
+        picked.append(jnp.concatenate(rows, axis=0) * factor[...])
+    mid = three_pass_dot(jnp.concatenate(picked, axis=1).T, tables[...])
     turn_cos, turn_sin = twiddle[:, :LANES], twiddle[:, LANES:]
     turned = []
     for k in range(per):
         real, imag = [], []
         for h in range(share):
             at = 2 * LANES * h
-            top = mid[k * nq : k * nq + local, at : at + 2 * LANES]
-            bottom = mid[k * nq + local : k * nq + 2 * local, at : at + 2 * LANES]
-            real.append(top[:, :LANES] - bottom[:, LANES:])
-            imag.append(top[:, LANES:] + bottom[:, :LANES])
+            upper = mid[k * nq : k * nq + local, at : at + 2 * LANES]
+            lower = mid[k * nq + local : k * nq + 2 * local, at : at + 2 * LANES]
+            real.append(upper[:, :LANES] - lower[:, LANES:])
+            imag.append(upper[:, LANES:] + lower[:, :LANES])
         real = jnp.concatenate(real, axis=0)
         imag = jnp.concatenate(imag, axis=0)
         pair = [real * turn_cos - imag * turn_sin, -(real * turn_sin + imag * turn_cos)]
         turned.append(jnp.concatenate(pair, axis=0))
-    wave = dot(circle[...], jnp.concatenate(turned, axis=1))
+    wave = three_pass_dot(circle[...], jnp.concatenate(turned, axis=1))
     for k in range(per):
         for q in range(nq):
             out[k : k + 1, q * LANES : (q + 1) * LANES] = wave[
@@ -742,26 +752,22 @@
         bytes_accessed=100_000,
     )(*columns)
     columns = hop(columns, "rad", rad, 1)
-    blocks = call(
+    j_of_block = np.arange(devices) * local // nq
+    mixed = np.concatenate(cos_sin(j_of_block, l_id, LANES), axis=1)
+    *blocks, tables, factor = call(
         functools.partial(couple_kernel, per, local, fast, slow),
-        tuple(pltpu.VMEM((azi * per, nq), F32) for _ in range(rad)),
+        (
+            *(pltpu.VMEM((azi * per, nq), F32) for _ in range(rad)),
+            pltpu.VMEM((devices, nq // local * 2 * LANES), F32),
+            pltpu.VMEM((devices, nq), F32),
+        ),
         name="couple",
         flops=100_000_000,
         bytes_accessed=1_000_000,
-    )(kernel, *columns)
+    )(kernel, jnp.asarray(mixed), *columns)
     blocks = hop(blocks, "rad", rad, 1)
     blocks = route(blocks, fast, per, 1, "block_fast")
     blocks = route(blocks, slow, per, fast, "block_slow", ring=True)
-    j_of_block = np.arange(devices) * local // nq
-    mixed = np.concatenate(cos_sin(j_of_block, l_id, LANES), axis=1)
-    turn = np.concatenate(cos_sin(k_id, l_id, length), axis=1)
-    potential = call(
-        functools.partial(inverse_kernel, per, local, fast),
-        shape_of((per, length)),
-        name="inverse",
-        flops=100_000_000,
-        bytes_accessed=1_000_000,
-    )(*blocks, jnp.asarray(circle), jnp.asarray(turn), jnp.asarray(mixed))
 
     moved, top = call(
         functools.partial(advect_kernel, per, nz),
@@ -783,11 +789,19 @@
         bytes_accessed=12 * nz * slab * seg,
     )(cycle_shift, remainder, bulk, sides)
     moved = exchange(moved, "azi")
+    turn = np.concatenate(cos_sin(k_id, l_id, length), axis=1)
+    potential = call(
+        functools.partial(inverse_kernel, per, local),
+        shape_of((per, length)),
+        name="inverse",
+        flops=100_000_000,
+        bytes_accessed=1_000_000,
+    )(jnp.asarray(circle), jnp.asarray(turn), tables, factor, *blocks)
     results = call(
         functools.partial(settle_kernel, per),
         tuple(pltpu.HBM((nz, slab, seg), F32) for _ in range(3)),
         out_specs=(far,) * 3,
-        scratch=(pltpu.VMEM((3, nz, slab, seg), F32), pltpu.SemaphoreType.DMA((3,))),
+        scratch=(pltpu.VMEM((3, nz, slab, seg), F32), pltpu.SemaphoreType.DMA((6,))),
         name="settle",
         flops=20 * 3 * nz * slab * seg,
         bytes_accessed=18 * nz * slab * seg,

time: 101 us -> 100 us (0.990)
  no operation moved by 1% of the time
where the time goes in v7:
time: 100 us; the launch traced here: 99.7 us
  waiting for transfers between devices  41.4 us (41%)
  starting transfers between devices  38.5 us (38%)
  Pallas kernels  18.8 us (19%)
    ppermute x20, waiting for transfers between devices, hop(): lax.ppermute(buffers[o], axis, [(i, i + (sent_to(i // step % size, o, siz...  41.4 us
    ppermute x20, starting transfers between devices, hop(): lax.ppermute(buffers[o], axis, [(i, i + (sent_to(i // step % size, o, siz...  25.9 us
    pallas_call x15, Pallas kernels, run(): return kernel(*near)  18.8 us
    all_to_all x2, starting transfers between devices, exchange(): return lax.all_to_all(array, axes, 0, 0, tiled=True)  11.9 us
  transfers between devices with their start and end apart: 24, of which 17 were waited for; matrix products, arithmetic and copies ran while one was open for 0% of the time, Pallas kernels for 6%

profile of v7, /device:TPU:0, one launch (start us, length us, event | category | flops | bytes accessed | tf_op | source)
XLA Modules:
  0.0 99.7 jit_solution(7190380912614726765)
XLA Ops:
  0.6 1.3 %shard_map.148 = (f32[3,4,2,1024]{3,2,1,0:T(2,128)S(1)}, f32[3,4,2,1024]{3,2,1,0:T(2,128)S(1)}) custom-call(f32[4,32,1024]{2,1,0:T(8,128)} %rho.3, f32[4,32,1024]{2,1,0:T(8,128)} %ur.3, f32[4,32,1024]{2,1,0:T(8,128)} %up.3), custom_call_target="tpu_custom_call" | custom-call | bytes 786432 | tf_op jit(solution)/shard_map/pallas_call | solution.py:617
  1.9 0.6 collective-permute-start
  2.5 0.1 collective-permute-start.1
  2.5 2.1 %shard_map.147 = (f32[3,4,40,1152]{3,2,1,0:T(8,128)S(1)}, f32[3,4,40,1152]{3,2,1,0:T(8,128)S(1)}) custom-call(f32[4,32,1024]{2,1,0:T(8,128)} %rho.3, f32[4,32,1024]{2,1,0:T(8,128)} %ur.3, f32[4,32,1024]{2,1,0:T(8,128)} %up.3), custom_call_target="tpu_custom_call" | custom-call | bytes 1572864 | tf_op jit(solution)/shard_map/pallas_call | solution.py:617
  4.7 0.0 collective-permute-done.low
  4.7 0.0 collective-permute-done.1.high
  4.7 0.0 copy-start.1
  4.7 0.0 copy-start.2
  4.7 0.0 copy-start.4
  4.7 0.0 copy-start.5
  4.7 0.0 copy-start.6
  4.8 0.0 copy-start.7
  4.8 4.4 %shard_map.149 = (bf16[16,192,128]{2,1,0:T(8,128)(2,1)}, f32[16,24,128]{2,1,0:T(8,128)S(1)}, f32[3,4,40,1152]{3,2,1,0:T(8,128)S(1)}, f32[3,4,40,1152]{3,2,1,0:T(8,128)S(1)}) custom-call(f32[3,4,40,1152]{3,2,1,0:T(8,128)S(1)} %get-tuple-element.47.field_in, ...), custom_call_target="tpu_custom_call", output_to_operand_aliasing={{2}: (0, {}), {3}: (1, {})} | custom-call | flops 39321600 | bytes 3145728 | tf_op jit(solution)/shard_map/pallas_call | solution.py:617
  9.2 8.3 %all-to-all-start = ((bf16[16,192,128]{2,1,0:T(8,128)(2,1)}), bf16[16,192,128]{2,1,0:T(8,128)(2,1)S(1)}, u32[]{:S(2)}, u32[]{:S(2)}) async-start(bf16[16,192,128]{2,1,0:T(8,128)(2,1)} %get-tuple-element.51), calls=%async_computation | async-start | bytes 1572864 | tf_op jit(solution)/shard_map/all_to_all | solution.py:623
  17.5 0.0 copy-start
  17.5 0.0 copy-start.3
  17.5 0.1 shard_map.150
  17.6 2.0 %collective-permute-start.2 = (f32[96,128]{1,0:T(8,128)S(1)}, f32[96,128]{1,0:T(8,128)S(1)}, u32[]{:S(2)}, u32[]{:S(2)}) collective-permute-start(f32[96,128]{1,0:T(8,128)S(1)} %get-tuple-element.54), channel_id=1, source_target_pairs={{0,4},{1,5},{2,6},{3,7},{4,8},{5,9},{6,10},{7,11},{8,12},{9,13},{1... | collective-permute-start | bytes 147464 | tf_op jit(solution)/shard_map/ppermute | solution.py:695
  19.6 2.4 %collective-permute-start.3 = (f32[96,128]{1,0:T(8,128)S(1)}, f32[96,128]{1,0:T(8,128)S(1)}, u32[]{:S(2)}, u32[]{:S(2)}) collective-permute-start(f32[96,128]{1,0:T(8,128)S(1)} %get-tuple-element.55), channel_id=1, source_target_pairs={{0,8},{1,9},{2,10},{3,11},{4,12},{5,13},{6,14},{7,15},{8,0},{9,1},... | collective-permute-start | bytes 147464 | tf_op jit(solution)/shard_map/ppermute | solution.py:695
  21.9 1.5 %collective-permute-start.4 = (f32[96,128]{1,0:T(8,128)S(1)}, f32[96,128]{1,0:T(8,128)S(1)}, u32[]{:S(2)}, u32[]{:S(2)}) collective-permute-start(f32[96,128]{1,0:T(8,128)S(1)} %get-tuple-element.56), channel_id=1, source_target_pairs={{0,12},{1,13},{2,14},{3,15},{4,0},{5,1},{6,2},{7,3},{8,4},{9,5},{1... | collective-permute-start | bytes 147464 | tf_op jit(solution)/shard_map/ppermute | solution.py:695
  23.4 13.3 %collective-permute-done.2.rest_1_ = f32[96,128]{1,0:T(8,128)S(1)} collective-permute-done((f32[96,128]{1,0:T(8,128)S(1)}, f32[96,128]{1,0:T(8,128)S(1)}, u32[]{:S(2)}, u32[]{:S(2)}) %collective-permute-start.2) | collective-permute-done | bytes 49184 | tf_op jit(solution)/shard_map/ppermute | solution.py:695
  36.6 4.8 %collective-permute-done.3.rest_2_ = f32[96,128]{1,0:T(8,128)S(1)} collective-permute-done((f32[96,128]{1,0:T(8,128)S(1)}, f32[96,128]{1,0:T(8,128)S(1)}, u32[]{:S(2)}, u32[]{:S(2)}) %collective-permute-start.3) | collective-permute-done | bytes 49184 | tf_op jit(solution)/shard_map/ppermute | solution.py:695
  41.5 0.0 collective-permute-done.4.rest_3_
  41.5 1.5 %collective-permute-start.5 = (f32[96,128]{1,0:T(8,128)S(1)}, f32[96,128]{1,0:T(8,128)S(1)}, u32[]{:S(2)}, u32[]{:S(2)}) collective-permute-start(f32[96,128]{1,0:T(8,128)S(1)} %get-tuple-element.58), channel_id=1, source_target_pairs={{0,1},{1,0},{2,3},{3,2},{4,5},{5,4},{6,7},{7,6},{8,9},{9,8},{10,11... | collective-permute-start | bytes 147464 | tf_op jit(solution)/shard_map/ppermute | solution.py:695
  43.1 1.5 %collective-permute-start.6 = (f32[96,128]{1,0:T(8,128)S(1)}, f32[96,128]{1,0:T(8,128)S(1)}, u32[]{:S(2)}, u32[]{:S(2)}) collective-permute-start(f32[96,128]{1,0:T(8,128)S(1)} %get-tuple-element.59), channel_id=1, source_target_pairs={{0,2},{1,3},{2,0},{3,1},{4,6},{5,7},{6,4},{7,5},{8,10},{9,11},{10,... | collective-permute-start | bytes 147464 | tf_op jit(solution)/shard_map/ppermute | solution.py:695
  44.5 0.6 collective-permute-start.7
  45.1 0.8 collective-permute-done.5
  45.9 1.2 %collective-permute-done.6 = f32[96,128]{1,0:T(8,128)S(1)} collective-permute-done((f32[96,128]{1,0:T(8,128)S(1)}, f32[96,128]{1,0:T(8,128)S(1)}, u32[]{:S(2)}, u32[]{:S(2)}) %collective-permute-start.6) | collective-permute-done | bytes 49184 | tf_op jit(solution)/shard_map/ppermute | solution.py:695
  47.2 2.4 %collective-permute-done.7 = f32[96,128]{1,0:T(8,128)S(1)} collective-permute-done((f32[96,128]{1,0:T(8,128)S(1)}, f32[96,128]{1,0:T(8,128)S(1)}, u32[]{:S(2)}, u32[]{:S(2)}) %collective-permute-start.7) | collective-permute-done | bytes 49184 | tf_op jit(solution)/shard_map/ppermute | solution.py:695
  49.6 1.5 %shard_map.152 = (f32[128,128]{1,0:T(8,128)S(1)}, f32[16,24,128]{2,1,0:T(8,128)S(1)}) custom-call(s32[32]{0:T(128)S(1)} %copy-done.6, f32[32]{0:T(128)S(1)} %copy-done.7, f32[128,256]{1,0:T(8,128)S(1)} %copy-done.2, f32[128,256]{1,0:T(8,128)S(1)} %copy-done.1, f32[32,128]{1,0:T(8,128)S(1)} %copy-done.5, f32[32,256]{1,0:T(8,128)S(1)} %copy-done.4, ...), custom_call_target="tpu_custom_call" | custom-call | flops 100000000 | bytes 1000000 | tf_op jit(solution)/shard_map/pallas_call | solution.py:617
  51.1 0.0 all-to-all-done.bulk
  51.1 5.7 %shard_map.153 = (bf16[16,24,1024]{2,1,0:T(8,128)(2,1)}, f32[8,128]{1,0:T(8,128)S(1)}) custom-call(s32[32]{0:T(128)S(1)} %copy-done.6, f32[32]{0:T(128)S(1)} %copy-done.7, bf16[16,192,128]{2,1,0:T(8,128)(2,1)S(1)} %all-to-all-done.bulk, f32[16,24,128]{2,1,0:T(8,128)S(1)} %get-tuple-element.61.sides), custom_call_target="tpu_custom_call" | custom-call | flops 19660800 | bytes 1572864 | tf_op jit(solution)/shard_map/pallas_call | solution.py:617
  56.8 3.6 %all-to-all-start.1 = ((bf16[16,24,1024]{2,1,0:T(8,128)(2,1)}), bf16[16,24,1024]{2,1,0:T(8,128)(2,1)S(1)}, u32[]{:S(2)}, u32[]{:S(2)}) async-start(bf16[16,24,1024]{2,1,0:T(8,128)(2,1)} %get-tuple-element.62), calls=%async_computation.1 | async-start | bytes 1572864 | tf_op jit(solution)/shard_map/all_to_all | solution.py:623
  60.4 1.9 %collective-permute-start.8 = (f32[32,128]{1,0:T(8,128)S(1)}, f32[32,128]{1,0:T(8,128)S(1)}, u32[]{:S(2)}, u32[]{:S(2)}) collective-permute-start(f32[32,128]{1,0:T(8,128)S(1)} %get-tuple-element.69), channel_id=1, source_target_pairs={{0,1},{1,0},{2,3},{3,2},{4,5},{5,4},{6,7},{7,6},{8,9},{9,8},{10,11... | collective-permute-start | bytes 49160 | tf_op jit(solution)/shard_map/ppermute | solution.py:695
  62.3 1.5 %collective-permute-start.9 = (f32[32,128]{1,0:T(8,128)S(1)}, f32[32,128]{1,0:T(8,128)S(1)}, u32[]{:S(2)}, u32[]{:S(2)}) collective-permute-start(f32[32,128]{1,0:T(8,128)S(1)} %get-tuple-element.70), channel_id=1, source_target_pairs={{0,2},{1,3},{2,0},{3,1},{4,6},{5,7},{6,4},{7,5},{8,10},{9,11},{10,... | collective-permute-start | bytes 49160 | tf_op jit(solution)/shard_map/ppermute | solution.py:695
  63.8 0.2 collective-permute-start.10
  64.0 1.6 %collective-permute-done.8.rest_1_ = f32[32,128]{1,0:T(8,128)S(1)} collective-permute-done((f32[32,128]{1,0:T(8,128)S(1)}, f32[32,128]{1,0:T(8,128)S(1)}, u32[]{:S(2)}, u32[]{:S(2)}) %collective-permute-start.8) | collective-permute-done | bytes 16416 | tf_op jit(solution)/shard_map/ppermute | solution.py:695
  65.6 1.3 %collective-permute-done.9.rest_2_ = f32[32,128]{1,0:T(8,128)S(1)} collective-permute-done((f32[32,128]{1,0:T(8,128)S(1)}, f32[32,128]{1,0:T(8,128)S(1)}, u32[]{:S(2)}, u32[]{:S(2)}) %collective-permute-start.9) | collective-permute-done | bytes 16416 | tf_op jit(solution)/shard_map/ppermute | solution.py:695
  66.9 1.7 %collective-permute-done.10.rest_3_ = f32[32,128]{1,0:T(8,128)S(1)} collective-permute-done((f32[32,128]{1,0:T(8,128)S(1)}, f32[32,128]{1,0:T(8,128)S(1)}, u32[]{:S(2)}, u32[]{:S(2)}) %collective-permute-start.10) | collective-permute-done | bytes 16416 | tf_op jit(solution)/shard_map/ppermute | solution.py:695
  68.6 1.5 %collective-permute-start.11 = (f32[32,128]{1,0:T(8,128)S(1)}, f32[32,128]{1,0:T(8,128)S(1)}, u32[]{:S(2)}, u32[]{:S(2)}) collective-permute-start(f32[32,128]{1,0:T(8,128)S(1)} %get-tuple-element.73), channel_id=1, source_target_pairs={{0,4},{1,5},{2,6},{3,7},{4,8},{5,9},{6,10},{7,11},{8,12},{9,13},{1... | collective-permute-start | bytes 49160 | tf_op jit(solution)/shard_map/ppermute | solution.py:695
  70.2 2.4 %collective-permute-start.12 = (f32[32,128]{1,0:T(8,128)S(1)}, f32[32,128]{1,0:T(8,128)S(1)}, u32[]{:S(2)}, u32[]{:S(2)}) collective-permute-start(f32[32,128]{1,0:T(8,128)S(1)} %get-tuple-element.74), channel_id=1, source_target_pairs={{0,8},{1,9},{2,10},{3,11},{4,12},{5,13},{6,14},{7,15},{8,0},{9,1},... | collective-permute-start | bytes 49160 | tf_op jit(solution)/shard_map/ppermute | solution.py:695
  72.6 1.4 %collective-permute-start.13 = (f32[32,128]{1,0:T(8,128)S(1)}, f32[32,128]{1,0:T(8,128)S(1)}, u32[]{:S(2)}, u32[]{:S(2)}) collective-permute-start(f32[32,128]{1,0:T(8,128)S(1)} %get-tuple-element.75), channel_id=1, source_target_pairs={{0,12},{1,13},{2,14},{3,15},{4,0},{5,1},{6,2},{7,3},{8,4},{9,5},{1... | collective-permute-start | bytes 49160 | tf_op jit(solution)/shard_map/ppermute | solution.py:695
  73.9 2.3 %collective-permute-done.11.rest_1_ = f32[32,128]{1,0:T(8,128)S(1)} collective-permute-done((f32[32,128]{1,0:T(8,128)S(1)}, f32[32,128]{1,0:T(8,128)S(1)}, u32[]{:S(2)}, u32[]{:S(2)}) %collective-permute-start.11) | collective-permute-done | bytes 16416 | tf_op jit(solution)/shard_map/ppermute | solution.py:695
  76.2 3.6 %collective-permute-done.12.rest_2_ = f32[32,128]{1,0:T(8,128)S(1)} collective-permute-done((f32[32,128]{1,0:T(8,128)S(1)}, f32[32,128]{1,0:T(8,128)S(1)}, u32[]{:S(2)}, u32[]{:S(2)}) %collective-permute-start.12) | collective-permute-done | bytes 16416 | tf_op jit(solution)/shard_map/ppermute | solution.py:695
  79.9 0.0 collective-permute-done.13.rest_3_
  79.9 0.1 collective-permute-start.14
  80.0 1.2 %collective-permute-done.14.rest_1_ = f32[64,128]{1,0:T(8,128)S(1)} collective-permute-done((f32[64,128]{1,0:T(8,128)S(1)}, f32[64,128]{1,0:T(8,128)S(1)}, u32[]{:S(2)}, u32[]{:S(2)}) %collective-permute-start.14) | collective-permute-done | bytes 32800 | tf_op jit(solution)/shard_map/ppermute | solution.py:695
  81.2 0.7 shard_map.158
  81.9 0.2 collective-permute-start.15
  82.1 1.0 %collective-permute-done.15.rest_1_ = f32[32,128]{1,0:T(8,128)S(1)} collective-permute-done((f32[32,128]{1,0:T(8,128)S(1)}, f32[32,128]{1,0:T(8,128)S(1)}, u32[]{:S(2)}, u32[]{:S(2)}) %collective-permute-start.15) | collective-permute-done | bytes 16416 | tf_op jit(solution)/shard_map/ppermute | solution.py:695
  83.1 1.5 %collective-permute-start.16 = (f32[16,128]{1,0:T(8,128)S(1)}, f32[16,128]{1,0:T(8,128)S(1)}, u32[]{:S(2)}, u32[]{:S(2)}) collective-permute-start(f32[16,128]{1,0:T(8,128)S(1)} %get-tuple-element.83), channel_id=1, source_target_pairs={{0,1},{1,0},{2,3},{3,2},{4,5},{5,4},{6,7},{7,6},{8,9},{9,8},{10,11... | collective-permute-start | bytes 24584 | tf_op jit(solution)/shard_map/ppermute | solution.py:695
  84.7 1.5 %collective-permute-start.17 = (f32[16,128]{1,0:T(8,128)S(1)}, f32[16,128]{1,0:T(8,128)S(1)}, u32[]{:S(2)}, u32[]{:S(2)}) collective-permute-start(f32[16,128]{1,0:T(8,128)S(1)} %get-tuple-element.84), channel_id=1, source_target_pairs={{0,2},{1,3},{2,0},{3,1},{4,6},{5,7},{6,4},{7,5},{8,10},{9,11},{10,... | collective-permute-start | bytes 24584 | tf_op jit(solution)/shard_map/ppermute | solution.py:695
  86.1 0.6 collective-permute-start.18
  86.7 0.2 collective-permute-done.16.rest_1_
  86.9 1.5 %collective-permute-done.17.rest_2_ = f32[16,128]{1,0:T(8,128)S(1)} collective-permute-done((f32[16,128]{1,0:T(8,128)S(1)}, f32[16,128]{1,0:T(8,128)S(1)}, u32[]{:S(2)}, u32[]{:S(2)}) %collective-permute-start.17) | collective-permute-done | bytes 8224 | tf_op jit(solution)/shard_map/ppermute | solution.py:695
  88.3 2.4 %collective-permute-done.18.rest_3_ = f32[16,128]{1,0:T(8,128)S(1)} collective-permute-done((f32[16,128]{1,0:T(8,128)S(1)}, f32[16,128]{1,0:T(8,128)S(1)}, u32[]{:S(2)}, u32[]{:S(2)}) %collective-permute-start.18) | collective-permute-done | bytes 8224 | tf_op jit(solution)/shard_map/ppermute | solution.py:695
  90.7 0.8 collective-permute-start.19
  91.5 1.5 %collective-permute-start.20 = (f32[16,128]{1,0:T(8,128)S(1)}, f32[16,128]{1,0:T(8,128)S(1)}, u32[]{:S(2)}, u32[]{:S(2)}) collective-permute-start(f32[16,128]{1,0:T(8,128)S(1)} %get-tuple-element.88), channel_id=1, source_target_pairs={{0,8},{1,9},{2,10},{3,11},{4,12},{5,13},{6,14},{7,15},{8,0},{9,1},... | collective-permute-start | bytes 24584 | tf_op jit(solution)/shard_map/ppermute | solution.py:695
  93.0 1.6 %collective-permute-start.21 = (f32[16,128]{1,0:T(8,128)S(1)}, f32[16,128]{1,0:T(8,128)S(1)}, u32[]{:S(2)}, u32[]{:S(2)}) collective-permute-start(f32[16,128]{1,0:T(8,128)S(1)} %get-tuple-element.89), channel_id=1, source_target_pairs={{0,12},{1,13},{2,14},{3,15},{4,0},{5,1},{6,2},{7,3},{8,4},{9,5},{1... | collective-permute-start | bytes 24584 | tf_op jit(solution)/shard_map/ppermute | solution.py:695
  94.6 1.6 %collective-permute-done.19.rest_1_ = f32[16,128]{1,0:T(8,128)S(1)} collective-permute-done((f32[16,128]{1,0:T(8,128)S(1)}, f32[16,128]{1,0:T(8,128)S(1)}, u32[]{:S(2)}, u32[]{:S(2)}) %collective-permute-start.19) | collective-permute-done | bytes 8224 | tf_op jit(solution)/shard_map/ppermute | solution.py:695
  96.2 0.6 collective-permute-done.21.rest_3_
  96.8 1.4 %shard_map.161 = f32[2,16384]{1,0:T(2,128)} custom-call(f32[128,256]{1,0:T(8,128)S(1)} %copy-done.2, f32[128,256]{1,0:T(8,128)S(1)} %copy-done.1, f32[32,512]{1,0:T(8,128)S(1)} %get-tuple-element.78.tables, f32[32,128]{1,0:T(8,128)S(1)} %get-tuple-element.79.factor, f32[16,128]{1,0:T(8,128)S(1)} %get-tuple-element.86.rest_0_, ...), custom_call_target="tpu_custom_call" | custom-call | flops 100000000 | bytes 1000000 | tf_op jit(solution)/shard_map/pallas_call | solution.py:617
  98.2 0.0 all-to-all-done.1.bulk
  98.2 1.5 %shard_map.154 = (f32[4,32,1024]{2,1,0:T(8,128)}, f32[4,32,1024]{2,1,0:T(8,128)}, f32[4,32,1024]{2,1,0:T(8,128)}) custom-call(bf16[16,24,1024]{2,1,0:T(8,128)(2,1)S(1)} %all-to-all-done.1.bulk, f32[8,128]{1,0:T(8,128)S(1)} %get-tuple-element.63.top), custom_call_target="tpu_custom_call" | custom-call | flops 7864320 | bytes 2359296 | tf_op jit(solution)/shard_map/pallas_call | solution.py:617
  (15 shorter events, 0.2 us)
Async XLA Ops:
  1.9 2.8 %collective-permute-start = (f32[3,4,2,1024]{3,2,1,0:T(2,128)S(1)}, f32[3,4,2,1024]{3,2,1,0:T(2,128)S(1)}, u32[]{:S(2)}, u32[]{:S(2)}) collective-permute-start(f32[3,4,2,1024]{3,2,1,0:T(2,128)S(1)} %get-tuple-element.49), channel_id=1, source_target_pairs={{0,16},{16,0},{1,17},{17,1},{2,18},{18,2},{3,19},{19,3},{4,20},{20... | collective-permute-start | bytes 294920 | tf_op jit(solution)/shard_map/ppermute | solution.py:666
  2.5 2.2 %collective-permute-start.1 = (f32[3,4,2,1024]{3,2,1,0:T(2,128)S(1)}, f32[3,4,2,1024]{3,2,1,0:T(2,128)S(1)}, u32[]{:S(2)}, u32[]{:S(2)}) collective-permute-start(f32[3,4,2,1024]{3,2,1,0:T(2,128)S(1)} %get-tuple-element.50), channel_id=1, source_target_pairs={{16,0},{0,16},{17,1},{1,17},{18,2},{2,18},{19,3},{3,19},{20,4},{4,... | collective-permute-start | bytes 294920 | tf_op jit(solution)/shard_map/ppermute | solution.py:667
  4.7 44.8 %copy-start.1 = (f32[128,256]{1,0:T(8,128)S(1)}, f32[128,256]{1,0:T(8,128)}, u32[]{:S(2)}) copy-start(f32[128,256]{1,0:T(8,128)} %constant.11.clone.twiddle) | copy-start | bytes 393220
  4.7 44.8 %copy-start.2 = (f32[128,256]{1,0:T(8,128)S(1)}, f32[128,256]{1,0:T(8,128)}, u32[]{:S(2)}) copy-start(f32[128,256]{1,0:T(8,128)} %constant.10.clone.circle) | copy-start | bytes 393220
  4.7 44.8 %copy-start.4 = (f32[32,256]{1,0:T(8,128)S(1)}, f32[32,256]{1,0:T(8,128)}, u32[]{:S(2)}) copy-start(f32[32,256]{1,0:T(8,128)} %constant.13.clone.steps) | copy-start | bytes 98308
  4.7 44.8 %copy-start.5 = (f32[32,128]{1,0:T(8,128)S(1)}, f32[32,128]{1,0:T(8,128)}, u32[]{:S(2)}) copy-start(f32[32,128]{1,0:T(8,128)} %constant.12.clone.short) | copy-start | bytes 49156
  4.7 44.8 %copy-start.6 = (s32[32]{0:T(128)S(1)}, s32[32]{0:T(128)}, u32[]{:S(2)}) copy-start(s32[32]{0:T(128)} %far_shift.3) | copy-start | bytes 388
  4.8 44.8 %copy-start.7 = (f32[32]{0:T(128)S(1)}, f32[32]{0:T(128)}, u32[]{:S(2)}) copy-start(f32[32]{0:T(128)} %far_remainder.3) | copy-start | bytes 388
  9.2 41.9 %all-to-all-start = ((bf16[16,192,128]{2,1,0:T(8,128)(2,1)}), bf16[16,192,128]{2,1,0:T(8,128)(2,1)S(1)}, u32[]{:S(2)}, u32[]{:S(2)}) async-start(bf16[16,192,128]{2,1,0:T(8,128)(2,1)} %get-tuple-element.51), calls=%async_computation | async-start | bytes 1572864 | tf_op jit(solution)/shard_map/all_to_all | solution.py:623
  17.5 63.7 %copy-start = (bf16[64,64,64]{2,1,0:T(8,128)(2,1)S(1)}, bf16[64,64,64]{2,1,0:T(8,128)(2,1)}, u32[]{:S(2)}) copy-start(bf16[64,64,64]{2,1,0:T(8,128)(2,1)} %kernel.1) | copy-start | bytes 1572868
  17.5 63.7 %copy-start.3 = (f32[32,256]{1,0:T(8,128)S(1)}, f32[32,256]{1,0:T(8,128)}, u32[]{:S(2)}) copy-start(f32[32,256]{1,0:T(8,128)} %constant.14.clone.mixed) | copy-start | bytes 98308
  17.6 19.1 %collective-permute-start.2 = (f32[96,128]{1,0:T(8,128)S(1)}, f32[96,128]{1,0:T(8,128)S(1)}, u32[]{:S(2)}, u32[]{:S(2)}) collective-permute-start(f32[96,128]{1,0:T(8,128)S(1)} %get-tuple-element.54), channel_id=1, source_target_pairs={{0,4},{1,5},{2,6},{3,7},{4,8},{5,9},{6,10},{7,11},{8,12},{9,13},{1... | collective-permute-start | bytes 147464 | tf_op jit(solution)/shard_map/ppermute | solution.py:695
  19.6 21.9 %collective-permute-start.3 = (f32[96,128]{1,0:T(8,128)S(1)}, f32[96,128]{1,0:T(8,128)S(1)}, u32[]{:S(2)}, u32[]{:S(2)}) collective-permute-start(f32[96,128]{1,0:T(8,128)S(1)} %get-tuple-element.55), channel_id=1, source_target_pairs={{0,8},{1,9},{2,10},{3,11},{4,12},{5,13},{6,14},{7,15},{8,0},{9,1},... | collective-permute-start | bytes 147464 | tf_op jit(solution)/shard_map/ppermute | solution.py:695
  21.9 19.6 %collective-permute-start.4 = (f32[96,128]{1,0:T(8,128)S(1)}, f32[96,128]{1,0:T(8,128)S(1)}, u32[]{:S(2)}, u32[]{:S(2)}) collective-permute-start(f32[96,128]{1,0:T(8,128)S(1)} %get-tuple-element.56), channel_id=1, source_target_pairs={{0,12},{1,13},{2,14},{3,15},{4,0},{5,1},{6,2},{7,3},{8,4},{9,5},{1... | collective-permute-start | bytes 147464 | tf_op jit(solution)/shard_map/ppermute | solution.py:695
  41.5 4.4 %collective-permute-start.5 = (f32[96,128]{1,0:T(8,128)S(1)}, f32[96,128]{1,0:T(8,128)S(1)}, u32[]{:S(2)}, u32[]{:S(2)}) collective-permute-start(f32[96,128]{1,0:T(8,128)S(1)} %get-tuple-element.58), channel_id=1, source_target_pairs={{0,1},{1,0},{2,3},{3,2},{4,5},{5,4},{6,7},{7,6},{8,9},{9,8},{10,11... | collective-permute-start | bytes 147464 | tf_op jit(solution)/shard_map/ppermute | solution.py:695
  43.1 4.1 %collective-permute-start.6 = (f32[96,128]{1,0:T(8,128)S(1)}, f32[96,128]{1,0:T(8,128)S(1)}, u32[]{:S(2)}, u32[]{:S(2)}) collective-permute-start(f32[96,128]{1,0:T(8,128)S(1)} %get-tuple-element.59), channel_id=1, source_target_pairs={{0,2},{1,3},{2,0},{3,1},{4,6},{5,7},{6,4},{7,5},{8,10},{9,11},{10,... | collective-permute-start | bytes 147464 | tf_op jit(solution)/shard_map/ppermute | solution.py:695
  44.5 5.0 %collective-permute-start.7 = (f32[96,128]{1,0:T(8,128)S(1)}, f32[96,128]{1,0:T(8,128)S(1)}, u32[]{:S(2)}, u32[]{:S(2)}) collective-permute-start(f32[96,128]{1,0:T(8,128)S(1)} %get-tuple-element.60), channel_id=1, source_target_pairs={{0,3},{1,2},{2,1},{3,0},{4,7},{5,6},{6,5},{7,4},{8,11},{9,10},{10,... | collective-permute-start | bytes 147464 | tf_op jit(solution)/shard_map/ppermute | solution.py:695
  56.8 41.4 %all-to-all-start.1 = ((bf16[16,24,1024]{2,1,0:T(8,128)(2,1)}), bf16[16,24,1024]{2,1,0:T(8,128)(2,1)S(1)}, u32[]{:S(2)}, u32[]{:S(2)}) async-start(bf16[16,24,1024]{2,1,0:T(8,128)(2,1)} %get-tuple-element.62), calls=%async_computation.1 | async-start | bytes 1572864 | tf_op jit(solution)/shard_map/all_to_all | solution.py:623
  60.4 5.1 %collective-permute-start.8 = (f32[32,128]{1,0:T(8,128)S(1)}, f32[32,128]{1,0:T(8,128)S(1)}, u32[]{:S(2)}, u32[]{:S(2)}) collective-permute-start(f32[32,128]{1,0:T(8,128)S(1)} %get-tuple-element.69), channel_id=1, source_target_pairs={{0,1},{1,0},{2,3},{3,2},{4,5},{5,4},{6,7},{7,6},{8,9},{9,8},{10,11... | collective-permute-start | bytes 49160 | tf_op jit(solution)/shard_map/ppermute | solution.py:695
  62.3 4.6 %collective-permute-start.9 = (f32[32,128]{1,0:T(8,128)S(1)}, f32[32,128]{1,0:T(8,128)S(1)}, u32[]{:S(2)}, u32[]{:S(2)}) collective-permute-start(f32[32,128]{1,0:T(8,128)S(1)} %get-tuple-element.70), channel_id=1, source_target_pairs={{0,2},{1,3},{2,0},{3,1},{4,6},{5,7},{6,4},{7,5},{8,10},{9,11},{10,... | collective-permute-start | bytes 49160 | tf_op jit(solution)/shard_map/ppermute | solution.py:695
  63.8 4.8 %collective-permute-start.10 = (f32[32,128]{1,0:T(8,128)S(1)}, f32[32,128]{1,0:T(8,128)S(1)}, u32[]{:S(2)}, u32[]{:S(2)}) collective-permute-start(f32[32,128]{1,0:T(8,128)S(1)} %get-tuple-element.71), channel_id=1, source_target_pairs={{0,3},{1,2},{2,1},{3,0},{4,7},{5,6},{6,5},{7,4},{8,11},{9,10},{10,... | collective-permute-start | bytes 49160 | tf_op jit(solution)/shard_map/ppermute | solution.py:695
  68.6 7.6 %collective-permute-start.11 = (f32[32,128]{1,0:T(8,128)S(1)}, f32[32,128]{1,0:T(8,128)S(1)}, u32[]{:S(2)}, u32[]{:S(2)}) collective-permute-start(f32[32,128]{1,0:T(8,128)S(1)} %get-tuple-element.73), channel_id=1, source_target_pairs={{0,4},{1,5},{2,6},{3,7},{4,8},{5,9},{6,10},{7,11},{8,12},{9,13},{1... | collective-permute-start | bytes 49160 | tf_op jit(solution)/shard_map/ppermute | solution.py:695
  70.2 9.7 %collective-permute-start.12 = (f32[32,128]{1,0:T(8,128)S(1)}, f32[32,128]{1,0:T(8,128)S(1)}, u32[]{:S(2)}, u32[]{:S(2)}) collective-permute-start(f32[32,128]{1,0:T(8,128)S(1)} %get-tuple-element.74), channel_id=1, source_target_pairs={{0,8},{1,9},{2,10},{3,11},{4,12},{5,13},{6,14},{7,15},{8,0},{9,1},... | collective-permute-start | bytes 49160 | tf_op jit(solution)/shard_map/ppermute | solution.py:695
  72.6 7.3 %collective-permute-start.13 = (f32[32,128]{1,0:T(8,128)S(1)}, f32[32,128]{1,0:T(8,128)S(1)}, u32[]{:S(2)}, u32[]{:S(2)}) collective-permute-start(f32[32,128]{1,0:T(8,128)S(1)} %get-tuple-element.75), channel_id=1, source_target_pairs={{0,12},{1,13},{2,14},{3,15},{4,0},{5,1},{6,2},{7,3},{8,4},{9,5},{1... | collective-permute-start | bytes 49160 | tf_op jit(solution)/shard_map/ppermute | solution.py:695
  79.9 1.3 %collective-permute-start.14 = (f32[64,128]{1,0:T(8,128)S(1)}, f32[64,128]{1,0:T(8,128)S(1)}, u32[]{:S(2)}, u32[]{:S(2)}) collective-permute-start(f32[64,128]{1,0:T(8,128)S(1)} %get-tuple-element.77), channel_id=1, source_target_pairs={{0,16},{16,0},{1,17},{17,1},{2,18},{18,2},{3,19},{19,3},{4,20},{20... | collective-permute-start | bytes 98312 | tf_op jit(solution)/shard_map/ppermute | solution.py:695
  81.9 1.2 %collective-permute-start.15 = (f32[32,128]{1,0:T(8,128)S(1)}, f32[32,128]{1,0:T(8,128)S(1)}, u32[]{:S(2)}, u32[]{:S(2)}) collective-permute-start(f32[32,128]{1,0:T(8,128)S(1)} %get-tuple-element.81), channel_id=1, source_target_pairs={{0,16},{16,0},{1,17},{17,1},{2,18},{18,2},{3,19},{19,3},{4,20},{20... | collective-permute-start | bytes 49160 | tf_op jit(solution)/shard_map/ppermute | solution.py:695
  83.1 3.7 %collective-permute-start.16 = (f32[16,128]{1,0:T(8,128)S(1)}, f32[16,128]{1,0:T(8,128)S(1)}, u32[]{:S(2)}, u32[]{:S(2)}) collective-permute-start(f32[16,128]{1,0:T(8,128)S(1)} %get-tuple-element.83), channel_id=1, source_target_pairs={{0,1},{1,0},{2,3},{3,2},{4,5},{5,4},{6,7},{7,6},{8,9},{9,8},{10,11... | collective-permute-start | bytes 24584 | tf_op jit(solution)/shard_map/ppermute | solution.py:695
  84.7 3.7 %collective-permute-start.17 = (f32[16,128]{1,0:T(8,128)S(1)}, f32[16,128]{1,0:T(8,128)S(1)}, u32[]{:S(2)}, u32[]{:S(2)}) collective-permute-start(f32[16,128]{1,0:T(8,128)S(1)} %get-tuple-element.84), channel_id=1, source_target_pairs={{0,2},{1,3},{2,0},{3,1},{4,6},{5,7},{6,4},{7,5},{8,10},{9,11},{10,... | collective-permute-start | bytes 24584 | tf_op jit(solution)/shard_map/ppermute | solution.py:695
  86.1 4.5 %collective-permute-start.18 = (f32[16,128]{1,0:T(8,128)S(1)}, f32[16,128]{1,0:T(8,128)S(1)}, u32[]{:S(2)}, u32[]{:S(2)}) collective-permute-start(f32[16,128]{1,0:T(8,128)S(1)} %get-tuple-element.85), channel_id=1, source_target_pairs={{0,3},{1,2},{2,1},{3,0},{4,7},{5,6},{6,5},{7,4},{8,11},{9,10},{10,... | collective-permute-start | bytes 24584 | tf_op jit(solution)/shard_map/ppermute | solution.py:695
  90.7 5.5 %collective-permute-start.19 = (f32[16,128]{1,0:T(8,128)S(1)}, f32[16,128]{1,0:T(8,128)S(1)}, u32[]{:S(2)}, u32[]{:S(2)}) collective-permute-start(f32[16,128]{1,0:T(8,128)S(1)} %get-tuple-element.87), channel_id=1, source_target_pairs={{0,4},{1,5},{2,6},{3,7},{4,8},{5,9},{6,10},{7,11},{8,12},{9,13},{1... | collective-permute-start | bytes 24584 | tf_op jit(solution)/shard_map/ppermute | solution.py:695
  91.5 4.7 %collective-permute-start.20 = (f32[16,128]{1,0:T(8,128)S(1)}, f32[16,128]{1,0:T(8,128)S(1)}, u32[]{:S(2)}, u32[]{:S(2)}) collective-permute-start(f32[16,128]{1,0:T(8,128)S(1)} %get-tuple-element.88), channel_id=1, source_target_pairs={{0,8},{1,9},{2,10},{3,11},{4,12},{5,13},{6,14},{7,15},{8,0},{9,1},... | collective-permute-start | bytes 24584 | tf_op jit(solution)/shard_map/ppermute | solution.py:695
  93.0 3.8 %collective-permute-start.21 = (f32[16,128]{1,0:T(8,128)S(1)}, f32[16,128]{1,0:T(8,128)S(1)}, u32[]{:S(2)}, u32[]{:S(2)}) collective-permute-start(f32[16,128]{1,0:T(8,128)S(1)} %get-tuple-element.89), channel_id=1, source_target_pairs={{0,12},{1,13},{2,14},{3,15},{4,0},{5,1},{6,2},{7,3},{8,4},{9,5},{1... | collective-permute-start | bytes 24584 | tf_op jit(solution)/shard_map/ppermute | solution.py:695

commit v8 on v7

--- a/solution.py
+++ b/solution.py
@@ -263,7 +263,7 @@
                 over[c, a, z * per : (z + 1) * per, :] = turned
         return jnp.maximum(peak, mine)
 
-    peak = lax.fori_loop(0, sources, widen, jnp.zeros((1, 1), F32), unroll=2)
+    peak = lax.fori_loop(0, sources, widen, jnp.zeros((1, 1), F32), unroll=8)
     top[...] = jnp.broadcast_to(peak, top.shape)
     lane = lane_iota((group, LANES))
     cycle = row_iota((group, LANES)) % per
@@ -277,7 +277,7 @@
             ring[c, before] = ring[c, before] + jnp.where(lane >= LANES - 2, extra, 0.0)
         return carry
 
-    lax.fori_loop(0, sources, spill, 0, unroll=4)
+    lax.fori_loop(0, sources, spill, 0, unroll=16)
     for copy in scalars:
         copy.wait()
     x = jnp.zeros((group, LANES), F32)
@@ -309,7 +309,7 @@
                 )
         return carry
 
-    lax.fori_loop(0, sources, tap, 0, unroll=2)
+    lax.fori_loop(0, sources, tap, 0, unroll=8)
     scale = (TOP / GAIN) / peak
 
     def send(dest):
@@ -338,7 +338,7 @@
         return tuple(carry)
 
     start = tuple(turned_tile(c, k, -1) for c in range(3) for k in range(per))
-    lax.fori_loop(0, sources, turn, start, unroll=2)
+    lax.fori_loop(0, sources, turn, start, unroll=8)
     for dest in range(sources):
         send(dest).wait()
 

time: 100 us -> 98.4 us (0.984)
  Pallas kernels: 18.8 us -> 17.2 us
    pallas_call x15, Pallas kernels: 18.8 us -> 17.2 us  [run(): return kernel(*near)]
where the time goes in v8:
time: 98.4 us; the launch traced here: 98.1 us
  waiting for transfers between devices  41.4 us (42%)
  starting transfers between devices  38.5 us (39%)
  Pallas kernels  17.2 us (17%)
    ppermute x20, waiting for transfers between devices, hop(): lax.ppermute(buffers[o], axis, [(i, i + (sent_to(i // step % size, o, siz...  41.4 us
    ppermute x20, starting transfers between devices, hop(): lax.ppermute(buffers[o], axis, [(i, i + (sent_to(i // step % size, o, siz...  25.9 us
    pallas_call x15, Pallas kernels, run(): return kernel(*near)  17.2 us
    all_to_all x2, starting transfers between devices, exchange(): return lax.all_to_all(array, axes, 0, 0, tiled=True)  11.9 us
  transfers between devices with their start and end apart: 24, of which 17 were waited for; matrix products, arithmetic and copies ran while one was open for 0% of the time, Pallas kernels for 6%

profile of v8, /device:TPU:0, one launch (start us, length us, event | category | flops | bytes accessed | tf_op | source)
XLA Modules:
  0.0 98.1 jit_solution(444352518553612513)
XLA Ops:
  0.6 1.3 %shard_map.148 = (f32[3,4,2,1024]{3,2,1,0:T(2,128)S(1)}, f32[3,4,2,1024]{3,2,1,0:T(2,128)S(1)}) custom-call(f32[4,32,1024]{2,1,0:T(8,128)} %rho.3, f32[4,32,1024]{2,1,0:T(8,128)} %ur.3, f32[4,32,1024]{2,1,0:T(8,128)} %up.3), custom_call_target="tpu_custom_call" | custom-call | bytes 786432 | tf_op jit(solution)/shard_map/pallas_call | solution.py:617
  1.9 0.6 collective-permute-start
  2.5 0.1 collective-permute-start.1
  2.5 2.1 %shard_map.147 = (f32[3,4,40,1152]{3,2,1,0:T(8,128)S(1)}, f32[3,4,40,1152]{3,2,1,0:T(8,128)S(1)}) custom-call(f32[4,32,1024]{2,1,0:T(8,128)} %rho.3, f32[4,32,1024]{2,1,0:T(8,128)} %ur.3, f32[4,32,1024]{2,1,0:T(8,128)} %up.3), custom_call_target="tpu_custom_call" | custom-call | bytes 1572864 | tf_op jit(solution)/shard_map/pallas_call | solution.py:617
  4.7 0.0 collective-permute-done.low
  4.7 0.0 collective-permute-done.1.high
  4.7 0.0 copy-start.1
  4.7 0.0 copy-start.2
  4.7 0.0 copy-start.4
  4.7 0.0 copy-start.5
  4.7 0.0 copy-start.6
  4.8 0.0 copy-start.7
  4.8 4.4 %shard_map.149 = (bf16[16,192,128]{2,1,0:T(8,128)(2,1)}, f32[16,24,128]{2,1,0:T(8,128)S(1)}, f32[3,4,40,1152]{3,2,1,0:T(8,128)S(1)}, f32[3,4,40,1152]{3,2,1,0:T(8,128)S(1)}) custom-call(f32[3,4,40,1152]{3,2,1,0:T(8,128)S(1)} %get-tuple-element.47.field_in, ...), custom_call_target="tpu_custom_call", output_to_operand_aliasing={{2}: (0, {}), {3}: (1, {})} | custom-call | flops 39321600 | bytes 3145728 | tf_op jit(solution)/shard_map/pallas_call | solution.py:617
  9.2 8.3 %all-to-all-start = ((bf16[16,192,128]{2,1,0:T(8,128)(2,1)}), bf16[16,192,128]{2,1,0:T(8,128)(2,1)S(1)}, u32[]{:S(2)}, u32[]{:S(2)}) async-start(bf16[16,192,128]{2,1,0:T(8,128)(2,1)} %get-tuple-element.51), calls=%async_computation | async-start | bytes 1572864 | tf_op jit(solution)/shard_map/all_to_all | solution.py:623
  17.5 0.0 copy-start
  17.5 0.0 copy-start.3
  17.5 0.1 shard_map.150
  17.6 2.0 %collective-permute-start.2 = (f32[96,128]{1,0:T(8,128)S(1)}, f32[96,128]{1,0:T(8,128)S(1)}, u32[]{:S(2)}, u32[]{:S(2)}) collective-permute-start(f32[96,128]{1,0:T(8,128)S(1)} %get-tuple-element.54), channel_id=1, source_target_pairs={{0,4},{1,5},{2,6},{3,7},{4,8},{5,9},{6,10},{7,11},{8,12},{9,13},{1... | collective-permute-start | bytes 147464 | tf_op jit(solution)/shard_map/ppermute | solution.py:695
  19.6 2.4 %collective-permute-start.3 = (f32[96,128]{1,0:T(8,128)S(1)}, f32[96,128]{1,0:T(8,128)S(1)}, u32[]{:S(2)}, u32[]{:S(2)}) collective-permute-start(f32[96,128]{1,0:T(8,128)S(1)} %get-tuple-element.55), channel_id=1, source_target_pairs={{0,8},{1,9},{2,10},{3,11},{4,12},{5,13},{6,14},{7,15},{8,0},{9,1},... | collective-permute-start | bytes 147464 | tf_op jit(solution)/shard_map/ppermute | solution.py:695
  21.9 1.5 %collective-permute-start.4 = (f32[96,128]{1,0:T(8,128)S(1)}, f32[96,128]{1,0:T(8,128)S(1)}, u32[]{:S(2)}, u32[]{:S(2)}) collective-permute-start(f32[96,128]{1,0:T(8,128)S(1)} %get-tuple-element.56), channel_id=1, source_target_pairs={{0,12},{1,13},{2,14},{3,15},{4,0},{5,1},{6,2},{7,3},{8,4},{9,5},{1... | collective-permute-start | bytes 147464 | tf_op jit(solution)/shard_map/ppermute | solution.py:695
  23.4 13.3 %collective-permute-done.2.rest_1_ = f32[96,128]{1,0:T(8,128)S(1)} collective-permute-done((f32[96,128]{1,0:T(8,128)S(1)}, f32[96,128]{1,0:T(8,128)S(1)}, u32[]{:S(2)}, u32[]{:S(2)}) %collective-permute-start.2) | collective-permute-done | bytes 49184 | tf_op jit(solution)/shard_map/ppermute | solution.py:695
  36.6 4.8 %collective-permute-done.3.rest_2_ = f32[96,128]{1,0:T(8,128)S(1)} collective-permute-done((f32[96,128]{1,0:T(8,128)S(1)}, f32[96,128]{1,0:T(8,128)S(1)}, u32[]{:S(2)}, u32[]{:S(2)}) %collective-permute-start.3) | collective-permute-done | bytes 49184 | tf_op jit(solution)/shard_map/ppermute | solution.py:695
  41.5 0.0 collective-permute-done.4.rest_3_
  41.5 1.5 %collective-permute-start.5 = (f32[96,128]{1,0:T(8,128)S(1)}, f32[96,128]{1,0:T(8,128)S(1)}, u32[]{:S(2)}, u32[]{:S(2)}) collective-permute-start(f32[96,128]{1,0:T(8,128)S(1)} %get-tuple-element.58), channel_id=1, source_target_pairs={{0,1},{1,0},{2,3},{3,2},{4,5},{5,4},{6,7},{7,6},{8,9},{9,8},{10,11... | collective-permute-start | bytes 147464 | tf_op jit(solution)/shard_map/ppermute | solution.py:695
  43.1 1.5 %collective-permute-start.6 = (f32[96,128]{1,0:T(8,128)S(1)}, f32[96,128]{1,0:T(8,128)S(1)}, u32[]{:S(2)}, u32[]{:S(2)}) collective-permute-start(f32[96,128]{1,0:T(8,128)S(1)} %get-tuple-element.59), channel_id=1, source_target_pairs={{0,2},{1,3},{2,0},{3,1},{4,6},{5,7},{6,4},{7,5},{8,10},{9,11},{10,... | collective-permute-start | bytes 147464 | tf_op jit(solution)/shard_map/ppermute | solution.py:695
  44.5 0.6 collective-permute-start.7
  45.1 0.8 collective-permute-done.5
  45.9 1.2 %collective-permute-done.6 = f32[96,128]{1,0:T(8,128)S(1)} collective-permute-done((f32[96,128]{1,0:T(8,128)S(1)}, f32[96,128]{1,0:T(8,128)S(1)}, u32[]{:S(2)}, u32[]{:S(2)}) %collective-permute-start.6) | collective-permute-done | bytes 49184 | tf_op jit(solution)/shard_map/ppermute | solution.py:695
  47.2 2.4 %collective-permute-done.7 = f32[96,128]{1,0:T(8,128)S(1)} collective-permute-done((f32[96,128]{1,0:T(8,128)S(1)}, f32[96,128]{1,0:T(8,128)S(1)}, u32[]{:S(2)}, u32[]{:S(2)}) %collective-permute-start.7) | collective-permute-done | bytes 49184 | tf_op jit(solution)/shard_map/ppermute | solution.py:695
  49.6 1.5 %shard_map.152 = (f32[128,128]{1,0:T(8,128)S(1)}, f32[16,24,128]{2,1,0:T(8,128)S(1)}) custom-call(s32[32]{0:T(128)S(1)} %copy-done.6, f32[32]{0:T(128)S(1)} %copy-done.7, f32[128,256]{1,0:T(8,128)S(1)} %copy-done.2, f32[128,256]{1,0:T(8,128)S(1)} %copy-done.1, f32[32,128]{1,0:T(8,128)S(1)} %copy-done.5, f32[32,256]{1,0:T(8,128)S(1)} %copy-done.4, ...), custom_call_target="tpu_custom_call" | custom-call | flops 100000000 | bytes 1000000 | tf_op jit(solution)/shard_map/pallas_call | solution.py:617
  51.1 0.0 all-to-all-done.bulk
  51.1 4.1 %shard_map.153 = (bf16[16,24,1024]{2,1,0:T(8,128)(2,1)}, f32[8,128]{1,0:T(8,128)S(1)}) custom-call(s32[32]{0:T(128)S(1)} %copy-done.6, f32[32]{0:T(128)S(1)} %copy-done.7, bf16[16,192,128]{2,1,0:T(8,128)(2,1)S(1)} %all-to-all-done.bulk, f32[16,24,128]{2,1,0:T(8,128)S(1)} %get-tuple-element.61.sides), custom_call_target="tpu_custom_call" | custom-call | flops 19660800 | bytes 1572864 | tf_op jit(solution)/shard_map/pallas_call | solution.py:617
  55.1 3.6 %all-to-all-start.1 = ((bf16[16,24,1024]{2,1,0:T(8,128)(2,1)}), bf16[16,24,1024]{2,1,0:T(8,128)(2,1)S(1)}, u32[]{:S(2)}, u32[]{:S(2)}) async-start(bf16[16,24,1024]{2,1,0:T(8,128)(2,1)} %get-tuple-element.62), calls=%async_computation.1 | async-start | bytes 1572864 | tf_op jit(solution)/shard_map/all_to_all | solution.py:623
  58.8 1.9 %collective-permute-start.8 = (f32[32,128]{1,0:T(8,128)S(1)}, f32[32,128]{1,0:T(8,128)S(1)}, u32[]{:S(2)}, u32[]{:S(2)}) collective-permute-start(f32[32,128]{1,0:T(8,128)S(1)} %get-tuple-element.69), channel_id=1, source_target_pairs={{0,1},{1,0},{2,3},{3,2},{4,5},{5,4},{6,7},{7,6},{8,9},{9,8},{10,11... | collective-permute-start | bytes 49160 | tf_op jit(solution)/shard_map/ppermute | solution.py:695
  60.7 1.5 %collective-permute-start.9 = (f32[32,128]{1,0:T(8,128)S(1)}, f32[32,128]{1,0:T(8,128)S(1)}, u32[]{:S(2)}, u32[]{:S(2)}) collective-permute-start(f32[32,128]{1,0:T(8,128)S(1)} %get-tuple-element.70), channel_id=1, source_target_pairs={{0,2},{1,3},{2,0},{3,1},{4,6},{5,7},{6,4},{7,5},{8,10},{9,11},{10,... | collective-permute-start | bytes 49160 | tf_op jit(solution)/shard_map/ppermute | solution.py:695
  62.1 0.2 collective-permute-start.10
  62.3 1.6 %collective-permute-done.8.rest_1_ = f32[32,128]{1,0:T(8,128)S(1)} collective-permute-done((f32[32,128]{1,0:T(8,128)S(1)}, f32[32,128]{1,0:T(8,128)S(1)}, u32[]{:S(2)}, u32[]{:S(2)}) %collective-permute-start.8) | collective-permute-done | bytes 16416 | tf_op jit(solution)/shard_map/ppermute | solution.py:695
  63.9 1.3 %collective-permute-done.9.rest_2_ = f32[32,128]{1,0:T(8,128)S(1)} collective-permute-done((f32[32,128]{1,0:T(8,128)S(1)}, f32[32,128]{1,0:T(8,128)S(1)}, u32[]{:S(2)}, u32[]{:S(2)}) %collective-permute-start.9) | collective-permute-done | bytes 16416 | tf_op jit(solution)/shard_map/ppermute | solution.py:695
  65.2 1.7 %collective-permute-done.10.rest_3_ = f32[32,128]{1,0:T(8,128)S(1)} collective-permute-done((f32[32,128]{1,0:T(8,128)S(1)}, f32[32,128]{1,0:T(8,128)S(1)}, u32[]{:S(2)}, u32[]{:S(2)}) %collective-permute-start.10) | collective-permute-done | bytes 16416 | tf_op jit(solution)/shard_map/ppermute | solution.py:695
  67.0 1.5 %collective-permute-start.11 = (f32[32,128]{1,0:T(8,128)S(1)}, f32[32,128]{1,0:T(8,128)S(1)}, u32[]{:S(2)}, u32[]{:S(2)}) collective-permute-start(f32[32,128]{1,0:T(8,128)S(1)} %get-tuple-element.73), channel_id=1, source_target_pairs={{0,4},{1,5},{2,6},{3,7},{4,8},{5,9},{6,10},{7,11},{8,12},{9,13},{1... | collective-permute-start | bytes 49160 | tf_op jit(solution)/shard_map/ppermute | solution.py:695
  68.5 2.4 %collective-permute-start.12 = (f32[32,128]{1,0:T(8,128)S(1)}, f32[32,128]{1,0:T(8,128)S(1)}, u32[]{:S(2)}, u32[]{:S(2)}) collective-permute-start(f32[32,128]{1,0:T(8,128)S(1)} %get-tuple-element.74), channel_id=1, source_target_pairs={{0,8},{1,9},{2,10},{3,11},{4,12},{5,13},{6,14},{7,15},{8,0},{9,1},... | collective-permute-start | bytes 49160 | tf_op jit(solution)/shard_map/ppermute | solution.py:695
  70.9 1.4 %collective-permute-start.13 = (f32[32,128]{1,0:T(8,128)S(1)}, f32[32,128]{1,0:T(8,128)S(1)}, u32[]{:S(2)}, u32[]{:S(2)}) collective-permute-start(f32[32,128]{1,0:T(8,128)S(1)} %get-tuple-element.75), channel_id=1, source_target_pairs={{0,12},{1,13},{2,14},{3,15},{4,0},{5,1},{6,2},{7,3},{8,4},{9,5},{1... | collective-permute-start | bytes 49160 | tf_op jit(solution)/shard_map/ppermute | solution.py:695
  72.3 2.3 %collective-permute-done.11.rest_1_ = f32[32,128]{1,0:T(8,128)S(1)} collective-permute-done((f32[32,128]{1,0:T(8,128)S(1)}, f32[32,128]{1,0:T(8,128)S(1)}, u32[]{:S(2)}, u32[]{:S(2)}) %collective-permute-start.11) | collective-permute-done | bytes 16416 | tf_op jit(solution)/shard_map/ppermute | solution.py:695
  74.6 3.6 %collective-permute-done.12.rest_2_ = f32[32,128]{1,0:T(8,128)S(1)} collective-permute-done((f32[32,128]{1,0:T(8,128)S(1)}, f32[32,128]{1,0:T(8,128)S(1)}, u32[]{:S(2)}, u32[]{:S(2)}) %collective-permute-start.12) | collective-permute-done | bytes 16416 | tf_op jit(solution)/shard_map/ppermute | solution.py:695
  78.2 0.0 collective-permute-done.13.rest_3_
  78.2 0.1 collective-permute-start.14
  78.3 1.2 %collective-permute-done.14.rest_1_ = f32[64,128]{1,0:T(8,128)S(1)} collective-permute-done((f32[64,128]{1,0:T(8,128)S(1)}, f32[64,128]{1,0:T(8,128)S(1)}, u32[]{:S(2)}, u32[]{:S(2)}) %collective-permute-start.14) | collective-permute-done | bytes 32800 | tf_op jit(solution)/shard_map/ppermute | solution.py:695
  79.5 0.7 shard_map.158
  80.2 0.2 collective-permute-start.15
  80.4 1.0 %collective-permute-done.15.rest_1_ = f32[32,128]{1,0:T(8,128)S(1)} collective-permute-done((f32[32,128]{1,0:T(8,128)S(1)}, f32[32,128]{1,0:T(8,128)S(1)}, u32[]{:S(2)}, u32[]{:S(2)}) %collective-permute-start.15) | collective-permute-done | bytes 16416 | tf_op jit(solution)/shard_map/ppermute | solution.py:695
  81.5 1.5 %collective-permute-start.16 = (f32[16,128]{1,0:T(8,128)S(1)}, f32[16,128]{1,0:T(8,128)S(1)}, u32[]{:S(2)}, u32[]{:S(2)}) collective-permute-start(f32[16,128]{1,0:T(8,128)S(1)} %get-tuple-element.83), channel_id=1, source_target_pairs={{0,1},{1,0},{2,3},{3,2},{4,5},{5,4},{6,7},{7,6},{8,9},{9,8},{10,11... | collective-permute-start | bytes 24584 | tf_op jit(solution)/shard_map/ppermute | solution.py:695
  83.0 1.5 %collective-permute-start.17 = (f32[16,128]{1,0:T(8,128)S(1)}, f32[16,128]{1,0:T(8,128)S(1)}, u32[]{:S(2)}, u32[]{:S(2)}) collective-permute-start(f32[16,128]{1,0:T(8,128)S(1)} %get-tuple-element.84), channel_id=1, source_target_pairs={{0,2},{1,3},{2,0},{3,1},{4,6},{5,7},{6,4},{7,5},{8,10},{9,11},{10,... | collective-permute-start | bytes 24584 | tf_op jit(solution)/shard_map/ppermute | solution.py:695
  84.5 0.6 collective-permute-start.18
  85.0 0.2 collective-permute-done.16.rest_1_
  85.2 1.5 %collective-permute-done.17.rest_2_ = f32[16,128]{1,0:T(8,128)S(1)} collective-permute-done((f32[16,128]{1,0:T(8,128)S(1)}, f32[16,128]{1,0:T(8,128)S(1)}, u32[]{:S(2)}, u32[]{:S(2)}) %collective-permute-start.17) | collective-permute-done | bytes 8224 | tf_op jit(solution)/shard_map/ppermute | solution.py:695
  86.7 2.4 %collective-permute-done.18.rest_3_ = f32[16,128]{1,0:T(8,128)S(1)} collective-permute-done((f32[16,128]{1,0:T(8,128)S(1)}, f32[16,128]{1,0:T(8,128)S(1)}, u32[]{:S(2)}, u32[]{:S(2)}) %collective-permute-start.18) | collective-permute-done | bytes 8224 | tf_op jit(solution)/shard_map/ppermute | solution.py:695
  89.1 0.8 collective-permute-start.19
  89.9 1.5 %collective-permute-start.20 = (f32[16,128]{1,0:T(8,128)S(1)}, f32[16,128]{1,0:T(8,128)S(1)}, u32[]{:S(2)}, u32[]{:S(2)}) collective-permute-start(f32[16,128]{1,0:T(8,128)S(1)} %get-tuple-element.88), channel_id=1, source_target_pairs={{0,8},{1,9},{2,10},{3,11},{4,12},{5,13},{6,14},{7,15},{8,0},{9,1},... | collective-permute-start | bytes 24584 | tf_op jit(solution)/shard_map/ppermute | solution.py:695
  91.4 1.6 %collective-permute-start.21 = (f32[16,128]{1,0:T(8,128)S(1)}, f32[16,128]{1,0:T(8,128)S(1)}, u32[]{:S(2)}, u32[]{:S(2)}) collective-permute-start(f32[16,128]{1,0:T(8,128)S(1)} %get-tuple-element.89), channel_id=1, source_target_pairs={{0,12},{1,13},{2,14},{3,15},{4,0},{5,1},{6,2},{7,3},{8,4},{9,5},{1... | collective-permute-start | bytes 24584 | tf_op jit(solution)/shard_map/ppermute | solution.py:695
  92.9 1.6 %collective-permute-done.19.rest_1_ = f32[16,128]{1,0:T(8,128)S(1)} collective-permute-done((f32[16,128]{1,0:T(8,128)S(1)}, f32[16,128]{1,0:T(8,128)S(1)}, u32[]{:S(2)}, u32[]{:S(2)}) %collective-permute-start.19) | collective-permute-done | bytes 8224 | tf_op jit(solution)/shard_map/ppermute | solution.py:695
  94.6 0.0 collective-permute-done.20.rest_2_
  94.6 0.6 collective-permute-done.21.rest_3_
  95.1 1.4 %shard_map.161 = f32[2,16384]{1,0:T(2,128)} custom-call(f32[128,256]{1,0:T(8,128)S(1)} %copy-done.2, f32[128,256]{1,0:T(8,128)S(1)} %copy-done.1, f32[32,512]{1,0:T(8,128)S(1)} %get-tuple-element.78.tables, f32[32,128]{1,0:T(8,128)S(1)} %get-tuple-element.79.factor, f32[16,128]{1,0:T(8,128)S(1)} %get-tuple-element.86.rest_0_, ...), custom_call_target="tpu_custom_call" | custom-call | flops 100000000 | bytes 1000000 | tf_op jit(solution)/shard_map/pallas_call | solution.py:617
  96.5 1.5 %shard_map.154 = (f32[4,32,1024]{2,1,0:T(8,128)}, f32[4,32,1024]{2,1,0:T(8,128)}, f32[4,32,1024]{2,1,0:T(8,128)}) custom-call(bf16[16,24,1024]{2,1,0:T(8,128)(2,1)S(1)} %all-to-all-done.1.bulk, f32[8,128]{1,0:T(8,128)S(1)} %get-tuple-element.63.top), custom_call_target="tpu_custom_call" | custom-call | flops 7864320 | bytes 2359296 | tf_op jit(solution)/shard_map/pallas_call | solution.py:617
  (15 shorter events, 0.2 us)
Async XLA Ops:
  1.9 2.8 %collective-permute-start = (f32[3,4,2,1024]{3,2,1,0:T(2,128)S(1)}, f32[3,4,2,1024]{3,2,1,0:T(2,128)S(1)}, u32[]{:S(2)}, u32[]{:S(2)}) collective-permute-start(f32[3,4,2,1024]{3,2,1,0:T(2,128)S(1)} %get-tuple-element.49), channel_id=1, source_target_pairs={{0,16},{16,0},{1,17},{17,1},{2,18},{18,2},{3,19},{19,3},{4,20},{20... | collective-permute-start | bytes 294920 | tf_op jit(solution)/shard_map/ppermute | solution.py:666
  2.5 2.2 %collective-permute-start.1 = (f32[3,4,2,1024]{3,2,1,0:T(2,128)S(1)}, f32[3,4,2,1024]{3,2,1,0:T(2,128)S(1)}, u32[]{:S(2)}, u32[]{:S(2)}) collective-permute-start(f32[3,4,2,1024]{3,2,1,0:T(2,128)S(1)} %get-tuple-element.50), channel_id=1, source_target_pairs={{16,0},{0,16},{17,1},{1,17},{18,2},{2,18},{19,3},{3,19},{20,4},{4,... | collective-permute-start | bytes 294920 | tf_op jit(solution)/shard_map/ppermute | solution.py:667
  4.7 44.8 %copy-start.1 = (f32[128,256]{1,0:T(8,128)S(1)}, f32[128,256]{1,0:T(8,128)}, u32[]{:S(2)}) copy-start(f32[128,256]{1,0:T(8,128)} %constant.11.clone.twiddle) | copy-start | bytes 393220
  4.7 44.8 %copy-start.2 = (f32[128,256]{1,0:T(8,128)S(1)}, f32[128,256]{1,0:T(8,128)}, u32[]{:S(2)}) copy-start(f32[128,256]{1,0:T(8,128)} %constant.10.clone.circle) | copy-start | bytes 393220
  4.7 44.8 %copy-start.4 = (f32[32,256]{1,0:T(8,128)S(1)}, f32[32,256]{1,0:T(8,128)}, u32[]{:S(2)}) copy-start(f32[32,256]{1,0:T(8,128)} %constant.13.clone.steps) | copy-start | bytes 98308
  4.7 44.8 %copy-start.5 = (f32[32,128]{1,0:T(8,128)S(1)}, f32[32,128]{1,0:T(8,128)}, u32[]{:S(2)}) copy-start(f32[32,128]{1,0:T(8,128)} %constant.12.clone.short) | copy-start | bytes 49156
  4.7 44.8 %copy-start.6 = (s32[32]{0:T(128)S(1)}, s32[32]{0:T(128)}, u32[]{:S(2)}) copy-start(s32[32]{0:T(128)} %far_shift.3) | copy-start | bytes 388
  4.8 44.8 %copy-start.7 = (f32[32]{0:T(128)S(1)}, f32[32]{0:T(128)}, u32[]{:S(2)}) copy-start(f32[32]{0:T(128)} %far_remainder.3) | copy-start | bytes 388
  9.2 41.9 %all-to-all-start = ((bf16[16,192,128]{2,1,0:T(8,128)(2,1)}), bf16[16,192,128]{2,1,0:T(8,128)(2,1)S(1)}, u32[]{:S(2)}, u32[]{:S(2)}) async-start(bf16[16,192,128]{2,1,0:T(8,128)(2,1)} %get-tuple-element.51), calls=%async_computation | async-start | bytes 1572864 | tf_op jit(solution)/shard_map/all_to_all | solution.py:623
  17.5 62.0 %copy-start = (bf16[64,64,64]{2,1,0:T(8,128)(2,1)S(1)}, bf16[64,64,64]{2,1,0:T(8,128)(2,1)}, u32[]{:S(2)}) copy-start(bf16[64,64,64]{2,1,0:T(8,128)(2,1)} %kernel.1) | copy-start | bytes 1572868
  17.5 62.0 %copy-start.3 = (f32[32,256]{1,0:T(8,128)S(1)}, f32[32,256]{1,0:T(8,128)}, u32[]{:S(2)}) copy-start(f32[32,256]{1,0:T(8,128)} %constant.14.clone.mixed) | copy-start | bytes 98308
  17.6 19.1 %collective-permute-start.2 = (f32[96,128]{1,0:T(8,128)S(1)}, f32[96,128]{1,0:T(8,128)S(1)}, u32[]{:S(2)}, u32[]{:S(2)}) collective-permute-start(f32[96,128]{1,0:T(8,128)S(1)} %get-tuple-element.54), channel_id=1, source_target_pairs={{0,4},{1,5},{2,6},{3,7},{4,8},{5,9},{6,10},{7,11},{8,12},{9,13},{1... | collective-permute-start | bytes 147464 | tf_op jit(solution)/shard_map/ppermute | solution.py:695
  19.6 21.9 %collective-permute-start.3 = (f32[96,128]{1,0:T(8,128)S(1)}, f32[96,128]{1,0:T(8,128)S(1)}, u32[]{:S(2)}, u32[]{:S(2)}) collective-permute-start(f32[96,128]{1,0:T(8,128)S(1)} %get-tuple-element.55), channel_id=1, source_target_pairs={{0,8},{1,9},{2,10},{3,11},{4,12},{5,13},{6,14},{7,15},{8,0},{9,1},... | collective-permute-start | bytes 147464 | tf_op jit(solution)/shard_map/ppermute | solution.py:695
  21.9 19.6 %collective-permute-start.4 = (f32[96,128]{1,0:T(8,128)S(1)}, f32[96,128]{1,0:T(8,128)S(1)}, u32[]{:S(2)}, u32[]{:S(2)}) collective-permute-start(f32[96,128]{1,0:T(8,128)S(1)} %get-tuple-element.56), channel_id=1, source_target_pairs={{0,12},{1,13},{2,14},{3,15},{4,0},{5,1},{6,2},{7,3},{8,4},{9,5},{1... | collective-permute-start | bytes 147464 | tf_op jit(solution)/shard_map/ppermute | solution.py:695
  41.5 4.4 %collective-permute-start.5 = (f32[96,128]{1,0:T(8,128)S(1)}, f32[96,128]{1,0:T(8,128)S(1)}, u32[]{:S(2)}, u32[]{:S(2)}) collective-permute-start(f32[96,128]{1,0:T(8,128)S(1)} %get-tuple-element.58), channel_id=1, source_target_pairs={{0,1},{1,0},{2,3},{3,2},{4,5},{5,4},{6,7},{7,6},{8,9},{9,8},{10,11... | collective-permute-start | bytes 147464 | tf_op jit(solution)/shard_map/ppermute | solution.py:695
  43.1 4.1 %collective-permute-start.6 = (f32[96,128]{1,0:T(8,128)S(1)}, f32[96,128]{1,0:T(8,128)S(1)}, u32[]{:S(2)}, u32[]{:S(2)}) collective-permute-start(f32[96,128]{1,0:T(8,128)S(1)} %get-tuple-element.59), channel_id=1, source_target_pairs={{0,2},{1,3},{2,0},{3,1},{4,6},{5,7},{6,4},{7,5},{8,10},{9,11},{10,... | collective-permute-start | bytes 147464 | tf_op jit(solution)/shard_map/ppermute | solution.py:695
  44.5 5.0 %collective-permute-start.7 = (f32[96,128]{1,0:T(8,128)S(1)}, f32[96,128]{1,0:T(8,128)S(1)}, u32[]{:S(2)}, u32[]{:S(2)}) collective-permute-start(f32[96,128]{1,0:T(8,128)S(1)} %get-tuple-element.60), channel_id=1, source_target_pairs={{0,3},{1,2},{2,1},{3,0},{4,7},{5,6},{6,5},{7,4},{8,11},{9,10},{10,... | collective-permute-start | bytes 147464 | tf_op jit(solution)/shard_map/ppermute | solution.py:695
  55.1 41.4 %all-to-all-start.1 = ((bf16[16,24,1024]{2,1,0:T(8,128)(2,1)}), bf16[16,24,1024]{2,1,0:T(8,128)(2,1)S(1)}, u32[]{:S(2)}, u32[]{:S(2)}) async-start(bf16[16,24,1024]{2,1,0:T(8,128)(2,1)} %get-tuple-element.62), calls=%async_computation.1 | async-start | bytes 1572864 | tf_op jit(solution)/shard_map/all_to_all | solution.py:623
  58.8 5.1 %collective-permute-start.8 = (f32[32,128]{1,0:T(8,128)S(1)}, f32[32,128]{1,0:T(8,128)S(1)}, u32[]{:S(2)}, u32[]{:S(2)}) collective-permute-start(f32[32,128]{1,0:T(8,128)S(1)} %get-tuple-element.69), channel_id=1, source_target_pairs={{0,1},{1,0},{2,3},{3,2},{4,5},{5,4},{6,7},{7,6},{8,9},{9,8},{10,11... | collective-permute-start | bytes 49160 | tf_op jit(solution)/shard_map/ppermute | solution.py:695
  60.7 4.6 %collective-permute-start.9 = (f32[32,128]{1,0:T(8,128)S(1)}, f32[32,128]{1,0:T(8,128)S(1)}, u32[]{:S(2)}, u32[]{:S(2)}) collective-permute-start(f32[32,128]{1,0:T(8,128)S(1)} %get-tuple-element.70), channel_id=1, source_target_pairs={{0,2},{1,3},{2,0},{3,1},{4,6},{5,7},{6,4},{7,5},{8,10},{9,11},{10,... | collective-permute-start | bytes 49160 | tf_op jit(solution)/shard_map/ppermute | solution.py:695
  62.1 4.8 %collective-permute-start.10 = (f32[32,128]{1,0:T(8,128)S(1)}, f32[32,128]{1,0:T(8,128)S(1)}, u32[]{:S(2)}, u32[]{:S(2)}) collective-permute-start(f32[32,128]{1,0:T(8,128)S(1)} %get-tuple-element.71), channel_id=1, source_target_pairs={{0,3},{1,2},{2,1},{3,0},{4,7},{5,6},{6,5},{7,4},{8,11},{9,10},{10,... | collective-permute-start | bytes 49160 | tf_op jit(solution)/shard_map/ppermute | solution.py:695
  67.0 7.6 %collective-permute-start.11 = (f32[32,128]{1,0:T(8,128)S(1)}, f32[32,128]{1,0:T(8,128)S(1)}, u32[]{:S(2)}, u32[]{:S(2)}) collective-permute-start(f32[32,128]{1,0:T(8,128)S(1)} %get-tuple-element.73), channel_id=1, source_target_pairs={{0,4},{1,5},{2,6},{3,7},{4,8},{5,9},{6,10},{7,11},{8,12},{9,13},{1... | collective-permute-start | bytes 49160 | tf_op jit(solution)/shard_map/ppermute | solution.py:695
  68.5 9.7 %collective-permute-start.12 = (f32[32,128]{1,0:T(8,128)S(1)}, f32[32,128]{1,0:T(8,128)S(1)}, u32[]{:S(2)}, u32[]{:S(2)}) collective-permute-start(f32[32,128]{1,0:T(8,128)S(1)} %get-tuple-element.74), channel_id=1, source_target_pairs={{0,8},{1,9},{2,10},{3,11},{4,12},{5,13},{6,14},{7,15},{8,0},{9,1},... | collective-permute-start | bytes 49160 | tf_op jit(solution)/shard_map/ppermute | solution.py:695
  70.9 7.3 %collective-permute-start.13 = (f32[32,128]{1,0:T(8,128)S(1)}, f32[32,128]{1,0:T(8,128)S(1)}, u32[]{:S(2)}, u32[]{:S(2)}) collective-permute-start(f32[32,128]{1,0:T(8,128)S(1)} %get-tuple-element.75), channel_id=1, source_target_pairs={{0,12},{1,13},{2,14},{3,15},{4,0},{5,1},{6,2},{7,3},{8,4},{9,5},{1... | collective-permute-start | bytes 49160 | tf_op jit(solution)/shard_map/ppermute | solution.py:695
  78.2 1.3 %collective-permute-start.14 = (f32[64,128]{1,0:T(8,128)S(1)}, f32[64,128]{1,0:T(8,128)S(1)}, u32[]{:S(2)}, u32[]{:S(2)}) collective-permute-start(f32[64,128]{1,0:T(8,128)S(1)} %get-tuple-element.77), channel_id=1, source_target_pairs={{0,16},{16,0},{1,17},{17,1},{2,18},{18,2},{3,19},{19,3},{4,20},{20... | collective-permute-start | bytes 98312 | tf_op jit(solution)/shard_map/ppermute | solution.py:695
  80.2 1.2 %collective-permute-start.15 = (f32[32,128]{1,0:T(8,128)S(1)}, f32[32,128]{1,0:T(8,128)S(1)}, u32[]{:S(2)}, u32[]{:S(2)}) collective-permute-start(f32[32,128]{1,0:T(8,128)S(1)} %get-tuple-element.81), channel_id=1, source_target_pairs={{0,16},{16,0},{1,17},{17,1},{2,18},{18,2},{3,19},{19,3},{4,20},{20... | collective-permute-start | bytes 49160 | tf_op jit(solution)/shard_map/ppermute | solution.py:695
  81.5 3.7 %collective-permute-start.16 = (f32[16,128]{1,0:T(8,128)S(1)}, f32[16,128]{1,0:T(8,128)S(1)}, u32[]{:S(2)}, u32[]{:S(2)}) collective-permute-start(f32[16,128]{1,0:T(8,128)S(1)} %get-tuple-element.83), channel_id=1, source_target_pairs={{0,1},{1,0},{2,3},{3,2},{4,5},{5,4},{6,7},{7,6},{8,9},{9,8},{10,11... | collective-permute-start | bytes 24584 | tf_op jit(solution)/shard_map/ppermute | solution.py:695
  83.0 3.7 %collective-permute-start.17 = (f32[16,128]{1,0:T(8,128)S(1)}, f32[16,128]{1,0:T(8,128)S(1)}, u32[]{:S(2)}, u32[]{:S(2)}) collective-permute-start(f32[16,128]{1,0:T(8,128)S(1)} %get-tuple-element.84), channel_id=1, source_target_pairs={{0,2},{1,3},{2,0},{3,1},{4,6},{5,7},{6,4},{7,5},{8,10},{9,11},{10,... | collective-permute-start | bytes 24584 | tf_op jit(solution)/shard_map/ppermute | solution.py:695
  84.5 4.5 %collective-permute-start.18 = (f32[16,128]{1,0:T(8,128)S(1)}, f32[16,128]{1,0:T(8,128)S(1)}, u32[]{:S(2)}, u32[]{:S(2)}) collective-permute-start(f32[16,128]{1,0:T(8,128)S(1)} %get-tuple-element.85), channel_id=1, source_target_pairs={{0,3},{1,2},{2,1},{3,0},{4,7},{5,6},{6,5},{7,4},{8,11},{9,10},{10,... | collective-permute-start | bytes 24584 | tf_op jit(solution)/shard_map/ppermute | solution.py:695
  89.1 5.5 %collective-permute-start.19 = (f32[16,128]{1,0:T(8,128)S(1)}, f32[16,128]{1,0:T(8,128)S(1)}, u32[]{:S(2)}, u32[]{:S(2)}) collective-permute-start(f32[16,128]{1,0:T(8,128)S(1)} %get-tuple-element.87), channel_id=1, source_target_pairs={{0,4},{1,5},{2,6},{3,7},{4,8},{5,9},{6,10},{7,11},{8,12},{9,13},{1... | collective-permute-start | bytes 24584 | tf_op jit(solution)/shard_map/ppermute | solution.py:695
  89.9 4.7 %collective-permute-start.20 = (f32[16,128]{1,0:T(8,128)S(1)}, f32[16,128]{1,0:T(8,128)S(1)}, u32[]{:S(2)}, u32[]{:S(2)}) collective-permute-start(f32[16,128]{1,0:T(8,128)S(1)} %get-tuple-element.88), channel_id=1, source_target_pairs={{0,8},{1,9},{2,10},{3,11},{4,12},{5,13},{6,14},{7,15},{8,0},{9,1},... | collective-permute-start | bytes 24584 | tf_op jit(solution)/shard_map/ppermute | solution.py:695
  91.4 3.8 %collective-permute-start.21 = (f32[16,128]{1,0:T(8,128)S(1)}, f32[16,128]{1,0:T(8,128)S(1)}, u32[]{:S(2)}, u32[]{:S(2)}) collective-permute-start(f32[16,128]{1,0:T(8,128)S(1)} %get-tuple-element.89), channel_id=1, source_target_pairs={{0,12},{1,13},{2,14},{3,15},{4,0},{5,1},{6,2},{7,3},{8,4},{9,5},{1... | collective-permute-start | bytes 24584 | tf_op jit(solution)/shard_map/ppermute | solution.py:695

commit v9 on v8

--- a/solution.py
+++ b/solution.py
@@ -56,19 +56,22 @@
     return -(-(per * tiles + per) // SUB) * SUB
 
 
-def edges_kernel(rho, ur, up, tail, head, last, first, sems):
-    slab = rho.shape[1]
-    copies = []
-    for c, far in enumerate((rho, ur, up)):
-        ends = (far.at[:, pl.ds(slab - SUB, SUB), :], last.at[c]), (far.at[:, pl.ds(0, SUB), :], first.at[c])
-        copies += [pltpu.make_async_copy(*end, sems.at[2 * c + i]) for i, end in enumerate(ends)]
+def load_kernel(rho, ur, up, field, tail, head, sems):
+    nz, slab, seg = rho.shape
+    lines, width = field.shape[2:]
+    copies = [
+        pltpu.make_async_copy(far, field.at[c, :, pl.ds(0, slab), pl.ds(0, seg)], sems.at[c])
+        for c, far in enumerate((rho, ur, up))
+    ]
     for copy in copies:
         copy.start()
     for c in range(3):
-        copies[2 * c].wait()
-        tail[c] = last[c, :, SUB - 2 :, :]
-        copies[2 * c + 1].wait()
-        head[c] = first[c, :, 0:2, :]
+        for z in range(nz):
+            field[c, z, :, seg:width] = jnp.zeros((lines, width - seg), F32)
+    for c in range(3):
+        copies[c].wait()
+        tail[c] = field[c, :, slab - 2 : slab, 0:seg]
+        head[c] = field[c, :, 0:2, 0:seg]
 
 
 def advance(ref, tile, z, slab, scale):
@@ -113,20 +116,8 @@
             stage[c, z, pl.ds(pl.multiple_of(tile * SUB, SUB), SUB), :] = value
 
 
-def interior_kernel(rho, ur, up, field, stage, sems):
-    nz, slab, seg = rho.shape
-    copies = [
-        pltpu.make_async_copy(far, field.at[c, :, pl.ds(0, slab), pl.ds(0, seg)], sems.at[c])
-        for c, far in enumerate((rho, ur, up))
-    ]
-    for copy in copies:
-        copy.start()
-    lines, width = field.shape[2:]
-    for c in range(3):
-        for z in range(nz):
-            field[c, z, :, seg:width] = jnp.zeros((lines, width - seg), F32)
-    for copy in copies:
-        copy.wait()
+def interior_kernel(field, stage):
+    slab = field.shape[2] - SUB
 
     def section(tile, carry):
         store_section(field, stage, slab, tile)
@@ -607,7 +598,7 @@
 
     def run(*operands):
         places = [
-            None if x.ndim == 1 else pltpu.HBM if name in ("edges", "interior") else pltpu.VMEM
+            None if x.ndim == 1 else pltpu.HBM if name == "load" else pltpu.VMEM
             for x in operands
         ]
         near = [
@@ -651,29 +642,18 @@
     anywhere = pl.BlockSpec(memory_space=pl.ANY)
     far = pl.BlockSpec(memory_space=pltpu.HBM)
     edge = pltpu.VMEM((3, nz, 2, seg), F32)
-    tail, head = call(
-        edges_kernel,
-        (edge, edge),
+    padded = pltpu.VMEM((3, nz, slab + SUB, width), F32)
+    field, tail, head = call(
+        load_kernel,
+        (padded, edge, edge),
         in_specs=[far] * 3,
-        scratch=(
-            pltpu.VMEM((3, nz, SUB, seg), F32),
-            pltpu.VMEM((3, nz, SUB, seg), F32),
-            pltpu.SemaphoreType.DMA((6,)),
-        ),
-        name="edges",
-        bytes_accessed=24 * nz * SUB * seg,
+        scratch=(pltpu.SemaphoreType.DMA((3,)),),
+        name="load",
+        bytes_accessed=12 * nz * slab * seg,
     )(*fields)
     low = lax.ppermute(tail, "rad", [(i, (i + 1) % rad) for i in range(rad)])
     high = lax.ppermute(head, "rad", [((i + 1) % rad, i) for i in range(rad)])
-    padded = pltpu.VMEM((3, nz, slab + SUB, width), F32)
-    field, stage = call(
-        interior_kernel,
-        (padded, padded),
-        in_specs=[far] * 3,
-        scratch=(pltpu.SemaphoreType.DMA((3,)),),
-        name="interior",
-        bytes_accessed=12 * nz * slab * seg,
-    )(*fields)
+    stage = call(interior_kernel, padded, name="interior", bytes_accessed=12 * nz * slab * seg)(field)
     bulk, surf, *_ = call(
         functools.partial(hydro_kernel, per, seg),
         (pltpu.HBM((azi, rows, LANES), BF16), pltpu.VMEM((azi, side, LANES), F32), padded, padded),

time: 98.4 us -> 97.5 us (level)
  Pallas kernels: 17.2 us -> 15.9 us
    pallas_call x15, Pallas kernels: 17.2 us -> 15.9 us  [run(): return kernel(*near)]
  transfers between devices with their start and end apart: 24 -> 24, of which waited for: 17 -> 19; matrix products, arithmetic and copies ran while one was open for 0% -> 0% of each run, Pallas kernels for 6% -> 5%
where the time goes in v9:
time: 97.5 us; the launch traced here: 97.2 us
  waiting for transfers between devices  42.1 us (43%)
  starting transfers between devices  38.2 us (39%)
  Pallas kernels  15.9 us (16%)
    ppermute x20, waiting for transfers between devices, hop(): lax.ppermute(buffers[o], axis, [(i, i + (sent_to(i // step % size, o, siz...  41.7 us
    ppermute x20, starting transfers between devices, hop(): lax.ppermute(buffers[o], axis, [(i, i + (sent_to(i // step % size, o, siz...  26 us
    pallas_call x15, Pallas kernels, run(): return kernel(*near)  15.9 us
    all_to_all x2, starting transfers between devices, exchange(): return lax.all_to_all(array, axes, 0, 0, tiled=True)  11.6 us
  transfers between devices with their start and end apart: 24, of which 19 were waited for; matrix products, arithmetic and copies ran while one was open for 0% of the time, Pallas kernels for 5%

profile of v9, /device:TPU:0, one launch (start us, length us, event | category | flops | bytes accessed | tf_op | source)
XLA Modules:
  0.0 97.2 jit_solution(3420942519879033044)
XLA Ops:
  0.6 1.4 %shard_map.147 = (f32[3,4,40,1152]{3,2,1,0:T(8,128)S(1)}, f32[3,4,2,1024]{3,2,1,0:T(2,128)S(1)}, f32[3,4,2,1024]{3,2,1,0:T(2,128)S(1)}) custom-call(f32[4,32,1024]{2,1,0:T(8,128)} %rho.1, f32[4,32,1024]{2,1,0:T(8,128)} %ur.1, f32[4,32,1024]{2,1,0:T(8,128)} %up.1), custom_call_target="tpu_custom_call" | custom-call | bytes 1572864 | tf_op jit(solution)/shard_map/pallas_call | solution.py:608
  2.0 0.6 collective-permute-start
  2.6 0.1 collective-permute-start.1
  2.7 0.7 shard_map.148.stage_in
  3.4 0.0 copy-start.1
  3.4 0.0 copy-start.2
  3.4 0.0 copy-start.4
  3.5 0.0 copy-start.5
  3.5 0.0 copy-start.6
  3.5 0.0 copy-start.7
  3.5 0.1 collective-permute-done.low
  3.5 0.4 collective-permute-done.1.high
  3.9 4.4 %shard_map.149 = (bf16[16,192,128]{2,1,0:T(8,128)(2,1)}, f32[16,24,128]{2,1,0:T(8,128)S(1)}, f32[3,4,40,1152]{3,2,1,0:T(8,128)S(1)}, f32[3,4,40,1152]{3,2,1,0:T(8,128)S(1)}) custom-call(f32[3,4,40,1152]{3,2,1,0:T(8,128)S(1)} %get-tuple-element.46.field.field_in, ...), custom_call_target="tpu_custom_call", output_to_operand_aliasing={{2}: (0, {}), {3}: (1, {})} | custom-call | flops 39321600 | bytes 3145728 | tf_op jit(solution)/shard_map/pallas_call | solution.py:608
  8.3 8.0 %all-to-all-start = ((bf16[16,192,128]{2,1,0:T(8,128)(2,1)}), bf16[16,192,128]{2,1,0:T(8,128)(2,1)S(1)}, u32[]{:S(2)}, u32[]{:S(2)}) async-start(bf16[16,192,128]{2,1,0:T(8,128)(2,1)} %get-tuple-element.49), calls=%async_computation | async-start | bytes 1572864 | tf_op jit(solution)/shard_map/all_to_all | solution.py:614
  16.3 0.0 copy-start
  16.3 0.0 copy-start.3
  16.4 0.1 shard_map.150
  16.4 2.0 %collective-permute-start.2 = (f32[96,128]{1,0:T(8,128)S(1)}, f32[96,128]{1,0:T(8,128)S(1)}, u32[]{:S(2)}, u32[]{:S(2)}) collective-permute-start(f32[96,128]{1,0:T(8,128)S(1)} %get-tuple-element.52), channel_id=1, source_target_pairs={{0,4},{1,5},{2,6},{3,7},{4,8},{5,9},{6,10},{7,11},{8,12},{9,13},{1... | collective-permute-start | bytes 147464 | tf_op jit(solution)/shard_map/ppermute | solution.py:675
  18.4 2.4 %collective-permute-start.3 = (f32[96,128]{1,0:T(8,128)S(1)}, f32[96,128]{1,0:T(8,128)S(1)}, u32[]{:S(2)}, u32[]{:S(2)}) collective-permute-start(f32[96,128]{1,0:T(8,128)S(1)} %get-tuple-element.53), channel_id=1, source_target_pairs={{0,8},{1,9},{2,10},{3,11},{4,12},{5,13},{6,14},{7,15},{8,0},{9,1},... | collective-permute-start | bytes 147464 | tf_op jit(solution)/shard_map/ppermute | solution.py:675
  20.8 1.5 %collective-permute-start.4 = (f32[96,128]{1,0:T(8,128)S(1)}, f32[96,128]{1,0:T(8,128)S(1)}, u32[]{:S(2)}, u32[]{:S(2)}) collective-permute-start(f32[96,128]{1,0:T(8,128)S(1)} %get-tuple-element.54), channel_id=1, source_target_pairs={{0,12},{1,13},{2,14},{3,15},{4,0},{5,1},{6,2},{7,3},{8,4},{9,5},{1... | collective-permute-start | bytes 147464 | tf_op jit(solution)/shard_map/ppermute | solution.py:675
  22.2 13.4 %collective-permute-done.2.rest_1_ = f32[96,128]{1,0:T(8,128)S(1)} collective-permute-done((f32[96,128]{1,0:T(8,128)S(1)}, f32[96,128]{1,0:T(8,128)S(1)}, u32[]{:S(2)}, u32[]{:S(2)}) %collective-permute-start.2) | collective-permute-done | bytes 49184 | tf_op jit(solution)/shard_map/ppermute | solution.py:675
  35.6 5.0 %collective-permute-done.3.rest_2_ = f32[96,128]{1,0:T(8,128)S(1)} collective-permute-done((f32[96,128]{1,0:T(8,128)S(1)}, f32[96,128]{1,0:T(8,128)S(1)}, u32[]{:S(2)}, u32[]{:S(2)}) %collective-permute-start.3) | collective-permute-done | bytes 49184 | tf_op jit(solution)/shard_map/ppermute | solution.py:675
  40.6 1.5 %collective-permute-start.5 = (f32[96,128]{1,0:T(8,128)S(1)}, f32[96,128]{1,0:T(8,128)S(1)}, u32[]{:S(2)}, u32[]{:S(2)}) collective-permute-start(f32[96,128]{1,0:T(8,128)S(1)} %get-tuple-element.56), channel_id=1, source_target_pairs={{0,1},{1,0},{2,3},{3,2},{4,5},{5,4},{6,7},{7,6},{8,9},{9,8},{10,11... | collective-permute-start | bytes 147464 | tf_op jit(solution)/shard_map/ppermute | solution.py:675
  42.2 1.5 %collective-permute-start.6 = (f32[96,128]{1,0:T(8,128)S(1)}, f32[96,128]{1,0:T(8,128)S(1)}, u32[]{:S(2)}, u32[]{:S(2)}) collective-permute-start(f32[96,128]{1,0:T(8,128)S(1)} %get-tuple-element.57), channel_id=1, source_target_pairs={{0,2},{1,3},{2,0},{3,1},{4,6},{5,7},{6,4},{7,5},{8,10},{9,11},{10,... | collective-permute-start | bytes 147464 | tf_op jit(solution)/shard_map/ppermute | solution.py:675
  43.6 0.6 collective-permute-start.7
  44.2 0.9 collective-permute-done.5
  45.1 1.2 %collective-permute-done.6 = f32[96,128]{1,0:T(8,128)S(1)} collective-permute-done((f32[96,128]{1,0:T(8,128)S(1)}, f32[96,128]{1,0:T(8,128)S(1)}, u32[]{:S(2)}, u32[]{:S(2)}) %collective-permute-start.6) | collective-permute-done | bytes 49184 | tf_op jit(solution)/shard_map/ppermute | solution.py:675
  46.3 2.3 %collective-permute-done.7 = f32[96,128]{1,0:T(8,128)S(1)} collective-permute-done((f32[96,128]{1,0:T(8,128)S(1)}, f32[96,128]{1,0:T(8,128)S(1)}, u32[]{:S(2)}, u32[]{:S(2)}) %collective-permute-start.7) | collective-permute-done | bytes 49184 | tf_op jit(solution)/shard_map/ppermute | solution.py:675
  48.7 1.5 %shard_map.152 = (f32[128,128]{1,0:T(8,128)S(1)}, f32[16,24,128]{2,1,0:T(8,128)S(1)}) custom-call(s32[32]{0:T(128)S(1)} %copy-done.6, f32[32]{0:T(128)S(1)} %copy-done.7, f32[128,256]{1,0:T(8,128)S(1)} %copy-done.2, f32[128,256]{1,0:T(8,128)S(1)} %copy-done.1, f32[32,128]{1,0:T(8,128)S(1)} %copy-done.5, f32[32,256]{1,0:T(8,128)S(1)} %copy-done.4, ...), custom_call_target="tpu_custom_call" | custom-call | flops 100000000 | bytes 1000000 | tf_op jit(solution)/shard_map/pallas_call | solution.py:608
  50.2 0.0 all-to-all-done.bulk
  50.2 4.1 %shard_map.153 = (bf16[16,24,1024]{2,1,0:T(8,128)(2,1)}, f32[8,128]{1,0:T(8,128)S(1)}) custom-call(s32[32]{0:T(128)S(1)} %copy-done.6, f32[32]{0:T(128)S(1)} %copy-done.7, bf16[16,192,128]{2,1,0:T(8,128)(2,1)S(1)} %all-to-all-done.bulk, f32[16,24,128]{2,1,0:T(8,128)S(1)} %get-tuple-element.59.sides), custom_call_target="tpu_custom_call" | custom-call | flops 19660800 | bytes 1572864 | tf_op jit(solution)/shard_map/pallas_call | solution.py:608
  54.2 3.6 %all-to-all-start.1 = ((bf16[16,24,1024]{2,1,0:T(8,128)(2,1)}), bf16[16,24,1024]{2,1,0:T(8,128)(2,1)S(1)}, u32[]{:S(2)}, u32[]{:S(2)}) async-start(bf16[16,24,1024]{2,1,0:T(8,128)(2,1)} %get-tuple-element.60), calls=%async_computation.1 | async-start | bytes 1572864 | tf_op jit(solution)/shard_map/all_to_all | solution.py:614
  57.9 1.9 %collective-permute-start.8 = (f32[32,128]{1,0:T(8,128)S(1)}, f32[32,128]{1,0:T(8,128)S(1)}, u32[]{:S(2)}, u32[]{:S(2)}) collective-permute-start(f32[32,128]{1,0:T(8,128)S(1)} %get-tuple-element.67), channel_id=1, source_target_pairs={{0,1},{1,0},{2,3},{3,2},{4,5},{5,4},{6,7},{7,6},{8,9},{9,8},{10,11... | collective-permute-start | bytes 49160 | tf_op jit(solution)/shard_map/ppermute | solution.py:675
  59.8 1.5 %collective-permute-start.9 = (f32[32,128]{1,0:T(8,128)S(1)}, f32[32,128]{1,0:T(8,128)S(1)}, u32[]{:S(2)}, u32[]{:S(2)}) collective-permute-start(f32[32,128]{1,0:T(8,128)S(1)} %get-tuple-element.68), channel_id=1, source_target_pairs={{0,2},{1,3},{2,0},{3,1},{4,6},{5,7},{6,4},{7,5},{8,10},{9,11},{10,... | collective-permute-start | bytes 49160 | tf_op jit(solution)/shard_map/ppermute | solution.py:675
  61.2 0.2 collective-permute-start.10
  61.5 1.6 %collective-permute-done.8.rest_1_ = f32[32,128]{1,0:T(8,128)S(1)} collective-permute-done((f32[32,128]{1,0:T(8,128)S(1)}, f32[32,128]{1,0:T(8,128)S(1)}, u32[]{:S(2)}, u32[]{:S(2)}) %collective-permute-start.8) | collective-permute-done | bytes 16416 | tf_op jit(solution)/shard_map/ppermute | solution.py:675
  63.0 1.3 %collective-permute-done.9.rest_2_ = f32[32,128]{1,0:T(8,128)S(1)} collective-permute-done((f32[32,128]{1,0:T(8,128)S(1)}, f32[32,128]{1,0:T(8,128)S(1)}, u32[]{:S(2)}, u32[]{:S(2)}) %collective-permute-start.9) | collective-permute-done | bytes 16416 | tf_op jit(solution)/shard_map/ppermute | solution.py:675
  64.4 1.7 %collective-permute-done.10.rest_3_ = f32[32,128]{1,0:T(8,128)S(1)} collective-permute-done((f32[32,128]{1,0:T(8,128)S(1)}, f32[32,128]{1,0:T(8,128)S(1)}, u32[]{:S(2)}, u32[]{:S(2)}) %collective-permute-start.10) | collective-permute-done | bytes 16416 | tf_op jit(solution)/shard_map/ppermute | solution.py:675
  66.1 1.5 %collective-permute-start.11 = (f32[32,128]{1,0:T(8,128)S(1)}, f32[32,128]{1,0:T(8,128)S(1)}, u32[]{:S(2)}, u32[]{:S(2)}) collective-permute-start(f32[32,128]{1,0:T(8,128)S(1)} %get-tuple-element.71), channel_id=1, source_target_pairs={{0,4},{1,5},{2,6},{3,7},{4,8},{5,9},{6,10},{7,11},{8,12},{9,13},{1... | collective-permute-start | bytes 49160 | tf_op jit(solution)/shard_map/ppermute | solution.py:675
  67.6 2.4 %collective-permute-start.12 = (f32[32,128]{1,0:T(8,128)S(1)}, f32[32,128]{1,0:T(8,128)S(1)}, u32[]{:S(2)}, u32[]{:S(2)}) collective-permute-start(f32[32,128]{1,0:T(8,128)S(1)} %get-tuple-element.72), channel_id=1, source_target_pairs={{0,8},{1,9},{2,10},{3,11},{4,12},{5,13},{6,14},{7,15},{8,0},{9,1},... | collective-permute-start | bytes 49160 | tf_op jit(solution)/shard_map/ppermute | solution.py:675
  70.0 1.4 %collective-permute-start.13 = (f32[32,128]{1,0:T(8,128)S(1)}, f32[32,128]{1,0:T(8,128)S(1)}, u32[]{:S(2)}, u32[]{:S(2)}) collective-permute-start(f32[32,128]{1,0:T(8,128)S(1)} %get-tuple-element.73), channel_id=1, source_target_pairs={{0,12},{1,13},{2,14},{3,15},{4,0},{5,1},{6,2},{7,3},{8,4},{9,5},{1... | collective-permute-start | bytes 49160 | tf_op jit(solution)/shard_map/ppermute | solution.py:675
  71.4 2.3 %collective-permute-done.11.rest_1_ = f32[32,128]{1,0:T(8,128)S(1)} collective-permute-done((f32[32,128]{1,0:T(8,128)S(1)}, f32[32,128]{1,0:T(8,128)S(1)}, u32[]{:S(2)}, u32[]{:S(2)}) %collective-permute-start.11) | collective-permute-done | bytes 16416 | tf_op jit(solution)/shard_map/ppermute | solution.py:675
  73.7 3.6 %collective-permute-done.12.rest_2_ = f32[32,128]{1,0:T(8,128)S(1)} collective-permute-done((f32[32,128]{1,0:T(8,128)S(1)}, f32[32,128]{1,0:T(8,128)S(1)}, u32[]{:S(2)}, u32[]{:S(2)}) %collective-permute-start.12) | collective-permute-done | bytes 16416 | tf_op jit(solution)/shard_map/ppermute | solution.py:675
  77.3 0.0 collective-permute-done.13.rest_3_
  77.3 0.1 collective-permute-start.14
  77.4 1.2 %collective-permute-done.14.rest_1_ = f32[64,128]{1,0:T(8,128)S(1)} collective-permute-done((f32[64,128]{1,0:T(8,128)S(1)}, f32[64,128]{1,0:T(8,128)S(1)}, u32[]{:S(2)}, u32[]{:S(2)}) %collective-permute-start.14) | collective-permute-done | bytes 32800 | tf_op jit(solution)/shard_map/ppermute | solution.py:675
  78.6 0.7 shard_map.158
  79.3 0.2 collective-permute-start.15
  79.5 1.0 %collective-permute-done.15.rest_1_ = f32[32,128]{1,0:T(8,128)S(1)} collective-permute-done((f32[32,128]{1,0:T(8,128)S(1)}, f32[32,128]{1,0:T(8,128)S(1)}, u32[]{:S(2)}, u32[]{:S(2)}) %collective-permute-start.15) | collective-permute-done | bytes 16416 | tf_op jit(solution)/shard_map/ppermute | solution.py:675
  80.6 1.5 %collective-permute-start.16 = (f32[16,128]{1,0:T(8,128)S(1)}, f32[16,128]{1,0:T(8,128)S(1)}, u32[]{:S(2)}, u32[]{:S(2)}) collective-permute-start(f32[16,128]{1,0:T(8,128)S(1)} %get-tuple-element.81), channel_id=1, source_target_pairs={{0,1},{1,0},{2,3},{3,2},{4,5},{5,4},{6,7},{7,6},{8,9},{9,8},{10,11... | collective-permute-start | bytes 24584 | tf_op jit(solution)/shard_map/ppermute | solution.py:675
  82.1 1.5 %collective-permute-start.17 = (f32[16,128]{1,0:T(8,128)S(1)}, f32[16,128]{1,0:T(8,128)S(1)}, u32[]{:S(2)}, u32[]{:S(2)}) collective-permute-start(f32[16,128]{1,0:T(8,128)S(1)} %get-tuple-element.82), channel_id=1, source_target_pairs={{0,2},{1,3},{2,0},{3,1},{4,6},{5,7},{6,4},{7,5},{8,10},{9,11},{10,... | collective-permute-start | bytes 24584 | tf_op jit(solution)/shard_map/ppermute | solution.py:675
  83.6 0.6 collective-permute-start.18
  84.1 0.2 collective-permute-done.16.rest_1_
  84.3 1.5 %collective-permute-done.17.rest_2_ = f32[16,128]{1,0:T(8,128)S(1)} collective-permute-done((f32[16,128]{1,0:T(8,128)S(1)}, f32[16,128]{1,0:T(8,128)S(1)}, u32[]{:S(2)}, u32[]{:S(2)}) %collective-permute-start.17) | collective-permute-done | bytes 8224 | tf_op jit(solution)/shard_map/ppermute | solution.py:675
  85.8 2.4 %collective-permute-done.18.rest_3_ = f32[16,128]{1,0:T(8,128)S(1)} collective-permute-done((f32[16,128]{1,0:T(8,128)S(1)}, f32[16,128]{1,0:T(8,128)S(1)}, u32[]{:S(2)}, u32[]{:S(2)}) %collective-permute-start.18) | collective-permute-done | bytes 8224 | tf_op jit(solution)/shard_map/ppermute | solution.py:675
  88.2 0.8 collective-permute-start.19
  89.0 1.5 %collective-permute-start.20 = (f32[16,128]{1,0:T(8,128)S(1)}, f32[16,128]{1,0:T(8,128)S(1)}, u32[]{:S(2)}, u32[]{:S(2)}) collective-permute-start(f32[16,128]{1,0:T(8,128)S(1)} %get-tuple-element.86), channel_id=1, source_target_pairs={{0,8},{1,9},{2,10},{3,11},{4,12},{5,13},{6,14},{7,15},{8,0},{9,1},... | collective-permute-start | bytes 24584 | tf_op jit(solution)/shard_map/ppermute | solution.py:675
  90.5 1.6 %collective-permute-start.21 = (f32[16,128]{1,0:T(8,128)S(1)}, f32[16,128]{1,0:T(8,128)S(1)}, u32[]{:S(2)}, u32[]{:S(2)}) collective-permute-start(f32[16,128]{1,0:T(8,128)S(1)} %get-tuple-element.87), channel_id=1, source_target_pairs={{0,12},{1,13},{2,14},{3,15},{4,0},{5,1},{6,2},{7,3},{8,4},{9,5},{1... | collective-permute-start | bytes 24584 | tf_op jit(solution)/shard_map/ppermute | solution.py:675
  92.1 1.6 %collective-permute-done.19.rest_1_ = f32[16,128]{1,0:T(8,128)S(1)} collective-permute-done((f32[16,128]{1,0:T(8,128)S(1)}, f32[16,128]{1,0:T(8,128)S(1)}, u32[]{:S(2)}, u32[]{:S(2)}) %collective-permute-start.19) | collective-permute-done | bytes 8224 | tf_op jit(solution)/shard_map/ppermute | solution.py:675
  93.7 0.0 collective-permute-done.20.rest_2_
  93.7 0.6 collective-permute-done.21.rest_3_
  94.2 1.4 %shard_map.161 = f32[2,16384]{1,0:T(2,128)} custom-call(f32[128,256]{1,0:T(8,128)S(1)} %copy-done.2, f32[128,256]{1,0:T(8,128)S(1)} %copy-done.1, f32[32,512]{1,0:T(8,128)S(1)} %get-tuple-element.76.tables, f32[32,128]{1,0:T(8,128)S(1)} %get-tuple-element.77.factor, f32[16,128]{1,0:T(8,128)S(1)} %get-tuple-element.84.rest_0_, ...), custom_call_target="tpu_custom_call" | custom-call | flops 100000000 | bytes 1000000 | tf_op jit(solution)/shard_map/pallas_call | solution.py:608
  95.6 0.0 all-to-all-done.1.bulk
  95.7 1.5 %shard_map.154 = (f32[4,32,1024]{2,1,0:T(8,128)}, f32[4,32,1024]{2,1,0:T(8,128)}, f32[4,32,1024]{2,1,0:T(8,128)}) custom-call(bf16[16,24,1024]{2,1,0:T(8,128)(2,1)S(1)} %all-to-all-done.1.bulk, f32[8,128]{1,0:T(8,128)S(1)} %get-tuple-element.61.top), custom_call_target="tpu_custom_call" | custom-call | flops 7864320 | bytes 2359296 | tf_op jit(solution)/shard_map/pallas_call | solution.py:608
  (15 shorter events, 0.2 us)
Async XLA Ops:
  2.0 1.5 %collective-permute-start = (f32[3,4,2,1024]{3,2,1,0:T(2,128)S(1)}, f32[3,4,2,1024]{3,2,1,0:T(2,128)S(1)}, u32[]{:S(2)}, u32[]{:S(2)}) collective-permute-start(f32[3,4,2,1024]{3,2,1,0:T(2,128)S(1)} %get-tuple-element.47), channel_id=1, source_target_pairs={{0,16},{16,0},{1,17},{17,1},{2,18},{18,2},{3,19},{19,3},{4,20},{20... | collective-permute-start | bytes 294920 | tf_op jit(solution)/shard_map/ppermute | solution.py:654
  2.6 1.3 %collective-permute-start.1 = (f32[3,4,2,1024]{3,2,1,0:T(2,128)S(1)}, f32[3,4,2,1024]{3,2,1,0:T(2,128)S(1)}, u32[]{:S(2)}, u32[]{:S(2)}) collective-permute-start(f32[3,4,2,1024]{3,2,1,0:T(2,128)S(1)} %get-tuple-element.48), channel_id=1, source_target_pairs={{16,0},{0,16},{17,1},{1,17},{18,2},{2,18},{19,3},{3,19},{20,4},{4,... | collective-permute-start | bytes 294920 | tf_op jit(solution)/shard_map/ppermute | solution.py:655
  3.4 45.2 %copy-start.1 = (f32[128,256]{1,0:T(8,128)S(1)}, f32[128,256]{1,0:T(8,128)}, u32[]{:S(2)}) copy-start(f32[128,256]{1,0:T(8,128)} %constant.11.clone.twiddle) | copy-start | bytes 393220
  3.4 45.2 %copy-start.2 = (f32[128,256]{1,0:T(8,128)S(1)}, f32[128,256]{1,0:T(8,128)}, u32[]{:S(2)}) copy-start(f32[128,256]{1,0:T(8,128)} %constant.10.clone.circle) | copy-start | bytes 393220
  3.4 45.2 %copy-start.4 = (f32[32,256]{1,0:T(8,128)S(1)}, f32[32,256]{1,0:T(8,128)}, u32[]{:S(2)}) copy-start(f32[32,256]{1,0:T(8,128)} %constant.13.clone.steps) | copy-start | bytes 98308
  3.5 45.2 %copy-start.5 = (f32[32,128]{1,0:T(8,128)S(1)}, f32[32,128]{1,0:T(8,128)}, u32[]{:S(2)}) copy-start(f32[32,128]{1,0:T(8,128)} %constant.12.clone.short) | copy-start | bytes 49156
  3.5 45.2 %copy-start.6 = (s32[32]{0:T(128)S(1)}, s32[32]{0:T(128)}, u32[]{:S(2)}) copy-start(s32[32]{0:T(128)} %far_shift.3) | copy-start | bytes 388
  3.5 45.2 %copy-start.7 = (f32[32]{0:T(128)S(1)}, f32[32]{0:T(128)}, u32[]{:S(2)}) copy-start(f32[32]{0:T(128)} %far_remainder.3) | copy-start | bytes 388
  8.3 41.9 %all-to-all-start = ((bf16[16,192,128]{2,1,0:T(8,128)(2,1)}), bf16[16,192,128]{2,1,0:T(8,128)(2,1)S(1)}, u32[]{:S(2)}, u32[]{:S(2)}) async-start(bf16[16,192,128]{2,1,0:T(8,128)(2,1)} %get-tuple-element.49), calls=%async_computation | async-start | bytes 1572864 | tf_op jit(solution)/shard_map/all_to_all | solution.py:614
  16.3 62.3 %copy-start = (bf16[64,64,64]{2,1,0:T(8,128)(2,1)S(1)}, bf16[64,64,64]{2,1,0:T(8,128)(2,1)}, u32[]{:S(2)}) copy-start(bf16[64,64,64]{2,1,0:T(8,128)(2,1)} %kernel.1) | copy-start | bytes 1572868
  16.3 62.3 %copy-start.3 = (f32[32,256]{1,0:T(8,128)S(1)}, f32[32,256]{1,0:T(8,128)}, u32[]{:S(2)}) copy-start(f32[32,256]{1,0:T(8,128)} %constant.14.clone.mixed) | copy-start | bytes 98308
  16.4 19.2 %collective-permute-start.2 = (f32[96,128]{1,0:T(8,128)S(1)}, f32[96,128]{1,0:T(8,128)S(1)}, u32[]{:S(2)}, u32[]{:S(2)}) collective-permute-start(f32[96,128]{1,0:T(8,128)S(1)} %get-tuple-element.52), channel_id=1, source_target_pairs={{0,4},{1,5},{2,6},{3,7},{4,8},{5,9},{6,10},{7,11},{8,12},{9,13},{1... | collective-permute-start | bytes 147464 | tf_op jit(solution)/shard_map/ppermute | solution.py:675
  18.4 22.2 %collective-permute-start.3 = (f32[96,128]{1,0:T(8,128)S(1)}, f32[96,128]{1,0:T(8,128)S(1)}, u32[]{:S(2)}, u32[]{:S(2)}) collective-permute-start(f32[96,128]{1,0:T(8,128)S(1)} %get-tuple-element.53), channel_id=1, source_target_pairs={{0,8},{1,9},{2,10},{3,11},{4,12},{5,13},{6,14},{7,15},{8,0},{9,1},... | collective-permute-start | bytes 147464 | tf_op jit(solution)/shard_map/ppermute | solution.py:675
  20.8 19.8 %collective-permute-start.4 = (f32[96,128]{1,0:T(8,128)S(1)}, f32[96,128]{1,0:T(8,128)S(1)}, u32[]{:S(2)}, u32[]{:S(2)}) collective-permute-start(f32[96,128]{1,0:T(8,128)S(1)} %get-tuple-element.54), channel_id=1, source_target_pairs={{0,12},{1,13},{2,14},{3,15},{4,0},{5,1},{6,2},{7,3},{8,4},{9,5},{1... | collective-permute-start | bytes 147464 | tf_op jit(solution)/shard_map/ppermute | solution.py:675
  40.6 4.5 %collective-permute-start.5 = (f32[96,128]{1,0:T(8,128)S(1)}, f32[96,128]{1,0:T(8,128)S(1)}, u32[]{:S(2)}, u32[]{:S(2)}) collective-permute-start(f32[96,128]{1,0:T(8,128)S(1)} %get-tuple-element.56), channel_id=1, source_target_pairs={{0,1},{1,0},{2,3},{3,2},{4,5},{5,4},{6,7},{7,6},{8,9},{9,8},{10,11... | collective-permute-start | bytes 147464 | tf_op jit(solution)/shard_map/ppermute | solution.py:675
  42.2 4.1 %collective-permute-start.6 = (f32[96,128]{1,0:T(8,128)S(1)}, f32[96,128]{1,0:T(8,128)S(1)}, u32[]{:S(2)}, u32[]{:S(2)}) collective-permute-start(f32[96,128]{1,0:T(8,128)S(1)} %get-tuple-element.57), channel_id=1, source_target_pairs={{0,2},{1,3},{2,0},{3,1},{4,6},{5,7},{6,4},{7,5},{8,10},{9,11},{10,... | collective-permute-start | bytes 147464 | tf_op jit(solution)/shard_map/ppermute | solution.py:675
  43.6 5.0 %collective-permute-start.7 = (f32[96,128]{1,0:T(8,128)S(1)}, f32[96,128]{1,0:T(8,128)S(1)}, u32[]{:S(2)}, u32[]{:S(2)}) collective-permute-start(f32[96,128]{1,0:T(8,128)S(1)} %get-tuple-element.58), channel_id=1, source_target_pairs={{0,3},{1,2},{2,1},{3,0},{4,7},{5,6},{6,5},{7,4},{8,11},{9,10},{10,... | collective-permute-start | bytes 147464 | tf_op jit(solution)/shard_map/ppermute | solution.py:675
  54.2 41.4 %all-to-all-start.1 = ((bf16[16,24,1024]{2,1,0:T(8,128)(2,1)}), bf16[16,24,1024]{2,1,0:T(8,128)(2,1)S(1)}, u32[]{:S(2)}, u32[]{:S(2)}) async-start(bf16[16,24,1024]{2,1,0:T(8,128)(2,1)} %get-tuple-element.60), calls=%async_computation.1 | async-start | bytes 1572864 | tf_op jit(solution)/shard_map/all_to_all | solution.py:614
  57.9 5.1 %collective-permute-start.8 = (f32[32,128]{1,0:T(8,128)S(1)}, f32[32,128]{1,0:T(8,128)S(1)}, u32[]{:S(2)}, u32[]{:S(2)}) collective-permute-start(f32[32,128]{1,0:T(8,128)S(1)} %get-tuple-element.67), channel_id=1, source_target_pairs={{0,1},{1,0},{2,3},{3,2},{4,5},{5,4},{6,7},{7,6},{8,9},{9,8},{10,11... | collective-permute-start | bytes 49160 | tf_op jit(solution)/shard_map/ppermute | solution.py:675
  59.8 4.6 %collective-permute-start.9 = (f32[32,128]{1,0:T(8,128)S(1)}, f32[32,128]{1,0:T(8,128)S(1)}, u32[]{:S(2)}, u32[]{:S(2)}) collective-permute-start(f32[32,128]{1,0:T(8,128)S(1)} %get-tuple-element.68), channel_id=1, source_target_pairs={{0,2},{1,3},{2,0},{3,1},{4,6},{5,7},{6,4},{7,5},{8,10},{9,11},{10,... | collective-permute-start | bytes 49160 | tf_op jit(solution)/shard_map/ppermute | solution.py:675
  61.2 4.8 %collective-permute-start.10 = (f32[32,128]{1,0:T(8,128)S(1)}, f32[32,128]{1,0:T(8,128)S(1)}, u32[]{:S(2)}, u32[]{:S(2)}) collective-permute-start(f32[32,128]{1,0:T(8,128)S(1)} %get-tuple-element.69), channel_id=1, source_target_pairs={{0,3},{1,2},{2,1},{3,0},{4,7},{5,6},{6,5},{7,4},{8,11},{9,10},{10,... | collective-permute-start | bytes 49160 | tf_op jit(solution)/shard_map/ppermute | solution.py:675
  66.1 7.6 %collective-permute-start.11 = (f32[32,128]{1,0:T(8,128)S(1)}, f32[32,128]{1,0:T(8,128)S(1)}, u32[]{:S(2)}, u32[]{:S(2)}) collective-permute-start(f32[32,128]{1,0:T(8,128)S(1)} %get-tuple-element.71), channel_id=1, source_target_pairs={{0,4},{1,5},{2,6},{3,7},{4,8},{5,9},{6,10},{7,11},{8,12},{9,13},{1... | collective-permute-start | bytes 49160 | tf_op jit(solution)/shard_map/ppermute | solution.py:675
  67.6 9.7 %collective-permute-start.12 = (f32[32,128]{1,0:T(8,128)S(1)}, f32[32,128]{1,0:T(8,128)S(1)}, u32[]{:S(2)}, u32[]{:S(2)}) collective-permute-start(f32[32,128]{1,0:T(8,128)S(1)} %get-tuple-element.72), channel_id=1, source_target_pairs={{0,8},{1,9},{2,10},{3,11},{4,12},{5,13},{6,14},{7,15},{8,0},{9,1},... | collective-permute-start | bytes 49160 | tf_op jit(solution)/shard_map/ppermute | solution.py:675
  70.0 7.3 %collective-permute-start.13 = (f32[32,128]{1,0:T(8,128)S(1)}, f32[32,128]{1,0:T(8,128)S(1)}, u32[]{:S(2)}, u32[]{:S(2)}) collective-permute-start(f32[32,128]{1,0:T(8,128)S(1)} %get-tuple-element.73), channel_id=1, source_target_pairs={{0,12},{1,13},{2,14},{3,15},{4,0},{5,1},{6,2},{7,3},{8,4},{9,5},{1... | collective-permute-start | bytes 49160 | tf_op jit(solution)/shard_map/ppermute | solution.py:675
  77.3 1.3 %collective-permute-start.14 = (f32[64,128]{1,0:T(8,128)S(1)}, f32[64,128]{1,0:T(8,128)S(1)}, u32[]{:S(2)}, u32[]{:S(2)}) collective-permute-start(f32[64,128]{1,0:T(8,128)S(1)} %get-tuple-element.75), channel_id=1, source_target_pairs={{0,16},{16,0},{1,17},{17,1},{2,18},{18,2},{3,19},{19,3},{4,20},{20... | collective-permute-start | bytes 98312 | tf_op jit(solution)/shard_map/ppermute | solution.py:675
  79.3 1.2 %collective-permute-start.15 = (f32[32,128]{1,0:T(8,128)S(1)}, f32[32,128]{1,0:T(8,128)S(1)}, u32[]{:S(2)}, u32[]{:S(2)}) collective-permute-start(f32[32,128]{1,0:T(8,128)S(1)} %get-tuple-element.79), channel_id=1, source_target_pairs={{0,16},{16,0},{1,17},{17,1},{2,18},{18,2},{3,19},{19,3},{4,20},{20... | collective-permute-start | bytes 49160 | tf_op jit(solution)/shard_map/ppermute | solution.py:675
  80.6 3.7 %collective-permute-start.16 = (f32[16,128]{1,0:T(8,128)S(1)}, f32[16,128]{1,0:T(8,128)S(1)}, u32[]{:S(2)}, u32[]{:S(2)}) collective-permute-start(f32[16,128]{1,0:T(8,128)S(1)} %get-tuple-element.81), channel_id=1, source_target_pairs={{0,1},{1,0},{2,3},{3,2},{4,5},{5,4},{6,7},{7,6},{8,9},{9,8},{10,11... | collective-permute-start | bytes 24584 | tf_op jit(solution)/shard_map/ppermute | solution.py:675
  82.1 3.7 %collective-permute-start.17 = (f32[16,128]{1,0:T(8,128)S(1)}, f32[16,128]{1,0:T(8,128)S(1)}, u32[]{:S(2)}, u32[]{:S(2)}) collective-permute-start(f32[16,128]{1,0:T(8,128)S(1)} %get-tuple-element.82), channel_id=1, source_target_pairs={{0,2},{1,3},{2,0},{3,1},{4,6},{5,7},{6,4},{7,5},{8,10},{9,11},{10,... | collective-permute-start | bytes 24584 | tf_op jit(solution)/shard_map/ppermute | solution.py:675
  83.6 4.5 %collective-permute-start.18 = (f32[16,128]{1,0:T(8,128)S(1)}, f32[16,128]{1,0:T(8,128)S(1)}, u32[]{:S(2)}, u32[]{:S(2)}) collective-permute-start(f32[16,128]{1,0:T(8,128)S(1)} %get-tuple-element.83), channel_id=1, source_target_pairs={{0,3},{1,2},{2,1},{3,0},{4,7},{5,6},{6,5},{7,4},{8,11},{9,10},{10,... | collective-permute-start | bytes 24584 | tf_op jit(solution)/shard_map/ppermute | solution.py:675
  88.2 5.5 %collective-permute-start.19 = (f32[16,128]{1,0:T(8,128)S(1)}, f32[16,128]{1,0:T(8,128)S(1)}, u32[]{:S(2)}, u32[]{:S(2)}) collective-permute-start(f32[16,128]{1,0:T(8,128)S(1)} %get-tuple-element.85), channel_id=1, source_target_pairs={{0,4},{1,5},{2,6},{3,7},{4,8},{5,9},{6,10},{7,11},{8,12},{9,13},{1... | collective-permute-start | bytes 24584 | tf_op jit(solution)/shard_map/ppermute | solution.py:675
  89.0 4.7 %collective-permute-start.20 = (f32[16,128]{1,0:T(8,128)S(1)}, f32[16,128]{1,0:T(8,128)S(1)}, u32[]{:S(2)}, u32[]{:S(2)}) collective-permute-start(f32[16,128]{1,0:T(8,128)S(1)} %get-tuple-element.86), channel_id=1, source_target_pairs={{0,8},{1,9},{2,10},{3,11},{4,12},{5,13},{6,14},{7,15},{8,0},{9,1},... | collective-permute-start | bytes 24584 | tf_op jit(solution)/shard_map/ppermute | solution.py:675
  90.5 3.8 %collective-permute-start.21 = (f32[16,128]{1,0:T(8,128)S(1)}, f32[16,128]{1,0:T(8,128)S(1)}, u32[]{:S(2)}, u32[]{:S(2)}) collective-permute-start(f32[16,128]{1,0:T(8,128)S(1)} %get-tuple-element.87), channel_id=1, source_target_pairs={{0,12},{1,13},{2,14},{3,15},{4,0},{5,1},{6,2},{7,3},{8,4},{9,5},{1... | collective-permute-start | bytes 24584 | tf_op jit(solution)/shard_map/ppermute | solution.py:675

commit v10 on v9

--- a/solution.py
+++ b/solution.py
@@ -345,11 +345,13 @@
         copy.start()
     me = lax.axis_index("azi")
     azi = lax.axis_index("azi")
+    slow = sides.shape[0] // fast
+    used = hops[0].shape[0] // slow
     for o_fast, hop in enumerate(hops):
-        for o_slow in range(hop.shape[0]):
-            from_slow = came_from(azi // fast, o_slow, hop.shape[0], True)
+        for o_slow in range(slow):
+            from_slow = came_from(azi // fast, o_slow, slow, True)
             from_fast = came_from(azi % fast, o_fast, fast, False)
-            sides[from_slow * fast + from_fast] = hop[o_slow]
+            sides[from_slow * fast + from_fast, 0:used, :] = hop[o_slow * used : (o_slow + 1) * used, :]
     sources = sides.shape[0]
     nq = circle.shape[0]
     tiles = nq // sources
@@ -438,6 +440,18 @@
         out[...] = pick(choices, sent_to(index, offset, size, ring))
 
 
+def trim_kernel(size, used, where, ring, surf, *rest):
+    outs, sorted_rows = rest[:-1], rest[-1]
+    inner = surf.shape[0] // size
+    for dest in range(size):
+        for i in range(inner):
+            sorted_rows[dest, i * used : (i + 1) * used, :] = surf[dest * inner + i, 0:used, :]
+    choices = [sorted_rows[dest] for dest in range(size)]
+    index = where()
+    for offset, out in enumerate(outs):
+        out[...] = pick(choices, sent_to(index, offset, size, ring))
+
+
 def halve_kernel(inner, *rest):
     rad_count = lax.axis_size("rad")
     outs, sorted_rows = rest[-1 - rad_count : -1], rest[-1]
@@ -671,13 +685,14 @@
 
     def hop(buffers, axis, size, step, ring=False):
         around = range(lax.axis_size(axis))
-        return [buffers[0]] + [
-            lax.ppermute(buffers[o], axis, [
+        moved = [buffers[0]]
+        for o in range(1, size):
+            pairs = [
                 (i, i + (sent_to(i // step % size, o, size, ring) - i // step % size) * step)
                 for i in around
-            ])
-            for o in range(1, size)
-        ]
+            ]
+            moved.append(lax.ppermute(buffers[o], axis, pairs))
+        return moved
 
     def route(buffers, size, inner, step, name, ring=False):
         count = buffers[0].shape[0]
@@ -692,11 +707,17 @@
         )(*buffers)
         return hop(buffers, "azi", size, step, ring)
 
-    surf = [surf.reshape(azi * side, LANES)]
-    surf = route(surf, slow, fast * side, fast, "surf_slow", ring=True)
+    used = per * tiles + per
+    surf = call(
+        functools.partial(trim_kernel, slow, used, lambda: lax.axis_index("azi") // fast, True),
+        tuple(pltpu.VMEM((fast * used, LANES), F32) for _ in range(slow)),
+        scratch=(pltpu.VMEM((slow, fast * used, LANES), F32),),
+        name="route_surf_slow",
+        bytes_accessed=100_000,
+    )(surf)
+    surf = hop(surf, "azi", slow, fast, ring=True)
     bulk = exchange(bulk, "azi")
-    surf = route(surf, fast, side, 1, "surf_fast")
-    surf = [x.reshape(slow, side, LANES) for x in surf]
+    surf = route(surf, fast, used, 1, "surf_fast")
 
     k_id, l_id = np.arange(nq), np.arange(LANES)
     circle = np.concatenate(cos_sin(k_id, k_id, nq), axis=1)

time: 97.5 us -> 96.3 us (0.988)
  waiting for transfers between devices: 42.1 us -> 40.7 us
    ppermute x20, waiting for transfers between devices: 41.7 us -> 40.3 us  [hop(): moved.append(lax.ppermute(buffers[o], axis, pairs))]
where the time goes in v10:
time: 96.3 us; the launch traced here: 96 us
  waiting for transfers between devices  40.7 us (42%)
  starting transfers between devices  38.5 us (40%)
  Pallas kernels  15.9 us (17%)
    ppermute x20, waiting for transfers between devices, hop(): moved.append(lax.ppermute(buffers[o], axis, pairs))  40.3 us
    ppermute x20, starting transfers between devices, hop(): moved.append(lax.ppermute(buffers[o], axis, pairs))  26 us
    pallas_call x15, Pallas kernels, run(): return kernel(*near)  15.9 us
    all_to_all x2, starting transfers between devices, exchange(): return lax.all_to_all(array, axes, 0, 0, tiled=True)  11.8 us
  transfers between devices with their start and end apart: 24, of which 19 were waited for; matrix products, arithmetic and copies ran while one was open for 0% of the time, Pallas kernels for 5%

profile of v10, /device:TPU:0, one launch (start us, length us, event | category | flops | bytes accessed | tf_op | source)
XLA Modules:
  0.0 96.0 jit_solution(9264334229439318800)
XLA Ops:
  0.6 1.4 %shard_map.147 = (f32[3,4,40,1152]{3,2,1,0:T(8,128)S(1)}, f32[3,4,2,1024]{3,2,1,0:T(2,128)S(1)}, f32[3,4,2,1024]{3,2,1,0:T(2,128)S(1)}) custom-call(f32[4,32,1024]{2,1,0:T(8,128)} %rho.1, f32[4,32,1024]{2,1,0:T(8,128)} %ur.1, f32[4,32,1024]{2,1,0:T(8,128)} %up.1), custom_call_target="tpu_custom_call" | custom-call | bytes 1572864 | tf_op jit(solution)/shard_map/pallas_call | solution.py:622
  2.0 0.6 collective-permute-start
  2.6 0.1 collective-permute-start.1
  2.7 0.7 shard_map.148.stage_in
  3.4 0.0 copy-start.1
  3.4 0.0 copy-start.2
  3.4 0.0 copy-start.3
  3.5 0.0 copy-start.5
  3.5 0.0 copy-start.6
  3.5 0.0 copy-start.7
  3.5 0.1 collective-permute-done.low
  3.5 0.4 collective-permute-done.1.high
  3.9 4.4 %shard_map.149 = (bf16[16,192,128]{2,1,0:T(8,128)(2,1)}, f32[16,24,128]{2,1,0:T(8,128)S(1)}, f32[3,4,40,1152]{3,2,1,0:T(8,128)S(1)}, f32[3,4,40,1152]{3,2,1,0:T(8,128)S(1)}) custom-call(f32[3,4,40,1152]{3,2,1,0:T(8,128)S(1)} %get-tuple-element.46.field.field_in, ...), custom_call_target="tpu_custom_call", output_to_operand_aliasing={{2}: (0, {}), {3}: (1, {})} | custom-call | flops 39321600 | bytes 3145728 | tf_op jit(solution)/shard_map/pallas_call | solution.py:622
  8.3 0.0 copy-start
  8.3 0.0 copy-start.4
  8.3 8.1 %all-to-all-start = ((bf16[16,192,128]{2,1,0:T(8,128)(2,1)}), bf16[16,192,128]{2,1,0:T(8,128)(2,1)S(1)}, u32[]{:S(2)}, u32[]{:S(2)}) async-start(bf16[16,192,128]{2,1,0:T(8,128)(2,1)} %get-tuple-element.49), calls=%async_computation | async-start | bytes 1572864 | tf_op jit(solution)/shard_map/all_to_all | solution.py:628
  16.5 2.0 %collective-permute-start.2 = (f32[72,128]{1,0:T(8,128)S(1)}, f32[72,128]{1,0:T(8,128)S(1)}, u32[]{:S(2)}, u32[]{:S(2)}) collective-permute-start(f32[72,128]{1,0:T(8,128)S(1)} %get-tuple-element.52), channel_id=1, source_target_pairs={{0,4},{1,5},{2,6},{3,7},{4,8},{5,9},{6,10},{7,11},{8,12},{9,13},{1... | collective-permute-start | bytes 110600 | tf_op jit(solution)/shard_map/ppermute | solution.py:694
  18.5 2.4 %collective-permute-start.3 = (f32[72,128]{1,0:T(8,128)S(1)}, f32[72,128]{1,0:T(8,128)S(1)}, u32[]{:S(2)}, u32[]{:S(2)}) collective-permute-start(f32[72,128]{1,0:T(8,128)S(1)} %get-tuple-element.53), channel_id=1, source_target_pairs={{0,8},{1,9},{2,10},{3,11},{4,12},{5,13},{6,14},{7,15},{8,0},{9,1},... | collective-permute-start | bytes 110600 | tf_op jit(solution)/shard_map/ppermute | solution.py:694
  20.9 1.5 %collective-permute-start.4 = (f32[72,128]{1,0:T(8,128)S(1)}, f32[72,128]{1,0:T(8,128)S(1)}, u32[]{:S(2)}, u32[]{:S(2)}) collective-permute-start(f32[72,128]{1,0:T(8,128)S(1)} %get-tuple-element.54), channel_id=1, source_target_pairs={{0,12},{1,13},{2,14},{3,15},{4,0},{5,1},{6,2},{7,3},{8,4},{9,5},{1... | collective-permute-start | bytes 110600 | tf_op jit(solution)/shard_map/ppermute | solution.py:694
  22.3 13.0 %collective-permute-done.2.rest_1_ = f32[72,128]{1,0:T(8,128)S(1)} collective-permute-done((f32[72,128]{1,0:T(8,128)S(1)}, f32[72,128]{1,0:T(8,128)S(1)}, u32[]{:S(2)}, u32[]{:S(2)}) %collective-permute-start.2) | collective-permute-done | bytes 36896 | tf_op jit(solution)/shard_map/ppermute | solution.py:694
  35.4 4.4 %collective-permute-done.3.rest_2_ = f32[72,128]{1,0:T(8,128)S(1)} collective-permute-done((f32[72,128]{1,0:T(8,128)S(1)}, f32[72,128]{1,0:T(8,128)S(1)}, u32[]{:S(2)}, u32[]{:S(2)}) %collective-permute-start.3) | collective-permute-done | bytes 36896 | tf_op jit(solution)/shard_map/ppermute | solution.py:694
  39.8 0.0 collective-permute-done.4.rest_3_
  39.9 1.5 %collective-permute-start.5 = (f32[72,128]{1,0:T(8,128)S(1)}, f32[72,128]{1,0:T(8,128)S(1)}, u32[]{:S(2)}, u32[]{:S(2)}) collective-permute-start(f32[72,128]{1,0:T(8,128)S(1)} %get-tuple-element.56), channel_id=1, source_target_pairs={{0,1},{1,0},{2,3},{3,2},{4,5},{5,4},{6,7},{7,6},{8,9},{9,8},{10,11... | collective-permute-start | bytes 110600 | tf_op jit(solution)/shard_map/ppermute | solution.py:694
  41.4 1.5 %collective-permute-start.6 = (f32[72,128]{1,0:T(8,128)S(1)}, f32[72,128]{1,0:T(8,128)S(1)}, u32[]{:S(2)}, u32[]{:S(2)}) collective-permute-start(f32[72,128]{1,0:T(8,128)S(1)} %get-tuple-element.57), channel_id=1, source_target_pairs={{0,2},{1,3},{2,0},{3,1},{4,6},{5,7},{6,4},{7,5},{8,10},{9,11},{10,... | collective-permute-start | bytes 110600 | tf_op jit(solution)/shard_map/ppermute | solution.py:694
  42.9 0.6 collective-permute-start.7
  43.4 0.8 collective-permute-done.5.rest_1_
  44.2 1.2 %collective-permute-done.6.rest_2_ = f32[72,128]{1,0:T(8,128)S(1)} collective-permute-done((f32[72,128]{1,0:T(8,128)S(1)}, f32[72,128]{1,0:T(8,128)S(1)}, u32[]{:S(2)}, u32[]{:S(2)}) %collective-permute-start.6) | collective-permute-done | bytes 36896 | tf_op jit(solution)/shard_map/ppermute | solution.py:694
  45.4 2.3 %collective-permute-done.7.rest_3_ = f32[72,128]{1,0:T(8,128)S(1)} collective-permute-done((f32[72,128]{1,0:T(8,128)S(1)}, f32[72,128]{1,0:T(8,128)S(1)}, u32[]{:S(2)}, u32[]{:S(2)}) %collective-permute-start.7) | collective-permute-done | bytes 36896 | tf_op jit(solution)/shard_map/ppermute | solution.py:694
  47.8 1.5 %shard_map.152 = (f32[128,128]{1,0:T(8,128)S(1)}, f32[16,24,128]{2,1,0:T(8,128)S(1)}) custom-call(s32[32]{0:T(128)S(1)} %copy-done.6, f32[32]{0:T(128)S(1)} %copy-done.7, f32[128,256]{1,0:T(8,128)S(1)} %copy-done.2, f32[128,256]{1,0:T(8,128)S(1)} %copy-done.1, f32[32,128]{1,0:T(8,128)S(1)} %copy-done.5, f32[32,256]{1,0:T(8,128)S(1)} %copy-done.3, ...), custom_call_target="tpu_custom_call" | custom-call | flops 100000000 | bytes 1000000 | tf_op jit(solution)/shard_map/pallas_call | solution.py:622
  49.3 0.0 all-to-all-done.bulk
  49.3 4.1 %shard_map.153 = (bf16[16,24,1024]{2,1,0:T(8,128)(2,1)}, f32[8,128]{1,0:T(8,128)S(1)}) custom-call(s32[32]{0:T(128)S(1)} %copy-done.6, f32[32]{0:T(128)S(1)} %copy-done.7, bf16[16,192,128]{2,1,0:T(8,128)(2,1)S(1)} %all-to-all-done.bulk, f32[16,24,128]{2,1,0:T(8,128)S(1)} %get-tuple-element.59.sides), custom_call_target="tpu_custom_call" | custom-call | flops 19660800 | bytes 1572864 | tf_op jit(solution)/shard_map/pallas_call | solution.py:622
  53.3 3.6 %all-to-all-start.1 = ((bf16[16,24,1024]{2,1,0:T(8,128)(2,1)}), bf16[16,24,1024]{2,1,0:T(8,128)(2,1)S(1)}, u32[]{:S(2)}, u32[]{:S(2)}) async-start(bf16[16,24,1024]{2,1,0:T(8,128)(2,1)} %get-tuple-element.60), calls=%async_computation.1 | async-start | bytes 1572864 | tf_op jit(solution)/shard_map/all_to_all | solution.py:628
  57.0 1.9 %collective-permute-start.8 = (f32[32,128]{1,0:T(8,128)S(1)}, f32[32,128]{1,0:T(8,128)S(1)}, u32[]{:S(2)}, u32[]{:S(2)}) collective-permute-start(f32[32,128]{1,0:T(8,128)S(1)} %get-tuple-element.67), channel_id=1, source_target_pairs={{0,1},{1,0},{2,3},{3,2},{4,5},{5,4},{6,7},{7,6},{8,9},{9,8},{10,11... | collective-permute-start | bytes 49160 | tf_op jit(solution)/shard_map/ppermute | solution.py:694
  58.9 1.5 %collective-permute-start.9 = (f32[32,128]{1,0:T(8,128)S(1)}, f32[32,128]{1,0:T(8,128)S(1)}, u32[]{:S(2)}, u32[]{:S(2)}) collective-permute-start(f32[32,128]{1,0:T(8,128)S(1)} %get-tuple-element.68), channel_id=1, source_target_pairs={{0,2},{1,3},{2,0},{3,1},{4,6},{5,7},{6,4},{7,5},{8,10},{9,11},{10,... | collective-permute-start | bytes 49160 | tf_op jit(solution)/shard_map/ppermute | solution.py:694
  60.3 0.2 collective-permute-start.10
  60.6 2.0 %collective-permute-done.8.rest_1_ = f32[32,128]{1,0:T(8,128)S(1)} collective-permute-done((f32[32,128]{1,0:T(8,128)S(1)}, f32[32,128]{1,0:T(8,128)S(1)}, u32[]{:S(2)}, u32[]{:S(2)}) %collective-permute-start.8) | collective-permute-done | bytes 16416 | tf_op jit(solution)/shard_map/ppermute | solution.py:694
  62.5 0.8 collective-permute-done.9.rest_2_
  63.3 1.7 %collective-permute-done.10.rest_3_ = f32[32,128]{1,0:T(8,128)S(1)} collective-permute-done((f32[32,128]{1,0:T(8,128)S(1)}, f32[32,128]{1,0:T(8,128)S(1)}, u32[]{:S(2)}, u32[]{:S(2)}) %collective-permute-start.10) | collective-permute-done | bytes 16416 | tf_op jit(solution)/shard_map/ppermute | solution.py:694
  65.1 1.6 %collective-permute-start.11 = (f32[32,128]{1,0:T(8,128)S(1)}, f32[32,128]{1,0:T(8,128)S(1)}, u32[]{:S(2)}, u32[]{:S(2)}) collective-permute-start(f32[32,128]{1,0:T(8,128)S(1)} %get-tuple-element.71), channel_id=1, source_target_pairs={{0,4},{1,5},{2,6},{3,7},{4,8},{5,9},{6,10},{7,11},{8,12},{9,13},{1... | collective-permute-start | bytes 49160 | tf_op jit(solution)/shard_map/ppermute | solution.py:694
  66.7 2.4 %collective-permute-start.12 = (f32[32,128]{1,0:T(8,128)S(1)}, f32[32,128]{1,0:T(8,128)S(1)}, u32[]{:S(2)}, u32[]{:S(2)}) collective-permute-start(f32[32,128]{1,0:T(8,128)S(1)} %get-tuple-element.72), channel_id=1, source_target_pairs={{0,8},{1,9},{2,10},{3,11},{4,12},{5,13},{6,14},{7,15},{8,0},{9,1},... | collective-permute-start | bytes 49160 | tf_op jit(solution)/shard_map/ppermute | solution.py:694
  69.1 1.4 %collective-permute-start.13 = (f32[32,128]{1,0:T(8,128)S(1)}, f32[32,128]{1,0:T(8,128)S(1)}, u32[]{:S(2)}, u32[]{:S(2)}) collective-permute-start(f32[32,128]{1,0:T(8,128)S(1)} %get-tuple-element.73), channel_id=1, source_target_pairs={{0,12},{1,13},{2,14},{3,15},{4,0},{5,1},{6,2},{7,3},{8,4},{9,5},{1... | collective-permute-start | bytes 49160 | tf_op jit(solution)/shard_map/ppermute | solution.py:694
  70.5 2.0 %collective-permute-done.11.rest_1_ = f32[32,128]{1,0:T(8,128)S(1)} collective-permute-done((f32[32,128]{1,0:T(8,128)S(1)}, f32[32,128]{1,0:T(8,128)S(1)}, u32[]{:S(2)}, u32[]{:S(2)}) %collective-permute-start.11) | collective-permute-done | bytes 16416 | tf_op jit(solution)/shard_map/ppermute | solution.py:694
  72.5 3.6 %collective-permute-done.12.rest_2_ = f32[32,128]{1,0:T(8,128)S(1)} collective-permute-done((f32[32,128]{1,0:T(8,128)S(1)}, f32[32,128]{1,0:T(8,128)S(1)}, u32[]{:S(2)}, u32[]{:S(2)}) %collective-permute-start.12) | collective-permute-done | bytes 16416 | tf_op jit(solution)/shard_map/ppermute | solution.py:694
  76.2 0.0 collective-permute-done.13.rest_3_
  76.2 0.1 collective-permute-start.14
  76.3 1.2 %collective-permute-done.14.rest_1_ = f32[64,128]{1,0:T(8,128)S(1)} collective-permute-done((f32[64,128]{1,0:T(8,128)S(1)}, f32[64,128]{1,0:T(8,128)S(1)}, u32[]{:S(2)}, u32[]{:S(2)}) %collective-permute-start.14) | collective-permute-done | bytes 32800 | tf_op jit(solution)/shard_map/ppermute | solution.py:694
  77.5 0.7 shard_map.158
  78.1 0.2 collective-permute-start.15
  78.4 1.0 %collective-permute-done.15.rest_1_ = f32[32,128]{1,0:T(8,128)S(1)} collective-permute-done((f32[32,128]{1,0:T(8,128)S(1)}, f32[32,128]{1,0:T(8,128)S(1)}, u32[]{:S(2)}, u32[]{:S(2)}) %collective-permute-start.15) | collective-permute-done | bytes 16416 | tf_op jit(solution)/shard_map/ppermute | solution.py:694
  79.4 1.5 %collective-permute-start.16 = (f32[16,128]{1,0:T(8,128)S(1)}, f32[16,128]{1,0:T(8,128)S(1)}, u32[]{:S(2)}, u32[]{:S(2)}) collective-permute-start(f32[16,128]{1,0:T(8,128)S(1)} %get-tuple-element.81), channel_id=1, source_target_pairs={{0,1},{1,0},{2,3},{3,2},{4,5},{5,4},{6,7},{7,6},{8,9},{9,8},{10,11... | collective-permute-start | bytes 24584 | tf_op jit(solution)/shard_map/ppermute | solution.py:694
  81.0 1.5 %collective-permute-start.17 = (f32[16,128]{1,0:T(8,128)S(1)}, f32[16,128]{1,0:T(8,128)S(1)}, u32[]{:S(2)}, u32[]{:S(2)}) collective-permute-start(f32[16,128]{1,0:T(8,128)S(1)} %get-tuple-element.82), channel_id=1, source_target_pairs={{0,2},{1,3},{2,0},{3,1},{4,6},{5,7},{6,4},{7,5},{8,10},{9,11},{10,... | collective-permute-start | bytes 24584 | tf_op jit(solution)/shard_map/ppermute | solution.py:694
  82.4 0.6 collective-permute-start.18
  83.0 0.2 collective-permute-done.16.rest_1_
  83.1 1.5 %collective-permute-done.17.rest_2_ = f32[16,128]{1,0:T(8,128)S(1)} collective-permute-done((f32[16,128]{1,0:T(8,128)S(1)}, f32[16,128]{1,0:T(8,128)S(1)}, u32[]{:S(2)}, u32[]{:S(2)}) %collective-permute-start.17) | collective-permute-done | bytes 8224 | tf_op jit(solution)/shard_map/ppermute | solution.py:694
  84.6 2.4 %collective-permute-done.18.rest_3_ = f32[16,128]{1,0:T(8,128)S(1)} collective-permute-done((f32[16,128]{1,0:T(8,128)S(1)}, f32[16,128]{1,0:T(8,128)S(1)}, u32[]{:S(2)}, u32[]{:S(2)}) %collective-permute-start.18) | collective-permute-done | bytes 8224 | tf_op jit(solution)/shard_map/ppermute | solution.py:694
  87.0 0.8 collective-permute-start.19
  87.8 1.5 %collective-permute-start.20 = (f32[16,128]{1,0:T(8,128)S(1)}, f32[16,128]{1,0:T(8,128)S(1)}, u32[]{:S(2)}, u32[]{:S(2)}) collective-permute-start(f32[16,128]{1,0:T(8,128)S(1)} %get-tuple-element.86), channel_id=1, source_target_pairs={{0,8},{1,9},{2,10},{3,11},{4,12},{5,13},{6,14},{7,15},{8,0},{9,1},... | collective-permute-start | bytes 24584 | tf_op jit(solution)/shard_map/ppermute | solution.py:694
  89.3 1.6 %collective-permute-start.21 = (f32[16,128]{1,0:T(8,128)S(1)}, f32[16,128]{1,0:T(8,128)S(1)}, u32[]{:S(2)}, u32[]{:S(2)}) collective-permute-start(f32[16,128]{1,0:T(8,128)S(1)} %get-tuple-element.87), channel_id=1, source_target_pairs={{0,12},{1,13},{2,14},{3,15},{4,0},{5,1},{6,2},{7,3},{8,4},{9,5},{1... | collective-permute-start | bytes 24584 | tf_op jit(solution)/shard_map/ppermute | solution.py:694
  90.9 1.6 %collective-permute-done.19.rest_1_ = f32[16,128]{1,0:T(8,128)S(1)} collective-permute-done((f32[16,128]{1,0:T(8,128)S(1)}, f32[16,128]{1,0:T(8,128)S(1)}, u32[]{:S(2)}, u32[]{:S(2)}) %collective-permute-start.19) | collective-permute-done | bytes 8224 | tf_op jit(solution)/shard_map/ppermute | solution.py:694
  92.5 0.0 collective-permute-done.20.rest_2_
  92.5 0.6 collective-permute-done.21.rest_3_
  93.1 1.4 %shard_map.161 = f32[2,16384]{1,0:T(2,128)} custom-call(f32[128,256]{1,0:T(8,128)S(1)} %copy-done.2, f32[128,256]{1,0:T(8,128)S(1)} %copy-done.1, f32[32,512]{1,0:T(8,128)S(1)} %get-tuple-element.76.tables, f32[32,128]{1,0:T(8,128)S(1)} %get-tuple-element.77.factor, f32[16,128]{1,0:T(8,128)S(1)} %get-tuple-element.84.rest_0_, ...), custom_call_target="tpu_custom_call" | custom-call | flops 100000000 | bytes 1000000 | tf_op jit(solution)/shard_map/pallas_call | solution.py:622
  94.5 0.0 all-to-all-done.1.bulk
  94.5 1.5 %shard_map.154 = (f32[4,32,1024]{2,1,0:T(8,128)}, f32[4,32,1024]{2,1,0:T(8,128)}, f32[4,32,1024]{2,1,0:T(8,128)}) custom-call(bf16[16,24,1024]{2,1,0:T(8,128)(2,1)S(1)} %all-to-all-done.1.bulk, f32[8,128]{1,0:T(8,128)S(1)} %get-tuple-element.61.top), custom_call_target="tpu_custom_call" | custom-call | flops 7864320 | bytes 2359296 | tf_op jit(solution)/shard_map/pallas_call | solution.py:622
  (15 shorter events, 0.2 us)
Async XLA Ops:
  2.0 1.5 %collective-permute-start = (f32[3,4,2,1024]{3,2,1,0:T(2,128)S(1)}, f32[3,4,2,1024]{3,2,1,0:T(2,128)S(1)}, u32[]{:S(2)}, u32[]{:S(2)}) collective-permute-start(f32[3,4,2,1024]{3,2,1,0:T(2,128)S(1)} %get-tuple-element.47), channel_id=1, source_target_pairs={{0,16},{16,0},{1,17},{17,1},{2,18},{18,2},{3,19},{19,3},{4,20},{20... | collective-permute-start | bytes 294920 | tf_op jit(solution)/shard_map/ppermute | solution.py:668
  2.6 1.3 %collective-permute-start.1 = (f32[3,4,2,1024]{3,2,1,0:T(2,128)S(1)}, f32[3,4,2,1024]{3,2,1,0:T(2,128)S(1)}, u32[]{:S(2)}, u32[]{:S(2)}) collective-permute-start(f32[3,4,2,1024]{3,2,1,0:T(2,128)S(1)} %get-tuple-element.48), channel_id=1, source_target_pairs={{16,0},{0,16},{17,1},{1,17},{18,2},{2,18},{19,3},{3,19},{20,4},{4,... | collective-permute-start | bytes 294920 | tf_op jit(solution)/shard_map/ppermute | solution.py:669
  3.4 44.3 %copy-start.1 = (f32[128,256]{1,0:T(8,128)S(1)}, f32[128,256]{1,0:T(8,128)}, u32[]{:S(2)}) copy-start(f32[128,256]{1,0:T(8,128)} %constant.11.clone.twiddle) | copy-start | bytes 393220
  3.4 44.3 %copy-start.2 = (f32[128,256]{1,0:T(8,128)S(1)}, f32[128,256]{1,0:T(8,128)}, u32[]{:S(2)}) copy-start(f32[128,256]{1,0:T(8,128)} %constant.10.clone.circle) | copy-start | bytes 393220
  3.4 44.3 %copy-start.3 = (f32[32,256]{1,0:T(8,128)S(1)}, f32[32,256]{1,0:T(8,128)}, u32[]{:S(2)}) copy-start(f32[32,256]{1,0:T(8,128)} %constant.13.clone.steps) | copy-start | bytes 98308
  3.5 44.3 %copy-start.5 = (f32[32,128]{1,0:T(8,128)S(1)}, f32[32,128]{1,0:T(8,128)}, u32[]{:S(2)}) copy-start(f32[32,128]{1,0:T(8,128)} %constant.12.clone.short) | copy-start | bytes 49156
  3.5 44.3 %copy-start.6 = (s32[32]{0:T(128)S(1)}, s32[32]{0:T(128)}, u32[]{:S(2)}) copy-start(s32[32]{0:T(128)} %far_shift.3) | copy-start | bytes 388
  3.5 44.3 %copy-start.7 = (f32[32]{0:T(128)S(1)}, f32[32]{0:T(128)}, u32[]{:S(2)}) copy-start(f32[32]{0:T(128)} %far_remainder.3) | copy-start | bytes 388
  8.3 69.2 %copy-start = (bf16[64,64,64]{2,1,0:T(8,128)(2,1)S(1)}, bf16[64,64,64]{2,1,0:T(8,128)(2,1)}, u32[]{:S(2)}) copy-start(bf16[64,64,64]{2,1,0:T(8,128)(2,1)} %kernel.1) | copy-start | bytes 1572868
  8.3 69.1 %copy-start.4 = (f32[32,256]{1,0:T(8,128)S(1)}, f32[32,256]{1,0:T(8,128)}, u32[]{:S(2)}) copy-start(f32[32,256]{1,0:T(8,128)} %constant.14.clone.mixed) | copy-start | bytes 98308
  8.3 40.9 %all-to-all-start = ((bf16[16,192,128]{2,1,0:T(8,128)(2,1)}), bf16[16,192,128]{2,1,0:T(8,128)(2,1)S(1)}, u32[]{:S(2)}, u32[]{:S(2)}) async-start(bf16[16,192,128]{2,1,0:T(8,128)(2,1)} %get-tuple-element.49), calls=%async_computation | async-start | bytes 1572864 | tf_op jit(solution)/shard_map/all_to_all | solution.py:628
  16.5 18.8 %collective-permute-start.2 = (f32[72,128]{1,0:T(8,128)S(1)}, f32[72,128]{1,0:T(8,128)S(1)}, u32[]{:S(2)}, u32[]{:S(2)}) collective-permute-start(f32[72,128]{1,0:T(8,128)S(1)} %get-tuple-element.52), channel_id=1, source_target_pairs={{0,4},{1,5},{2,6},{3,7},{4,8},{5,9},{6,10},{7,11},{8,12},{9,13},{1... | collective-permute-start | bytes 110600 | tf_op jit(solution)/shard_map/ppermute | solution.py:694
  18.5 21.3 %collective-permute-start.3 = (f32[72,128]{1,0:T(8,128)S(1)}, f32[72,128]{1,0:T(8,128)S(1)}, u32[]{:S(2)}, u32[]{:S(2)}) collective-permute-start(f32[72,128]{1,0:T(8,128)S(1)} %get-tuple-element.53), channel_id=1, source_target_pairs={{0,8},{1,9},{2,10},{3,11},{4,12},{5,13},{6,14},{7,15},{8,0},{9,1},... | collective-permute-start | bytes 110600 | tf_op jit(solution)/shard_map/ppermute | solution.py:694
  20.9 18.9 %collective-permute-start.4 = (f32[72,128]{1,0:T(8,128)S(1)}, f32[72,128]{1,0:T(8,128)S(1)}, u32[]{:S(2)}, u32[]{:S(2)}) collective-permute-start(f32[72,128]{1,0:T(8,128)S(1)} %get-tuple-element.54), channel_id=1, source_target_pairs={{0,12},{1,13},{2,14},{3,15},{4,0},{5,1},{6,2},{7,3},{8,4},{9,5},{1... | collective-permute-start | bytes 110600 | tf_op jit(solution)/shard_map/ppermute | solution.py:694
  39.9 4.3 %collective-permute-start.5 = (f32[72,128]{1,0:T(8,128)S(1)}, f32[72,128]{1,0:T(8,128)S(1)}, u32[]{:S(2)}, u32[]{:S(2)}) collective-permute-start(f32[72,128]{1,0:T(8,128)S(1)} %get-tuple-element.56), channel_id=1, source_target_pairs={{0,1},{1,0},{2,3},{3,2},{4,5},{5,4},{6,7},{7,6},{8,9},{9,8},{10,11... | collective-permute-start | bytes 110600 | tf_op jit(solution)/shard_map/ppermute | solution.py:694
  41.4 4.0 %collective-permute-start.6 = (f32[72,128]{1,0:T(8,128)S(1)}, f32[72,128]{1,0:T(8,128)S(1)}, u32[]{:S(2)}, u32[]{:S(2)}) collective-permute-start(f32[72,128]{1,0:T(8,128)S(1)} %get-tuple-element.57), channel_id=1, source_target_pairs={{0,2},{1,3},{2,0},{3,1},{4,6},{5,7},{6,4},{7,5},{8,10},{9,11},{10,... | collective-permute-start | bytes 110600 | tf_op jit(solution)/shard_map/ppermute | solution.py:694
  42.9 4.9 %collective-permute-start.7 = (f32[72,128]{1,0:T(8,128)S(1)}, f32[72,128]{1,0:T(8,128)S(1)}, u32[]{:S(2)}, u32[]{:S(2)}) collective-permute-start(f32[72,128]{1,0:T(8,128)S(1)} %get-tuple-element.58), channel_id=1, source_target_pairs={{0,3},{1,2},{2,1},{3,0},{4,7},{5,6},{6,5},{7,4},{8,11},{9,10},{10,... | collective-permute-start | bytes 110600 | tf_op jit(solution)/shard_map/ppermute | solution.py:694
  53.3 41.1 %all-to-all-start.1 = ((bf16[16,24,1024]{2,1,0:T(8,128)(2,1)}), bf16[16,24,1024]{2,1,0:T(8,128)(2,1)S(1)}, u32[]{:S(2)}, u32[]{:S(2)}) async-start(bf16[16,24,1024]{2,1,0:T(8,128)(2,1)} %get-tuple-element.60), calls=%async_computation.1 | async-start | bytes 1572864 | tf_op jit(solution)/shard_map/all_to_all | solution.py:628
  57.0 5.5 %collective-permute-start.8 = (f32[32,128]{1,0:T(8,128)S(1)}, f32[32,128]{1,0:T(8,128)S(1)}, u32[]{:S(2)}, u32[]{:S(2)}) collective-permute-start(f32[32,128]{1,0:T(8,128)S(1)} %get-tuple-element.67), channel_id=1, source_target_pairs={{0,1},{1,0},{2,3},{3,2},{4,5},{5,4},{6,7},{7,6},{8,9},{9,8},{10,11... | collective-permute-start | bytes 49160 | tf_op jit(solution)/shard_map/ppermute | solution.py:694
  58.9 4.5 %collective-permute-start.9 = (f32[32,128]{1,0:T(8,128)S(1)}, f32[32,128]{1,0:T(8,128)S(1)}, u32[]{:S(2)}, u32[]{:S(2)}) collective-permute-start(f32[32,128]{1,0:T(8,128)S(1)} %get-tuple-element.68), channel_id=1, source_target_pairs={{0,2},{1,3},{2,0},{3,1},{4,6},{5,7},{6,4},{7,5},{8,10},{9,11},{10,... | collective-permute-start | bytes 49160 | tf_op jit(solution)/shard_map/ppermute | solution.py:694
  60.3 4.7 %collective-permute-start.10 = (f32[32,128]{1,0:T(8,128)S(1)}, f32[32,128]{1,0:T(8,128)S(1)}, u32[]{:S(2)}, u32[]{:S(2)}) collective-permute-start(f32[32,128]{1,0:T(8,128)S(1)} %get-tuple-element.69), channel_id=1, source_target_pairs={{0,3},{1,2},{2,1},{3,0},{4,7},{5,6},{6,5},{7,4},{8,11},{9,10},{10,... | collective-permute-start | bytes 49160 | tf_op jit(solution)/shard_map/ppermute | solution.py:694
  65.1 7.4 %collective-permute-start.11 = (f32[32,128]{1,0:T(8,128)S(1)}, f32[32,128]{1,0:T(8,128)S(1)}, u32[]{:S(2)}, u32[]{:S(2)}) collective-permute-start(f32[32,128]{1,0:T(8,128)S(1)} %get-tuple-element.71), channel_id=1, source_target_pairs={{0,4},{1,5},{2,6},{3,7},{4,8},{5,9},{6,10},{7,11},{8,12},{9,13},{1... | collective-permute-start | bytes 49160 | tf_op jit(solution)/shard_map/ppermute | solution.py:694
  66.7 9.4 %collective-permute-start.12 = (f32[32,128]{1,0:T(8,128)S(1)}, f32[32,128]{1,0:T(8,128)S(1)}, u32[]{:S(2)}, u32[]{:S(2)}) collective-permute-start(f32[32,128]{1,0:T(8,128)S(1)} %get-tuple-element.72), channel_id=1, source_target_pairs={{0,8},{1,9},{2,10},{3,11},{4,12},{5,13},{6,14},{7,15},{8,0},{9,1},... | collective-permute-start | bytes 49160 | tf_op jit(solution)/shard_map/ppermute | solution.py:694
  69.1 7.0 %collective-permute-start.13 = (f32[32,128]{1,0:T(8,128)S(1)}, f32[32,128]{1,0:T(8,128)S(1)}, u32[]{:S(2)}, u32[]{:S(2)}) collective-permute-start(f32[32,128]{1,0:T(8,128)S(1)} %get-tuple-element.73), channel_id=1, source_target_pairs={{0,12},{1,13},{2,14},{3,15},{4,0},{5,1},{6,2},{7,3},{8,4},{9,5},{1... | collective-permute-start | bytes 49160 | tf_op jit(solution)/shard_map/ppermute | solution.py:694
  76.2 1.3 %collective-permute-start.14 = (f32[64,128]{1,0:T(8,128)S(1)}, f32[64,128]{1,0:T(8,128)S(1)}, u32[]{:S(2)}, u32[]{:S(2)}) collective-permute-start(f32[64,128]{1,0:T(8,128)S(1)} %get-tuple-element.75), channel_id=1, source_target_pairs={{0,16},{16,0},{1,17},{17,1},{2,18},{18,2},{3,19},{19,3},{4,20},{20... | collective-permute-start | bytes 98312 | tf_op jit(solution)/shard_map/ppermute | solution.py:694
  78.1 1.2 %collective-permute-start.15 = (f32[32,128]{1,0:T(8,128)S(1)}, f32[32,128]{1,0:T(8,128)S(1)}, u32[]{:S(2)}, u32[]{:S(2)}) collective-permute-start(f32[32,128]{1,0:T(8,128)S(1)} %get-tuple-element.79), channel_id=1, source_target_pairs={{0,16},{16,0},{1,17},{17,1},{2,18},{18,2},{3,19},{19,3},{4,20},{20... | collective-permute-start | bytes 49160 | tf_op jit(solution)/shard_map/ppermute | solution.py:694
  79.4 3.7 %collective-permute-start.16 = (f32[16,128]{1,0:T(8,128)S(1)}, f32[16,128]{1,0:T(8,128)S(1)}, u32[]{:S(2)}, u32[]{:S(2)}) collective-permute-start(f32[16,128]{1,0:T(8,128)S(1)} %get-tuple-element.81), channel_id=1, source_target_pairs={{0,1},{1,0},{2,3},{3,2},{4,5},{5,4},{6,7},{7,6},{8,9},{9,8},{10,11... | collective-permute-start | bytes 24584 | tf_op jit(solution)/shard_map/ppermute | solution.py:694
  81.0 3.7 %collective-permute-start.17 = (f32[16,128]{1,0:T(8,128)S(1)}, f32[16,128]{1,0:T(8,128)S(1)}, u32[]{:S(2)}, u32[]{:S(2)}) collective-permute-start(f32[16,128]{1,0:T(8,128)S(1)} %get-tuple-element.82), channel_id=1, source_target_pairs={{0,2},{1,3},{2,0},{3,1},{4,6},{5,7},{6,4},{7,5},{8,10},{9,11},{10,... | collective-permute-start | bytes 24584 | tf_op jit(solution)/shard_map/ppermute | solution.py:694
  82.4 4.5 %collective-permute-start.18 = (f32[16,128]{1,0:T(8,128)S(1)}, f32[16,128]{1,0:T(8,128)S(1)}, u32[]{:S(2)}, u32[]{:S(2)}) collective-permute-start(f32[16,128]{1,0:T(8,128)S(1)} %get-tuple-element.83), channel_id=1, source_target_pairs={{0,3},{1,2},{2,1},{3,0},{4,7},{5,6},{6,5},{7,4},{8,11},{9,10},{10,... | collective-permute-start | bytes 24584 | tf_op jit(solution)/shard_map/ppermute | solution.py:694
  87.0 5.5 %collective-permute-start.19 = (f32[16,128]{1,0:T(8,128)S(1)}, f32[16,128]{1,0:T(8,128)S(1)}, u32[]{:S(2)}, u32[]{:S(2)}) collective-permute-start(f32[16,128]{1,0:T(8,128)S(1)} %get-tuple-element.85), channel_id=1, source_target_pairs={{0,4},{1,5},{2,6},{3,7},{4,8},{5,9},{6,10},{7,11},{8,12},{9,13},{1... | collective-permute-start | bytes 24584 | tf_op jit(solution)/shard_map/ppermute | solution.py:694
  87.8 4.7 %collective-permute-start.20 = (f32[16,128]{1,0:T(8,128)S(1)}, f32[16,128]{1,0:T(8,128)S(1)}, u32[]{:S(2)}, u32[]{:S(2)}) collective-permute-start(f32[16,128]{1,0:T(8,128)S(1)} %get-tuple-element.86), channel_id=1, source_target_pairs={{0,8},{1,9},{2,10},{3,11},{4,12},{5,13},{6,14},{7,15},{8,0},{9,1},... | collective-permute-start | bytes 24584 | tf_op jit(solution)/shard_map/ppermute | solution.py:694
  89.3 3.8 %collective-permute-start.21 = (f32[16,128]{1,0:T(8,128)S(1)}, f32[16,128]{1,0:T(8,128)S(1)}, u32[]{:S(2)}, u32[]{:S(2)}) collective-permute-start(f32[16,128]{1,0:T(8,128)S(1)} %get-tuple-element.87), channel_id=1, source_target_pairs={{0,12},{1,13},{2,14},{3,15},{4,0},{5,1},{6,2},{7,3},{8,4},{9,5},{1... | collective-permute-start | bytes 24584 | tf_op jit(solution)/shard_map/ppermute | solution.py:694

commit v11 on v10

--- a/solution.py
+++ b/solution.py
@@ -123,7 +123,7 @@
         store_section(field, stage, slab, tile)
         return carry
 
-    lax.fori_loop(1, slab // SUB - 1, section, 0)
+    lax.fori_loop(1, slab // SUB - 1, section, 0, unroll=True)
 
 
 def hydro_kernel(
@@ -148,7 +148,7 @@
         store_section(field, stage, slab, lax.rem(index + last - 1, last + 1))
         return carry
 
-    lax.fori_loop(0, 3, section, 0)
+    lax.fori_loop(0, 3, section, 0, unroll=True)
 
     @pl.when(rad == 0)
     def _():
@@ -171,7 +171,7 @@
                 largest = jnp.maximum(largest, jnp.abs(value))
         return largest
 
-    largest = lax.fori_loop(0, last, second_section, jnp.zeros((SUB, width), F32))
+    largest = lax.fori_loop(0, last, second_section, jnp.zeros((SUB, width), F32), unroll=2)
     peak = jnp.maximum(jnp.max(largest, keepdims=True), 1e-30)
     scale = TOP / peak
     dests = SUB // per
@@ -216,7 +216,7 @@
         send(tile).start()
         return carry
 
-    lax.fori_loop(0, last, pack, 0)
+    lax.fori_loop(0, last, pack, 0, unroll=True)
     for index in range(last):
         send(index).wait()
 

time: 96.3 us -> 96 us (level)
  no operation moved by 1% of the time
where the time goes in v11:
time: 96 us; the launch traced here: 95.7 us
  waiting for transfers between devices  40.9 us (43%)
  starting transfers between devices  38.5 us (40%)
  Pallas kernels  15.5 us (16%)
    ppermute x20, waiting for transfers between devices, hop(): moved.append(lax.ppermute(buffers[o], axis, pairs))  40.3 us
    ppermute x20, starting transfers between devices, hop(): moved.append(lax.ppermute(buffers[o], axis, pairs))  26 us
    pallas_call x15, Pallas kernels, run(): return kernel(*near)  15.5 us
    all_to_all x2, starting transfers between devices, exchange(): return lax.all_to_all(array, axes, 0, 0, tiled=True)  11.8 us
  transfers between devices with their start and end apart: 24, of which 19 were waited for; matrix products, arithmetic and copies ran while one was open for 0% of the time, Pallas kernels for 5%

profile of v11, /device:TPU:0, one launch (start us, length us, event | category | flops | bytes accessed | tf_op | source)
XLA Modules:
  0.0 95.7 jit_solution(18001709161755131248)
XLA Ops:
  0.6 1.4 %shard_map.147 = (f32[3,4,40,1152]{3,2,1,0:T(8,128)S(1)}, f32[3,4,2,1024]{3,2,1,0:T(2,128)S(1)}, f32[3,4,2,1024]{3,2,1,0:T(2,128)S(1)}) custom-call(f32[4,32,1024]{2,1,0:T(8,128)} %rho.1, f32[4,32,1024]{2,1,0:T(8,128)} %ur.1, f32[4,32,1024]{2,1,0:T(8,128)} %up.1), custom_call_target="tpu_custom_call" | custom-call | bytes 1572864 | tf_op jit(solution)/shard_map/pallas_call | solution.py:622
  2.0 0.6 collective-permute-start
  2.6 0.1 collective-permute-start.1
  2.7 0.6 shard_map.148.stage_in
  3.3 0.0 copy-start.1
  3.3 0.0 copy-start.2
  3.3 0.0 copy-start.3
  3.4 0.0 copy-start.5
  3.4 0.0 copy-start.6
  3.4 0.0 copy-start.7
  3.4 0.2 collective-permute-done.low
  3.5 0.4 collective-permute-done.1.high
  3.9 4.1 %shard_map.149 = (bf16[16,192,128]{2,1,0:T(8,128)(2,1)}, f32[16,24,128]{2,1,0:T(8,128)S(1)}, f32[3,4,40,1152]{3,2,1,0:T(8,128)S(1)}, f32[3,4,40,1152]{3,2,1,0:T(8,128)S(1)}) custom-call(f32[3,4,40,1152]{3,2,1,0:T(8,128)S(1)} %get-tuple-element.46.field.field_in, ...), custom_call_target="tpu_custom_call", output_to_operand_aliasing={{2}: (0, {}), {3}: (1, {})} | custom-call | flops 39321600 | bytes 3145728 | tf_op jit(solution)/shard_map/pallas_call | solution.py:622
  8.0 0.0 copy-start
  8.0 0.0 copy-start.4
  8.0 8.1 %all-to-all-start = ((bf16[16,192,128]{2,1,0:T(8,128)(2,1)}), bf16[16,192,128]{2,1,0:T(8,128)(2,1)S(1)}, u32[]{:S(2)}, u32[]{:S(2)}) async-start(bf16[16,192,128]{2,1,0:T(8,128)(2,1)} %get-tuple-element.49), calls=%async_computation | async-start | bytes 1572864 | tf_op jit(solution)/shard_map/all_to_all | solution.py:628
  16.2 2.0 %collective-permute-start.2 = (f32[72,128]{1,0:T(8,128)S(1)}, f32[72,128]{1,0:T(8,128)S(1)}, u32[]{:S(2)}, u32[]{:S(2)}) collective-permute-start(f32[72,128]{1,0:T(8,128)S(1)} %get-tuple-element.52), channel_id=1, source_target_pairs={{0,4},{1,5},{2,6},{3,7},{4,8},{5,9},{6,10},{7,11},{8,12},{9,13},{1... | collective-permute-start | bytes 110600 | tf_op jit(solution)/shard_map/ppermute | solution.py:694
  18.2 2.4 %collective-permute-start.3 = (f32[72,128]{1,0:T(8,128)S(1)}, f32[72,128]{1,0:T(8,128)S(1)}, u32[]{:S(2)}, u32[]{:S(2)}) collective-permute-start(f32[72,128]{1,0:T(8,128)S(1)} %get-tuple-element.53), channel_id=1, source_target_pairs={{0,8},{1,9},{2,10},{3,11},{4,12},{5,13},{6,14},{7,15},{8,0},{9,1},... | collective-permute-start | bytes 110600 | tf_op jit(solution)/shard_map/ppermute | solution.py:694
  20.6 1.5 %collective-permute-start.4 = (f32[72,128]{1,0:T(8,128)S(1)}, f32[72,128]{1,0:T(8,128)S(1)}, u32[]{:S(2)}, u32[]{:S(2)}) collective-permute-start(f32[72,128]{1,0:T(8,128)S(1)} %get-tuple-element.54), channel_id=1, source_target_pairs={{0,12},{1,13},{2,14},{3,15},{4,0},{5,1},{6,2},{7,3},{8,4},{9,5},{1... | collective-permute-start | bytes 110600 | tf_op jit(solution)/shard_map/ppermute | solution.py:694
  22.0 13.0 %collective-permute-done.2.rest_1_ = f32[72,128]{1,0:T(8,128)S(1)} collective-permute-done((f32[72,128]{1,0:T(8,128)S(1)}, f32[72,128]{1,0:T(8,128)S(1)}, u32[]{:S(2)}, u32[]{:S(2)}) %collective-permute-start.2) | collective-permute-done | bytes 36896 | tf_op jit(solution)/shard_map/ppermute | solution.py:694
  35.1 4.4 %collective-permute-done.3.rest_2_ = f32[72,128]{1,0:T(8,128)S(1)} collective-permute-done((f32[72,128]{1,0:T(8,128)S(1)}, f32[72,128]{1,0:T(8,128)S(1)}, u32[]{:S(2)}, u32[]{:S(2)}) %collective-permute-start.3) | collective-permute-done | bytes 36896 | tf_op jit(solution)/shard_map/ppermute | solution.py:694
  39.5 0.0 collective-permute-done.4.rest_3_
  39.6 1.5 %collective-permute-start.5 = (f32[72,128]{1,0:T(8,128)S(1)}, f32[72,128]{1,0:T(8,128)S(1)}, u32[]{:S(2)}, u32[]{:S(2)}) collective-permute-start(f32[72,128]{1,0:T(8,128)S(1)} %get-tuple-element.56), channel_id=1, source_target_pairs={{0,1},{1,0},{2,3},{3,2},{4,5},{5,4},{6,7},{7,6},{8,9},{9,8},{10,11... | collective-permute-start | bytes 110600 | tf_op jit(solution)/shard_map/ppermute | solution.py:694
  41.1 1.5 %collective-permute-start.6 = (f32[72,128]{1,0:T(8,128)S(1)}, f32[72,128]{1,0:T(8,128)S(1)}, u32[]{:S(2)}, u32[]{:S(2)}) collective-permute-start(f32[72,128]{1,0:T(8,128)S(1)} %get-tuple-element.57), channel_id=1, source_target_pairs={{0,2},{1,3},{2,0},{3,1},{4,6},{5,7},{6,4},{7,5},{8,10},{9,11},{10,... | collective-permute-start | bytes 110600 | tf_op jit(solution)/shard_map/ppermute | solution.py:694
  42.6 0.6 collective-permute-start.7
  43.1 0.8 collective-permute-done.5.rest_1_
  43.9 1.2 %collective-permute-done.6.rest_2_ = f32[72,128]{1,0:T(8,128)S(1)} collective-permute-done((f32[72,128]{1,0:T(8,128)S(1)}, f32[72,128]{1,0:T(8,128)S(1)}, u32[]{:S(2)}, u32[]{:S(2)}) %collective-permute-start.6) | collective-permute-done | bytes 36896 | tf_op jit(solution)/shard_map/ppermute | solution.py:694
  45.1 2.3 %collective-permute-done.7.rest_3_ = f32[72,128]{1,0:T(8,128)S(1)} collective-permute-done((f32[72,128]{1,0:T(8,128)S(1)}, f32[72,128]{1,0:T(8,128)S(1)}, u32[]{:S(2)}, u32[]{:S(2)}) %collective-permute-start.7) | collective-permute-done | bytes 36896 | tf_op jit(solution)/shard_map/ppermute | solution.py:694
  47.5 1.5 %shard_map.152 = (f32[128,128]{1,0:T(8,128)S(1)}, f32[16,24,128]{2,1,0:T(8,128)S(1)}) custom-call(s32[32]{0:T(128)S(1)} %copy-done.6, f32[32]{0:T(128)S(1)} %copy-done.7, f32[128,256]{1,0:T(8,128)S(1)} %copy-done.2, f32[128,256]{1,0:T(8,128)S(1)} %copy-done.1, f32[32,128]{1,0:T(8,128)S(1)} %copy-done.5, f32[32,256]{1,0:T(8,128)S(1)} %copy-done.3, ...), custom_call_target="tpu_custom_call" | custom-call | flops 100000000 | bytes 1000000 | tf_op jit(solution)/shard_map/pallas_call | solution.py:622
  49.0 0.0 all-to-all-done.bulk
  49.0 4.1 %shard_map.153 = (bf16[16,24,1024]{2,1,0:T(8,128)(2,1)}, f32[8,128]{1,0:T(8,128)S(1)}) custom-call(s32[32]{0:T(128)S(1)} %copy-done.6, f32[32]{0:T(128)S(1)} %copy-done.7, bf16[16,192,128]{2,1,0:T(8,128)(2,1)S(1)} %all-to-all-done.bulk, f32[16,24,128]{2,1,0:T(8,128)S(1)} %get-tuple-element.59.sides), custom_call_target="tpu_custom_call" | custom-call | flops 19660800 | bytes 1572864 | tf_op jit(solution)/shard_map/pallas_call | solution.py:622
  53.0 3.6 %all-to-all-start.1 = ((bf16[16,24,1024]{2,1,0:T(8,128)(2,1)}), bf16[16,24,1024]{2,1,0:T(8,128)(2,1)S(1)}, u32[]{:S(2)}, u32[]{:S(2)}) async-start(bf16[16,24,1024]{2,1,0:T(8,128)(2,1)} %get-tuple-element.60), calls=%async_computation.1 | async-start | bytes 1572864 | tf_op jit(solution)/shard_map/all_to_all | solution.py:628
  56.7 1.9 %collective-permute-start.8 = (f32[32,128]{1,0:T(8,128)S(1)}, f32[32,128]{1,0:T(8,128)S(1)}, u32[]{:S(2)}, u32[]{:S(2)}) collective-permute-start(f32[32,128]{1,0:T(8,128)S(1)} %get-tuple-element.67), channel_id=1, source_target_pairs={{0,1},{1,0},{2,3},{3,2},{4,5},{5,4},{6,7},{7,6},{8,9},{9,8},{10,11... | collective-permute-start | bytes 49160 | tf_op jit(solution)/shard_map/ppermute | solution.py:694
  58.6 1.5 %collective-permute-start.9 = (f32[32,128]{1,0:T(8,128)S(1)}, f32[32,128]{1,0:T(8,128)S(1)}, u32[]{:S(2)}, u32[]{:S(2)}) collective-permute-start(f32[32,128]{1,0:T(8,128)S(1)} %get-tuple-element.68), channel_id=1, source_target_pairs={{0,2},{1,3},{2,0},{3,1},{4,6},{5,7},{6,4},{7,5},{8,10},{9,11},{10,... | collective-permute-start | bytes 49160 | tf_op jit(solution)/shard_map/ppermute | solution.py:694
  60.1 0.2 collective-permute-start.10
  60.3 2.0 %collective-permute-done.8.rest_1_ = f32[32,128]{1,0:T(8,128)S(1)} collective-permute-done((f32[32,128]{1,0:T(8,128)S(1)}, f32[32,128]{1,0:T(8,128)S(1)}, u32[]{:S(2)}, u32[]{:S(2)}) %collective-permute-start.8) | collective-permute-done | bytes 16416 | tf_op jit(solution)/shard_map/ppermute | solution.py:694
  62.2 0.8 collective-permute-done.9.rest_2_
  63.0 1.7 %collective-permute-done.10.rest_3_ = f32[32,128]{1,0:T(8,128)S(1)} collective-permute-done((f32[32,128]{1,0:T(8,128)S(1)}, f32[32,128]{1,0:T(8,128)S(1)}, u32[]{:S(2)}, u32[]{:S(2)}) %collective-permute-start.10) | collective-permute-done | bytes 16416 | tf_op jit(solution)/shard_map/ppermute | solution.py:694
  64.8 1.6 %collective-permute-start.11 = (f32[32,128]{1,0:T(8,128)S(1)}, f32[32,128]{1,0:T(8,128)S(1)}, u32[]{:S(2)}, u32[]{:S(2)}) collective-permute-start(f32[32,128]{1,0:T(8,128)S(1)} %get-tuple-element.71), channel_id=1, source_target_pairs={{0,4},{1,5},{2,6},{3,7},{4,8},{5,9},{6,10},{7,11},{8,12},{9,13},{1... | collective-permute-start | bytes 49160 | tf_op jit(solution)/shard_map/ppermute | solution.py:694
  66.4 2.4 %collective-permute-start.12 = (f32[32,128]{1,0:T(8,128)S(1)}, f32[32,128]{1,0:T(8,128)S(1)}, u32[]{:S(2)}, u32[]{:S(2)}) collective-permute-start(f32[32,128]{1,0:T(8,128)S(1)} %get-tuple-element.72), channel_id=1, source_target_pairs={{0,8},{1,9},{2,10},{3,11},{4,12},{5,13},{6,14},{7,15},{8,0},{9,1},... | collective-permute-start | bytes 49160 | tf_op jit(solution)/shard_map/ppermute | solution.py:694
  68.8 1.4 %collective-permute-start.13 = (f32[32,128]{1,0:T(8,128)S(1)}, f32[32,128]{1,0:T(8,128)S(1)}, u32[]{:S(2)}, u32[]{:S(2)}) collective-permute-start(f32[32,128]{1,0:T(8,128)S(1)} %get-tuple-element.73), channel_id=1, source_target_pairs={{0,12},{1,13},{2,14},{3,15},{4,0},{5,1},{6,2},{7,3},{8,4},{9,5},{1... | collective-permute-start | bytes 49160 | tf_op jit(solution)/shard_map/ppermute | solution.py:694
  70.2 2.0 %collective-permute-done.11.rest_1_ = f32[32,128]{1,0:T(8,128)S(1)} collective-permute-done((f32[32,128]{1,0:T(8,128)S(1)}, f32[32,128]{1,0:T(8,128)S(1)}, u32[]{:S(2)}, u32[]{:S(2)}) %collective-permute-start.11) | collective-permute-done | bytes 16416 | tf_op jit(solution)/shard_map/ppermute | solution.py:694
  72.2 3.6 %collective-permute-done.12.rest_2_ = f32[32,128]{1,0:T(8,128)S(1)} collective-permute-done((f32[32,128]{1,0:T(8,128)S(1)}, f32[32,128]{1,0:T(8,128)S(1)}, u32[]{:S(2)}, u32[]{:S(2)}) %collective-permute-start.12) | collective-permute-done | bytes 16416 | tf_op jit(solution)/shard_map/ppermute | solution.py:694
  75.9 0.0 collective-permute-done.13.rest_3_
  75.9 0.1 collective-permute-start.14
  76.0 1.2 %collective-permute-done.14.rest_1_ = f32[64,128]{1,0:T(8,128)S(1)} collective-permute-done((f32[64,128]{1,0:T(8,128)S(1)}, f32[64,128]{1,0:T(8,128)S(1)}, u32[]{:S(2)}, u32[]{:S(2)}) %collective-permute-start.14) | collective-permute-done | bytes 32800 | tf_op jit(solution)/shard_map/ppermute | solution.py:694
  77.2 0.7 shard_map.158
  77.8 0.2 collective-permute-start.15
  78.1 1.0 %collective-permute-done.15.rest_1_ = f32[32,128]{1,0:T(8,128)S(1)} collective-permute-done((f32[32,128]{1,0:T(8,128)S(1)}, f32[32,128]{1,0:T(8,128)S(1)}, u32[]{:S(2)}, u32[]{:S(2)}) %collective-permute-start.15) | collective-permute-done | bytes 16416 | tf_op jit(solution)/shard_map/ppermute | solution.py:694
  79.1 1.5 %collective-permute-start.16 = (f32[16,128]{1,0:T(8,128)S(1)}, f32[16,128]{1,0:T(8,128)S(1)}, u32[]{:S(2)}, u32[]{:S(2)}) collective-permute-start(f32[16,128]{1,0:T(8,128)S(1)} %get-tuple-element.81), channel_id=1, source_target_pairs={{0,1},{1,0},{2,3},{3,2},{4,5},{5,4},{6,7},{7,6},{8,9},{9,8},{10,11... | collective-permute-start | bytes 24584 | tf_op jit(solution)/shard_map/ppermute | solution.py:694
  80.7 1.5 %collective-permute-start.17 = (f32[16,128]{1,0:T(8,128)S(1)}, f32[16,128]{1,0:T(8,128)S(1)}, u32[]{:S(2)}, u32[]{:S(2)}) collective-permute-start(f32[16,128]{1,0:T(8,128)S(1)} %get-tuple-element.82), channel_id=1, source_target_pairs={{0,2},{1,3},{2,0},{3,1},{4,6},{5,7},{6,4},{7,5},{8,10},{9,11},{10,... | collective-permute-start | bytes 24584 | tf_op jit(solution)/shard_map/ppermute | solution.py:694
  82.1 0.6 collective-permute-start.18
  82.7 0.2 collective-permute-done.16.rest_1_
  82.8 1.5 %collective-permute-done.17.rest_2_ = f32[16,128]{1,0:T(8,128)S(1)} collective-permute-done((f32[16,128]{1,0:T(8,128)S(1)}, f32[16,128]{1,0:T(8,128)S(1)}, u32[]{:S(2)}, u32[]{:S(2)}) %collective-permute-start.17) | collective-permute-done | bytes 8224 | tf_op jit(solution)/shard_map/ppermute | solution.py:694
  84.3 2.4 %collective-permute-done.18.rest_3_ = f32[16,128]{1,0:T(8,128)S(1)} collective-permute-done((f32[16,128]{1,0:T(8,128)S(1)}, f32[16,128]{1,0:T(8,128)S(1)}, u32[]{:S(2)}, u32[]{:S(2)}) %collective-permute-start.18) | collective-permute-done | bytes 8224 | tf_op jit(solution)/shard_map/ppermute | solution.py:694
  86.7 0.8 collective-permute-start.19
  87.5 1.5 %collective-permute-start.20 = (f32[16,128]{1,0:T(8,128)S(1)}, f32[16,128]{1,0:T(8,128)S(1)}, u32[]{:S(2)}, u32[]{:S(2)}) collective-permute-start(f32[16,128]{1,0:T(8,128)S(1)} %get-tuple-element.86), channel_id=1, source_target_pairs={{0,8},{1,9},{2,10},{3,11},{4,12},{5,13},{6,14},{7,15},{8,0},{9,1},... | collective-permute-start | bytes 24584 | tf_op jit(solution)/shard_map/ppermute | solution.py:694
  89.0 1.6 %collective-permute-start.21 = (f32[16,128]{1,0:T(8,128)S(1)}, f32[16,128]{1,0:T(8,128)S(1)}, u32[]{:S(2)}, u32[]{:S(2)}) collective-permute-start(f32[16,128]{1,0:T(8,128)S(1)} %get-tuple-element.87), channel_id=1, source_target_pairs={{0,12},{1,13},{2,14},{3,15},{4,0},{5,1},{6,2},{7,3},{8,4},{9,5},{1... | collective-permute-start | bytes 24584 | tf_op jit(solution)/shard_map/ppermute | solution.py:694
  90.6 1.6 %collective-permute-done.19.rest_1_ = f32[16,128]{1,0:T(8,128)S(1)} collective-permute-done((f32[16,128]{1,0:T(8,128)S(1)}, f32[16,128]{1,0:T(8,128)S(1)}, u32[]{:S(2)}, u32[]{:S(2)}) %collective-permute-start.19) | collective-permute-done | bytes 8224 | tf_op jit(solution)/shard_map/ppermute | solution.py:694
  92.2 0.0 collective-permute-done.20.rest_2_
  92.2 0.6 collective-permute-done.21.rest_3_
  92.8 1.4 %shard_map.161 = f32[2,16384]{1,0:T(2,128)} custom-call(f32[128,256]{1,0:T(8,128)S(1)} %copy-done.2, f32[128,256]{1,0:T(8,128)S(1)} %copy-done.1, f32[32,512]{1,0:T(8,128)S(1)} %get-tuple-element.76.tables, f32[32,128]{1,0:T(8,128)S(1)} %get-tuple-element.77.factor, f32[16,128]{1,0:T(8,128)S(1)} %get-tuple-element.84.rest_0_, ...), custom_call_target="tpu_custom_call" | custom-call | flops 100000000 | bytes 1000000 | tf_op jit(solution)/shard_map/pallas_call | solution.py:622
  94.2 0.0 all-to-all-done.1.bulk
  94.2 1.5 %shard_map.154 = (f32[4,32,1024]{2,1,0:T(8,128)}, f32[4,32,1024]{2,1,0:T(8,128)}, f32[4,32,1024]{2,1,0:T(8,128)}) custom-call(bf16[16,24,1024]{2,1,0:T(8,128)(2,1)S(1)} %all-to-all-done.1.bulk, f32[8,128]{1,0:T(8,128)S(1)} %get-tuple-element.61.top), custom_call_target="tpu_custom_call" | custom-call | flops 7864320 | bytes 2359296 | tf_op jit(solution)/shard_map/pallas_call | solution.py:622
  (15 shorter events, 0.2 us)
Async XLA Ops:
  2.0 1.5 %collective-permute-start = (f32[3,4,2,1024]{3,2,1,0:T(2,128)S(1)}, f32[3,4,2,1024]{3,2,1,0:T(2,128)S(1)}, u32[]{:S(2)}, u32[]{:S(2)}) collective-permute-start(f32[3,4,2,1024]{3,2,1,0:T(2,128)S(1)} %get-tuple-element.47), channel_id=1, source_target_pairs={{0,16},{16,0},{1,17},{17,1},{2,18},{18,2},{3,19},{19,3},{4,20},{20... | collective-permute-start | bytes 294920 | tf_op jit(solution)/shard_map/ppermute | solution.py:668
  2.6 1.3 %collective-permute-start.1 = (f32[3,4,2,1024]{3,2,1,0:T(2,128)S(1)}, f32[3,4,2,1024]{3,2,1,0:T(2,128)S(1)}, u32[]{:S(2)}, u32[]{:S(2)}) collective-permute-start(f32[3,4,2,1024]{3,2,1,0:T(2,128)S(1)} %get-tuple-element.48), channel_id=1, source_target_pairs={{16,0},{0,16},{17,1},{1,17},{18,2},{2,18},{19,3},{3,19},{20,4},{4,... | collective-permute-start | bytes 294920 | tf_op jit(solution)/shard_map/ppermute | solution.py:669
  3.3 44.1 %copy-start.1 = (f32[128,256]{1,0:T(8,128)S(1)}, f32[128,256]{1,0:T(8,128)}, u32[]{:S(2)}) copy-start(f32[128,256]{1,0:T(8,128)} %constant.11.clone.twiddle) | copy-start | bytes 393220
  3.3 44.1 %copy-start.2 = (f32[128,256]{1,0:T(8,128)S(1)}, f32[128,256]{1,0:T(8,128)}, u32[]{:S(2)}) copy-start(f32[128,256]{1,0:T(8,128)} %constant.10.clone.circle) | copy-start | bytes 393220
  3.3 44.1 %copy-start.3 = (f32[32,256]{1,0:T(8,128)S(1)}, f32[32,256]{1,0:T(8,128)}, u32[]{:S(2)}) copy-start(f32[32,256]{1,0:T(8,128)} %constant.13.clone.steps) | copy-start | bytes 98308
  3.4 44.1 %copy-start.5 = (f32[32,128]{1,0:T(8,128)S(1)}, f32[32,128]{1,0:T(8,128)}, u32[]{:S(2)}) copy-start(f32[32,128]{1,0:T(8,128)} %constant.12.clone.short) | copy-start | bytes 49156
  3.4 44.1 %copy-start.6 = (s32[32]{0:T(128)S(1)}, s32[32]{0:T(128)}, u32[]{:S(2)}) copy-start(s32[32]{0:T(128)} %far_shift.3) | copy-start | bytes 388
  3.4 44.1 %copy-start.7 = (f32[32]{0:T(128)S(1)}, f32[32]{0:T(128)}, u32[]{:S(2)}) copy-start(f32[32]{0:T(128)} %far_remainder.3) | copy-start | bytes 388
  8.0 69.2 %copy-start = (bf16[64,64,64]{2,1,0:T(8,128)(2,1)S(1)}, bf16[64,64,64]{2,1,0:T(8,128)(2,1)}, u32[]{:S(2)}) copy-start(bf16[64,64,64]{2,1,0:T(8,128)(2,1)} %kernel.1) | copy-start | bytes 1572868
  8.0 69.1 %copy-start.4 = (f32[32,256]{1,0:T(8,128)S(1)}, f32[32,256]{1,0:T(8,128)}, u32[]{:S(2)}) copy-start(f32[32,256]{1,0:T(8,128)} %constant.14.clone.mixed) | copy-start | bytes 98308
  8.0 40.9 %all-to-all-start = ((bf16[16,192,128]{2,1,0:T(8,128)(2,1)}), bf16[16,192,128]{2,1,0:T(8,128)(2,1)S(1)}, u32[]{:S(2)}, u32[]{:S(2)}) async-start(bf16[16,192,128]{2,1,0:T(8,128)(2,1)} %get-tuple-element.49), calls=%async_computation | async-start | bytes 1572864 | tf_op jit(solution)/shard_map/all_to_all | solution.py:628
  16.2 18.8 %collective-permute-start.2 = (f32[72,128]{1,0:T(8,128)S(1)}, f32[72,128]{1,0:T(8,128)S(1)}, u32[]{:S(2)}, u32[]{:S(2)}) collective-permute-start(f32[72,128]{1,0:T(8,128)S(1)} %get-tuple-element.52), channel_id=1, source_target_pairs={{0,4},{1,5},{2,6},{3,7},{4,8},{5,9},{6,10},{7,11},{8,12},{9,13},{1... | collective-permute-start | bytes 110600 | tf_op jit(solution)/shard_map/ppermute | solution.py:694
  18.2 21.3 %collective-permute-start.3 = (f32[72,128]{1,0:T(8,128)S(1)}, f32[72,128]{1,0:T(8,128)S(1)}, u32[]{:S(2)}, u32[]{:S(2)}) collective-permute-start(f32[72,128]{1,0:T(8,128)S(1)} %get-tuple-element.53), channel_id=1, source_target_pairs={{0,8},{1,9},{2,10},{3,11},{4,12},{5,13},{6,14},{7,15},{8,0},{9,1},... | collective-permute-start | bytes 110600 | tf_op jit(solution)/shard_map/ppermute | solution.py:694
  20.6 19.0 %collective-permute-start.4 = (f32[72,128]{1,0:T(8,128)S(1)}, f32[72,128]{1,0:T(8,128)S(1)}, u32[]{:S(2)}, u32[]{:S(2)}) collective-permute-start(f32[72,128]{1,0:T(8,128)S(1)} %get-tuple-element.54), channel_id=1, source_target_pairs={{0,12},{1,13},{2,14},{3,15},{4,0},{5,1},{6,2},{7,3},{8,4},{9,5},{1... | collective-permute-start | bytes 110600 | tf_op jit(solution)/shard_map/ppermute | solution.py:694
  39.6 4.3 %collective-permute-start.5 = (f32[72,128]{1,0:T(8,128)S(1)}, f32[72,128]{1,0:T(8,128)S(1)}, u32[]{:S(2)}, u32[]{:S(2)}) collective-permute-start(f32[72,128]{1,0:T(8,128)S(1)} %get-tuple-element.56), channel_id=1, source_target_pairs={{0,1},{1,0},{2,3},{3,2},{4,5},{5,4},{6,7},{7,6},{8,9},{9,8},{10,11... | collective-permute-start | bytes 110600 | tf_op jit(solution)/shard_map/ppermute | solution.py:694
  41.1 4.0 %collective-permute-start.6 = (f32[72,128]{1,0:T(8,128)S(1)}, f32[72,128]{1,0:T(8,128)S(1)}, u32[]{:S(2)}, u32[]{:S(2)}) collective-permute-start(f32[72,128]{1,0:T(8,128)S(1)} %get-tuple-element.57), channel_id=1, source_target_pairs={{0,2},{1,3},{2,0},{3,1},{4,6},{5,7},{6,4},{7,5},{8,10},{9,11},{10,... | collective-permute-start | bytes 110600 | tf_op jit(solution)/shard_map/ppermute | solution.py:694
  42.6 4.9 %collective-permute-start.7 = (f32[72,128]{1,0:T(8,128)S(1)}, f32[72,128]{1,0:T(8,128)S(1)}, u32[]{:S(2)}, u32[]{:S(2)}) collective-permute-start(f32[72,128]{1,0:T(8,128)S(1)} %get-tuple-element.58), channel_id=1, source_target_pairs={{0,3},{1,2},{2,1},{3,0},{4,7},{5,6},{6,5},{7,4},{8,11},{9,10},{10,... | collective-permute-start | bytes 110600 | tf_op jit(solution)/shard_map/ppermute | solution.py:694
  53.0 41.2 %all-to-all-start.1 = ((bf16[16,24,1024]{2,1,0:T(8,128)(2,1)}), bf16[16,24,1024]{2,1,0:T(8,128)(2,1)S(1)}, u32[]{:S(2)}, u32[]{:S(2)}) async-start(bf16[16,24,1024]{2,1,0:T(8,128)(2,1)} %get-tuple-element.60), calls=%async_computation.1 | async-start | bytes 1572864 | tf_op jit(solution)/shard_map/all_to_all | solution.py:628
  56.7 5.5 %collective-permute-start.8 = (f32[32,128]{1,0:T(8,128)S(1)}, f32[32,128]{1,0:T(8,128)S(1)}, u32[]{:S(2)}, u32[]{:S(2)}) collective-permute-start(f32[32,128]{1,0:T(8,128)S(1)} %get-tuple-element.67), channel_id=1, source_target_pairs={{0,1},{1,0},{2,3},{3,2},{4,5},{5,4},{6,7},{7,6},{8,9},{9,8},{10,11... | collective-permute-start | bytes 49160 | tf_op jit(solution)/shard_map/ppermute | solution.py:694
  58.6 4.5 %collective-permute-start.9 = (f32[32,128]{1,0:T(8,128)S(1)}, f32[32,128]{1,0:T(8,128)S(1)}, u32[]{:S(2)}, u32[]{:S(2)}) collective-permute-start(f32[32,128]{1,0:T(8,128)S(1)} %get-tuple-element.68), channel_id=1, source_target_pairs={{0,2},{1,3},{2,0},{3,1},{4,6},{5,7},{6,4},{7,5},{8,10},{9,11},{10,... | collective-permute-start | bytes 49160 | tf_op jit(solution)/shard_map/ppermute | solution.py:694
  60.1 4.7 %collective-permute-start.10 = (f32[32,128]{1,0:T(8,128)S(1)}, f32[32,128]{1,0:T(8,128)S(1)}, u32[]{:S(2)}, u32[]{:S(2)}) collective-permute-start(f32[32,128]{1,0:T(8,128)S(1)} %get-tuple-element.69), channel_id=1, source_target_pairs={{0,3},{1,2},{2,1},{3,0},{4,7},{5,6},{6,5},{7,4},{8,11},{9,10},{10,... | collective-permute-start | bytes 49160 | tf_op jit(solution)/shard_map/ppermute | solution.py:694
  64.8 7.4 %collective-permute-start.11 = (f32[32,128]{1,0:T(8,128)S(1)}, f32[32,128]{1,0:T(8,128)S(1)}, u32[]{:S(2)}, u32[]{:S(2)}) collective-permute-start(f32[32,128]{1,0:T(8,128)S(1)} %get-tuple-element.71), channel_id=1, source_target_pairs={{0,4},{1,5},{2,6},{3,7},{4,8},{5,9},{6,10},{7,11},{8,12},{9,13},{1... | collective-permute-start | bytes 49160 | tf_op jit(solution)/shard_map/ppermute | solution.py:694
  66.4 9.4 %collective-permute-start.12 = (f32[32,128]{1,0:T(8,128)S(1)}, f32[32,128]{1,0:T(8,128)S(1)}, u32[]{:S(2)}, u32[]{:S(2)}) collective-permute-start(f32[32,128]{1,0:T(8,128)S(1)} %get-tuple-element.72), channel_id=1, source_target_pairs={{0,8},{1,9},{2,10},{3,11},{4,12},{5,13},{6,14},{7,15},{8,0},{9,1},... | collective-permute-start | bytes 49160 | tf_op jit(solution)/shard_map/ppermute | solution.py:694
  68.8 7.0 %collective-permute-start.13 = (f32[32,128]{1,0:T(8,128)S(1)}, f32[32,128]{1,0:T(8,128)S(1)}, u32[]{:S(2)}, u32[]{:S(2)}) collective-permute-start(f32[32,128]{1,0:T(8,128)S(1)} %get-tuple-element.73), channel_id=1, source_target_pairs={{0,12},{1,13},{2,14},{3,15},{4,0},{5,1},{6,2},{7,3},{8,4},{9,5},{1... | collective-permute-start | bytes 49160 | tf_op jit(solution)/shard_map/ppermute | solution.py:694
  75.9 1.3 %collective-permute-start.14 = (f32[64,128]{1,0:T(8,128)S(1)}, f32[64,128]{1,0:T(8,128)S(1)}, u32[]{:S(2)}, u32[]{:S(2)}) collective-permute-start(f32[64,128]{1,0:T(8,128)S(1)} %get-tuple-element.75), channel_id=1, source_target_pairs={{0,16},{16,0},{1,17},{17,1},{2,18},{18,2},{3,19},{19,3},{4,20},{20... | collective-permute-start | bytes 98312 | tf_op jit(solution)/shard_map/ppermute | solution.py:694
  77.8 1.2 %collective-permute-start.15 = (f32[32,128]{1,0:T(8,128)S(1)}, f32[32,128]{1,0:T(8,128)S(1)}, u32[]{:S(2)}, u32[]{:S(2)}) collective-permute-start(f32[32,128]{1,0:T(8,128)S(1)} %get-tuple-element.79), channel_id=1, source_target_pairs={{0,16},{16,0},{1,17},{17,1},{2,18},{18,2},{3,19},{19,3},{4,20},{20... | collective-permute-start | bytes 49160 | tf_op jit(solution)/shard_map/ppermute | solution.py:694
  79.1 3.7 %collective-permute-start.16 = (f32[16,128]{1,0:T(8,128)S(1)}, f32[16,128]{1,0:T(8,128)S(1)}, u32[]{:S(2)}, u32[]{:S(2)}) collective-permute-start(f32[16,128]{1,0:T(8,128)S(1)} %get-tuple-element.81), channel_id=1, source_target_pairs={{0,1},{1,0},{2,3},{3,2},{4,5},{5,4},{6,7},{7,6},{8,9},{9,8},{10,11... | collective-permute-start | bytes 24584 | tf_op jit(solution)/shard_map/ppermute | solution.py:694
  80.7 3.7 %collective-permute-start.17 = (f32[16,128]{1,0:T(8,128)S(1)}, f32[16,128]{1,0:T(8,128)S(1)}, u32[]{:S(2)}, u32[]{:S(2)}) collective-permute-start(f32[16,128]{1,0:T(8,128)S(1)} %get-tuple-element.82), channel_id=1, source_target_pairs={{0,2},{1,3},{2,0},{3,1},{4,6},{5,7},{6,4},{7,5},{8,10},{9,11},{10,... | collective-permute-start | bytes 24584 | tf_op jit(solution)/shard_map/ppermute | solution.py:694
  82.1 4.5 %collective-permute-start.18 = (f32[16,128]{1,0:T(8,128)S(1)}, f32[16,128]{1,0:T(8,128)S(1)}, u32[]{:S(2)}, u32[]{:S(2)}) collective-permute-start(f32[16,128]{1,0:T(8,128)S(1)} %get-tuple-element.83), channel_id=1, source_target_pairs={{0,3},{1,2},{2,1},{3,0},{4,7},{5,6},{6,5},{7,4},{8,11},{9,10},{10,... | collective-permute-start | bytes 24584 | tf_op jit(solution)/shard_map/ppermute | solution.py:694
  86.7 5.5 %collective-permute-start.19 = (f32[16,128]{1,0:T(8,128)S(1)}, f32[16,128]{1,0:T(8,128)S(1)}, u32[]{:S(2)}, u32[]{:S(2)}) collective-permute-start(f32[16,128]{1,0:T(8,128)S(1)} %get-tuple-element.85), channel_id=1, source_target_pairs={{0,4},{1,5},{2,6},{3,7},{4,8},{5,9},{6,10},{7,11},{8,12},{9,13},{1... | collective-permute-start | bytes 24584 | tf_op jit(solution)/shard_map/ppermute | solution.py:694
  87.5 4.7 %collective-permute-start.20 = (f32[16,128]{1,0:T(8,128)S(1)}, f32[16,128]{1,0:T(8,128)S(1)}, u32[]{:S(2)}, u32[]{:S(2)}) collective-permute-start(f32[16,128]{1,0:T(8,128)S(1)} %get-tuple-element.86), channel_id=1, source_target_pairs={{0,8},{1,9},{2,10},{3,11},{4,12},{5,13},{6,14},{7,15},{8,0},{9,1},... | collective-permute-start | bytes 24584 | tf_op jit(solution)/shard_map/ppermute | solution.py:694
  89.0 3.8 %collective-permute-start.21 = (f32[16,128]{1,0:T(8,128)S(1)}, f32[16,128]{1,0:T(8,128)S(1)}, u32[]{:S(2)}, u32[]{:S(2)}) collective-permute-start(f32[16,128]{1,0:T(8,128)S(1)} %get-tuple-element.87), channel_id=1, source_target_pairs={{0,12},{1,13},{2,14},{3,15},{4,0},{5,1},{6,2},{7,3},{8,4},{9,5},{1... | collective-permute-start | bytes 24584 | tf_op jit(solution)/shard_map/ppermute | solution.py:694

commit v12 on v11

--- a/solution.py
+++ b/solution.py
@@ -254,7 +254,7 @@
                 over[c, a, z * per : (z + 1) * per, :] = turned
         return jnp.maximum(peak, mine)
 
-    peak = lax.fori_loop(0, sources, widen, jnp.zeros((1, 1), F32), unroll=8)
+    peak = lax.fori_loop(0, sources, widen, jnp.zeros((1, 1), F32), unroll=True)
     top[...] = jnp.broadcast_to(peak, top.shape)
     lane = lane_iota((group, LANES))
     cycle = row_iota((group, LANES)) % per
@@ -268,7 +268,7 @@
             ring[c, before] = ring[c, before] + jnp.where(lane >= LANES - 2, extra, 0.0)
         return carry
 
-    lax.fori_loop(0, sources, spill, 0, unroll=16)
+    lax.fori_loop(0, sources, spill, 0, unroll=True)
     for copy in scalars:
         copy.wait()
     x = jnp.zeros((group, LANES), F32)
@@ -300,7 +300,7 @@
                 )
         return carry
 
-    lax.fori_loop(0, sources, tap, 0, unroll=8)
+    lax.fori_loop(0, sources, tap, 0, unroll=True)
     scale = (TOP / GAIN) / peak
 
     def send(dest):
@@ -329,7 +329,7 @@
         return tuple(carry)
 
     start = tuple(turned_tile(c, k, -1) for c in range(3) for k in range(per))
-    lax.fori_loop(0, sources, turn, start, unroll=8)
+    lax.fori_loop(0, sources, turn, start, unroll=True)
     for dest in range(sources):
         send(dest).wait()
 

time: 96 us -> 96.2 us (level)
  no operation moved by 1% of the time
where the time goes in v12:
time: 96.2 us; the launch traced here: 95.8 us
  waiting for transfers between devices  40.8 us (42%)
  starting transfers between devices  38.5 us (40%)
  Pallas kernels  15.6 us (16%)
    ppermute x20, waiting for transfers between devices, hop(): moved.append(lax.ppermute(buffers[o], axis, pairs))  40.3 us
    ppermute x20, starting transfers between devices, hop(): moved.append(lax.ppermute(buffers[o], axis, pairs))  26.1 us
    pallas_call x15, Pallas kernels, run(): return kernel(*near)  15.6 us
    all_to_all x2, starting transfers between devices, exchange(): return lax.all_to_all(array, axes, 0, 0, tiled=True)  11.8 us
  transfers between devices with their start and end apart: 24, of which 19 were waited for; matrix products, arithmetic and copies ran while one was open for 0% of the time, Pallas kernels for 5%

profile of v12, /device:TPU:0, one launch (start us, length us, event | category | flops | bytes accessed | tf_op | source)
XLA Modules:
  0.0 95.8 jit_solution(40847049690029085)
XLA Ops:
  0.6 1.4 %shard_map.147 = (f32[3,4,40,1152]{3,2,1,0:T(8,128)S(1)}, f32[3,4,2,1024]{3,2,1,0:T(2,128)S(1)}, f32[3,4,2,1024]{3,2,1,0:T(2,128)S(1)}) custom-call(f32[4,32,1024]{2,1,0:T(8,128)} %rho.1, f32[4,32,1024]{2,1,0:T(8,128)} %ur.1, f32[4,32,1024]{2,1,0:T(8,128)} %up.1), custom_call_target="tpu_custom_call" | custom-call | bytes 1572864 | tf_op jit(solution)/shard_map/pallas_call | solution.py:622
  2.0 0.6 collective-permute-start
  2.6 0.1 collective-permute-start.1
  2.7 0.6 shard_map.148.stage_in
  3.3 0.0 copy-start.1
  3.3 0.0 copy-start.2
  3.3 0.0 copy-start.3
  3.4 0.0 copy-start.5
  3.4 0.0 copy-start.6
  3.4 0.0 copy-start.7
  3.4 0.2 collective-permute-done.low
  3.5 0.4 collective-permute-done.1.high
  3.9 4.1 %shard_map.149 = (bf16[16,192,128]{2,1,0:T(8,128)(2,1)}, f32[16,24,128]{2,1,0:T(8,128)S(1)}, f32[3,4,40,1152]{3,2,1,0:T(8,128)S(1)}, f32[3,4,40,1152]{3,2,1,0:T(8,128)S(1)}) custom-call(f32[3,4,40,1152]{3,2,1,0:T(8,128)S(1)} %get-tuple-element.46.field.field_in, ...), custom_call_target="tpu_custom_call", output_to_operand_aliasing={{2}: (0, {}), {3}: (1, {})} | custom-call | flops 39321600 | bytes 3145728 | tf_op jit(solution)/shard_map/pallas_call | solution.py:622
  8.0 0.0 copy-start
  8.0 0.0 copy-start.4
  8.0 8.1 %all-to-all-start = ((bf16[16,192,128]{2,1,0:T(8,128)(2,1)}), bf16[16,192,128]{2,1,0:T(8,128)(2,1)S(1)}, u32[]{:S(2)}, u32[]{:S(2)}) async-start(bf16[16,192,128]{2,1,0:T(8,128)(2,1)} %get-tuple-element.49), calls=%async_computation | async-start | bytes 1572864 | tf_op jit(solution)/shard_map/all_to_all | solution.py:628
  16.2 2.0 %collective-permute-start.2 = (f32[72,128]{1,0:T(8,128)S(1)}, f32[72,128]{1,0:T(8,128)S(1)}, u32[]{:S(2)}, u32[]{:S(2)}) collective-permute-start(f32[72,128]{1,0:T(8,128)S(1)} %get-tuple-element.52), channel_id=1, source_target_pairs={{0,4},{1,5},{2,6},{3,7},{4,8},{5,9},{6,10},{7,11},{8,12},{9,13},{1... | collective-permute-start | bytes 110600 | tf_op jit(solution)/shard_map/ppermute | solution.py:694
  18.2 2.4 %collective-permute-start.3 = (f32[72,128]{1,0:T(8,128)S(1)}, f32[72,128]{1,0:T(8,128)S(1)}, u32[]{:S(2)}, u32[]{:S(2)}) collective-permute-start(f32[72,128]{1,0:T(8,128)S(1)} %get-tuple-element.53), channel_id=1, source_target_pairs={{0,8},{1,9},{2,10},{3,11},{4,12},{5,13},{6,14},{7,15},{8,0},{9,1},... | collective-permute-start | bytes 110600 | tf_op jit(solution)/shard_map/ppermute | solution.py:694
  20.6 1.5 %collective-permute-start.4 = (f32[72,128]{1,0:T(8,128)S(1)}, f32[72,128]{1,0:T(8,128)S(1)}, u32[]{:S(2)}, u32[]{:S(2)}) collective-permute-start(f32[72,128]{1,0:T(8,128)S(1)} %get-tuple-element.54), channel_id=1, source_target_pairs={{0,12},{1,13},{2,14},{3,15},{4,0},{5,1},{6,2},{7,3},{8,4},{9,5},{1... | collective-permute-start | bytes 110600 | tf_op jit(solution)/shard_map/ppermute | solution.py:694
  22.0 13.0 %collective-permute-done.2.rest_1_ = f32[72,128]{1,0:T(8,128)S(1)} collective-permute-done((f32[72,128]{1,0:T(8,128)S(1)}, f32[72,128]{1,0:T(8,128)S(1)}, u32[]{:S(2)}, u32[]{:S(2)}) %collective-permute-start.2) | collective-permute-done | bytes 36896 | tf_op jit(solution)/shard_map/ppermute | solution.py:694
  35.1 4.4 %collective-permute-done.3.rest_2_ = f32[72,128]{1,0:T(8,128)S(1)} collective-permute-done((f32[72,128]{1,0:T(8,128)S(1)}, f32[72,128]{1,0:T(8,128)S(1)}, u32[]{:S(2)}, u32[]{:S(2)}) %collective-permute-start.3) | collective-permute-done | bytes 36896 | tf_op jit(solution)/shard_map/ppermute | solution.py:694
  39.5 0.0 collective-permute-done.4.rest_3_
  39.6 1.5 %collective-permute-start.5 = (f32[72,128]{1,0:T(8,128)S(1)}, f32[72,128]{1,0:T(8,128)S(1)}, u32[]{:S(2)}, u32[]{:S(2)}) collective-permute-start(f32[72,128]{1,0:T(8,128)S(1)} %get-tuple-element.56), channel_id=1, source_target_pairs={{0,1},{1,0},{2,3},{3,2},{4,5},{5,4},{6,7},{7,6},{8,9},{9,8},{10,11... | collective-permute-start | bytes 110600 | tf_op jit(solution)/shard_map/ppermute | solution.py:694
  41.1 1.5 %collective-permute-start.6 = (f32[72,128]{1,0:T(8,128)S(1)}, f32[72,128]{1,0:T(8,128)S(1)}, u32[]{:S(2)}, u32[]{:S(2)}) collective-permute-start(f32[72,128]{1,0:T(8,128)S(1)} %get-tuple-element.57), channel_id=1, source_target_pairs={{0,2},{1,3},{2,0},{3,1},{4,6},{5,7},{6,4},{7,5},{8,10},{9,11},{10,... | collective-permute-start | bytes 110600 | tf_op jit(solution)/shard_map/ppermute | solution.py:694
  42.6 0.6 collective-permute-start.7
  43.1 0.8 collective-permute-done.5.rest_1_
  43.9 1.2 %collective-permute-done.6.rest_2_ = f32[72,128]{1,0:T(8,128)S(1)} collective-permute-done((f32[72,128]{1,0:T(8,128)S(1)}, f32[72,128]{1,0:T(8,128)S(1)}, u32[]{:S(2)}, u32[]{:S(2)}) %collective-permute-start.6) | collective-permute-done | bytes 36896 | tf_op jit(solution)/shard_map/ppermute | solution.py:694
  45.1 2.3 %collective-permute-done.7.rest_3_ = f32[72,128]{1,0:T(8,128)S(1)} collective-permute-done((f32[72,128]{1,0:T(8,128)S(1)}, f32[72,128]{1,0:T(8,128)S(1)}, u32[]{:S(2)}, u32[]{:S(2)}) %collective-permute-start.7) | collective-permute-done | bytes 36896 | tf_op jit(solution)/shard_map/ppermute | solution.py:694
  47.5 1.5 %shard_map.152 = (f32[128,128]{1,0:T(8,128)S(1)}, f32[16,24,128]{2,1,0:T(8,128)S(1)}) custom-call(s32[32]{0:T(128)S(1)} %copy-done.6, f32[32]{0:T(128)S(1)} %copy-done.7, f32[128,256]{1,0:T(8,128)S(1)} %copy-done.2, f32[128,256]{1,0:T(8,128)S(1)} %copy-done.1, f32[32,128]{1,0:T(8,128)S(1)} %copy-done.5, f32[32,256]{1,0:T(8,128)S(1)} %copy-done.3, ...), custom_call_target="tpu_custom_call" | custom-call | flops 100000000 | bytes 1000000 | tf_op jit(solution)/shard_map/pallas_call | solution.py:622
  49.0 0.0 all-to-all-done.bulk
  49.0 4.2 %shard_map.153 = (bf16[16,24,1024]{2,1,0:T(8,128)(2,1)}, f32[8,128]{1,0:T(8,128)S(1)}) custom-call(s32[32]{0:T(128)S(1)} %copy-done.6, f32[32]{0:T(128)S(1)} %copy-done.7, bf16[16,192,128]{2,1,0:T(8,128)(2,1)S(1)} %all-to-all-done.bulk, f32[16,24,128]{2,1,0:T(8,128)S(1)} %get-tuple-element.59.sides), custom_call_target="tpu_custom_call" | custom-call | flops 19660800 | bytes 1572864 | tf_op jit(solution)/shard_map/pallas_call | solution.py:622
  53.1 3.6 %all-to-all-start.1 = ((bf16[16,24,1024]{2,1,0:T(8,128)(2,1)}), bf16[16,24,1024]{2,1,0:T(8,128)(2,1)S(1)}, u32[]{:S(2)}, u32[]{:S(2)}) async-start(bf16[16,24,1024]{2,1,0:T(8,128)(2,1)} %get-tuple-element.60), calls=%async_computation.1 | async-start | bytes 1572864 | tf_op jit(solution)/shard_map/all_to_all | solution.py:628
  56.8 1.9 %collective-permute-start.8 = (f32[32,128]{1,0:T(8,128)S(1)}, f32[32,128]{1,0:T(8,128)S(1)}, u32[]{:S(2)}, u32[]{:S(2)}) collective-permute-start(f32[32,128]{1,0:T(8,128)S(1)} %get-tuple-element.67), channel_id=1, source_target_pairs={{0,1},{1,0},{2,3},{3,2},{4,5},{5,4},{6,7},{7,6},{8,9},{9,8},{10,11... | collective-permute-start | bytes 49160 | tf_op jit(solution)/shard_map/ppermute | solution.py:694
  58.7 1.5 %collective-permute-start.9 = (f32[32,128]{1,0:T(8,128)S(1)}, f32[32,128]{1,0:T(8,128)S(1)}, u32[]{:S(2)}, u32[]{:S(2)}) collective-permute-start(f32[32,128]{1,0:T(8,128)S(1)} %get-tuple-element.68), channel_id=1, source_target_pairs={{0,2},{1,3},{2,0},{3,1},{4,6},{5,7},{6,4},{7,5},{8,10},{9,11},{10,... | collective-permute-start | bytes 49160 | tf_op jit(solution)/shard_map/ppermute | solution.py:694
  60.2 0.2 collective-permute-start.10
  60.4 2.0 %collective-permute-done.8.rest_1_ = f32[32,128]{1,0:T(8,128)S(1)} collective-permute-done((f32[32,128]{1,0:T(8,128)S(1)}, f32[32,128]{1,0:T(8,128)S(1)}, u32[]{:S(2)}, u32[]{:S(2)}) %collective-permute-start.8) | collective-permute-done | bytes 16416 | tf_op jit(solution)/shard_map/ppermute | solution.py:694
  62.4 0.8 collective-permute-done.9.rest_2_
  63.1 1.7 %collective-permute-done.10.rest_3_ = f32[32,128]{1,0:T(8,128)S(1)} collective-permute-done((f32[32,128]{1,0:T(8,128)S(1)}, f32[32,128]{1,0:T(8,128)S(1)}, u32[]{:S(2)}, u32[]{:S(2)}) %collective-permute-start.10) | collective-permute-done | bytes 16416 | tf_op jit(solution)/shard_map/ppermute | solution.py:694
  64.9 1.6 %collective-permute-start.11 = (f32[32,128]{1,0:T(8,128)S(1)}, f32[32,128]{1,0:T(8,128)S(1)}, u32[]{:S(2)}, u32[]{:S(2)}) collective-permute-start(f32[32,128]{1,0:T(8,128)S(1)} %get-tuple-element.71), channel_id=1, source_target_pairs={{0,4},{1,5},{2,6},{3,7},{4,8},{5,9},{6,10},{7,11},{8,12},{9,13},{1... | collective-permute-start | bytes 49160 | tf_op jit(solution)/shard_map/ppermute | solution.py:694
  66.5 2.4 %collective-permute-start.12 = (f32[32,128]{1,0:T(8,128)S(1)}, f32[32,128]{1,0:T(8,128)S(1)}, u32[]{:S(2)}, u32[]{:S(2)}) collective-permute-start(f32[32,128]{1,0:T(8,128)S(1)} %get-tuple-element.72), channel_id=1, source_target_pairs={{0,8},{1,9},{2,10},{3,11},{4,12},{5,13},{6,14},{7,15},{8,0},{9,1},... | collective-permute-start | bytes 49160 | tf_op jit(solution)/shard_map/ppermute | solution.py:694
  69.0 1.4 %collective-permute-start.13 = (f32[32,128]{1,0:T(8,128)S(1)}, f32[32,128]{1,0:T(8,128)S(1)}, u32[]{:S(2)}, u32[]{:S(2)}) collective-permute-start(f32[32,128]{1,0:T(8,128)S(1)} %get-tuple-element.73), channel_id=1, source_target_pairs={{0,12},{1,13},{2,14},{3,15},{4,0},{5,1},{6,2},{7,3},{8,4},{9,5},{1... | collective-permute-start | bytes 49160 | tf_op jit(solution)/shard_map/ppermute | solution.py:694
  70.3 2.0 %collective-permute-done.11.rest_1_ = f32[32,128]{1,0:T(8,128)S(1)} collective-permute-done((f32[32,128]{1,0:T(8,128)S(1)}, f32[32,128]{1,0:T(8,128)S(1)}, u32[]{:S(2)}, u32[]{:S(2)}) %collective-permute-start.11) | collective-permute-done | bytes 16416 | tf_op jit(solution)/shard_map/ppermute | solution.py:694
  72.3 3.6 %collective-permute-done.12.rest_2_ = f32[32,128]{1,0:T(8,128)S(1)} collective-permute-done((f32[32,128]{1,0:T(8,128)S(1)}, f32[32,128]{1,0:T(8,128)S(1)}, u32[]{:S(2)}, u32[]{:S(2)}) %collective-permute-start.12) | collective-permute-done | bytes 16416 | tf_op jit(solution)/shard_map/ppermute | solution.py:694
  76.0 0.0 collective-permute-done.13.rest_3_
  76.0 0.1 collective-permute-start.14
  76.1 1.2 %collective-permute-done.14.rest_1_ = f32[64,128]{1,0:T(8,128)S(1)} collective-permute-done((f32[64,128]{1,0:T(8,128)S(1)}, f32[64,128]{1,0:T(8,128)S(1)}, u32[]{:S(2)}, u32[]{:S(2)}) %collective-permute-start.14) | collective-permute-done | bytes 32800 | tf_op jit(solution)/shard_map/ppermute | solution.py:694
  77.3 0.7 shard_map.158
  78.0 0.2 collective-permute-start.15
  78.2 1.0 %collective-permute-done.15.rest_1_ = f32[32,128]{1,0:T(8,128)S(1)} collective-permute-done((f32[32,128]{1,0:T(8,128)S(1)}, f32[32,128]{1,0:T(8,128)S(1)}, u32[]{:S(2)}, u32[]{:S(2)}) %collective-permute-start.15) | collective-permute-done | bytes 16416 | tf_op jit(solution)/shard_map/ppermute | solution.py:694
  79.2 1.5 %collective-permute-start.16 = (f32[16,128]{1,0:T(8,128)S(1)}, f32[16,128]{1,0:T(8,128)S(1)}, u32[]{:S(2)}, u32[]{:S(2)}) collective-permute-start(f32[16,128]{1,0:T(8,128)S(1)} %get-tuple-element.81), channel_id=1, source_target_pairs={{0,1},{1,0},{2,3},{3,2},{4,5},{5,4},{6,7},{7,6},{8,9},{9,8},{10,11... | collective-permute-start | bytes 24584 | tf_op jit(solution)/shard_map/ppermute | solution.py:694
  80.8 1.5 %collective-permute-start.17 = (f32[16,128]{1,0:T(8,128)S(1)}, f32[16,128]{1,0:T(8,128)S(1)}, u32[]{:S(2)}, u32[]{:S(2)}) collective-permute-start(f32[16,128]{1,0:T(8,128)S(1)} %get-tuple-element.82), channel_id=1, source_target_pairs={{0,2},{1,3},{2,0},{3,1},{4,6},{5,7},{6,4},{7,5},{8,10},{9,11},{10,... | collective-permute-start | bytes 24584 | tf_op jit(solution)/shard_map/ppermute | solution.py:694
  82.2 0.6 collective-permute-start.18
  82.8 0.2 collective-permute-done.16.rest_1_
  83.0 1.5 %collective-permute-done.17.rest_2_ = f32[16,128]{1,0:T(8,128)S(1)} collective-permute-done((f32[16,128]{1,0:T(8,128)S(1)}, f32[16,128]{1,0:T(8,128)S(1)}, u32[]{:S(2)}, u32[]{:S(2)}) %collective-permute-start.17) | collective-permute-done | bytes 8224 | tf_op jit(solution)/shard_map/ppermute | solution.py:694
  84.4 2.4 %collective-permute-done.18.rest_3_ = f32[16,128]{1,0:T(8,128)S(1)} collective-permute-done((f32[16,128]{1,0:T(8,128)S(1)}, f32[16,128]{1,0:T(8,128)S(1)}, u32[]{:S(2)}, u32[]{:S(2)}) %collective-permute-start.18) | collective-permute-done | bytes 8224 | tf_op jit(solution)/shard_map/ppermute | solution.py:694
  86.8 0.8 collective-permute-start.19
  87.6 1.5 %collective-permute-start.20 = (f32[16,128]{1,0:T(8,128)S(1)}, f32[16,128]{1,0:T(8,128)S(1)}, u32[]{:S(2)}, u32[]{:S(2)}) collective-permute-start(f32[16,128]{1,0:T(8,128)S(1)} %get-tuple-element.86), channel_id=1, source_target_pairs={{0,8},{1,9},{2,10},{3,11},{4,12},{5,13},{6,14},{7,15},{8,0},{9,1},... | collective-permute-start | bytes 24584 | tf_op jit(solution)/shard_map/ppermute | solution.py:694
  89.1 1.6 %collective-permute-start.21 = (f32[16,128]{1,0:T(8,128)S(1)}, f32[16,128]{1,0:T(8,128)S(1)}, u32[]{:S(2)}, u32[]{:S(2)}) collective-permute-start(f32[16,128]{1,0:T(8,128)S(1)} %get-tuple-element.87), channel_id=1, source_target_pairs={{0,12},{1,13},{2,14},{3,15},{4,0},{5,1},{6,2},{7,3},{8,4},{9,5},{1... | collective-permute-start | bytes 24584 | tf_op jit(solution)/shard_map/ppermute | solution.py:694
  90.7 1.6 %collective-permute-done.19.rest_1_ = f32[16,128]{1,0:T(8,128)S(1)} collective-permute-done((f32[16,128]{1,0:T(8,128)S(1)}, f32[16,128]{1,0:T(8,128)S(1)}, u32[]{:S(2)}, u32[]{:S(2)}) %collective-permute-start.19) | collective-permute-done | bytes 8224 | tf_op jit(solution)/shard_map/ppermute | solution.py:694
  92.3 0.0 collective-permute-done.20.rest_2_
  92.3 0.6 collective-permute-done.21.rest_3_
  92.9 1.4 %shard_map.161 = f32[2,16384]{1,0:T(2,128)} custom-call(f32[128,256]{1,0:T(8,128)S(1)} %copy-done.2, f32[128,256]{1,0:T(8,128)S(1)} %copy-done.1, f32[32,512]{1,0:T(8,128)S(1)} %get-tuple-element.76.tables, f32[32,128]{1,0:T(8,128)S(1)} %get-tuple-element.77.factor, f32[16,128]{1,0:T(8,128)S(1)} %get-tuple-element.84.rest_0_, ...), custom_call_target="tpu_custom_call" | custom-call | flops 100000000 | bytes 1000000 | tf_op jit(solution)/shard_map/pallas_call | solution.py:622
  94.3 0.0 all-to-all-done.1.bulk
  94.3 1.5 %shard_map.154 = (f32[4,32,1024]{2,1,0:T(8,128)}, f32[4,32,1024]{2,1,0:T(8,128)}, f32[4,32,1024]{2,1,0:T(8,128)}) custom-call(bf16[16,24,1024]{2,1,0:T(8,128)(2,1)S(1)} %all-to-all-done.1.bulk, f32[8,128]{1,0:T(8,128)S(1)} %get-tuple-element.61.top), custom_call_target="tpu_custom_call" | custom-call | flops 7864320 | bytes 2359296 | tf_op jit(solution)/shard_map/pallas_call | solution.py:622
  (15 shorter events, 0.2 us)
Async XLA Ops:
  2.0 1.5 %collective-permute-start = (f32[3,4,2,1024]{3,2,1,0:T(2,128)S(1)}, f32[3,4,2,1024]{3,2,1,0:T(2,128)S(1)}, u32[]{:S(2)}, u32[]{:S(2)}) collective-permute-start(f32[3,4,2,1024]{3,2,1,0:T(2,128)S(1)} %get-tuple-element.47), channel_id=1, source_target_pairs={{0,16},{16,0},{1,17},{17,1},{2,18},{18,2},{3,19},{19,3},{4,20},{20... | collective-permute-start | bytes 294920 | tf_op jit(solution)/shard_map/ppermute | solution.py:668
  2.6 1.3 %collective-permute-start.1 = (f32[3,4,2,1024]{3,2,1,0:T(2,128)S(1)}, f32[3,4,2,1024]{3,2,1,0:T(2,128)S(1)}, u32[]{:S(2)}, u32[]{:S(2)}) collective-permute-start(f32[3,4,2,1024]{3,2,1,0:T(2,128)S(1)} %get-tuple-element.48), channel_id=1, source_target_pairs={{16,0},{0,16},{17,1},{1,17},{18,2},{2,18},{19,3},{3,19},{20,4},{4,... | collective-permute-start | bytes 294920 | tf_op jit(solution)/shard_map/ppermute | solution.py:669
  3.3 44.1 %copy-start.1 = (f32[128,256]{1,0:T(8,128)S(1)}, f32[128,256]{1,0:T(8,128)}, u32[]{:S(2)}) copy-start(f32[128,256]{1,0:T(8,128)} %constant.11.clone.twiddle) | copy-start | bytes 393220
  3.3 44.1 %copy-start.2 = (f32[128,256]{1,0:T(8,128)S(1)}, f32[128,256]{1,0:T(8,128)}, u32[]{:S(2)}) copy-start(f32[128,256]{1,0:T(8,128)} %constant.10.clone.circle) | copy-start | bytes 393220
  3.3 44.1 %copy-start.3 = (f32[32,256]{1,0:T(8,128)S(1)}, f32[32,256]{1,0:T(8,128)}, u32[]{:S(2)}) copy-start(f32[32,256]{1,0:T(8,128)} %constant.13.clone.steps) | copy-start | bytes 98308
  3.4 44.1 %copy-start.5 = (f32[32,128]{1,0:T(8,128)S(1)}, f32[32,128]{1,0:T(8,128)}, u32[]{:S(2)}) copy-start(f32[32,128]{1,0:T(8,128)} %constant.12.clone.short) | copy-start | bytes 49156
  3.4 44.1 %copy-start.6 = (s32[32]{0:T(128)S(1)}, s32[32]{0:T(128)}, u32[]{:S(2)}) copy-start(s32[32]{0:T(128)} %far_shift.3) | copy-start | bytes 388
  3.4 44.1 %copy-start.7 = (f32[32]{0:T(128)S(1)}, f32[32]{0:T(128)}, u32[]{:S(2)}) copy-start(f32[32]{0:T(128)} %far_remainder.3) | copy-start | bytes 388
  8.0 69.3 %copy-start = (bf16[64,64,64]{2,1,0:T(8,128)(2,1)S(1)}, bf16[64,64,64]{2,1,0:T(8,128)(2,1)}, u32[]{:S(2)}) copy-start(bf16[64,64,64]{2,1,0:T(8,128)(2,1)} %kernel.1) | copy-start | bytes 1572868
  8.0 69.3 %copy-start.4 = (f32[32,256]{1,0:T(8,128)S(1)}, f32[32,256]{1,0:T(8,128)}, u32[]{:S(2)}) copy-start(f32[32,256]{1,0:T(8,128)} %constant.14.clone.mixed) | copy-start | bytes 98308
  8.0 40.9 %all-to-all-start = ((bf16[16,192,128]{2,1,0:T(8,128)(2,1)}), bf16[16,192,128]{2,1,0:T(8,128)(2,1)S(1)}, u32[]{:S(2)}, u32[]{:S(2)}) async-start(bf16[16,192,128]{2,1,0:T(8,128)(2,1)} %get-tuple-element.49), calls=%async_computation | async-start | bytes 1572864 | tf_op jit(solution)/shard_map/all_to_all | solution.py:628
  16.2 18.8 %collective-permute-start.2 = (f32[72,128]{1,0:T(8,128)S(1)}, f32[72,128]{1,0:T(8,128)S(1)}, u32[]{:S(2)}, u32[]{:S(2)}) collective-permute-start(f32[72,128]{1,0:T(8,128)S(1)} %get-tuple-element.52), channel_id=1, source_target_pairs={{0,4},{1,5},{2,6},{3,7},{4,8},{5,9},{6,10},{7,11},{8,12},{9,13},{1... | collective-permute-start | bytes 110600 | tf_op jit(solution)/shard_map/ppermute | solution.py:694
  18.2 21.3 %collective-permute-start.3 = (f32[72,128]{1,0:T(8,128)S(1)}, f32[72,128]{1,0:T(8,128)S(1)}, u32[]{:S(2)}, u32[]{:S(2)}) collective-permute-start(f32[72,128]{1,0:T(8,128)S(1)} %get-tuple-element.53), channel_id=1, source_target_pairs={{0,8},{1,9},{2,10},{3,11},{4,12},{5,13},{6,14},{7,15},{8,0},{9,1},... | collective-permute-start | bytes 110600 | tf_op jit(solution)/shard_map/ppermute | solution.py:694
  20.6 19.0 %collective-permute-start.4 = (f32[72,128]{1,0:T(8,128)S(1)}, f32[72,128]{1,0:T(8,128)S(1)}, u32[]{:S(2)}, u32[]{:S(2)}) collective-permute-start(f32[72,128]{1,0:T(8,128)S(1)} %get-tuple-element.54), channel_id=1, source_target_pairs={{0,12},{1,13},{2,14},{3,15},{4,0},{5,1},{6,2},{7,3},{8,4},{9,5},{1... | collective-permute-start | bytes 110600 | tf_op jit(solution)/shard_map/ppermute | solution.py:694
  39.6 4.3 %collective-permute-start.5 = (f32[72,128]{1,0:T(8,128)S(1)}, f32[72,128]{1,0:T(8,128)S(1)}, u32[]{:S(2)}, u32[]{:S(2)}) collective-permute-start(f32[72,128]{1,0:T(8,128)S(1)} %get-tuple-element.56), channel_id=1, source_target_pairs={{0,1},{1,0},{2,3},{3,2},{4,5},{5,4},{6,7},{7,6},{8,9},{9,8},{10,11... | collective-permute-start | bytes 110600 | tf_op jit(solution)/shard_map/ppermute | solution.py:694
  41.1 4.0 %collective-permute-start.6 = (f32[72,128]{1,0:T(8,128)S(1)}, f32[72,128]{1,0:T(8,128)S(1)}, u32[]{:S(2)}, u32[]{:S(2)}) collective-permute-start(f32[72,128]{1,0:T(8,128)S(1)} %get-tuple-element.57), channel_id=1, source_target_pairs={{0,2},{1,3},{2,0},{3,1},{4,6},{5,7},{6,4},{7,5},{8,10},{9,11},{10,... | collective-permute-start | bytes 110600 | tf_op jit(solution)/shard_map/ppermute | solution.py:694
  42.6 4.9 %collective-permute-start.7 = (f32[72,128]{1,0:T(8,128)S(1)}, f32[72,128]{1,0:T(8,128)S(1)}, u32[]{:S(2)}, u32[]{:S(2)}) collective-permute-start(f32[72,128]{1,0:T(8,128)S(1)} %get-tuple-element.58), channel_id=1, source_target_pairs={{0,3},{1,2},{2,1},{3,0},{4,7},{5,6},{6,5},{7,4},{8,11},{9,10},{10,... | collective-permute-start | bytes 110600 | tf_op jit(solution)/shard_map/ppermute | solution.py:694
  53.1 41.2 %all-to-all-start.1 = ((bf16[16,24,1024]{2,1,0:T(8,128)(2,1)}), bf16[16,24,1024]{2,1,0:T(8,128)(2,1)S(1)}, u32[]{:S(2)}, u32[]{:S(2)}) async-start(bf16[16,24,1024]{2,1,0:T(8,128)(2,1)} %get-tuple-element.60), calls=%async_computation.1 | async-start | bytes 1572864 | tf_op jit(solution)/shard_map/all_to_all | solution.py:628
  56.8 5.5 %collective-permute-start.8 = (f32[32,128]{1,0:T(8,128)S(1)}, f32[32,128]{1,0:T(8,128)S(1)}, u32[]{:S(2)}, u32[]{:S(2)}) collective-permute-start(f32[32,128]{1,0:T(8,128)S(1)} %get-tuple-element.67), channel_id=1, source_target_pairs={{0,1},{1,0},{2,3},{3,2},{4,5},{5,4},{6,7},{7,6},{8,9},{9,8},{10,11... | collective-permute-start | bytes 49160 | tf_op jit(solution)/shard_map/ppermute | solution.py:694
  58.7 4.5 %collective-permute-start.9 = (f32[32,128]{1,0:T(8,128)S(1)}, f32[32,128]{1,0:T(8,128)S(1)}, u32[]{:S(2)}, u32[]{:S(2)}) collective-permute-start(f32[32,128]{1,0:T(8,128)S(1)} %get-tuple-element.68), channel_id=1, source_target_pairs={{0,2},{1,3},{2,0},{3,1},{4,6},{5,7},{6,4},{7,5},{8,10},{9,11},{10,... | collective-permute-start | bytes 49160 | tf_op jit(solution)/shard_map/ppermute | solution.py:694
  60.2 4.7 %collective-permute-start.10 = (f32[32,128]{1,0:T(8,128)S(1)}, f32[32,128]{1,0:T(8,128)S(1)}, u32[]{:S(2)}, u32[]{:S(2)}) collective-permute-start(f32[32,128]{1,0:T(8,128)S(1)} %get-tuple-element.69), channel_id=1, source_target_pairs={{0,3},{1,2},{2,1},{3,0},{4,7},{5,6},{6,5},{7,4},{8,11},{9,10},{10,... | collective-permute-start | bytes 49160 | tf_op jit(solution)/shard_map/ppermute | solution.py:694
  64.9 7.4 %collective-permute-start.11 = (f32[32,128]{1,0:T(8,128)S(1)}, f32[32,128]{1,0:T(8,128)S(1)}, u32[]{:S(2)}, u32[]{:S(2)}) collective-permute-start(f32[32,128]{1,0:T(8,128)S(1)} %get-tuple-element.71), channel_id=1, source_target_pairs={{0,4},{1,5},{2,6},{3,7},{4,8},{5,9},{6,10},{7,11},{8,12},{9,13},{1... | collective-permute-start | bytes 49160 | tf_op jit(solution)/shard_map/ppermute | solution.py:694
  66.5 9.4 %collective-permute-start.12 = (f32[32,128]{1,0:T(8,128)S(1)}, f32[32,128]{1,0:T(8,128)S(1)}, u32[]{:S(2)}, u32[]{:S(2)}) collective-permute-start(f32[32,128]{1,0:T(8,128)S(1)} %get-tuple-element.72), channel_id=1, source_target_pairs={{0,8},{1,9},{2,10},{3,11},{4,12},{5,13},{6,14},{7,15},{8,0},{9,1},... | collective-permute-start | bytes 49160 | tf_op jit(solution)/shard_map/ppermute | solution.py:694
  69.0 7.0 %collective-permute-start.13 = (f32[32,128]{1,0:T(8,128)S(1)}, f32[32,128]{1,0:T(8,128)S(1)}, u32[]{:S(2)}, u32[]{:S(2)}) collective-permute-start(f32[32,128]{1,0:T(8,128)S(1)} %get-tuple-element.73), channel_id=1, source_target_pairs={{0,12},{1,13},{2,14},{3,15},{4,0},{5,1},{6,2},{7,3},{8,4},{9,5},{1... | collective-permute-start | bytes 49160 | tf_op jit(solution)/shard_map/ppermute | solution.py:694
  76.0 1.3 %collective-permute-start.14 = (f32[64,128]{1,0:T(8,128)S(1)}, f32[64,128]{1,0:T(8,128)S(1)}, u32[]{:S(2)}, u32[]{:S(2)}) collective-permute-start(f32[64,128]{1,0:T(8,128)S(1)} %get-tuple-element.75), channel_id=1, source_target_pairs={{0,16},{16,0},{1,17},{17,1},{2,18},{18,2},{3,19},{19,3},{4,20},{20... | collective-permute-start | bytes 98312 | tf_op jit(solution)/shard_map/ppermute | solution.py:694
  78.0 1.2 %collective-permute-start.15 = (f32[32,128]{1,0:T(8,128)S(1)}, f32[32,128]{1,0:T(8,128)S(1)}, u32[]{:S(2)}, u32[]{:S(2)}) collective-permute-start(f32[32,128]{1,0:T(8,128)S(1)} %get-tuple-element.79), channel_id=1, source_target_pairs={{0,16},{16,0},{1,17},{17,1},{2,18},{18,2},{3,19},{19,3},{4,20},{20... | collective-permute-start | bytes 49160 | tf_op jit(solution)/shard_map/ppermute | solution.py:694
  79.2 3.7 %collective-permute-start.16 = (f32[16,128]{1,0:T(8,128)S(1)}, f32[16,128]{1,0:T(8,128)S(1)}, u32[]{:S(2)}, u32[]{:S(2)}) collective-permute-start(f32[16,128]{1,0:T(8,128)S(1)} %get-tuple-element.81), channel_id=1, source_target_pairs={{0,1},{1,0},{2,3},{3,2},{4,5},{5,4},{6,7},{7,6},{8,9},{9,8},{10,11... | collective-permute-start | bytes 24584 | tf_op jit(solution)/shard_map/ppermute | solution.py:694
  80.8 3.7 %collective-permute-start.17 = (f32[16,128]{1,0:T(8,128)S(1)}, f32[16,128]{1,0:T(8,128)S(1)}, u32[]{:S(2)}, u32[]{:S(2)}) collective-permute-start(f32[16,128]{1,0:T(8,128)S(1)} %get-tuple-element.82), channel_id=1, source_target_pairs={{0,2},{1,3},{2,0},{3,1},{4,6},{5,7},{6,4},{7,5},{8,10},{9,11},{10,... | collective-permute-start | bytes 24584 | tf_op jit(solution)/shard_map/ppermute | solution.py:694
  82.2 4.5 %collective-permute-start.18 = (f32[16,128]{1,0:T(8,128)S(1)}, f32[16,128]{1,0:T(8,128)S(1)}, u32[]{:S(2)}, u32[]{:S(2)}) collective-permute-start(f32[16,128]{1,0:T(8,128)S(1)} %get-tuple-element.83), channel_id=1, source_target_pairs={{0,3},{1,2},{2,1},{3,0},{4,7},{5,6},{6,5},{7,4},{8,11},{9,10},{10,... | collective-permute-start | bytes 24584 | tf_op jit(solution)/shard_map/ppermute | solution.py:694
  86.8 5.5 %collective-permute-start.19 = (f32[16,128]{1,0:T(8,128)S(1)}, f32[16,128]{1,0:T(8,128)S(1)}, u32[]{:S(2)}, u32[]{:S(2)}) collective-permute-start(f32[16,128]{1,0:T(8,128)S(1)} %get-tuple-element.85), channel_id=1, source_target_pairs={{0,4},{1,5},{2,6},{3,7},{4,8},{5,9},{6,10},{7,11},{8,12},{9,13},{1... | collective-permute-start | bytes 24584 | tf_op jit(solution)/shard_map/ppermute | solution.py:694
  87.6 4.7 %collective-permute-start.20 = (f32[16,128]{1,0:T(8,128)S(1)}, f32[16,128]{1,0:T(8,128)S(1)}, u32[]{:S(2)}, u32[]{:S(2)}) collective-permute-start(f32[16,128]{1,0:T(8,128)S(1)} %get-tuple-element.86), channel_id=1, source_target_pairs={{0,8},{1,9},{2,10},{3,11},{4,12},{5,13},{6,14},{7,15},{8,0},{9,1},... | collective-permute-start | bytes 24584 | tf_op jit(solution)/shard_map/ppermute | solution.py:694
  89.1 3.8 %collective-permute-start.21 = (f32[16,128]{1,0:T(8,128)S(1)}, f32[16,128]{1,0:T(8,128)S(1)}, u32[]{:S(2)}, u32[]{:S(2)}) collective-permute-start(f32[16,128]{1,0:T(8,128)S(1)} %get-tuple-element.87), channel_id=1, source_target_pairs={{0,12},{1,13},{2,14},{3,15},{4,0},{5,1},{6,2},{7,3},{8,4},{9,5},{1... | collective-permute-start | bytes 24584 | tf_op jit(solution)/shard_map/ppermute | solution.py:694
